TPU v7x, 32 devices: a whole 2x2x4 slice. The times are simulated.
32 devices in a mesh: fsdp: 4 (over y, x), ctx: 8 (over z, core).
Axes of the slice: x: 2, y: 2, z: 4, core: 2. Of those that a mesh axis runs over, the one named last changes fastest.
Arguments:
- tokens: bfloat16 [4096, 2048], P(('fsdp', 'ctx')), may hold values from -6 to 6
- w_qkv: bfloat16 [2048, 6144], P(('fsdp', 'ctx')), may hold values from -0.125 to 0.125
- w_out: bfloat16 [2048, 2048], P(('fsdp', 'ctx')), may hold values from -1 to 1
- w_gate_up: bfloat16 [2048, 16384], P(('fsdp', 'ctx')), may hold values from -0.125 to 0.125
- w_down: bfloat16 [8192, 2048], P(('fsdp', 'ctx')), may hold values from -0.0625 to 0.0625
- seq_lengths: int32 [4, 2], P('fsdp'), may hold values from 1 to 768, 1024 in all within a row
- block_order: int32 [4, 8], P('fsdp'), may hold values from 0 to 7, as said below
- cotangent: bfloat16 [4096, 2048], P(('fsdp', 'ctx')), may hold values from -6 to 6
Outputs:
- layer_out: bfloat16 [4096, 2048], P(('fsdp', 'ctx'))
- tokens_grad: float32 [4096, 2048], P(('fsdp', 'ctx'))
- qkv_grad: float32 [2048, 6144], P(('fsdp', 'ctx'))
- out_grad: float32 [2048, 2048], P(('fsdp', 'ctx'))
- gate_up_grad: float32 [2048, 16384], P(('fsdp', 'ctx'))
- down_grad: float32 [8192, 2048], P(('fsdp', 'ctx'))
Inputs may be any that keep to these rules, and one draw needn't show every extreme that they name: `seq_lengths`: the lengths of each group sum to 1024, and none is longer than 768. `block_order`: each row names every block of its group exactly once.
All inputs are finite; a program needn't handle non-finite values.
Results may differ from a plain program's by a relative error of at most 0.018.
Values may be sent and summed in bfloat16 or wider, within the bound.
A program may use at most 704 MiB of HBM per device.

v0:
```python
import jax
import jax.numpy as jnp
from jax import lax
from jax.sharding import PartitionSpec as P

HEADS = 16
HEAD_DIM = 128
BLOCK = 128


def normalize(values):
    average = jnp.mean(values, axis=-1, keepdims=True)
    centered = values - average
    variance = jnp.mean(centered * centered, axis=-1, keepdims=True)
    inv_root = lax.rsqrt(variance + 1e-05)
    return (centered * inv_root, inv_root)


def norm_back(upstream, normed, inv_root):
    first_mean = jnp.mean(upstream, axis=-1, keepdims=True)
    second_mean = jnp.mean(upstream * normed, axis=-1, keepdims=True)
    return inv_root * (upstream - first_mean - normed * second_mean)


def places(token_index, lengths):
    seq_ends = jnp.cumsum(lengths)
    sequence = jnp.sum((token_index[:, None] >= seq_ends[None, :]).astype(jnp.int32), axis=1)
    before = jnp.arange(lengths.shape[0], dtype=jnp.int32)
    seq_start = jnp.sum(jnp.where(before[None, :] < sequence[:, None], lengths[None, :], 0), axis=1)
    return (sequence, token_index - seq_start)


def initial_index(row_index, order_row):
    slot_index = row_index // BLOCK
    slot_table = jnp.arange(order_row.shape[0], dtype=jnp.int32)
    picked = jnp.sum(
        jnp.where(slot_table[None, :] == slot_index[:, None], order_row[None, :], 0), axis=1
    )
    return picked * BLOCK + row_index % BLOCK


def angle_tables(position):
    half_dim = HEAD_DIM // 2
    frequency = 10000.0 ** (-jnp.arange(half_dim, dtype=jnp.float32) * 2.0 / HEAD_DIM)
    angle_table = position.astype(jnp.float32)[:, None] * frequency[None, :]
    angle_table = jnp.concatenate([angle_table, angle_table], axis=-1)
    return (jnp.cos(angle_table)[:, None, :], jnp.sin(angle_table)[:, None, :])


def rotate(values, cosine_table, sine_table):
    half_dim = values.shape[-1] // 2
    turned = jnp.concatenate([-values[..., half_dim:], values[..., :half_dim]], axis=-1)
    return values * cosine_table + turned * sine_table


def unrotate(values, cosine_table, sine_table):
    half_dim = values.shape[-1] // 2
    scaled = values * sine_table
    turned = jnp.concatenate([scaled[..., half_dim:], -scaled[..., :half_dim]], axis=-1)
    return values * cosine_table + turned


def times_transposed(left, right):
    return lax.dot_general(
        left, right, (((1,), (1,)), ((), ())), preferred_element_type=jnp.float32
    )


def column_product(left, right):
    return lax.dot_general(
        left, right, (((0,), (0,)), ((), ())), preferred_element_type=jnp.float32
    )


def column_terms(left, right):
    return column_product(left, right)


def gather_all(first, second):
    return (
        lax.all_gather(first, ("fsdp", "ctx"), axis=0, tiled=True),
        lax.all_gather(second, ("fsdp", "ctx"), axis=0, tiled=True),
    )


def scatter_rows(term_fn, rows):
    return lax.psum_scatter(
        term_fn(jnp.int32(0), rows * lax.axis_size(("fsdp", "ctx"))),
        ("fsdp", "ctx"),
        scatter_dimension=0,
        tiled=True,
    )


def rows_plan(tokens, w_qkv, w_out, w_gate_up, w_down, lengths, order_row, cotangent):
    row_count = tokens.shape[0]
    model_width = tokens.shape[1]
    ff_width = w_gate_up.shape[1] // 2
    score_scale = HEAD_DIM ** (-0.5)
    local_index = lax.axis_index("ctx") * row_count + jnp.arange(row_count, dtype=jnp.int32)
    query_seq, query_pos = places(initial_index(local_index, order_row), lengths)
    cosine_table, sine_table = angle_tables(query_pos)

    def allowed_pairs(length):
        key_index = initial_index(jnp.arange(length, dtype=jnp.int32), order_row)
        key_seq, key_pos = places(key_index, lengths)
        same = (query_seq[:, None] == key_seq[None, :]) & (key_pos[None, :] <= query_pos[:, None])
        return same[None]

    inputs = tokens.astype(jnp.float32)
    normed_in, root_in = normalize(inputs)
    normed_in_low = normed_in.astype(jnp.bfloat16)
    qkv_full, out_full = gather_all(w_qkv, w_out)
    qkv = jnp.dot(normed_in_low, qkv_full, preferred_element_type=jnp.float32)
    head_shape = (row_count, HEADS, HEAD_DIM)
    queries = rotate(qkv[:, :model_width].reshape(head_shape), cosine_table, sine_table).astype(
        jnp.bfloat16
    )
    key_rows = rotate(
        qkv[:, model_width : 2 * model_width].reshape(head_shape), cosine_table, sine_table
    )
    key_rows = key_rows.astype(jnp.bfloat16).reshape(row_count, model_width)
    value_rows = qkv[:, 2 * model_width :].astype(jnp.bfloat16)
    row_max = jnp.full((HEADS, row_count), -1e30, jnp.float32)
    key_piece = lax.all_gather(key_rows, "ctx", axis=0, tiled=True)
    value_piece = lax.all_gather(value_rows, "ctx", axis=0, tiled=True)
    length = key_piece.shape[0]
    allowed = allowed_pairs(length)
    key_heads = key_piece.reshape(length, HEADS, HEAD_DIM)
    value_heads = value_piece.reshape(length, HEADS, HEAD_DIM)
    scores = (
        jnp.einsum("qhd,khd->hqk", queries, key_heads, preferred_element_type=jnp.float32)
        * score_scale
    )
    scores = jnp.where(allowed, scores, -1e30)
    new_max = jnp.maximum(row_max, jnp.max(scores, axis=-1))
    weights = jnp.where(allowed, jnp.exp(scores - new_max[..., None]), 0.0)
    row_total = jnp.sum(weights, axis=-1)
    block_mix = jnp.einsum(
        "hqk,khd->qhd",
        weights.astype(jnp.bfloat16),
        value_heads,
        preferred_element_type=jnp.float32,
    )
    accumulated = block_mix
    row_max, row_total, accumulated = (new_max, row_total, accumulated)
    log_total = row_max + jnp.log(row_total)
    attn_heads = accumulated / jnp.transpose(row_total)[..., None]
    mix_low = attn_heads.reshape(row_count, model_width).astype(jnp.bfloat16)
    residual = inputs + jnp.dot(mix_low, out_full, preferred_element_type=jnp.float32)
    normed_mid, root_mid = normalize(residual)
    normed_mid_low = normed_mid.astype(jnp.bfloat16)
    gate_up_full, down_full = gather_all(w_gate_up, w_down)
    gate_up = jnp.dot(normed_mid_low, gate_up_full, preferred_element_type=jnp.float32)
    gate_part = gate_up[:, :ff_width]
    up_part = gate_up[:, ff_width:]
    sigmoid_gate = jax.nn.sigmoid(gate_part)
    silu_gate = gate_part * sigmoid_gate
    activated = (silu_gate * up_part).astype(jnp.bfloat16)
    layer_out = (
        residual + jnp.dot(activated, down_full, preferred_element_type=jnp.float32)
    ).astype(jnp.bfloat16)

    def down_terms(offset, length):
        return column_terms(activated, cotangent)

    down_grad = scatter_rows(down_terms, w_down.shape[0])
    gate_up_back_w, down_back_w = gather_all(w_gate_up, w_down)
    act_grad = times_transposed(cotangent, down_back_w)
    gate_grad = act_grad * up_part * sigmoid_gate * (1.0 + gate_part * (1.0 - sigmoid_gate))
    up_grad = act_grad * silu_gate
    gate_up_back = jnp.concatenate([gate_grad, up_grad], axis=1).astype(jnp.bfloat16)
    mid_back = times_transposed(gate_up_back, gate_up_back_w)
    residual_back = cotangent.astype(jnp.float32) + norm_back(mid_back, normed_mid, root_mid)
    proj_back = residual_back.astype(jnp.bfloat16)
    qkv_back_w, out_back_w = gather_all(w_qkv, w_out)
    mix_back = times_transposed(proj_back, out_back_w).astype(jnp.bfloat16)
    mix_back_heads = mix_back.reshape(head_shape)
    delta = jnp.einsum("qhd,qhd->hq", mix_back_heads.astype(jnp.float32), attn_heads)
    key_piece = lax.all_gather(key_rows, "ctx", axis=0, tiled=True)
    value_piece = lax.all_gather(value_rows, "ctx", axis=0, tiled=True)
    length = key_piece.shape[0]
    allowed = allowed_pairs(length)
    key_heads = key_piece.reshape(length, HEADS, HEAD_DIM)
    value_heads = value_piece.reshape(length, HEADS, HEAD_DIM)
    scores = (
        jnp.einsum("qhd,khd->hqk", queries, key_heads, preferred_element_type=jnp.float32)
        * score_scale
    )
    probs = jnp.where(allowed, jnp.exp(scores - log_total[..., None]), 0.0)
    value_part = jnp.einsum(
        "hqk,qhd->khd",
        probs.astype(jnp.bfloat16),
        mix_back_heads,
        preferred_element_type=jnp.float32,
    )
    prob_back = jnp.einsum(
        "qhd,khd->hqk", mix_back_heads, value_heads, preferred_element_type=jnp.float32
    )
    score_back = (score_scale * probs * (prob_back - delta[..., None])).astype(jnp.bfloat16)
    query_grad = jnp.einsum(
        "hqk,khd->qhd", score_back, key_heads, preferred_element_type=jnp.float32
    )
    key_part = jnp.einsum("hqk,qhd->khd", score_back, queries, preferred_element_type=jnp.float32)
    key_grads = key_part.reshape(length, model_width)
    value_grads = value_part.reshape(length, model_width)
    query_grad, key_grads, value_grads = (query_grad, key_grads, value_grads)
    key_back, value_back = (
        lax.psum_scatter(
            key_grads.astype(jnp.bfloat16), "ctx", scatter_dimension=0, tiled=True
        ).astype(jnp.float32),
        lax.psum_scatter(
            value_grads.astype(jnp.bfloat16), "ctx", scatter_dimension=0, tiled=True
        ).astype(jnp.float32),
    )
    query_back = unrotate(query_grad, cosine_table, sine_table).reshape(row_count, model_width)
    key_back = unrotate(key_back.reshape(head_shape), cosine_table, sine_table).reshape(
        row_count, model_width
    )
    qkv_back = jnp.concatenate([query_back, key_back, value_back], axis=1).astype(jnp.bfloat16)
    in_back = times_transposed(qkv_back, qkv_back_w)
    tokens_grad = residual_back + norm_back(in_back, normed_in, root_in)

    def row_terms(offset, length):
        return jnp.concatenate(
            [
                column_terms(normed_in_low, qkv_back),
                column_terms(mix_low, proj_back),
                column_terms(normed_mid_low, gate_up_back),
            ],
            axis=1,
        )

    row_grads = scatter_rows(row_terms, w_out.shape[0])
    qkv_grad = row_grads[:, : 3 * model_width]
    out_grad = row_grads[:, 3 * model_width : 4 * model_width]
    gate_up_grad = row_grads[:, 4 * model_width :]
    return (layer_out, tokens_grad, qkv_grad, out_grad, gate_up_grad, down_grad)


def per_device(tokens, w_qkv, w_out, w_gate_up, w_down, seq_lengths, block_order, cotangent):
    lengths = seq_lengths[0]
    order_row = block_order[0]
    return rows_plan(tokens, w_qkv, w_out, w_gate_up, w_down, lengths, order_row, cotangent)


def solution(mesh):
    in_specs = (
        P(("fsdp", "ctx"), None),
        P(("fsdp", "ctx"), None),
        P(("fsdp", "ctx"), None),
        P(("fsdp", "ctx"), None),
        P(("fsdp", "ctx"), None),
        P("fsdp", None),
        P("fsdp", None),
        P(("fsdp", "ctx"), None),
    )
    out_specs = (
        P(("fsdp", "ctx"), None),
        P(("fsdp", "ctx"), None),
        P(("fsdp", "ctx"), None),
        P(("fsdp", "ctx"), None),
        P(("fsdp", "ctx"), None),
        P(("fsdp", "ctx"), None),
    )
    return jax.shard_map(
        per_device, mesh=mesh, in_specs=in_specs, out_specs=out_specs, check_vma=False
    )
```

profile of v0, /device:TPU:9, one launch (start us, length us, event | category | flops | bytes accessed | tf_op | source)
XLA Modules:
  0.0 3555.3 jit_solution(6140398392184267996)
XLA Ops:
  11.7 153.3 %all-gather.7.cloned.1.call-done = bf16[2048,6144]{1,0:T(8,128)(2,1)} async-done(((bf16[64,6144]{1,0:T(8,128)(2,1)}), bf16[2048,6144]{1,0:T(8,128)(2,1)}) %all-gather.7.cloned.1.call-update) | async-done | bytes 25165840 | tf_op jit(solution)/shard_map/all_gather | solution.py:81
  165.0 10.1 fusion.86
  189.1 40.4 %all-gather.11.cloned.1.call-done = bf16[1024,2048]{1,0:T(8,128)(2,1)} async-done(((bf16[128,2048]{1,0:T(8,128)(2,1)}), bf16[1024,2048]{1,0:T(8,128)(2,1)}) %all-gather.11.cloned.1.call-update) | async-done | bytes 4194320 | tf_op jit(solution)/shard_map/all_gather | solution.py:125
  245.8 31.6 all-gather.9.cloned.1.call-done
  277.4 8.6 fusion.96
  285.9 71.5 %all-gather.13.cloned.1.call-done = bf16[2048,2048]{1,0:T(8,128)(2,1)} async-done(((bf16[64,2048]{1,0:T(8,128)(2,1)}), bf16[2048,2048]{1,0:T(8,128)(2,1)}) %all-gather.13.cloned.1.call-update) | async-done | bytes 8388624 | tf_op jit(solution)/shard_map/all_gather | solution.py:82
  362.4 350.3 %all-gather.15.cloned.1.call-done = bf16[2048,16384]{1,0:T(8,128)(2,1)} async-done(((bf16[64,16384]{1,0:T(8,128)(2,1)}), bf16[2048,16384]{1,0:T(8,128)(2,1)}) %all-gather.15.cloned.1.call-update) | async-done | bytes 67108880 | tf_op jit(solution)/shard_map/all_gather | solution.py:81
  712.7 27.2 fusion.89
  740.0 168.0 %all-gather.17.cloned.1.call-done = bf16[8192,2048]{1,0:T(8,128)(2,1)} async-done(((bf16[256,2048]{1,0:T(8,128)(2,1)}), bf16[8192,2048]{1,0:T(8,128)(2,1)}) %all-gather.17.cloned.1.call-update) | async-done | bytes 33554448 | tf_op jit(solution)/shard_map/all_gather | solution.py:82
  907.9 21.4 multiply_convert_fusion.2
  929.3 29.8 fusion.92
  976.2 8.4 multiply_convert_fusion
  995.5 7.7 fusion.26
  1003.2 6.7 copy.68
  1009.9 8.1 fusion.57
  1018.1 47.2 %fusion.24 = f32[2048,16384]{1,0:T(8,128)} fusion(bf16[128,8192]{1,0:T(8,128)(2,1)} %get-tuple-element.13, bf16[128,8192]{1,0:T(8,128)(2,1)} %get-tuple-element.12, f32[128,2048]{1,0:T(8,128)S(1)} %get-tuple-element.34, f32[128]{0:T(128)S(1)} %add_rsqrt_fusion, f32[128]{0:T(128)S(1)} %broadcast_multiply_fusion.7), kind=kOutput, calls=%fused_computation.30 | convolution fusion | flops 8599109632 | bytes 139461632 | tf_op jit(solution)/shard_map/dot_general | solution.py:70
  1078.7 15.0 reduce-scatter.7.cloned.1.call-done
  1093.7 20.6 fusion.55
  1114.3 130.6 %pad_maximum_fusion = f32[2048,24576]{1,0:T(8,128)} fusion(f32[2048,16384]{1,0:T(8,128)} %fusion.24, f32[2048,2048]{1,0:T(8,128)} %fusion.57, f32[2048,6144]{1,0:T(8,128)} %fusion.55), kind=kLoop, calls=%fused_computation | loop fusion | flops 100663296 | bytes 402653184 | tf_op jit(solution)/shard_map/concatenate | solution.py:225
  1246.6 38.4 %fusion.98 = f32[8192,2048]{1,0:T(8,128)} fusion(bf16[128,8192]{1,0:T(8,128)(2,1)S(1)} %copy-done.9, bf16[128,2048]{1,0:T(8,128)(2,1)S(1)} %copy-done.16), kind=kOutput, calls=%fused_computation.149 | convolution fusion | flops 4294967296 | bytes 69730304 | tf_op jit(solution)/shard_map/dot_general | solution.py:70
  1286.5 23.7 fusion.29
  1310.2 19.0 fusion.91
  1331.9 1508.3 %reduce-scatter.9.cloned.1.call-done = f32[64,24576]{1,0:T(8,128)} async-done(((f32[2048,24576]{1,0:T(8,128)}), f32[64,24576]{1,0:T(8,128)}) %reduce-scatter.9.cloned.1.call-update) | async-done | bytes 6291472 | tf_op jit(solution)/shard_map/reduce_scatter | solution.py:87
  2849.4 698.8 %reduce-scatter.11.cloned.1.call-done = f32[256,2048]{1,0:T(8,128)} async-done(((f32[8192,2048]{1,0:T(8,128)}), f32[256,2048]{1,0:T(8,128)}) %reduce-scatter.11.cloned.1.call-update) | async-done | bytes 2097168 | tf_op jit(solution)/shard_map/reduce_scatter | solution.py:87
  (156 shorter events, 95.8 us)
Async XLA Ops:
  7.2 157.8 %all-gather.7.cloned.1.call-start = ((), (), s32[]{:S(2)}) async-start(), calls=%async_computation.4 | async-start | bytes 25952256 | tf_op jit(solution)/shard_map/all_gather | solution.py:81
  7.9 221.6 %all-gather.11.cloned.1.call-start = ((), (), s32[]{:S(2)}) async-start(), calls=%async_computation.6 | async-start | bytes 4718592 | tf_op jit(solution)/shard_map/all_gather | solution.py:125
  10.7 178.2 %copy-start.21 = (f32[128,128]{0,1:T(8,128)}, f32[128,128]{0,1:T(8,128)S(1)}, u32[]{:S(2)}) copy-start(f32[128,128]{0,1:T(8,128)S(1)} %get-tuple-element.28) | copy-start | bytes 196612
  10.7 178.2 %copy-start.23 = (f32[128,128]{0,1:T(8,128)}, f32[128,128]{0,1:T(8,128)S(1)}, u32[]{:S(2)}) copy-start(f32[128,128]{0,1:T(8,128)S(1)} %get-tuple-element.27) | copy-start | bytes 196612
  11.2 169.7 %copy-start.10 = (f32[128,2048]{1,0:T(8,128)}, f32[128,2048]{1,0:T(8,128)S(1)}, u32[]{:S(2)}) copy-start(f32[128,2048]{1,0:T(8,128)S(1)} %copy.62) | copy-start | bytes 3145732
  11.4 163.7 %copy-start.26 = (f32[128]{0:T(128)}, f32[128]{0:T(128)S(1)}, u32[]{:S(2)}) copy-start(f32[128]{0:T(128)S(1)} %broadcast_multiply_fusion.8) | copy-start | bytes 1540
  11.7 163.4 %copy-start.29 = (f32[128]{0:T(128)}, f32[128]{0:T(128)S(1)}, u32[]{:S(2)}) copy-start(f32[128]{0:T(128)S(1)} %add_rsqrt_fusion.1) | copy-start | bytes 1540
  183.8 93.5 %all-gather.9.cloned.1.call-start = ((), (), s32[]{:S(2)}) async-start(), calls=%async_computation.5 | async-start | bytes 4718592 | tf_op jit(solution)/shard_map/all_gather | solution.py:126
  186.0 171.4 %all-gather.13.cloned.1.call-start = ((), (), s32[]{:S(2)}) async-start(), calls=%async_computation.7 | async-start | bytes 8650752 | tf_op jit(solution)/shard_map/all_gather | solution.py:82
  186.6 526.2 %all-gather.15.cloned.1.call-start = ((), (), s32[]{:S(2)}) async-start(), calls=%async_computation.8 | async-start | bytes 69206016 | tf_op jit(solution)/shard_map/all_gather | solution.py:81
  187.1 720.8 %all-gather.17.cloned.1.call-start = ((), (), s32[]{:S(2)}) async-start(), calls=%async_computation.9 | async-start | bytes 34603008 | tf_op jit(solution)/shard_map/all_gather | solution.py:82
  187.7 877.6 %reduce-scatter.5.cloned.1.call-start = ((), (), s32[]{:S(2)}) async-start(), calls=%async_computation.10 | async-start | bytes 4718592 | tf_op jit(solution)/shard_map/reduce_scatter | solution.py:209
  285.9 76.2 %copy-start.13 = (bf16[128,16,128]{0,2,1:T(8,128)(2,1)}, bf16[128,16,128]{0,2,1:T(8,128)(2,1)S(1)}, u32[]{:S(2)}) copy-start(bf16[128,16,128]{0,2,1:T(8,128)(2,1)S(1)} %get-tuple-element.31) | copy-start | bytes 1572868
  362.1 656.0 %copy-start.1 = (f32[128,2048]{1,0:T(8,128)}, f32[128,2048]{1,0:T(8,128)S(1)}, u32[]{:S(2)}) copy-start(f32[128,2048]{1,0:T(8,128)S(1)} %get-tuple-element.34) | copy-start | bytes 3145732
  362.4 545.5 %copy-start.15 = (bf16[128,2048]{1,0:T(8,128)(2,1)S(1)}, bf16[128,2048]{1,0:T(8,128)(2,1)}, u32[]{:S(2)}) copy-start(bf16[128,2048]{1,0:T(8,128)(2,1)} %param.15) | copy-start | bytes 1572868
  961.0 48.9 %copy-start.5 = (f32[128,2048]{1,0:T(8,128)}, f32[128,2048]{1,0:T(8,128)S(1)}, u32[]{:S(2)}) copy-start(f32[128,2048]{1,0:T(8,128)S(1)} %multiply_add_fusion) | copy-start | bytes 3145732
  994.5 99.2 %reduce-scatter.7.cloned.1.call-start = ((), (), s32[]{:S(2)}) async-start(), calls=%async_computation.11 | async-start | bytes 4718592 | tf_op jit(solution)/shard_map/reduce_scatter | solution.py:212
  1018.0 48.5 %copy-start.22 = (f32[128,128]{0,1:T(8,128)S(1)}, f32[128,128]{0,1:T(8,128)}, u32[]{:S(2)}) copy-start(f32[128,128]{0,1:T(8,128)} %copy-done.21) | copy-start | bytes 196612
  1018.0 1822.2 %reduce-scatter.9.cloned.1.call-start = ((), (), s32[]{:S(2)}) async-start(), calls=%async_computation.12 | async-start | bytes 207618048 | tf_op jit(solution)/shard_map/reduce_scatter | solution.py:87
  1245.0 2303.2 %reduce-scatter.11.cloned.1.call-start = ((), (), s32[]{:S(2)}) async-start(), calls=%async_computation.13 | async-start | bytes 69206016 | tf_op jit(solution)/shard_map/reduce_scatter | solution.py:87
  1286.5 23.7 copy-start.19
  1286.5 23.7 copy-start.25
  1286.5 23.7 copy-start.28
  1286.5 23.7 copy-start.31
  (20 other events, 168.7 us)
Sparse Core Ops, SparseCore 0:
  11.0 153.9 all-gather.6
  183.9 45.4 all-gather.10
  231.6 45.6 all-gather.8
  280.2 77.1 all-gather.12
  360.2 352.4 all-gather.14
  715.5 192.3 all-gather.16
  994.6 48.2 reduce-scatter.4
  1045.2 48.3 reduce-scatter.6
  1245.1 1595.0 reduce-scatter.8
  2843.0 705.2 reduce-scatter.10
where the time goes:
time: 3560 us
  waiting for transfers between devices  3040 us (85%)
  matrix products  294 us (8%)
  other arithmetic  152 us (4%)
  local copies, waits for them, and re-layouts  54.4 us (2%)
    reduce_scatter x2, waiting for transfers between devices, scatter_rows(): lax.psum_scatter(term_fn(jnp.int32(0), rows * lax.axis_size(('fsdp', 'ctx...  2210 us
    all_gather x2, waiting for transfers between devices, gather_all(): lax.all_gather(first, ('fsdp', 'ctx'), axis=0, tiled=True)  504 us
    all_gather x2, waiting for transfers between devices, gather_all(): lax.all_gather(second, ('fsdp', 'ctx'), axis=0, tiled=True)  239 us
    concatenate x1, other arithmetic, row_terms(): jnp.concatenate([column_terms(normed_in_low, qkv_back), column_terms(mix_...  131 us
    dot_general x4, matrix products, column_product(): lax.dot_general(left, right, (((0,), (0,)), ((), ())), preferred_element_...  114 us
    dot_general x4, matrix products, times_transposed(): lax.dot_general(left, right, (((1,), (1,)), ((), ())), preferred_element_...  76.9 us
  transfers between devices with their start and end apart: 10, of which 9 were waited for; matrix products, arithmetic and copies ran while one was open for 7% of the time, Pallas kernels for 0%

commit v1 on v0

v1 whole, which is shorter than its diff:
```python
import jax
import jax.numpy as jnp
from jax import lax
from jax.sharding import PartitionSpec as P

HEADS = 16
HEAD_DIM = 128
BLOCK = 128


def normalize(values):
    average = jnp.mean(values, axis=-1, keepdims=True)
    centered = values - average
    variance = jnp.mean(centered * centered, axis=-1, keepdims=True)
    inv_root = lax.rsqrt(variance + 1e-05)
    return (centered * inv_root, inv_root)


def norm_back(upstream, normed, inv_root):
    first_mean = jnp.mean(upstream, axis=-1, keepdims=True)
    second_mean = jnp.mean(upstream * normed, axis=-1, keepdims=True)
    return inv_root * (upstream - first_mean - normed * second_mean)


def places(token_index, lengths):
    seq_ends = jnp.cumsum(lengths)
    sequence = jnp.sum((token_index[:, None] >= seq_ends[None, :]).astype(jnp.int32), axis=1)
    before = jnp.arange(lengths.shape[0], dtype=jnp.int32)
    seq_start = jnp.sum(jnp.where(before[None, :] < sequence[:, None], lengths[None, :], 0), axis=1)
    return (sequence, token_index - seq_start)


def initial_index(row_index, order_row):
    slot_index = row_index // BLOCK
    slot_table = jnp.arange(order_row.shape[0], dtype=jnp.int32)
    picked = jnp.sum(
        jnp.where(slot_table[None, :] == slot_index[:, None], order_row[None, :], 0), axis=1
    )
    return picked * BLOCK + row_index % BLOCK


def angle_tables(position):
    half_dim = HEAD_DIM // 2
    frequency = 10000.0 ** (-jnp.arange(half_dim, dtype=jnp.float32) * 2.0 / HEAD_DIM)
    angle_table = position.astype(jnp.float32)[:, None] * frequency[None, :]
    angle_table = jnp.concatenate([angle_table, angle_table], axis=-1)
    return (jnp.cos(angle_table)[:, None, :], jnp.sin(angle_table)[:, None, :])


def rotate(values, cosine_table, sine_table):
    half_dim = values.shape[-1] // 2
    turned = jnp.concatenate([-values[..., half_dim:], values[..., :half_dim]], axis=-1)
    return values * cosine_table + turned * sine_table


def unrotate(values, cosine_table, sine_table):
    half_dim = values.shape[-1] // 2
    scaled = values * sine_table
    turned = jnp.concatenate([scaled[..., half_dim:], -scaled[..., :half_dim]], axis=-1)
    return values * cosine_table + turned


def dot(left, right):
    return jnp.dot(left, right, preferred_element_type=jnp.float32)


def times_transposed(left, right):
    return lax.dot_general(
        left, right, (((1,), (1,)), ((), ())), preferred_element_type=jnp.float32
    )


def column_product(left, right):
    return lax.dot_general(
        left, right, (((0,), (0,)), ((), ())), preferred_element_type=jnp.float32
    )


def gather(values, axes):
    return lax.all_gather(values, axes, axis=0, tiled=True)


def scatter(values, axes):
    return lax.psum_scatter(values, axes, scatter_dimension=0, tiled=True)


def spread_columns(weight, outer, parts):
    rows, columns = weight.shape
    inner = columns // (outer * parts)
    pieces = weight.reshape(rows, outer, parts, inner).transpose(2, 0, 1, 3)
    pieces = lax.all_to_all(pieces, "ctx", split_axis=0, concat_axis=0, tiled=True)
    return pieces.reshape(parts * rows, outer * inner)


def collect_rows(grad, outer, parts):
    rows, columns = grad.shape
    inner = columns // outer
    pieces = grad.reshape(parts, rows // parts, columns)
    pieces = lax.all_to_all(pieces, "ctx", split_axis=0, concat_axis=0, tiled=True)
    pieces = pieces.reshape(parts, rows // parts, outer, inner).transpose(1, 2, 0, 3)
    return pieces.reshape(rows // parts, outer * parts * inner).astype(jnp.float32)


def per_device(tokens, w_qkv, w_out, w_gate_up, w_down, seq_lengths, block_order, cotangent):
    lengths = seq_lengths[0]
    order_row = block_order[0]
    parts = lax.axis_size("ctx")
    groups = lax.axis_size("fsdp")
    rows, width = tokens.shape
    length = rows * parts
    heads = HEADS // parts
    head_width = heads * HEAD_DIM
    low = jnp.bfloat16
    score_scale = HEAD_DIM ** (-0.5)

    qkv_cols = gather(spread_columns(w_qkv, 3, parts), "fsdp")
    out_full = gather(w_out, ("fsdp", "ctx"))
    gate_up_cols = gather(spread_columns(w_gate_up, 2 * groups, parts), "fsdp")
    down_rows = gather(w_down, "fsdp")
    cot_full = gather(cotangent, "ctx")

    inputs = tokens.astype(jnp.float32)
    normed_in, root_in = normalize(inputs)
    normed_in_full = gather(normed_in.astype(low), "ctx")

    row_index = jnp.arange(length, dtype=jnp.int32)
    seq, pos = places(initial_index(row_index, order_row), lengths)
    cosine_table, sine_table = angle_tables(pos)
    allowed = ((seq[:, None] == seq[None, :]) & (pos[None, :] <= pos[:, None]))[None]

    qkv = dot(normed_in_full, qkv_cols)
    head_shape = (length, heads, HEAD_DIM)
    queries = rotate(qkv[:, :head_width].reshape(head_shape), cosine_table, sine_table).astype(low)
    keys = rotate(
        qkv[:, head_width : 2 * head_width].reshape(head_shape), cosine_table, sine_table
    ).astype(low)
    values = qkv[:, 2 * head_width :].astype(low).reshape(head_shape)
    scores = jnp.einsum("qhd,khd->hqk", queries, keys, preferred_element_type=jnp.float32)
    scores = jnp.where(allowed, scores * score_scale, -1e30)
    row_max = jnp.max(scores, axis=-1)
    weights = jnp.where(allowed, jnp.exp(scores - row_max[..., None]), 0.0)
    row_total = jnp.sum(weights, axis=-1)
    mixed = jnp.einsum("hqk,khd->qhd", weights.astype(low), values, preferred_element_type=jnp.float32)
    log_total = row_max + jnp.log(row_total)
    attn_heads = mixed / jnp.transpose(row_total)[..., None]

    mix_pieces = attn_heads.astype(low).reshape(parts, rows, head_width)
    mix_pieces = lax.all_to_all(mix_pieces, "ctx", split_axis=0, concat_axis=0, tiled=True)
    mix_low = mix_pieces.transpose(1, 0, 2).reshape(rows, width)
    residual = inputs + dot(mix_low, out_full)
    normed_mid, root_mid = normalize(residual)
    normed_mid_full = gather(normed_mid.astype(low), "ctx")

    gate_up = dot(normed_mid_full, gate_up_cols)
    units = gate_up.shape[1] // 2
    gate_part = gate_up[:, :units]
    up_part = gate_up[:, units:]
    sigmoid_gate = jax.nn.sigmoid(gate_part)
    silu_gate = gate_part * sigmoid_gate
    activated = (silu_gate * up_part).astype(low)
    down_out = scatter(dot(activated, down_rows).astype(low), "ctx")
    layer_out = (residual + down_out.astype(jnp.float32)).astype(low)

    down_grad = scatter(column_product(activated, cot_full).astype(low), "fsdp").astype(jnp.float32)

    act_grad = times_transposed(cot_full, down_rows)
    gate_grad = act_grad * up_part * sigmoid_gate * (1.0 + gate_part * (1.0 - sigmoid_gate))
    up_grad = act_grad * silu_gate
    gate_up_back = jnp.concatenate([gate_grad, up_grad], axis=1).astype(low)
    mid_back = scatter(times_transposed(gate_up_back, gate_up_cols).astype(low), "ctx")
    gate_up_grad = scatter(column_product(normed_mid_full, gate_up_back).astype(low), "fsdp")

    residual_back = cotangent.astype(jnp.float32) + norm_back(
        mid_back.astype(jnp.float32), normed_mid, root_mid
    )
    proj_back = residual_back.astype(low)
    mix_back = times_transposed(proj_back, out_full).astype(low)
    out_grad = scatter(column_product(mix_low, proj_back).astype(low), ("fsdp", "ctx"))

    back_pieces = mix_back.reshape(rows, parts, head_width).transpose(1, 0, 2)
    back_pieces = lax.all_to_all(back_pieces, "ctx", split_axis=0, concat_axis=0, tiled=True)
    back_heads = back_pieces.reshape(head_shape)

    delta = jnp.einsum("qhd,qhd->hq", back_heads.astype(jnp.float32), attn_heads)
    probs = jnp.where(allowed, jnp.exp(scores - log_total[..., None]), 0.0)
    value_back = jnp.einsum(
        "hqk,qhd->khd", probs.astype(low), back_heads, preferred_element_type=jnp.float32
    )
    prob_back = jnp.einsum("qhd,khd->hqk", back_heads, values, preferred_element_type=jnp.float32)
    score_back = (score_scale * probs * (prob_back - delta[..., None])).astype(low)
    query_back = jnp.einsum("hqk,khd->qhd", score_back, keys, preferred_element_type=jnp.float32)
    key_back = jnp.einsum("hqk,qhd->khd", score_back, queries, preferred_element_type=jnp.float32)
    qkv_back = jnp.concatenate(
        [
            unrotate(query_back, cosine_table, sine_table).reshape(length, head_width),
            unrotate(key_back, cosine_table, sine_table).reshape(length, head_width),
            value_back.reshape(length, head_width),
        ],
        axis=1,
    ).astype(low)
    in_back = scatter(times_transposed(qkv_back, qkv_cols).astype(low), "ctx")
    tokens_grad = residual_back + norm_back(in_back.astype(jnp.float32), normed_in, root_in)
    qkv_grad = scatter(column_product(normed_in_full, qkv_back).astype(low), "fsdp")

    return (
        layer_out,
        tokens_grad,
        collect_rows(qkv_grad, 3, parts),
        out_grad.astype(jnp.float32),
        collect_rows(gate_up_grad, 2 * groups, parts),
        down_grad,
    )


def solution(mesh):
    both = P(("fsdp", "ctx"), None)
    one = P("fsdp", None)
    return jax.shard_map(
        per_device,
        mesh=mesh,
        in_specs=(both, both, both, both, both, one, one, both),
        out_specs=(both,) * 6,
        check_vma=False,
    )
```

time: 3560 us -> 1040 us (0.29)
  waiting for transfers between devices: 3040 us -> 711 us
  matrix products: 294 us -> 130 us
  other arithmetic: 152 us -> 24.4 us
  blocking collectives: 0 us -> 96.3 us
    reduce_scatter x4 -> x7, waiting for transfers between devices: 2220 us -> 406 us  [scatter(): return lax.psum_scatter(values, axes, scatter_dimension=0, tiled=True)]
    all_gather x6 -> x7, waiting for transfers between devices: 815 us -> 291 us  [gather(): return lax.all_gather(values, axes, axis=0, tiled=True)]
    concatenate x2 -> x0, other arithmetic: 132 us -> none  [the longest x1 131 us: row_terms(): jnp.concatenate([column_terms(normed_in_low, qkv_back), column_terms(mix_...]
    all_to_all x0 -> x3, blocking collectives: none -> 96.3 us  [the longest x2 75 us: spread_columns(): lax.all_to_all(pieces, 'ctx', split_axis=0, concat_axis=0, tiled=True)]
    dot_general x4, matrix products: 114 us -> 34 us  [column_product(): lax.dot_general(left, right, (((0,), (0,)), ((), ())), preferred_element_...]
    dot_general x10, matrix products: 103 us -> 55.7 us  [the longest x4 34.8 us: dot(): return jnp.dot(left, right, preferred_element_type=jnp.float32)]
    dot_general x4, matrix products: 76.9 us -> 40.3 us  [times_transposed(): lax.dot_general(left, right, (((1,), (1,)), ((), ())), preferred_element_...]
  transfers between devices with their start and end apart: 10 -> 17, of which waited for: 9 -> 14; matrix products, arithmetic and copies ran while one was open for 7% -> 11% of each run, Pallas kernels for 0% -> 0%
where the time goes in v1:
time: 1040 us; the launch traced here: 1030 us
  waiting for transfers between devices  711 us (68%)
  matrix products  130 us (12%)
  blocking collectives  96.3 us (9%)
  local copies, waits for them, and re-layouts  33.2 us (3%)
  other arithmetic  24.4 us (2%)
  starting transfers between devices  19.7 us (2%)
  between operations  14.7 us (1%)
    reduce_scatter x7, waiting for transfers between devices, scatter(): return lax.psum_scatter(values, axes, scatter_dimension=0, tiled=True)  406 us
    all_gather x7, waiting for transfers between devices, gather(): return lax.all_gather(values, axes, axis=0, tiled=True)  291 us
    all_to_all x2, blocking collectives, spread_columns(): lax.all_to_all(pieces, 'ctx', split_axis=0, concat_axis=0, tiled=True)  75 us
    dot_general x4, matrix products, times_transposed(): lax.dot_general(left, right, (((1,), (1,)), ((), ())), preferred_element_...  40.3 us
    dot_general x4, matrix products, dot(): return jnp.dot(left, right, preferred_element_type=jnp.float32)  34.8 us
    dot_general x4, matrix products, column_product(): lax.dot_general(left, right, (((0,), (0,)), ((), ())), preferred_element_...  34 us
    all_to_all x1, blocking collectives, per_device(): lax.all_to_all(mix_pieces, 'ctx', split_axis=0, concat_axis=0, tiled=True)  21.4 us
  transfers between devices with their start and end apart: 17, of which 14 were waited for; matrix products, arithmetic and copies ran while one was open for 11% of the time, Pallas kernels for 0%

profile of v1, /device:TPU:9, one launch (start us, length us, event | category | flops | bytes accessed | tf_op | source)
XLA Modules:
  0.0 1028.8 jit_solution(7652950163884755804)
XLA Ops:
  8.7 23.5 %all_to_all.30 = bf16[8,64,3,256]{3,1,2,0:T(8,128)(2,1)S(1)} all-to-all(bf16[8,64,3,256]{3,1,2,0:T(8,128)(2,1)S(1)} %copy.97), channel_id=1, replica_groups=mesh['fsdp'=4,'ctx'=8] {'ctx'}, dimensions={0} | all-to-all | bytes 1572864 | tf_op jit(solution)/shard_map/all_to_all | solution.py:91
  38.2 51.5 %all_to_all.31 = bf16[8,64,8,256]{3,2,1,0:T(8,128)(2,1)S(1)} all-to-all(bf16[8,64,8,256]{3,2,1,0:T(8,128)(2,1)S(1)} %bitcast.108), channel_id=1, replica_groups=mesh['fsdp'=4,'ctx'=8] {'ctx'}, dimensions={0} | all-to-all | bytes 4194304 | tf_op jit(solution)/shard_map/all_to_all | solution.py:91
  95.7 31.5 %all-gather.8.cloned.1.call-done = bf16[1024,2048]{1,0:T(8,128)(2,1)} async-done(((bf16[128,2048]{1,0:T(8,128)(2,1)}), bf16[1024,2048]{1,0:T(8,128)(2,1)}) %all-gather.8.cloned.1.call-update) | async-done | bytes 4194320 | tf_op jit(solution)/shard_map/all_gather | solution.py:80
  143.9 21.4 %all_to_all.32 = bf16[8,128,256]{1,2,0:T(8,128)(2,1)S(1)} all-to-all(bf16[8,128,256]{1,2,0:T(8,128)(2,1)S(1)} %copy.102), channel_id=1, replica_groups=mesh['fsdp'=4,'ctx'=8] {'ctx'}, dimensions={0} | all-to-all | bytes 1048576 | tf_op jit(solution)/shard_map/all_to_all | solution.py:148
  165.3 44.0 %all-gather.12.cloned.1.call-done = bf16[2048,2048]{1,0:T(8,128)(2,1)} async-done(((bf16[64,2048]{1,0:T(8,128)(2,1)}), bf16[2048,2048]{1,0:T(8,128)(2,1)}) %all-gather.12.cloned.1.call-update) | async-done | bytes 8388624 | tf_op jit(solution)/shard_map/all_gather | solution.py:80
  217.3 79.8 %all-gather.16.cloned.1.call-done = bf16[2048,2048]{1,0:T(8,128)(2,1)} async-done(((bf16[512,2048]{1,0:T(8,128)(2,1)}), bf16[2048,2048]{1,0:T(8,128)(2,1)}) %all-gather.16.cloned.1.call-update) | async-done | bytes 8388624 | tf_op jit(solution)/shard_map/all_gather | solution.py:80
  297.1 48.2 %all-gather.14.cloned.1.call-done = bf16[1024,2048]{1,0:T(8,128)(2,1)} async-done(((bf16[128,2048]{1,0:T(8,128)(2,1)}), bf16[1024,2048]{1,0:T(8,128)(2,1)}) %all-gather.14.cloned.1.call-update) | async-done | bytes 4194320 | tf_op jit(solution)/shard_map/all_gather | solution.py:80
  345.3 14.5 %fusion.74 = f32[1024,2048]{1,0:T(8,128)} fusion(bf16[1024,2048]{1,0:T(8,128)(2,1)} %all-gather.14.cloned.1.call-done, bf16[2048,2048]{1,0:T(8,128)(2,1)} %all-gather.16.cloned.1.call-done), kind=kOutput, calls=%fused_computation.131 | convolution fusion | flops 8589934592 | bytes 20971520 | tf_op jit(solution)/shard_map/dot_general | solution.py:64
  359.9 39.2 %all-gather.18.cloned.1.call-done = bf16[1024,2048]{1,0:T(8,128)(2,1)} async-done(((bf16[256,2048]{1,0:T(8,128)(2,1)}), bf16[1024,2048]{1,0:T(8,128)(2,1)}) %all-gather.18.cloned.1.call-update) | async-done | bytes 4194320 | tf_op jit(solution)/shard_map/all_gather | solution.py:80
  399.1 47.8 %all-gather.20.cloned.1.call-done = bf16[1024,2048]{1,0:T(8,128)(2,1)} async-done(((bf16[128,2048]{1,0:T(8,128)(2,1)}), bf16[1024,2048]{1,0:T(8,128)(2,1)}) %all-gather.20.cloned.1.call-update) | async-done | bytes 4194320 | tf_op jit(solution)/shard_map/all_gather | solution.py:80
  446.9 13.1 %multiply_convert_fusion.2 = (bf16[1024,1024]{1,0:T(8,128)(2,1)S(1)}, bf16[1024,1024]{1,0:T(8,128)(2,1)S(1)}, bf16[1024,1024]{1,0:T(8,128)(2,1)}) fusion(f32[1024,2048]{1,0:T(8,128)} %fusion.74, bf16[1024,2048]{1,0:T(8,128)(2,1)} %all-gather.20.cloned.1.call-done, bf16[1024,2048]{1,0:T(8,128)(2,1)} %all-gather.18.cloned.1.call-done), kind=kOutput, calls=%fused_computation.12 | convolution fusion | flops 4310695936 | bytes 23068672 | tf_op jit(solution)/shard_map/dot_general | solution.py:68
  462.1 12.6 %convolution_convert_fusion.2 = bf16[1024,2048]{1,0:T(8,128)(2,1)} fusion(bf16[2048,2048]{1,0:T(8,128)(2,1)} %all-gather.16.cloned.1.call-done, bf16[1024,1024]{1,0:T(8,128)(2,1)S(1)} %get-tuple-element.13, bf16[1024,1024]{1,0:T(8,128)(2,1)S(1)} %get-tuple-element.12), kind=kOutput, calls=%fused_computation.21 | convolution fusion | flops 8600420352 | bytes 16777216 | tf_op jit(solution)/shard_map/dot_general | solution.py:68
  474.9 9.3 convolution_convert_fusion.5
  484.2 39.0 %reduce-scatter.10.cloned.1.call-done = bf16[128,2048]{1,0:T(8,128)(2,1)} async-done(((bf16[1024,2048]{1,0:T(8,128)(2,1)}), bf16[128,2048]{1,0:T(8,128)(2,1)}) %reduce-scatter.10.cloned.1.call-update) | async-done | bytes 524304 | tf_op jit(solution)/shard_map/reduce_scatter | solution.py:84
  524.6 49.3 %reduce-scatter.8.cloned.1.call-done = bf16[128,2048]{1,0:T(8,128)(2,1)} async-done(((bf16[1024,2048]{1,0:T(8,128)(2,1)}), bf16[128,2048]{1,0:T(8,128)(2,1)}) %reduce-scatter.8.cloned.1.call-update) | async-done | bytes 524304 | tf_op jit(solution)/shard_map/reduce_scatter | solution.py:84
  591.9 11.8 %all-to-all-done.3 = bf16[8,128,256]{1,2,0:T(8,128)(2,1)} async-done(((bf16[8,128,256]{1,2,0:T(8,128)(2,1)}), bf16[8,128,256]{1,2,0:T(8,128)(2,1)}, u32[]{:S(2)}, u32[]{:S(2)}) %all-to-all-start.3) | async-done | bytes 524320 | tf_op jit(solution)/shard_map/all_to_all | solution.py:181
  632.3 14.0 %convolution_convert_fusion = bf16[2048,2048]{1,0:T(8,128)(2,1)} fusion(bf16[1024,2048]{1,0:T(8,128)(2,1)} %all-gather.14.cloned.1.call-done, bf16[1024,1024]{1,0:T(8,128)(2,1)} %copy-done.25, bf16[1024,1024]{1,0:T(8,128)(2,1)} %copy-done.24), kind=kOutput, calls=%fused_computation.4 | convolution fusion | flops 8602517504 | bytes 16777216 | tf_op jit(solution)/shard_map/dot_general | solution.py:74
  646.4 9.6 convolution_convert_fusion.4
  656.4 7.6 convolution_convert_fusion.3
  669.6 8.0 reduce-scatter.14.cloned.1.call-done
  683.2 83.8 %reduce-scatter.18.cloned.1.call-done = bf16[512,2048]{1,0:T(8,128)(2,1)} async-done(((bf16[2048,2048]{1,0:T(8,128)(2,1)}), bf16[512,2048]{1,0:T(8,128)(2,1)}) %reduce-scatter.18.cloned.1.call-update) | async-done | bytes 2097168 | tf_op jit(solution)/shard_map/reduce_scatter | solution.py:84
  772.9 49.6 %reduce-scatter.20.cloned.1.call-done = bf16[256,2048]{1,0:T(8,128)(2,1)} async-done(((bf16[1024,2048]{1,0:T(8,128)(2,1)}), bf16[256,2048]{1,0:T(8,128)(2,1)}) %reduce-scatter.20.cloned.1.call-update) | async-done | bytes 1048592 | tf_op jit(solution)/shard_map/reduce_scatter | solution.py:84
  831.3 43.0 %reduce-scatter.12.cloned.1.call-done = bf16[128,2048]{1,0:T(8,128)(2,1)} async-done(((bf16[1024,2048]{1,0:T(8,128)(2,1)}), bf16[128,2048]{1,0:T(8,128)(2,1)}) %reduce-scatter.12.cloned.1.call-update) | async-done | bytes 524304 | tf_op jit(solution)/shard_map/reduce_scatter | solution.py:84
  887.1 133.3 %reduce-scatter.16.cloned.1.call-done = bf16[64,2048]{1,0:T(8,128)(2,1)} async-done(((bf16[2048,2048]{1,0:T(8,128)(2,1)}), bf16[64,2048]{1,0:T(8,128)(2,1)}) %reduce-scatter.16.cloned.1.call-update) | async-done | bytes 262160 | tf_op jit(solution)/shard_map/reduce_scatter | solution.py:84
  (155 shorter events, 128.8 us)
Async XLA Ops:
  7.2 88.6 %all-gather.10.cloned.1.call-start = ((), (), s32[]{:S(2)}) async-start(), calls=%async_computation.14 | async-start | bytes 3932160 | tf_op jit(solution)/shard_map/all_gather | solution.py:80
  8.7 28.5 %copy-start.11 = (bf16[64,16384]{1,0:T(8,128)(2,1)S(1)}, bf16[64,16384]{1,0:T(8,128)(2,1)}, u32[]{:S(2)}) copy-start(bf16[64,16384]{1,0:T(8,128)(2,1)} %param.11) | copy-start | bytes 6291460
  33.9 93.3 %all-gather.8.cloned.1.call-start = ((), (), s32[]{:S(2)}) async-start(), calls=%async_computation.13 | async-start | bytes 4718592 | tf_op jit(solution)/shard_map/all_gather | solution.py:80
  36.4 172.9 %all-gather.12.cloned.1.call-start = ((), (), s32[]{:S(2)}) async-start(), calls=%async_computation.15 | async-start | bytes 8650752 | tf_op jit(solution)/shard_map/all_gather | solution.py:80
  37.1 259.9 %all-gather.16.cloned.1.call-start = ((), (), s32[]{:S(2)}) async-start(), calls=%async_computation.17 | async-start | bytes 10485760 | tf_op jit(solution)/shard_map/all_gather | solution.py:80
  91.7 253.6 %all-gather.14.cloned.1.call-start = ((), (), s32[]{:S(2)}) async-start(), calls=%async_computation.16 | async-start | bytes 4718592 | tf_op jit(solution)/shard_map/all_gather | solution.py:80
  94.5 39.5 %copy-start.1 = (f32[1024,128]{0,1:T(8,128)}, f32[1024,128]{0,1:T(8,128)S(1)}, u32[]{:S(2)}) copy-start(f32[1024,128]{0,1:T(8,128)S(1)} %get-tuple-element.34) | copy-start | bytes 1572868
  94.5 39.5 %copy-start.4 = (f32[1024,128]{0,1:T(8,128)}, f32[1024,128]{0,1:T(8,128)S(1)}, u32[]{:S(2)}) copy-start(f32[1024,128]{0,1:T(8,128)S(1)} %get-tuple-element.33) | copy-start | bytes 1572868
  95.7 43.3 %copy-start.6 = (pred[1024,1024]{0,1:T(8,128)(4,1)}, pred[1024,1024]{0,1:T(8,128)(4,1)S(1)}, u32[]{:S(2)}) copy-start(pred[1024,1024]{0,1:T(8,128)(4,1)S(1)} %compare_and_fusion) | copy-start | bytes 3145732
  215.3 183.8 %all-gather.18.cloned.1.call-start = ((), (), s32[]{:S(2)}) async-start(), calls=%async_computation.18 | async-start | bytes 5242880 | tf_op jit(solution)/shard_map/all_gather | solution.py:80
  215.9 231.1 %all-gather.20.cloned.1.call-start = ((), (), s32[]{:S(2)}) async-start(), calls=%async_computation.20 | async-start | bytes 4718592 | tf_op jit(solution)/shard_map/all_gather | solution.py:80
  216.6 306.5 %reduce-scatter.10.cloned.1.call-start = ((), (), s32[]{:S(2)}) async-start(), calls=%async_computation.21 | async-start | bytes 4718592 | tf_op jit(solution)/shard_map/reduce_scatter | solution.py:84
  474.7 99.2 %reduce-scatter.8.cloned.1.call-start = ((), (), s32[]{:S(2)}) async-start(), calls=%async_computation.19 | async-start | bytes 4718592 | tf_op jit(solution)/shard_map/reduce_scatter | solution.py:84
  583.6 25.8 %copy-start.7 = (pred[1024,1024]{0,1:T(8,128)(4,1)S(1)}, pred[1024,1024]{0,1:T(8,128)(4,1)}, u32[]{:S(2)}) copy-start(pred[1024,1024]{0,1:T(8,128)(4,1)} %copy-done.6) | copy-start | bytes 3145732
  585.8 17.9 %all-to-all-start.3 = ((bf16[8,128,256]{1,2,0:T(8,128)(2,1)}), bf16[8,128,256]{1,2,0:T(8,128)(2,1)}, u32[]{:S(2)}, u32[]{:S(2)}) async-start(bf16[8,128,256]{1,2,0:T(8,128)(2,1)} %bitcast.118), calls=%async_computation.5 | async-start | bytes 1048576 | tf_op jit(solution)/shard_map/all_to_all | solution.py:181
  591.9 85.7 %reduce-scatter.14.cloned.1.call-start = ((), (), s32[]{:S(2)}) async-start(), calls=%async_computation.23 | async-start | bytes 3932160 | tf_op jit(solution)/shard_map/reduce_scatter | solution.py:84
  632.0 135.0 %reduce-scatter.18.cloned.1.call-start = ((), (), s32[]{:S(2)}) async-start(), calls=%async_computation.25 | async-start | bytes 10485760 | tf_op jit(solution)/shard_map/reduce_scatter | solution.py:84
  646.3 176.2 %reduce-scatter.20.cloned.1.call-start = ((), (), s32[]{:S(2)}) async-start(), calls=%async_computation.26 | async-start | bytes 5242880 | tf_op jit(solution)/shard_map/reduce_scatter | solution.py:84
  656.0 218.3 %reduce-scatter.12.cloned.1.call-start = ((), (), s32[]{:S(2)}) async-start(), calls=%async_computation.22 | async-start | bytes 4718592 | tf_op jit(solution)/shard_map/reduce_scatter | solution.py:84
  664.0 356.3 %reduce-scatter.16.cloned.1.call-start = ((), (), s32[]{:S(2)}) async-start(), calls=%async_computation.24 | async-start | bytes 8650752 | tf_op jit(solution)/shard_map/reduce_scatter | solution.py:84
  677.6 89.4 %all-to-all-start.4 = ((bf16[8,64,768]{2,1,0:T(8,128)(2,1)}), bf16[8,64,768]{2,1,0:T(8,128)(2,1)S(1)}, u32[]{:S(2)}, u32[]{:S(2)}) async-start(bf16[8,64,768]{2,1,0:T(8,128)(2,1)} %bitcast.122), calls=%async_computation.8 | async-start | bytes 1572864 | tf_op jit(solution)/shard_map/all_to_all | solution.py:99
  767.0 111.1 %all-to-all-start.5 = ((bf16[8,64,2048]{2,1,0:T(8,128)(2,1)}), bf16[8,64,2048]{2,1,0:T(8,128)(2,1)}, u32[]{:S(2)}, u32[]{:S(2)}) async-start(bf16[8,64,2048]{2,1,0:T(8,128)(2,1)} %bitcast.117), calls=%async_computation.11 | async-start | bytes 4194304 | tf_op jit(solution)/shard_map/all_to_all | solution.py:99
  825.3 49.0 %copy-start.17 = (f32[128]{0:T(128)S(1)}, f32[128]{0:T(128)}, u32[]{:S(2)}) copy-start(f32[128]{0:T(128)} %copy-done.16) | copy-start | bytes 1540
  825.3 49.0 %copy-start.19 = (f32[128]{0:T(128)S(1)}, f32[128]{0:T(128)}, u32[]{:S(2)}) copy-start(f32[128]{0:T(128)} %copy-done.18) | copy-start | bytes 1540
  (19 other events, 83.8 us)
Sparse Core Ops, SparseCore 0:
  34.1 44.7 all-gather.9
  81.1 46.1 all-gather.7
  130.3 78.9 all-gather.11
  211.6 85.4 all-gather.15
  299.1 46.1 all-gather.13
  347.0 52.0 all-gather.17
  400.7 46.1 all-gather.19
  474.8 48.2 reduce-scatter.9
  525.5 48.3 reduce-scatter.7
  632.2 45.4 reduce-scatter.13
  680.7 86.3 reduce-scatter.17
  769.9 52.5 reduce-scatter.19
  825.4 48.8 reduce-scatter.11
  876.4 143.8 reduce-scatter.15

commit v2 on v1

v2 whole, which is shorter than its diff:
```python
import jax
import jax.numpy as jnp
from jax import lax
from jax.experimental import pallas as pl
from jax.experimental.pallas import tpu as pltpu
from jax.sharding import PartitionSpec as P

HEADS = 16
HEAD_DIM = 128
BLOCK = 128
LOW = jnp.bfloat16


def normalize(values):
    average = jnp.mean(values, axis=-1, keepdims=True)
    centered = values - average
    variance = jnp.mean(centered * centered, axis=-1, keepdims=True)
    inv_root = lax.rsqrt(variance + 1e-05)
    return (centered * inv_root, inv_root)


def norm_back(upstream, normed, inv_root):
    first_mean = jnp.mean(upstream, axis=-1, keepdims=True)
    second_mean = jnp.mean(upstream * normed, axis=-1, keepdims=True)
    return inv_root * (upstream - first_mean - normed * second_mean)


def places(token_index, lengths):
    seq_ends = jnp.cumsum(lengths)
    sequence = jnp.sum((token_index[:, None] >= seq_ends[None, :]).astype(jnp.int32), axis=1)
    before = jnp.arange(lengths.shape[0], dtype=jnp.int32)
    seq_start = jnp.sum(jnp.where(before[None, :] < sequence[:, None], lengths[None, :], 0), axis=1)
    return (sequence, token_index - seq_start)


def initial_index(row_index, order_row):
    slot_index = row_index // BLOCK
    slot_table = jnp.arange(order_row.shape[0], dtype=jnp.int32)
    picked = jnp.sum(
        jnp.where(slot_table[None, :] == slot_index[:, None], order_row[None, :], 0), axis=1
    )
    return picked * BLOCK + row_index % BLOCK


def angle_tables(position):
    half_dim = HEAD_DIM // 2
    frequency = 10000.0 ** (-jnp.arange(half_dim, dtype=jnp.float32) * 2.0 / HEAD_DIM)
    angle_table = position.astype(jnp.float32)[:, None] * frequency[None, :]
    angle_table = jnp.concatenate([angle_table, angle_table], axis=-1)
    return (jnp.cos(angle_table)[:, None, :], jnp.sin(angle_table)[:, None, :])


def rotate(values, cosine_table, sine_table):
    half_dim = values.shape[-1] // 2
    turned = jnp.concatenate([-values[..., half_dim:], values[..., :half_dim]], axis=-1)
    return values * cosine_table + turned * sine_table


def unrotate(values, cosine_table, sine_table):
    half_dim = values.shape[-1] // 2
    scaled = values * sine_table
    turned = jnp.concatenate([scaled[..., half_dim:], -scaled[..., :half_dim]], axis=-1)
    return values * cosine_table + turned


def dot(left, right):
    return jnp.dot(left, right, preferred_element_type=jnp.float32)


def times_transposed(left, right):
    return lax.dot_general(
        left, right, (((1,), (1,)), ((), ())), preferred_element_type=jnp.float32
    )


def column_product(left, right):
    return lax.dot_general(
        left, right, (((0,), (0,)), ((), ())), preferred_element_type=jnp.float32
    )


def gather(values, axes):
    return lax.all_gather(values, axes, axis=0, tiled=True)


def scatter(values, axes):
    return lax.psum_scatter(values, axes, scatter_dimension=0, tiled=True)


def by_part(weight, outer, parts):
    rows, columns = weight.shape
    inner = columns // (outer * parts)
    pieces = weight.reshape(rows, outer, parts, inner).transpose(2, 0, 1, 3)
    return pieces.reshape(parts, rows, outer * inner)


def from_parts(pieces, outer):
    parts, rows, columns = pieces.shape
    pieces = pieces.reshape(parts, rows, outer, columns // outer).transpose(1, 2, 0, 3)
    return pieces.reshape(rows, parts * columns).astype(jnp.float32)


def enter(axes):
    barrier = pltpu.get_barrier_semaphore()
    count = 0
    for axis, size in axes:
        me = lax.axis_index(axis)
        for step in range(1, size):
            pl.semaphore_signal(barrier, inc=1, device_id={axis: lax.rem(me + step, size)})
        count += size - 1
    pl.semaphore_wait(barrier, count)


def remote(src, dst, send, recv, axis, peer):
    return pltpu.make_async_remote_copy(
        src_ref=src, dst_ref=dst, send_sem=send, recv_sem=recv, device_id={axis: peer}
    )


class Exchange:
    def __init__(self, parts, shape):
        self.parts = parts
        self.out = jax.ShapeDtypeStruct((parts,) + shape, LOW)
        self.scratch = [
            pltpu.SemaphoreType.DMA((parts - 1,)),
            pltpu.SemaphoreType.DMA((parts - 1,)),
            pltpu.SemaphoreType.DMA,
        ]

    def run(self, src, dst, send, recv, local):
        me = lax.axis_index("ctx")
        copies = []
        for step in range(1, self.parts):
            peer = lax.rem(me + step, self.parts)
            copies.append(
                remote(src.at[peer], dst.at[me], send.at[step - 1], recv.at[step - 1], "ctx", peer)
            )
            copies[-1].start()
        own = pltpu.make_async_copy(src.at[me], dst.at[me], local)
        own.start()
        yield
        for copy in copies:
            copy.wait()
        own.wait()


class Gather:
    def __init__(self, parts, shape):
        self.parts = parts
        self.out = jax.ShapeDtypeStruct((parts,) + shape, LOW)
        chips = parts // 2
        self.scratch = [
            pltpu.SemaphoreType.DMA((2, chips)),
            pltpu.SemaphoreType.DMA((chips,)),
            pltpu.SemaphoreType.DMA((chips,)),
            pltpu.SemaphoreType.DMA((chips,)),
            pltpu.SemaphoreType.DMA,
        ]

    def run(self, src, dst, send, recv, pair_send, pair_recv, local):
        chips = self.parts // 2
        me = lax.axis_index("ctx")
        chip, core = me // 2, lax.rem(me, 2)
        partner = me + 1 - 2 * core

        def line(block, slot, origin, way):
            return remote(
                block, slot, send.at[way, origin], recv.at[origin], "ctx", me + 2 - 4 * way
            )

        def across(block, slot, origin):
            return remote(block, slot, pair_send.at[origin], pair_recv.at[origin], "ctx", partner)

        mine = dst.at[me]

        @pl.when(chip < chips - 1)
        def _():
            line(src, mine, chip, 0).start()

        @pl.when(chip > 0)
        def _():
            line(src, mine, chip, 1).start()

        across(src, mine, chip).start()
        own = pltpu.make_async_copy(src, mine, local)
        own.start()
        yield
        for step in range(1, chips):
            for way in range(2):
                origin = chip - step if way == 0 else chip + step

                @pl.when((origin >= 0) & (origin < chips))
                def _():
                    slot = dst.at[2 * origin + core]
                    line(slot, slot, origin, way).wait_recv()

                    @pl.when((chip < chips - 1) if way == 0 else (chip > 0))
                    def _():
                        line(slot, slot, origin, way).start()

                    across(slot, slot, origin).start()

            yield
        for step in range(chips):
            for way in range(2):
                origin = chip - step if way == 0 else chip + step
                ahead = (chip < chips - 1) if way == 0 else (chip > 0)

                @pl.when((origin >= 0) & (origin < chips) & ahead)
                def _():
                    slot = dst.at[2 * origin + core]
                    line(slot, slot, origin, way).wait_send()

        for origin in range(chips):
            across(dst.at[2 * origin + core], dst.at[2 * origin + core], origin).wait_send()
            other = dst.at[2 * origin + 1 - core]
            across(other, other, origin).wait_recv()
        own.wait()


class Scatter:
    def __init__(self, parts, shape):
        self.parts, self.shape = parts, shape
        self.out = jax.ShapeDtypeStruct(shape, jnp.float32)
        chips = parts // 2
        self.scratch = [
            pltpu.VMEM((chips,) + shape, LOW),
            pltpu.VMEM((2, chips) + shape, LOW),
            pltpu.VMEM((chips,) + shape, LOW),
            pltpu.SemaphoreType.DMA((chips,)),
            pltpu.SemaphoreType.DMA((chips,)),
            pltpu.SemaphoreType.DMA((chips,)),
            pltpu.SemaphoreType.DMA((2, chips)),
        ]

    def run(self, src, out, pair, come, stage, pair_send, pair_recv, send, recv):
        chips = self.parts // 2
        me = lax.axis_index("ctx")
        chip, core = me // 2, lax.rem(me, 2)
        partner = me + 1 - 2 * core
        rows = self.shape[0]
        slab = min(rows, 16)

        def across(goal):
            return remote(
                src.at[2 * goal + 1 - core],
                pair.at[goal],
                pair_send.at[goal],
                pair_recv.at[goal],
                "ctx",
                partner,
            )

        def line(goal, way):
            return remote(
                stage.at[goal],
                come.at[way, goal],
                send.at[goal],
                recv.at[way, goal],
                "ctx",
                me + 2 - 4 * way,
            )

        def wide(ref, *index):
            return ref[index].astype(jnp.float32)

        def slabs(part):
            def one(index, carry):
                part(pl.ds(pl.multiple_of(index * slab, slab), slab))
                return carry

            lax.fori_loop(0, rows // slab, one, 0)

        order = []
        for step in range((chips + 1) // 2):
            order += sorted({step, chips - 1 - step})
        for goal in order:
            across(goal).start()
        yield
        for step in range(chips - 1):
            for way in range(2):
                goal = chips - 1 - step if way == 0 else step
                first = (chip == 0) if way == 0 else (chip == chips - 1)

                def begin(at):
                    value = wide(src, 2 * goal + core, at) + wide(pair, goal, at)
                    stage[goal, at, :] = value.astype(LOW)

                def middle(at):
                    value = wide(src, 2 * goal + core, at) + wide(pair, goal, at)
                    value += wide(come, way, goal, at)
                    stage[goal, at, :] = value.astype(LOW)

                @pl.when((chip < goal) if way == 0 else (chip > goal))
                def _():
                    across(goal).wait_recv()

                    @pl.when(first)
                    def _():
                        slabs(begin)

                    @pl.when(jnp.logical_not(first))
                    def _():
                        line(goal, way).wait_recv()
                        slabs(middle)

                    line(goal, way).start()

            yield

        def own(at):
            out[at, :] = wide(src, me, at) + wide(pair, chip, at)

        across(chip).wait_recv()
        slabs(own)
        for way in range(2):

            def last(at):
                out[at, :] += wide(come, way, chip, at)

            @pl.when((chip > 0) if way == 0 else (chip < chips - 1))
            def _():
                line(chip, way).wait_recv()
                slabs(last)

            yield
        for goal in range(chips):
            across(goal).wait_send()

            @pl.when(chip != goal)
            def _():
                line(goal, 0).wait_send()


class Spread:
    def __init__(self, parts, groups, shape):
        self.parts, self.groups = parts, groups
        self.out = jax.ShapeDtypeStruct((groups, parts) + shape, LOW)
        self.scratch = [
            pltpu.SemaphoreType.DMA((parts - 1,)),
            pltpu.SemaphoreType.DMA((parts - 1,)),
            pltpu.SemaphoreType.DMA((groups - 1, parts)),
            pltpu.SemaphoreType.DMA((groups - 1, parts)),
            pltpu.SemaphoreType.DMA,
        ]

    def run(self, src, dst, send, recv, far_send, far_recv, local):
        parts, groups = self.parts, self.groups
        me, group = lax.axis_index("ctx"), lax.axis_index("fsdp")
        copies = []
        for step in range(1, parts):
            peer = lax.rem(me + step, parts)
            copies.append(
                remote(
                    src.at[peer],
                    dst.at[group, me],
                    send.at[step - 1],
                    recv.at[step - 1],
                    "ctx",
                    peer,
                )
            )
            copies[-1].start()
        own = pltpu.make_async_copy(src.at[me], dst.at[group, me], local)
        own.start()

        def pass_on(block, origin, step):
            out = []
            for hop in range(1, groups):
                copy = remote(
                    block,
                    dst.at[group, origin],
                    far_send.at[hop - 1, step],
                    far_recv.at[hop - 1, step],
                    "fsdp",
                    lax.rem(group + hop, groups),
                )
                copy.start()
                out.append(copy)
            return out

        far = pass_on(src.at[me], me, 0)
        yield
        for step in range(1, parts):
            copies[step - 1].wait_recv()
            origin = lax.rem(me - step + parts, parts)
            far += pass_on(dst.at[group, origin], origin, step)
            yield
        for copy in far:
            copy.wait()
            yield
        for copy in copies:
            copy.wait_send()
        own.wait()


def call(jobs, operands, name, identity, axes, body=None):
    counts = [len(job.scratch) for job in jobs]

    def kernel(*refs):
        n = len(jobs)
        ins, outs, rest = refs[:n], refs[n : 2 * n], refs[2 * n :]
        enter(axes)
        runs, at = [], 0
        for job, src, dst, count in zip(jobs, ins, outs, counts):
            runs.append(job.run(src, dst, *rest[at : at + count]))
            at += count
        while runs:
            going = []
            for run in runs:
                try:
                    next(run)
                    going.append(run)
                except StopIteration:
                    pass
            runs = going

    vmem = pl.BlockSpec(memory_space=pltpu.VMEM)
    return pl.pallas_call(
        kernel,
        out_shape=tuple(job.out for job in jobs),
        in_specs=[vmem] * len(jobs),
        out_specs=(vmem,) * len(jobs),
        scratch_shapes=[shape for job in jobs for shape in job.scratch],
        compiler_params=pltpu.CompilerParams(
            collective_id=identity, has_side_effects=True, vmem_limit_bytes=60 << 20
        ),
        name=name,
    )(*operands)


def per_device(tokens, w_qkv, w_out, w_gate_up, w_down, seq_lengths, block_order, cotangent):
    lengths = seq_lengths[0]
    order_row = block_order[0]
    parts = lax.axis_size("ctx")
    groups = lax.axis_size("fsdp")
    rows, width = tokens.shape
    length = rows * parts
    heads = HEADS // parts
    head_width = heads * HEAD_DIM
    score_scale = HEAD_DIM ** (-0.5)

    line = (("ctx", parts),)
    plane = (("ctx", parts), ("fsdp", groups))
    block = (rows, width)

    out_full = gather(w_out, ("fsdp", "ctx"))
    down_rows = gather(w_down, "fsdp")
    inputs = tokens.astype(jnp.float32)
    normed_in, root_in = normalize(inputs)
    qkv_pieces = by_part(w_qkv, 3, parts)
    gate_up_pieces = by_part(w_gate_up, 2 * groups, parts)
    qkv_cols, normed_in_full, gate_up_cols = call(
        [
            Spread(parts, groups, qkv_pieces.shape[1:]),
            Gather(parts, block),
            Exchange(parts, gate_up_pieces.shape[1:]),
        ],
        [qkv_pieces, normed_in.astype(LOW), gate_up_pieces],
        "start",
        1,
        plane,
    )
    qkv_cols = qkv_cols.reshape(width, 3 * head_width)
    normed_in_full = normed_in_full.reshape(length, width)
    gate_up_cols = gather(gate_up_cols.reshape(width // groups, -1), "fsdp")

    row_index = jnp.arange(length, dtype=jnp.int32)
    seq, pos = places(initial_index(row_index, order_row), lengths)
    cosine_table, sine_table = angle_tables(pos)
    allowed = ((seq[:, None] == seq[None, :]) & (pos[None, :] <= pos[:, None]))[None]

    qkv = dot(normed_in_full, qkv_cols)
    head_shape = (length, heads, HEAD_DIM)
    queries = rotate(qkv[:, :head_width].reshape(head_shape), cosine_table, sine_table).astype(LOW)
    keys = rotate(
        qkv[:, head_width : 2 * head_width].reshape(head_shape), cosine_table, sine_table
    ).astype(LOW)
    values = qkv[:, 2 * head_width :].astype(LOW).reshape(head_shape)
    scores = jnp.einsum("qhd,khd->hqk", queries, keys, preferred_element_type=jnp.float32)
    scores = jnp.where(allowed, scores * score_scale, -1e30)
    row_max = jnp.max(scores, axis=-1)
    weights = jnp.where(allowed, jnp.exp(scores - row_max[..., None]), 0.0)
    row_total = jnp.sum(weights, axis=-1)
    mixed = jnp.einsum("hqk,khd->qhd", weights.astype(LOW), values, preferred_element_type=jnp.float32)
    log_total = row_max + jnp.log(row_total)
    attn_heads = mixed / jnp.transpose(row_total)[..., None]

    mix_pieces = attn_heads.astype(LOW).reshape(parts, rows, head_width)
    (mix_pieces,) = call(
        [Exchange(parts, mix_pieces.shape[1:])], [mix_pieces], "mix", 2, line
    )
    mix_low = mix_pieces.transpose(1, 0, 2).reshape(rows, width)
    residual = inputs + dot(mix_low, out_full)
    normed_mid, root_mid = normalize(residual)
    normed_mid_full, cot_full = call(
        [Gather(parts, block), Gather(parts, block)],
        [normed_mid.astype(LOW), cotangent],
        "mid",
        3,
        line,
    )
    normed_mid_full = normed_mid_full.reshape(length, width)
    cot_full = cot_full.reshape(length, width)

    gate_up = dot(normed_mid_full, gate_up_cols)
    units = gate_up.shape[1] // 2
    gate_part = gate_up[:, :units]
    up_part = gate_up[:, units:]
    sigmoid_gate = jax.nn.sigmoid(gate_part)
    silu_gate = gate_part * sigmoid_gate
    activated = (silu_gate * up_part).astype(LOW)
    down_out = scatter(dot(activated, down_rows).astype(LOW), "ctx")
    layer_out = (residual + down_out.astype(jnp.float32)).astype(LOW)

    down_grad = scatter(column_product(activated, cot_full).astype(LOW), "fsdp").astype(jnp.float32)

    act_grad = times_transposed(cot_full, down_rows)
    gate_grad = act_grad * up_part * sigmoid_gate * (1.0 + gate_part * (1.0 - sigmoid_gate))
    up_grad = act_grad * silu_gate
    gate_up_back = jnp.concatenate([gate_grad, up_grad], axis=1).astype(LOW)
    mid_back_terms = times_transposed(gate_up_back, gate_up_cols).astype(LOW)
    gate_up_grad = scatter(column_product(normed_mid_full, gate_up_back).astype(LOW), "fsdp")

    (mid_back,) = call(
        [Scatter(parts, block)],
        [mid_back_terms.reshape((parts,) + block)],
        "mid_back",
        4,
        line,
    )
    residual_back = cotangent.astype(jnp.float32) + norm_back(mid_back, normed_mid, root_mid)
    proj_back = residual_back.astype(LOW)
    mix_back = times_transposed(proj_back, out_full).astype(LOW)

    back_pieces = mix_back.reshape(rows, parts, head_width).transpose(1, 0, 2)
    (back_pieces,) = call(
        [Exchange(parts, back_pieces.shape[1:])], [back_pieces], "mix_back", 5, line
    )
    back_heads = back_pieces.reshape(head_shape)

    delta = jnp.einsum("qhd,qhd->hq", back_heads.astype(jnp.float32), attn_heads)
    probs = jnp.where(allowed, jnp.exp(scores - log_total[..., None]), 0.0)
    value_back = jnp.einsum(
        "hqk,qhd->khd", probs.astype(LOW), back_heads, preferred_element_type=jnp.float32
    )
    prob_back = jnp.einsum("qhd,khd->hqk", back_heads, values, preferred_element_type=jnp.float32)
    score_back = (score_scale * probs * (prob_back - delta[..., None])).astype(LOW)
    query_back = jnp.einsum("hqk,khd->qhd", score_back, keys, preferred_element_type=jnp.float32)
    key_back = jnp.einsum("hqk,qhd->khd", score_back, queries, preferred_element_type=jnp.float32)
    qkv_back = jnp.concatenate(
        [
            unrotate(query_back, cosine_table, sine_table).reshape(length, head_width),
            unrotate(key_back, cosine_table, sine_table).reshape(length, head_width),
            value_back.reshape(length, head_width),
        ],
        axis=1,
    ).astype(LOW)
    in_back_terms = times_transposed(qkv_back, qkv_cols).astype(LOW)
    qkv_grad = scatter(column_product(normed_in_full, qkv_back).astype(LOW), "fsdp")
    shard = width // (parts * groups)
    mix_columns = mix_low.reshape(rows, groups, parts, shard).transpose(2, 0, 1, 3)
    in_back, proj_back_full, mix_columns, gate_up_grad = call(
        [
            Scatter(parts, block),
            Gather(parts, block),
            Exchange(parts, (rows, groups * shard)),
            Exchange(parts, gate_up_pieces.shape[1:]),
        ],
        [
            in_back_terms.reshape((parts,) + block),
            proj_back,
            mix_columns.reshape(parts, rows, groups * shard),
            gate_up_grad.reshape(gate_up_pieces.shape),
        ],
        "in_back",
        6,
        line,
    )
    out_grad = scatter(
        column_product(
            mix_columns.reshape(length, groups * shard), proj_back_full.reshape(length, width)
        ).astype(LOW),
        "fsdp",
    )
    tokens_grad = residual_back + norm_back(in_back, normed_in, root_in)
    (qkv_grad,) = call(
        [Exchange(parts, qkv_pieces.shape[1:])],
        [qkv_grad.reshape(qkv_pieces.shape)],
        "last",
        7,
        line,
    )

    return (
        layer_out,
        tokens_grad,
        from_parts(qkv_grad, 3),
        out_grad.astype(jnp.float32),
        from_parts(gate_up_grad, 2 * groups),
        down_grad,
    )


def solution(mesh):
    both = P(("fsdp", "ctx"), None)
    one = P("fsdp", None)
    return jax.shard_map(
        per_device,
        mesh=mesh,
        in_specs=(both, both, both, both, both, one, one, both),
        out_specs=(both,) * 6,
        check_vma=False,
    )
```

time: 1040 us -> 704 us (0.68)
  waiting for transfers between devices: 711 us -> 5.92 us
  Pallas kernels: 0 us -> 493 us
  blocking collectives: 96.3 us -> 0 us
  starting transfers between devices: 19.7 us -> 0.5 us
    pallas_call x0 -> x7, Pallas kernels: none -> 493 us  [call(): pl.pallas_call(kernel, out_shape=tuple((job.out for job in jobs)), in_spe...]
    reduce_scatter x7 -> x5, waiting for transfers between devices: 406 us -> 0.05 us  [scatter(): return lax.psum_scatter(values, axes, scatter_dimension=0, tiled=True)]
    all_gather x7 -> x3, waiting for transfers between devices: 291 us -> 4.41 us  [gather(): return lax.all_gather(values, axes, axis=0, tiled=True)]
    all_to_all x3 -> x0, blocking collectives: 96.3 us -> none  [the longest x2 75 us: spread_columns(): lax.all_to_all(pieces, 'ctx', split_axis=0, concat_axis=0, tiled=True)]
    all_to_all x3 -> x0, starting transfers between devices: 17.5 us -> none  [the longest x2 11.4 us: collect_rows(): lax.all_to_all(pieces, 'ctx', split_axis=0, concat_axis=0, tiled=True)]
    all_to_all x3 -> x0, waiting for transfers between devices: 11.8 us -> none  [the longest x1 11.8 us: per_device(): lax.all_to_all(back_pieces, 'ctx', split_axis=0, concat_axis=0, tiled=True)]
  transfers between devices with their start and end apart: 17 -> 8, of which waited for: 14 -> 1; matrix products, arithmetic and copies ran while one was open for 11% -> 23% of each run, Pallas kernels for 0% -> 70%
where the time goes in v2:
time: 704 us; the launch traced here: 700 us
  Pallas kernels  493 us (70%)
  matrix products  125 us (18%)
  local copies, waits for them, and re-layouts  36.7 us (5%)
  other arithmetic  24.2 us (3%)
  between operations  15.1 us (2%)
    pallas_call x7, Pallas kernels, call(): pl.pallas_call(kernel, out_shape=tuple((job.out for job in jobs)), in_spe...  493 us
    dot_general x4, matrix products, times_transposed(): lax.dot_general(left, right, (((1,), (1,)), ((), ())), preferred_element_...  42.2 us
    dot_general x4, matrix products, column_product(): lax.dot_general(left, right, (((0,), (0,)), ((), ())), preferred_element_...  33.4 us
    dot_general x4, matrix products, dot(): return jnp.dot(left, right, preferred_element_type=jnp.float32)  31.5 us
    unnamed x63, local copies, waits for them, and re-layouts  17.4 us
  transfers between devices with their start and end apart: 8, of which 1 were waited for; matrix products, arithmetic and copies ran while one was open for 23% of the time, Pallas kernels for 70%

profile of v2, /device:TPU:9, one launch (start us, length us, event | category | flops | bytes accessed | tf_op | source)
XLA Modules:
  0.0 700.0 jit_solution(16411098059645010004)
XLA Ops:
  18.6 158.6 %start.1 = (bf16[4,8,64,768]{3,2,1,0:T(8,128)(2,1)}, bf16[8,128,2048]{2,1,0:T(8,128)(2,1)}, bf16[8,64,2048]{2,1,0:T(8,128)(2,1)}) custom-call(bf16[8,64,768]{2,1,0:T(8,128)(2,1)} %reshape.342.refs_0_, bf16[128,2048]{1,0:T(8,128)(2,1)} %fusion.22.refs_1_, bf16[8,64,2048]{2,1,0:T(8,128)(2,1)} %reshape.344.refs_2_), custom_call_target="tpu_custom_call" | custom-call | tf_op jit(solution)/shard_map/start/pallas_call | solution.py:419
  178.2 6.2 fusion.71
  195.7 3.7 fusion.69
  200.6 23.0 %mix.1 = bf16[8,128,256]{2,1,0:T(8,128)(2,1)} custom-call(bf16[8,128,256]{2,1,0:T(8,128)(2,1)} %copy.119.refs_0_), custom_call_target="tpu_custom_call" | custom-call | tf_op jit(solution)/shard_map/mix/pallas_call | solution.py:419
  225.1 4.7 fusion.70
  231.1 73.7 %mid.1 = (bf16[8,128,2048]{2,1,0:T(8,128)(2,1)}, bf16[8,128,2048]{2,1,0:T(8,128)(2,1)}) custom-call(bf16[128,2048]{1,0:T(8,128)(2,1)} %fusion.37.refs_0_, bf16[128,2048]{1,0:T(8,128)(2,1)} %refs_1_.1), custom_call_target="tpu_custom_call" | custom-call | tf_op jit(solution)/shard_map/mid/pallas_call | solution.py:419
  304.9 14.4 %fusion.72 = f32[1024,2048]{1,0:T(8,128)} fusion(bf16[1024,2048]{1,0:T(8,128)(2,1)} %bitcast.158, bf16[2048,2048]{1,0:T(8,128)(2,1)} %all-gather.6.cloned.1.call-done), kind=kOutput, calls=%fused_computation.128 | convolution fusion | flops 8589934592 | bytes 20971520 | tf_op jit(solution)/shard_map/dot_general | solution.py:67
  319.3 4.4 all-gather.8.cloned.1.call-done
  323.7 14.0 %multiply_convert_fusion.2 = (bf16[1024,1024]{1,0:T(8,128)(2,1)}, bf16[1024,1024]{1,0:T(8,128)(2,1)}, bf16[1024,1024]{1,0:T(8,128)(2,1)S(1)}) fusion(f32[1024,2048]{1,0:T(8,128)} %fusion.72, bf16[1024,2048]{1,0:T(8,128)(2,1)} %bitcast.156, bf16[1024,2048]{1,0:T(8,128)(2,1)} %all-gather.8.cloned.1.call-done), kind=kOutput, calls=%fused_computation.12 | convolution fusion | flops 4310695936 | bytes 23068672 | tf_op jit(solution)/shard_map/dot_general | solution.py:71
  339.0 6.1 convolution_convert_fusion.4
  345.1 14.4 %convolution_convert_fusion = bf16[2048,2048]{1,0:T(8,128)(2,1)} fusion(bf16[1024,2048]{1,0:T(8,128)(2,1)} %bitcast.159, bf16[1024,1024]{1,0:T(8,128)(2,1)} %get-tuple-element.33, bf16[1024,1024]{1,0:T(8,128)(2,1)} %get-tuple-element.32), kind=kOutput, calls=%fused_computation.4 | convolution fusion | flops 8602517504 | bytes 16777216 | tf_op jit(solution)/shard_map/dot_general | solution.py:77
  359.6 9.4 %convolution_convert_fusion.3 = bf16[1024,2048]{1,0:T(8,128)(2,1)} fusion(bf16[1024,1024]{1,0:T(8,128)(2,1)} %copy-done.25, bf16[1024,2048]{1,0:T(8,128)(2,1)} %bitcast.157), kind=kOutput, calls=%fused_computation.23 | convolution fusion | flops 4297064448 | bytes 10485760 | tf_op jit(solution)/shard_map/dot_general | solution.py:77
  369.1 14.7 %convolution_convert_fusion.1 = bf16[1024,2048]{1,0:T(8,128)(2,1)} fusion(bf16[2048,2048]{1,0:T(8,128)(2,1)} %all-gather.6.cloned.1.call-done, bf16[1024,1024]{1,0:T(8,128)(2,1)} %get-tuple-element.33, bf16[1024,1024]{1,0:T(8,128)(2,1)} %get-tuple-element.32), kind=kOutput, calls=%fused_computation.21 | convolution fusion | flops 8600420352 | bytes 16777216 | tf_op jit(solution)/shard_map/dot_general | solution.py:71
  383.9 58.2 %mid_back.1 = f32[128,2048]{1,0:T(8,128)} custom-call(bf16[8,128,2048]{2,1,0:T(8,128)(2,1)} %bitcast.126), custom_call_target="tpu_custom_call" | custom-call | tf_op jit(solution)/shard_map/mid_back/pallas_call | solution.py:419
  443.8 3.2 fusion.63
  447.0 6.5 convolution_convert_fusion.6
  454.8 18.9 %mix_back.1 = bf16[8,128,256]{2,1,0:T(8,128)(2,1)} custom-call(bf16[8,128,256]{2,1,0:T(8,128)(2,1)} %bitcast.137), custom_call_target="tpu_custom_call" | custom-call | tf_op jit(solution)/shard_map/mix_back/pallas_call | solution.py:419
  480.3 6.4 multiply_convert_fusion
  495.7 4.9 convolution_convert_fusion.5
  501.7 7.0 convolution_convert_fusion.2
  508.7 131.0 %in_back.1 = (f32[128,2048]{1,0:T(8,128)}, bf16[8,128,2048]{2,1,0:T(8,128)(2,1)}, bf16[8,128,256]{2,1,0:T(8,128)(2,1)}, bf16[8,64,2048]{2,1,0:T(8,128)(2,1)}) custom-call(bf16[8,128,2048]{2,1,0:T(8,128)(2,1)} %bitcast.125, bf16[128,2048]{1,0:T(8,128)(2,1)} %copy-done.2, bf16[8,128,256]{2,1,0:T(8,128)(2,1)} %copy.99.refs_2_, bf16[8,64,2048]{2,1,0:T(8,128)(2,1)} %bitcast.130), custom_call_target="tpu_custom_call" | custom-call | tf_op jit(solution)/shard_map/in_back/pallas_call | solution.py:419
  639.7 4.6 fusion.11
  647.2 29.4 %last.1 = bf16[8,64,768]{2,1,0:T(8,128)(2,1)} custom-call(bf16[8,64,768]{2,1,0:T(8,128)(2,1)} %bitcast.141), custom_call_target="tpu_custom_call" | custom-call | tf_op jit(solution)/shard_map/last/pallas_call | solution.py:419
  685.0 4.4 copy.125
  (146 shorter events, 62.9 us)
Async XLA Ops:
  7.2 218.0 %all-gather.4.cloned.1.call-start = ((), (), s32[]{:S(2)}) async-start(), calls=%async_computation.5 | async-start | bytes 8650752 | tf_op jit(solution)/shard_map/all_gather | solution.py:83
  7.9 297.0 %all-gather.6.cloned.1.call-start = ((), (), s32[]{:S(2)}) async-start(), calls=%async_computation.6 | async-start | bytes 10485760 | tf_op jit(solution)/shard_map/all_gather | solution.py:83
  177.2 146.5 %all-gather.8.cloned.1.call-start = ((), (), s32[]{:S(2)}) async-start(), calls=%async_computation.7 | async-start | bytes 5242880 | tf_op jit(solution)/shard_map/all_gather | solution.py:83
  177.9 265.8 %reduce-scatter.6.cloned.1.call-start = ((), (), s32[]{:S(2)}) async-start(), calls=%async_computation.8 | async-start | bytes 4718592 | tf_op jit(solution)/shard_map/reduce_scatter | solution.py:87
  188.8 3.3 copy-start.10
  188.8 3.3 copy-start.12
  190.0 4.3 copy-start.6
  192.1 3.6 copy-start.1
  192.1 3.6 copy-start.14
  323.7 15.3 %copy-start.24 = (bf16[1024,2048]{1,0:T(8,128)(2,1)S(1)}, bf16[1024,2048]{1,0:T(8,128)(2,1)}, u32[]{:S(2)}) copy-start(bf16[1024,2048]{1,0:T(8,128)(2,1)} %all-gather.8.cloned.1.call-done) | copy-start | bytes 12582916
  345.1 163.7 %reduce-scatter.8.cloned.1.call-start = ((), (), s32[]{:S(2)}) async-start(), calls=%async_computation.9 | async-start | bytes 10485760 | tf_op jit(solution)/shard_map/reduce_scatter | solution.py:87
  359.6 284.9 %reduce-scatter.14.cloned.1.call-start = ((), (), s32[]{:S(2)}) async-start(), calls=%async_computation.12 | async-start | bytes 5242880 | tf_op jit(solution)/shard_map/reduce_scatter | solution.py:87
  369.1 278.1 %reduce-scatter.10.cloned.1.call-start = ((), (), s32[]{:S(2)}) async-start(), calls=%async_computation.10 | async-start | bytes 3932160 | tf_op jit(solution)/shard_map/reduce_scatter | solution.py:87
  447.0 6.5 copy-start.2
  473.7 6.6 copy-start.15
  480.3 6.4 copy-start.13
  489.3 3.0 copy-start.7
  489.3 3.1 copy-start.16
  492.5 3.2 copy-start.23
  500.6 190.5 %reduce-scatter.12.cloned.1.call-start = ((), (), s32[]{:S(2)}) async-start(), calls=%async_computation.11 | async-start | bytes 1310720 | tf_op jit(solution)/shard_map/reduce_scatter | solution.py:87
  685.0 4.4 copy-start.8
  685.0 4.4 copy-start.18
  685.0 4.4 copy-start.20
  685.0 4.7 copy-start.5
  (12 other events, 19.6 us)
Sparse Core Ops, SparseCore 0:
  11.0 124.7 all-gather.3
  177.3 91.8 all-gather.5
  271.1 52.5 all-gather.7
  345.2 48.6 reduce-scatter.5
  396.8 88.2 reduce-scatter.7
  487.9 52.5 reduce-scatter.13
  543.4 43.8 reduce-scatter.9
  644.5 32.6 reduce-scatter.11

commit v3 on v2

--- a/solution.py
+++ b/solution.py
@@ -85,19 +85,6 @@
 
 def scatter(values, axes):
     return lax.psum_scatter(values, axes, scatter_dimension=0, tiled=True)
-
-
-def by_part(weight, outer, parts):
-    rows, columns = weight.shape
-    inner = columns // (outer * parts)
-    pieces = weight.reshape(rows, outer, parts, inner).transpose(2, 0, 1, 3)
-    return pieces.reshape(parts, rows, outer * inner)
-
-
-def from_parts(pieces, outer):
-    parts, rows, columns = pieces.shape
-    pieces = pieces.reshape(parts, rows, outer, columns // outer).transpose(1, 2, 0, 3)
-    return pieces.reshape(rows, parts * columns).astype(jnp.float32)
 
 
 def enter(axes):
@@ -128,12 +115,20 @@
         ]
 
     def run(self, src, dst, send, recv, local):
-        me = lax.axis_index("ctx")
+        place = lax.axis_index("ctx")
+        me = lax.rem(place, self.parts)
         copies = []
         for step in range(1, self.parts):
             peer = lax.rem(me + step, self.parts)
             copies.append(
-                remote(src.at[peer], dst.at[me], send.at[step - 1], recv.at[step - 1], "ctx", peer)
+                remote(
+                    src.at[peer],
+                    dst.at[me],
+                    send.at[step - 1],
+                    recv.at[step - 1],
+                    "ctx",
+                    place - me + peer,
+                )
             )
             copies[-1].start()
         own = pltpu.make_async_copy(src.at[me], dst.at[me], local)
@@ -141,6 +136,7 @@
         yield
         for copy in copies:
             copy.wait()
+            yield
         own.wait()
 
 
@@ -219,27 +215,31 @@
 
 
 class Scatter:
+    cuts = 2
+
     def __init__(self, parts, shape):
         self.parts, self.shape = parts, shape
         self.out = jax.ShapeDtypeStruct(shape, jnp.float32)
         chips = parts // 2
+        piece = (self.cuts, shape[0] // self.cuts, shape[1])
         self.scratch = [
             pltpu.VMEM((chips,) + shape, LOW),
-            pltpu.VMEM((2, chips) + shape, LOW),
-            pltpu.VMEM((chips,) + shape, LOW),
+            pltpu.VMEM((2, chips) + piece, LOW),
+            pltpu.VMEM((chips,) + piece, LOW),
             pltpu.SemaphoreType.DMA((chips,)),
             pltpu.SemaphoreType.DMA((chips,)),
-            pltpu.SemaphoreType.DMA((chips,)),
-            pltpu.SemaphoreType.DMA((2, chips)),
+            pltpu.SemaphoreType.DMA((chips, self.cuts)),
+            pltpu.SemaphoreType.DMA((2, chips, self.cuts)),
         ]
 
     def run(self, src, out, pair, come, stage, pair_send, pair_recv, send, recv):
-        chips = self.parts // 2
+        chips, cuts = self.parts // 2, self.cuts
         me = lax.axis_index("ctx")
         chip, core = me // 2, lax.rem(me, 2)
         partner = me + 1 - 2 * core
-        rows = self.shape[0]
+        rows = self.shape[0] // cuts
         slab = min(rows, 16)
+        last = chips - 1
 
         def across(goal):
             return remote(
@@ -251,12 +251,12 @@
                 partner,
             )
 
-        def line(goal, way):
+        def line(goal, cut, way):
             return remote(
-                stage.at[goal],
-                come.at[way, goal],
-                send.at[goal],
-                recv.at[way, goal],
+                stage.at[goal, cut],
+                come.at[way, goal, cut],
+                send.at[goal, cut],
+                recv.at[way, goal, cut],
                 "ctx",
                 me + 2 - 4 * way,
             )
@@ -266,34 +266,42 @@
 
         def slabs(part):
             def one(index, carry):
-                part(pl.ds(pl.multiple_of(index * slab, slab), slab))
+                part(pl.multiple_of(index * slab, slab))
                 return carry
 
             lax.fori_loop(0, rows // slab, one, 0)
+
+        def both(goal, cut, at):
+            at = pl.ds(cut * rows + at, slab)
+            return wide(src, 2 * goal + core, at) + wide(pair, goal, at)
 
         order = []
         for step in range((chips + 1) // 2):
-            order += sorted({step, chips - 1 - step})
+            order += sorted({step, last - step})
         for goal in order:
             across(goal).start()
         yield
-        for step in range(chips - 1):
+        for step in range(last * cuts):
             for way in range(2):
-                goal = chips - 1 - step if way == 0 else step
-                first = (chip == 0) if way == 0 else (chip == chips - 1)
+                turn = step - (chip if way == 0 else last - chip)
+                goal = (last - turn // cuts) if way == 0 else turn // cuts
+                cut = step - (chip if way == 0 else last - chip) - (turn // cuts) * cuts
+                first = (chip == 0) if way == 0 else (chip == last)
+                ahead = last - chip if way == 0 else chip
 
                 def begin(at):
-                    value = wide(src, 2 * goal + core, at) + wide(pair, goal, at)
-                    stage[goal, at, :] = value.astype(LOW)
+                    value = both(goal, cut, at)
+                    stage[goal, cut, pl.ds(at, slab), :] = value.astype(LOW)
 
                 def middle(at):
-                    value = wide(src, 2 * goal + core, at) + wide(pair, goal, at)
-                    value += wide(come, way, goal, at)
-                    stage[goal, at, :] = value.astype(LOW)
-
-                @pl.when((chip < goal) if way == 0 else (chip > goal))
+                    value = both(goal, cut, at) + wide(come, way, goal, cut, pl.ds(at, slab))
+                    stage[goal, cut, pl.ds(at, slab), :] = value.astype(LOW)
+
+                @pl.when((turn >= 0) & (turn < ahead * cuts))
                 def _():
-                    across(goal).wait_recv()
+                    @pl.when(cut == 0)
+                    def _():
+                        across(goal).wait_recv()
 
                     @pl.when(first)
                     def _():
@@ -301,27 +309,32 @@
 
                     @pl.when(jnp.logical_not(first))
                     def _():
-                        line(goal, way).wait_recv()
+                        line(goal, cut, way).wait_recv()
                         slabs(middle)
 
-                    line(goal, way).start()
+                    line(goal, cut, way).start()
 
             yield
-
-        def own(at):
-            out[at, :] = wide(src, me, at) + wide(pair, chip, at)
-
         across(chip).wait_recv()
-        slabs(own)
-        for way in range(2):
-
-            def last(at):
-                out[at, :] += wide(come, way, chip, at)
-
-            @pl.when((chip > 0) if way == 0 else (chip < chips - 1))
-            def _():
-                line(chip, way).wait_recv()
-                slabs(last)
+        for cut in range(cuts):
+
+            def own(at):
+                out[pl.ds(cut * rows + at, slab), :] = both(chip, cut, at)
+
+            slabs(own)
+        yield
+        for cut in range(cuts):
+            for way in range(2):
+
+                def final(at):
+                    out[pl.ds(cut * rows + at, slab), :] += wide(
+                        come, way, chip, cut, pl.ds(at, slab)
+                    )
+
+                @pl.when((chip > 0) if way == 0 else (chip < last))
+                def _():
+                    line(chip, cut, way).wait_recv()
+                    slabs(final)
 
             yield
         for goal in range(chips):
@@ -329,7 +342,8 @@
 
             @pl.when(chip != goal)
             def _():
-                line(goal, 0).wait_send()
+                for cut in range(cuts):
+                    line(goal, cut, 0).wait_send()
 
 
 class Spread:
@@ -394,17 +408,29 @@
         own.wait()
 
 
-def call(jobs, operands, name, identity, axes, body=None):
+def call(jobs, operands, name, identity, axes, work=None):
     counts = [len(job.scratch) for job in jobs]
+    jobs_n = len(jobs)
+    extra = work.operands if work else []
+    extra_out = work.outs if work else []
+    extra_scratch = work.scratch if work else []
 
     def kernel(*refs):
-        n = len(jobs)
-        ins, outs, rest = refs[:n], refs[n : 2 * n], refs[2 * n :]
+        refs = list(refs)
+
+        def take(count):
+            taken = refs[:count]
+            del refs[:count]
+            return taken
+
+        ins, more = take(jobs_n), take(len(extra))
+        outs, more_outs = take(jobs_n), take(len(extra_out))
+        runs = []
+        for job, src, dst, count in zip(jobs, ins, outs, counts):
+            runs.append(job.run(src, dst, *take(count)))
+        if work:
+            runs.append(work.run(*more, *more_outs, *refs))
         enter(axes)
-        runs, at = [], 0
-        for job, src, dst, count in zip(jobs, ins, outs, counts):
-            runs.append(job.run(src, dst, *rest[at : at + count]))
-            at += count
         while runs:
             going = []
             for run in runs:
@@ -416,17 +442,104 @@
             runs = going
 
     vmem = pl.BlockSpec(memory_space=pltpu.VMEM)
+    anywhere = pl.BlockSpec(memory_space=pl.ANY)
     return pl.pallas_call(
         kernel,
-        out_shape=tuple(job.out for job in jobs),
-        in_specs=[vmem] * len(jobs),
-        out_specs=(vmem,) * len(jobs),
-        scratch_shapes=[shape for job in jobs for shape in job.scratch],
+        out_shape=tuple(job.out for job in jobs) + tuple(extra_out),
+        in_specs=[vmem] * jobs_n + [anywhere] * len(extra),
+        out_specs=(vmem,) * jobs_n + (anywhere,) * len(extra_out),
+        scratch_shapes=[shape for job in jobs for shape in job.scratch] + list(extra_scratch),
         compiler_params=pltpu.CompilerParams(
-            collective_id=identity, has_side_effects=True, vmem_limit_bytes=60 << 20
+            collective_id=identity, has_side_effects=True, vmem_limit_bytes=62 << 20
         ),
         name=name,
-    )(*operands)
+    )(*operands, *extra)
+
+
+class Grads:
+    tile = 256
+
+    def __init__(self, pairs):
+        self.pairs = pairs
+        length, wide = pairs[0][0].shape[0], max(right.shape[1] for _, right in pairs)
+        self.operands = [array for pair in pairs for array in pair]
+        self.outs = [jax.ShapeDtypeStruct((l.shape[1], r.shape[1]), LOW) for l, r in pairs]
+        self.scratch = [pltpu.VMEM(array.shape, LOW) for array in self.operands]
+        self.scratch += [
+            pltpu.VMEM((self.tile, length), LOW),
+            pltpu.VMEM((2, self.tile, wide), LOW),
+            pltpu.SemaphoreType.DMA((2 * len(pairs),)),
+            pltpu.SemaphoreType.DMA((2,)),
+        ]
+
+    def run(self, *refs):
+        n, tile = len(self.pairs), self.tile
+        sources, outs = refs[: 2 * n], refs[2 * n : 3 * n]
+        held = refs[3 * n : 5 * n]
+        turned, made, get, put = refs[5 * n :]
+        gets = [pltpu.make_async_copy(s, h, get.at[i]) for i, (s, h) in enumerate(zip(sources, held))]
+        for copy in gets:
+            copy.start()
+        yield
+        puts = []
+        for which in range(n):
+            left, right, out = held[2 * which], held[2 * which + 1], outs[which]
+            gets[2 * which].wait()
+            gets[2 * which + 1].wait()
+            columns = right.shape[1]
+            step = min(columns, 512)
+            for at in range(0, left.shape[1], tile):
+                slot = len(puts) % 2
+                if len(puts) >= 2:
+                    puts[-2].wait()
+                turned[...] = left[:, at : at + tile].T
+
+                def one(index, carry):
+                    where = pl.ds(pl.multiple_of(index * step, step), step)
+                    made[slot, :, where] = jnp.dot(
+                        turned[...], right[:, where], preferred_element_type=jnp.float32
+                    ).astype(LOW)
+                    return carry
+
+                lax.fori_loop(0, columns // step, one, 0)
+                part = made.at[slot] if columns == made.shape[2] else made.at[slot, :, :columns]
+                puts.append(pltpu.make_async_copy(part, out.at[at : at + tile, :], put.at[slot]))
+                puts[-1].start()
+                yield
+        for copy in puts[-2:]:
+            copy.wait()
+
+
+class Plan:
+    def __init__(self, parts, groups, width):
+        self.parts, self.groups = parts, groups
+        self.shard = width // (parts * groups)
+        self.run = HEAD_DIM // self.shard
+        self.heads = HEADS // parts
+        self.qkv_dims = (3, self.run, self.heads, parts // self.run, HEAD_DIM)
+
+    def qkv_pieces(self, weight):
+        rows = weight.shape[0]
+        pieces = weight.reshape((rows,) + self.qkv_dims).transpose(4, 2, 0, 1, 3, 5)
+        return pieces.reshape(self.parts, rows, 3 * self.heads * HEAD_DIM)
+
+    def qkv_rows(self, pieces):
+        parts, rows, columns = pieces.shape
+        runs = parts // self.run
+        pieces = pieces.reshape(runs, self.run, rows, 3, self.heads, HEAD_DIM)
+        return pieces.transpose(2, 3, 1, 4, 0, 5).reshape(rows, parts * columns).astype(jnp.float32)
+
+    def unit_pieces(self, weight):
+        rows, columns = weight.shape
+        inner = columns // (2 * self.groups * self.parts)
+        pieces = weight.reshape(rows, 2 * self.groups, self.parts, inner).transpose(2, 0, 1, 3)
+        return pieces.reshape(self.parts, rows, 2 * self.groups * inner)
+
+    def unit_rows(self, pieces):
+        parts, rows, columns = pieces.shape
+        outer = 2 * self.groups
+        pieces = pieces.reshape(parts, rows, outer, columns // outer).transpose(1, 2, 0, 3)
+        return pieces.reshape(rows, parts * columns).astype(jnp.float32)
 
 
 def per_device(tokens, w_qkv, w_out, w_gate_up, w_down, seq_lengths, block_order, cotangent):
@@ -436,34 +549,39 @@
     groups = lax.axis_size("fsdp")
     rows, width = tokens.shape
     length = rows * parts
-    heads = HEADS // parts
+    plan = Plan(parts, groups, width)
+    heads, shard, run = plan.heads, plan.shard, plan.run
     head_width = heads * HEAD_DIM
     score_scale = HEAD_DIM ** (-0.5)
-
     line = (("ctx", parts),)
     plane = (("ctx", parts), ("fsdp", groups))
     block = (rows, width)
 
-    out_full = gather(w_out, ("fsdp", "ctx"))
+    out_rows = gather(w_out, "fsdp")
     down_rows = gather(w_down, "fsdp")
+    gate_up_pieces = plan.unit_pieces(w_gate_up)
+    (gate_up_cols,) = call(
+        [Exchange(parts, gate_up_pieces.shape[1:])], [gate_up_pieces], "units", 1, line
+    )
+    gate_up_cols = gather(gate_up_cols.reshape(width // groups, -1), "fsdp")
     inputs = tokens.astype(jnp.float32)
     normed_in, root_in = normalize(inputs)
-    qkv_pieces = by_part(w_qkv, 3, parts)
-    gate_up_pieces = by_part(w_gate_up, 2 * groups, parts)
-    qkv_cols, normed_in_full, gate_up_cols = call(
+    qkv_pieces = plan.qkv_pieces(w_qkv)
+    qkv_cols, normed_in_full, out_cols = call(
         [
             Spread(parts, groups, qkv_pieces.shape[1:]),
             Gather(parts, block),
-            Exchange(parts, gate_up_pieces.shape[1:]),
+            Exchange(run, (heads * shard, width)),
         ],
-        [qkv_pieces, normed_in.astype(LOW), gate_up_pieces],
+        [qkv_pieces, normed_in.astype(LOW), out_rows.reshape(run, heads * shard, width)],
         "start",
-        1,
+        2,
         plane,
     )
     qkv_cols = qkv_cols.reshape(width, 3 * head_width)
     normed_in_full = normed_in_full.reshape(length, width)
-    gate_up_cols = gather(gate_up_cols.reshape(width // groups, -1), "fsdp")
+    out_cols = out_cols.reshape(run, heads, shard, width).transpose(1, 0, 2, 3)
+    out_cols = out_cols.reshape(head_width, width)
 
     row_index = jnp.arange(length, dtype=jnp.int32)
     seq, pos = places(initial_index(row_index, order_row), lengths)
@@ -485,23 +603,21 @@
     mixed = jnp.einsum("hqk,khd->qhd", weights.astype(LOW), values, preferred_element_type=jnp.float32)
     log_total = row_max + jnp.log(row_total)
     attn_heads = mixed / jnp.transpose(row_total)[..., None]
-
-    mix_pieces = attn_heads.astype(LOW).reshape(parts, rows, head_width)
-    (mix_pieces,) = call(
-        [Exchange(parts, mix_pieces.shape[1:])], [mix_pieces], "mix", 2, line
-    )
-    mix_low = mix_pieces.transpose(1, 0, 2).reshape(rows, width)
-    residual = inputs + dot(mix_low, out_full)
-    normed_mid, root_mid = normalize(residual)
-    normed_mid_full, cot_full = call(
-        [Gather(parts, block), Gather(parts, block)],
-        [normed_mid.astype(LOW), cotangent],
-        "mid",
+    mix_low = attn_heads.astype(LOW).reshape(length, head_width)
+
+    out_terms = dot(mix_low, out_cols).astype(LOW)
+    attn_out, cot_full = call(
+        [Scatter(parts, block), Gather(parts, block)],
+        [out_terms.reshape((parts,) + block), cotangent],
+        "out",
         3,
         line,
     )
+    cot_full = cot_full.reshape(length, width)
+    residual = inputs + attn_out
+    normed_mid, root_mid = normalize(residual)
+    (normed_mid_full,) = call([Gather(parts, block)], [normed_mid.astype(LOW)], "mid", 4, line)
     normed_mid_full = normed_mid_full.reshape(length, width)
-    cot_full = cot_full.reshape(length, width)
 
     gate_up = dot(normed_mid_full, gate_up_cols)
     units = gate_up.shape[1] // 2
@@ -510,35 +626,36 @@
     sigmoid_gate = jax.nn.sigmoid(gate_part)
     silu_gate = gate_part * sigmoid_gate
     activated = (silu_gate * up_part).astype(LOW)
-    down_out = scatter(dot(activated, down_rows).astype(LOW), "ctx")
-    layer_out = (residual + down_out.astype(jnp.float32)).astype(LOW)
-
-    down_grad = scatter(column_product(activated, cot_full).astype(LOW), "fsdp").astype(jnp.float32)
-
     act_grad = times_transposed(cot_full, down_rows)
     gate_grad = act_grad * up_part * sigmoid_gate * (1.0 + gate_part * (1.0 - sigmoid_gate))
     up_grad = act_grad * silu_gate
     gate_up_back = jnp.concatenate([gate_grad, up_grad], axis=1).astype(LOW)
     mid_back_terms = times_transposed(gate_up_back, gate_up_cols).astype(LOW)
-    gate_up_grad = scatter(column_product(normed_mid_full, gate_up_back).astype(LOW), "fsdp")
-
-    (mid_back,) = call(
+    mid_back, gate_up_grad, down_grad = call(
         [Scatter(parts, block)],
         [mid_back_terms.reshape((parts,) + block)],
         "mid_back",
-        4,
+        5,
         line,
-    )
+        Grads([(normed_mid_full, gate_up_back), (activated, cot_full)]),
+    )
+    gate_up_grad = scatter(gate_up_grad, "fsdp")
+    down_grad = scatter(down_grad, "fsdp").astype(jnp.float32)
     residual_back = cotangent.astype(jnp.float32) + norm_back(mid_back, normed_mid, root_mid)
     proj_back = residual_back.astype(LOW)
-    mix_back = times_transposed(proj_back, out_full).astype(LOW)
-
-    back_pieces = mix_back.reshape(rows, parts, head_width).transpose(1, 0, 2)
-    (back_pieces,) = call(
-        [Exchange(parts, back_pieces.shape[1:])], [back_pieces], "mix_back", 5, line
-    )
-    back_heads = back_pieces.reshape(head_shape)
-
+
+    down_terms = dot(activated, down_rows).astype(LOW)
+    proj_back_full, down_out = call(
+        [Gather(parts, block), Scatter(parts, block)],
+        [proj_back, down_terms.reshape((parts,) + block)],
+        "proj_back",
+        6,
+        line,
+    )
+    layer_out = (residual + down_out).astype(LOW)
+    proj_back_full = proj_back_full.reshape(length, width)
+
+    back_heads = times_transposed(proj_back_full, out_cols).astype(LOW).reshape(head_shape)
     delta = jnp.einsum("qhd,qhd->hq", back_heads.astype(jnp.float32), attn_heads)
     probs = jnp.where(allowed, jnp.exp(scores - log_total[..., None]), 0.0)
     value_back = jnp.einsum(
@@ -556,48 +673,40 @@
         ],
         axis=1,
     ).astype(LOW)
+    qkv_grad = scatter(column_product(normed_in_full, qkv_back).astype(LOW), "fsdp")
     in_back_terms = times_transposed(qkv_back, qkv_cols).astype(LOW)
-    qkv_grad = scatter(column_product(normed_in_full, qkv_back).astype(LOW), "fsdp")
-    shard = width // (parts * groups)
-    mix_columns = mix_low.reshape(rows, groups, parts, shard).transpose(2, 0, 1, 3)
-    in_back, proj_back_full, mix_columns, gate_up_grad = call(
+    out_grad = column_product(mix_low, proj_back_full).astype(LOW)
+    out_grad = out_grad.reshape(heads, run, shard, width).transpose(1, 0, 2, 3)
+    in_back, out_grad, gate_up_grad = call(
         [
             Scatter(parts, block),
-            Gather(parts, block),
-            Exchange(parts, (rows, groups * shard)),
+            Exchange(run, (heads * shard, width)),
             Exchange(parts, gate_up_pieces.shape[1:]),
         ],
         [
             in_back_terms.reshape((parts,) + block),
-            proj_back,
-            mix_columns.reshape(parts, rows, groups * shard),
+            out_grad.reshape(run, heads * shard, width),
             gate_up_grad.reshape(gate_up_pieces.shape),
         ],
         "in_back",
-        6,
+        7,
         line,
     )
-    out_grad = scatter(
-        column_product(
-            mix_columns.reshape(length, groups * shard), proj_back_full.reshape(length, width)
-        ).astype(LOW),
-        "fsdp",
-    )
+    out_grad = scatter(out_grad.reshape(groups * shard, width), "fsdp").astype(jnp.float32)
     tokens_grad = residual_back + norm_back(in_back, normed_in, root_in)
     (qkv_grad,) = call(
         [Exchange(parts, qkv_pieces.shape[1:])],
         [qkv_grad.reshape(qkv_pieces.shape)],
         "last",
-        7,
+        8,
         line,
     )
-
     return (
         layer_out,
         tokens_grad,
-        from_parts(qkv_grad, 3),
-        out_grad.astype(jnp.float32),
-        from_parts(gate_up_grad, 2 * groups),
+        plan.qkv_rows(qkv_grad),
+        out_grad,
+        plan.unit_rows(gate_up_grad),
         down_grad,
     )
 

time: 704 us -> 653 us (0.928)
  matrix products: 125 us -> 89 us
  Pallas kernels: 493 us -> 482 us
    dot_general x4 -> x2, matrix products: 33.4 us -> 8.5 us  [column_product(): lax.dot_general(left, right, (((0,), (0,)), ((), ())), preferred_element_...]
    pallas_call x7 -> x8, Pallas kernels: 493 us -> 482 us  [call(): pl.pallas_call(kernel, out_shape=tuple((job.out for job in jobs)) + tuple...]
    dot_general x4, matrix products: 42.2 us -> 32.9 us  [times_transposed(): lax.dot_general(left, right, (((1,), (1,)), ((), ())), preferred_element_...]
    unnamed x63 -> x83, local copies, waits for them, and re-layouts: 17.4 us -> 16.4 us
  transfers between devices with their start and end apart: 8 -> 7, of which waited for: 1 -> 0; matrix products, arithmetic and copies ran while one was open for 23% -> 17% of each run, Pallas kernels for 70% -> 66%
where the time goes in v3:
time: 653 us; the launch traced here: 649 us
  Pallas kernels  482 us (74%)
  matrix products  89 us (14%)
  local copies, waits for them, and re-layouts  32.9 us (5%)
  other arithmetic  27.3 us (4%)
  between operations  15.3 us (2%)
    pallas_call x8, Pallas kernels, call(): pl.pallas_call(kernel, out_shape=tuple((job.out for job in jobs)) + tuple...  482 us
    dot_general x4, matrix products, times_transposed(): lax.dot_general(left, right, (((1,), (1,)), ((), ())), preferred_element_...  32.9 us
    dot_general x4, matrix products, dot(): return jnp.dot(left, right, preferred_element_type=jnp.float32)  30.1 us
    unnamed x83, local copies, waits for them, and re-layouts  16.4 us
  transfers between devices with their start and end apart: 7, of which 0 were waited for; matrix products, arithmetic and copies ran while one was open for 17% of the time, Pallas kernels for 66%

profile of v3, /device:TPU:9, one launch (start us, length us, event | category | flops | bytes accessed | tf_op | source)
XLA Modules:
  0.0 648.7 jit_solution(8074166421794645681)
XLA Ops:
  12.9 52.2 %units.1 = bf16[8,64,2048]{2,1,0:T(8,128)(2,1)} custom-call(bf16[8,64,2048]{2,1,0:T(8,128)(2,1)} %reshape.374.refs_0_), custom_call_target="tpu_custom_call" | custom-call | tf_op jit(solution)/shard_map/units/pallas_call | solution.py:446
  74.5 93.3 %start.1 = (bf16[4,8,64,768]{3,2,1,0:T(8,128)(2,1)}, bf16[8,128,2048]{2,1,0:T(8,128)(2,1)}, bf16[2,128,2048]{2,1,0:T(8,128)(2,1)}) custom-call(bf16[8,64,768]{2,1,0:T(8,128)(2,1)} %reshape.358.refs_0_, bf16[128,2048]{1,0:T(8,128)(2,1)} %fusion.21.refs_1_, bf16[2,128,2048]{2,1,0:T(8,128)(2,1)} %bitcast.131), custom_call_target="tpu_custom_call" | custom-call | tf_op jit(solution)/shard_map/start/pallas_call | solution.py:446
  167.9 6.2 fusion.69
  182.3 3.7 fusion.68
  186.0 3.3 convolution_convert_fusion.1
  189.3 69.4 %out.1 = (f32[128,2048]{1,0:T(8,128)}, bf16[8,128,2048]{2,1,0:T(8,128)(2,1)}) custom-call(bf16[8,128,2048]{2,1,0:T(8,128)(2,1)} %bitcast.101, bf16[128,2048]{1,0:T(8,128)(2,1)} %refs_1_.1), custom_call_target="tpu_custom_call" | custom-call | tf_op jit(solution)/shard_map/out/pallas_call | solution.py:446
  261.4 41.0 %mid.1 = bf16[8,128,2048]{2,1,0:T(8,128)(2,1)} custom-call(bf16[128,2048]{1,0:T(8,128)(2,1)} %fusion.37.refs_0_), custom_call_target="tpu_custom_call" | custom-call | tf_op jit(solution)/shard_map/mid/pallas_call | solution.py:446
  302.4 14.6 %fusion.70 = f32[1024,2048]{1,0:T(8,128)} fusion(bf16[1024,2048]{1,0:T(8,128)(2,1)} %bitcast.104, bf16[2048,2048]{1,0:T(8,128)(2,1)} %all-gather.8.cloned.1.call-done), kind=kOutput, calls=%fused_computation.124 | convolution fusion | flops 8589934592 | bytes 20971520 | tf_op jit(solution)/shard_map/dot_general | solution.py:67
  317.0 13.1 %multiply_convert_fusion.3 = (bf16[1024,1024]{1,0:T(8,128)(2,1)S(1)}, bf16[1024,1024]{1,0:T(8,128)(2,1)S(1)}, bf16[1024,1024]{1,0:T(8,128)(2,1)}) fusion(f32[1024,2048]{1,0:T(8,128)} %fusion.70, bf16[1024,2048]{1,0:T(8,128)(2,1)} %bitcast.120, bf16[1024,2048]{1,0:T(8,128)(2,1)} %all-gather.6.cloned.1.call-done), kind=kOutput, calls=%fused_computation.12 | convolution fusion | flops 4310695936 | bytes 23068672 | tf_op jit(solution)/shard_map/dot_general | solution.py:71
  335.0 10.5 %convolution_convert_fusion = bf16[1024,2048]{1,0:T(8,128)(2,1)} fusion(bf16[2048,2048]{1,0:T(8,128)(2,1)S(1)} %copy-done.32, bf16[1024,1024]{1,0:T(8,128)(2,1)S(1)} %get-tuple-element.43, bf16[1024,1024]{1,0:T(8,128)(2,1)S(1)} %get-tuple-element.42), kind=kOutput, calls=%fused_computation.20 | convolution fusion | flops 8600420352 | bytes 16777216 | tf_op jit(solution)/shard_map/dot_general | solution.py:71
  345.6 56.8 %mid_back.1 = (f32[128,2048]{1,0:T(8,128)}, bf16[2048,2048]{1,0:T(8,128)(2,1)}, bf16[1024,2048]{1,0:T(8,128)(2,1)}) custom-call(bf16[8,128,2048]{2,1,0:T(8,128)(2,1)} %bitcast.122, bf16[1024,2048]{1,0:T(8,128)(2,1)} %bitcast.105, bf16[1024,2048]{1,0:T(8,128)(2,1)} %pad_maximum_fusion.refs_2_, bf16[1024,1024]{1,0:T(8,128)(2,1)} %get-tuple-element.44.refs_3_, ...), custom_call_target="tpu_custom_call" | custom-call | tf_op jit(solution)/shard_map/mid_back/pallas_call | solution.py:446
  403.9 3.3 fusion.61
  407.2 6.0 convolution_convert_fusion.3
  413.2 67.9 %proj_back.1 = (bf16[8,128,2048]{2,1,0:T(8,128)(2,1)}, f32[128,2048]{1,0:T(8,128)}) custom-call(bf16[128,2048]{1,0:T(8,128)(2,1)} %get-tuple-element.36.refs_0_, bf16[8,128,2048]{2,1,0:T(8,128)(2,1)} %bitcast.118), custom_call_target="tpu_custom_call" | custom-call | tf_op jit(solution)/shard_map/proj_back/pallas_call | solution.py:446
  481.1 4.2 fusion.33
  485.4 6.3 multiply_convert_fusion
  497.1 3.0 fusion.14
  500.9 4.9 convolution_convert_fusion.4
  506.9 3.6 convolution_convert_fusion.5
  511.5 5.0 convolution_convert_fusion.2
  516.6 77.6 %in_back.1 = (f32[128,2048]{1,0:T(8,128)}, bf16[2,128,2048]{2,1,0:T(8,128)(2,1)}, bf16[8,64,2048]{2,1,0:T(8,128)(2,1)}) custom-call(bf16[8,128,2048]{2,1,0:T(8,128)(2,1)} %bitcast.116, bf16[2,128,2048]{2,1,0:T(8,128)(2,1)} %bitcast.117, bf16[8,64,2048]{2,1,0:T(8,128)(2,1)} %bitcast.126), custom_call_target="tpu_custom_call" | custom-call | tf_op jit(solution)/shard_map/in_back/pallas_call | solution.py:446
  596.3 23.8 %last.1 = bf16[8,64,768]{2,1,0:T(8,128)(2,1)} custom-call(bf16[8,64,768]{2,1,0:T(8,128)(2,1)} %bitcast.135), custom_call_target="tpu_custom_call" | custom-call | tf_op jit(solution)/shard_map/last/pallas_call | solution.py:446
  624.3 3.1 reshape.389
  633.5 4.4 copy.83
  (159 shorter events, 56.2 us)
Async XLA Ops:
  7.2 67.4 %all-gather.4.cloned.1.call-start = ((), (), s32[]{:S(2)}) async-start(), calls=%async_computation.4 | async-start | bytes 1310720 | tf_op jit(solution)/shard_map/all_gather | solution.py:83
  7.9 294.5 %all-gather.8.cloned.1.call-start = ((), (), s32[]{:S(2)}) async-start(), calls=%async_computation.6 | async-start | bytes 10485760 | tf_op jit(solution)/shard_map/all_gather | solution.py:83
  12.9 53.0 %copy-start = (bf16[128,2048]{1,0:T(8,128)(2,1)S(1)}, bf16[128,2048]{1,0:T(8,128)(2,1)}, u32[]{:S(2)}) copy-start(bf16[128,2048]{1,0:T(8,128)(2,1)} %param.8) | copy-start | bytes 1572868
  12.9 53.5 %copy-start.30 = (s32[1,8]{1,0:T(1,128)S(1)}, s32[1,8]{1,0:T(1,128)}, u32[]{:S(2)}) copy-start(s32[1,8]{1,0:T(1,128)} %param.14) | copy-start | bytes 100
  12.9 53.6 %copy-start.31 = (s32[1,2]{1,0:T(1,128)S(1)}, s32[1,2]{1,0:T(1,128)}, u32[]{:S(2)}) copy-start(s32[1,2]{1,0:T(1,128)} %param.13) | copy-start | bytes 28
  12.9 55.1 %copy-start.21 = (bf16[64,6144]{1,0:T(8,128)(2,1)S(1)}, bf16[64,6144]{1,0:T(8,128)(2,1)}, u32[]{:S(2)}) copy-start(bf16[64,6144]{1,0:T(8,128)(2,1)} %param.9) | copy-start | bytes 2359300
  65.1 251.9 %all-gather.6.cloned.1.call-start = ((), (), s32[]{:S(2)}) async-start(), calls=%async_computation.5 | async-start | bytes 5242880 | tf_op jit(solution)/shard_map/all_gather | solution.py:83
  65.8 450.8 %reduce-scatter.5.cloned.1.call-start = ((), (), s32[]{:S(2)}) async-start(), calls=%async_computation.7 | async-start | bytes 10485760 | tf_op jit(solution)/shard_map/reduce_scatter | solution.py:87
  72.6 102.9 %copy-start.1 = (f32[1024,128]{0,1:T(8,128)}, f32[1024,128]{0,1:T(8,128)S(1)}, u32[]{:S(2)}) copy-start(f32[1024,128]{0,1:T(8,128)S(1)} %get-tuple-element.62) | copy-start | bytes 1572868
  72.6 102.9 %copy-start.4 = (f32[1024,128]{0,1:T(8,128)}, f32[1024,128]{0,1:T(8,128)S(1)}, u32[]{:S(2)}) copy-start(f32[1024,128]{0,1:T(8,128)S(1)} %get-tuple-element.61) | copy-start | bytes 1572868
  174.6 6.7 %copy-start.22 = (bf16[1024,256]{0,1:T(8,128)(2,1)}, bf16[1024,256]{0,1:T(8,128)(2,1)S(1)}, u32[]{:S(2)}) copy-start(bf16[1024,256]{0,1:T(8,128)(2,1)S(1)} %slice.79) | copy-start | bytes 1572868
  175.4 10.6 %copy-start.11 = (bf16[2,2,64,2048]{3,2,0,1:T(8,128)(2,1)}, bf16[2,2,64,2048]{3,2,0,1:T(8,128)(2,1)S(1)}, u32[]{:S(2)}) copy-start(bf16[2,2,64,2048]{3,2,0,1:T(8,128)(2,1)S(1)} %copy.51) | copy-start | bytes 3145732
  330.1 4.9 copy-start.32
  402.4 194.0 %reduce-scatter.7.cloned.1.call-start = ((), (), s32[]{:S(2)}) async-start(), calls=%async_computation.8 | async-start | bytes 3932160 | tf_op jit(solution)/shard_map/reduce_scatter | solution.py:87
  402.4 4.8 copy-start.12
  402.4 4.7 copy-start.34
  485.3 6.3 copy-start.17
  505.9 121.6 %reduce-scatter.11.cloned.1.call-start = ((), (), s32[]{:S(2)}) async-start(), calls=%async_computation.10 | async-start | bytes 5242880 | tf_op jit(solution)/shard_map/reduce_scatter | solution.py:87
  506.4 133.2 %reduce-scatter.9.cloned.1.call-start = ((), (), s32[]{:S(2)}) async-start(), calls=%async_computation.9 | async-start | bytes 1310720 | tf_op jit(solution)/shard_map/reduce_scatter | solution.py:87
  506.9 4.6 copy-start.25
  506.9 4.6 copy-start.35
  506.9 4.6 copy-start.37
  624.3 5.9 copy-start.13
  633.5 4.7 copy-start.9
  (23 other events, 65.5 us)
Sparse Core Ops, SparseCore 0:
  9.8 27.4 all-gather.3
  65.2 121.5 all-gather.7
  188.6 52.5 all-gather.5
  402.5 84.4 reduce-scatter.4
  506.0 43.2 reduce-scatter.6
  552.1 52.5 reduce-scatter.10
  607.6 27.9 reduce-scatter.8

commit v4 on v3

--- a/solution.py
+++ b/solution.py
@@ -394,18 +394,123 @@
             return out
 
         far = pass_on(src.at[me], me, 0)
+        eager = -(-parts // 2)
         yield
         for step in range(1, parts):
             copies[step - 1].wait_recv()
             origin = lax.rem(me - step + parts, parts)
             far += pass_on(dst.at[group, origin], origin, step)
-            yield
-        for copy in far:
+            if step % eager == 0:
+                yield
+        for at, copy in enumerate(far):
             copy.wait()
+            if at % 6 == 5:
+                yield
+        for copy in copies:
+            copy.wait_send()
+        own.wait()
+
+
+class Deliver:
+    def __init__(self, parts, shape, offsets):
+        self.parts, self.shape, self.offsets = parts, shape, offsets
+        self.out = jax.ShapeDtypeStruct((shape[0], parts * shape[1]), jnp.float32)
+        self.scratch = [
+            pltpu.VMEM((parts - 1,) + shape, LOW),
+            pltpu.SemaphoreType.DMA((parts - 1,)),
+            pltpu.SemaphoreType.DMA((parts - 1,)),
+        ]
+
+    def place(self, out, origin, read):
+        starts = self.offsets(origin)
+        step = self.shape[1] // len(starts)
+        for index, start in enumerate(starts):
+            out[:, pl.ds(pl.multiple_of(start, HEAD_DIM), step)] = read(
+                index * step, (index + 1) * step
+            )
+
+    def send(self, me, step, block, came, send, recv):
+        return remote(
+            block,
+            came.at[step - 1],
+            send.at[step - 1],
+            recv.at[step - 1],
+            "ctx",
+            lax.rem(me + step, self.parts),
+        )
+
+    def run(self, src, out, came, send, recv):
+        me = lax.axis_index("ctx")
+        copies = []
+        for step in range(1, self.parts):
+            block = src.at[lax.rem(me + step, self.parts)]
+            copies.append(self.send(me, step, block, came, send, recv))
+            copies[-1].start()
+        self.place(out, me, lambda lo, hi: src[me, :, lo:hi].astype(jnp.float32))
+        yield
+        yield from self.finish(me, out, copies, came)
+
+    def finish(self, me, out, copies, came):
+        for step in range(1, self.parts):
+            copies[step - 1].wait_recv()
+            origin = lax.rem(me - step + self.parts, self.parts)
+            self.place(out, origin, lambda lo, hi: came[step - 1, :, lo:hi].astype(jnp.float32))
             yield
         for copy in copies:
             copy.wait_send()
-        own.wait()
+
+
+class Collect(Deliver):
+    def __init__(self, parts, groups, shape, offsets):
+        super().__init__(parts, shape, offsets)
+        self.groups = groups
+        self.scratch = self.scratch + [
+            pltpu.VMEM((groups - 1, parts) + shape, LOW),
+            pltpu.VMEM((parts,) + shape, LOW),
+            pltpu.VMEM(shape, jnp.float32),
+            pltpu.SemaphoreType.DMA((groups - 1, parts)),
+            pltpu.SemaphoreType.DMA((groups - 1, parts)),
+        ]
+
+    def run(self, src, out, came, send, recv, far, stage, mine, far_send, far_recv):
+        parts, groups = self.parts, self.groups
+        me, group = lax.axis_index("ctx"), lax.axis_index("fsdp")
+        goals = [lax.rem(me + step, parts) for step in range(1, parts + 1)]
+        hops = []
+        for goal in goals:
+            for hop in range(1, groups):
+                peer = lax.rem(group + hop, groups)
+                hops.append(
+                    remote(
+                        src.at[peer, goal],
+                        far.at[hop - 1, goal],
+                        far_send.at[hop - 1, goal],
+                        far_recv.at[hop - 1, goal],
+                        "fsdp",
+                        peer,
+                    )
+                )
+                hops[-1].start()
+        yield
+        copies = []
+        for step in range(1, parts + 1):
+            goal = goals[step - 1]
+            for copy in hops[(step - 1) * (groups - 1) : step * (groups - 1)]:
+                copy.wait_recv()
+            value = src[group, goal].astype(jnp.float32)
+            for hop in range(groups - 1):
+                value += far[hop, goal].astype(jnp.float32)
+            if step < parts:
+                stage[goal] = value.astype(LOW)
+                copies.append(self.send(me, step, stage.at[goal], came, send, recv))
+                copies[-1].start()
+            else:
+                mine[...] = value
+            yield
+        self.place(out, me, lambda lo, hi: mine[:, lo:hi])
+        yield from self.finish(me, out, copies, came)
+        for copy in hops:
+            copy.wait_send()
 
 
 def call(jobs, operands, name, identity, axes, work=None):
@@ -523,11 +628,13 @@
         pieces = weight.reshape((rows,) + self.qkv_dims).transpose(4, 2, 0, 1, 3, 5)
         return pieces.reshape(self.parts, rows, 3 * self.heads * HEAD_DIM)
 
-    def qkv_rows(self, pieces):
-        parts, rows, columns = pieces.shape
-        runs = parts // self.run
-        pieces = pieces.reshape(runs, self.run, rows, 3, self.heads, HEAD_DIM)
-        return pieces.transpose(2, 3, 1, 4, 0, 5).reshape(rows, parts * columns).astype(jnp.float32)
+    def qkv_starts(self, part):
+        at, index = part // self.run, lax.rem(part, self.run)
+        return [
+            (kind * HEADS + (index * self.heads + head) * (self.parts // self.run) + at) * HEAD_DIM
+            for kind in range(3)
+            for head in range(self.heads)
+        ]
 
     def unit_pieces(self, weight):
         rows, columns = weight.shape
@@ -535,7 +642,19 @@
         pieces = weight.reshape(rows, 2 * self.groups, self.parts, inner).transpose(2, 0, 1, 3)
         return pieces.reshape(self.parts, rows, 2 * self.groups * inner)
 
+    def unit_job(self, shape):
+        step = shape[1] // (2 * self.groups)
+        if step % HEAD_DIM:
+            return Exchange(self.parts, shape)
+        return Deliver(
+            self.parts,
+            shape,
+            lambda part: [(at * self.parts + part) * step for at in range(2 * self.groups)],
+        )
+
     def unit_rows(self, pieces):
+        if pieces.ndim == 2:
+            return pieces
         parts, rows, columns = pieces.shape
         outer = 2 * self.groups
         pieces = pieces.reshape(parts, rows, outer, columns // outer).transpose(1, 2, 0, 3)
@@ -560,23 +679,30 @@
     out_rows = gather(w_out, "fsdp")
     down_rows = gather(w_down, "fsdp")
     gate_up_pieces = plan.unit_pieces(w_gate_up)
-    (gate_up_cols,) = call(
-        [Exchange(parts, gate_up_pieces.shape[1:])], [gate_up_pieces], "units", 1, line
-    )
-    gate_up_cols = gather(gate_up_cols.reshape(width // groups, -1), "fsdp")
     inputs = tokens.astype(jnp.float32)
     normed_in, root_in = normalize(inputs)
     qkv_pieces = plan.qkv_pieces(w_qkv)
-    qkv_cols, normed_in_full, out_cols = call(
+    qkv_cols, normed_in_full, gate_up_cols = call(
         [
             Spread(parts, groups, qkv_pieces.shape[1:]),
             Gather(parts, block),
-            Exchange(run, (heads * shard, width)),
+            Exchange(parts, gate_up_pieces.shape[1:]),
         ],
-        [qkv_pieces, normed_in.astype(LOW), out_rows.reshape(run, heads * shard, width)],
+        [qkv_pieces, normed_in.astype(LOW), gate_up_pieces],
         "start",
         2,
         plane,
+    )
+    gate_up_cols, down_rows, out_rows = lax.optimization_barrier(
+        (gate_up_cols, down_rows, out_rows)
+    )
+    gate_up_cols = gather(gate_up_cols.reshape(width // groups, -1), "fsdp")
+    (out_cols,) = call(
+        [Exchange(run, (heads * shard, width))],
+        [out_rows.reshape(run, heads * shard, width)],
+        "swap",
+        1,
+        line,
     )
     qkv_cols = qkv_cols.reshape(width, 3 * head_width)
     normed_in_full = normed_in_full.reshape(length, width)
@@ -630,17 +756,17 @@
     gate_grad = act_grad * up_part * sigmoid_gate * (1.0 + gate_part * (1.0 - sigmoid_gate))
     up_grad = act_grad * silu_gate
     gate_up_back = jnp.concatenate([gate_grad, up_grad], axis=1).astype(LOW)
+    down_grad = scatter(column_product(activated, cot_full).astype(LOW), "fsdp").astype(jnp.float32)
     mid_back_terms = times_transposed(gate_up_back, gate_up_cols).astype(LOW)
-    mid_back, gate_up_grad, down_grad = call(
+    mid_back, gate_up_grad = call(
         [Scatter(parts, block)],
         [mid_back_terms.reshape((parts,) + block)],
         "mid_back",
         5,
         line,
-        Grads([(normed_mid_full, gate_up_back), (activated, cot_full)]),
+        Grads([(normed_mid_full, gate_up_back)]),
     )
     gate_up_grad = scatter(gate_up_grad, "fsdp")
-    down_grad = scatter(down_grad, "fsdp").astype(jnp.float32)
     residual_back = cotangent.astype(jnp.float32) + norm_back(mid_back, normed_mid, root_mid)
     proj_back = residual_back.astype(LOW)
 
@@ -655,6 +781,16 @@
     layer_out = (residual + down_out).astype(LOW)
     proj_back_full = proj_back_full.reshape(length, width)
 
+    out_grad = column_product(mix_low, proj_back_full).astype(LOW)
+    out_grad = out_grad.reshape(heads, run, shard, width).transpose(1, 0, 2, 3)
+    (out_grad,) = call(
+        [Exchange(run, (heads * shard, width))],
+        [out_grad.reshape(run, heads * shard, width)],
+        "swap_back",
+        8,
+        line,
+    )
+    out_grad = scatter(out_grad.reshape(groups * shard, width), "fsdp").astype(jnp.float32)
     back_heads = times_transposed(proj_back_full, out_cols).astype(LOW).reshape(head_shape)
     delta = jnp.einsum("qhd,qhd->hq", back_heads.astype(jnp.float32), attn_heads)
     probs = jnp.where(allowed, jnp.exp(scores - log_total[..., None]), 0.0)
@@ -673,38 +809,28 @@
         ],
         axis=1,
     ).astype(LOW)
-    qkv_grad = scatter(column_product(normed_in_full, qkv_back).astype(LOW), "fsdp")
+    qkv_grad = column_product(normed_in_full, qkv_back).astype(LOW)
     in_back_terms = times_transposed(qkv_back, qkv_cols).astype(LOW)
-    out_grad = column_product(mix_low, proj_back_full).astype(LOW)
-    out_grad = out_grad.reshape(heads, run, shard, width).transpose(1, 0, 2, 3)
-    in_back, out_grad, gate_up_grad = call(
+    in_back, qkv_grad, gate_up_grad = call(
         [
             Scatter(parts, block),
-            Exchange(run, (heads * shard, width)),
-            Exchange(parts, gate_up_pieces.shape[1:]),
+            Collect(parts, groups, qkv_pieces.shape[1:], plan.qkv_starts),
+            plan.unit_job(gate_up_pieces.shape[1:]),
         ],
         [
             in_back_terms.reshape((parts,) + block),
-            out_grad.reshape(run, heads * shard, width),
+            qkv_grad.reshape((groups,) + qkv_pieces.shape),
             gate_up_grad.reshape(gate_up_pieces.shape),
         ],
         "in_back",
         7,
-        line,
-    )
-    out_grad = scatter(out_grad.reshape(groups * shard, width), "fsdp").astype(jnp.float32)
+        plane,
+    )
     tokens_grad = residual_back + norm_back(in_back, normed_in, root_in)
-    (qkv_grad,) = call(
-        [Exchange(parts, qkv_pieces.shape[1:])],
-        [qkv_grad.reshape(qkv_pieces.shape)],
-        "last",
-        8,
-        line,
-    )
     return (
         layer_out,
         tokens_grad,
-        plan.qkv_rows(qkv_grad),
+        qkv_grad,
         out_grad,
         plan.unit_rows(gate_up_grad),
         down_grad,

time: 653 us -> 740 us (1.13)
  waiting for transfers between devices: 1.98 us -> 131 us
  Pallas kernels: 482 us -> 438 us
  local copies, waits for them, and re-layouts: 32.9 us -> 23.8 us
  matrix products: 89 us -> 97.3 us
    reduce_scatter x4 -> x3, waiting for transfers between devices: 0.01 us -> 129 us  [scatter(): return lax.psum_scatter(values, axes, scatter_dimension=0, tiled=True)]
    pallas_call x8, Pallas kernels: 482 us -> 438 us  [call(): pl.pallas_call(kernel, out_shape=tuple((job.out for job in jobs)) + tuple...]
    convert_element_type x5 -> x0, local copies, waits for them, and re-layouts: 9.99 us -> none  [the longest x3 7.27 us: qkv_rows(): pieces.transpose(2, 3, 1, 4, 0, 5).reshape(rows, parts * columns)]
    dot_general x2 -> x3, matrix products: 8.5 us -> 17.9 us  [column_product(): lax.dot_general(left, right, (((0,), (0,)), ((), ())), preferred_element_...]
    unnamed x83 -> x73, local copies, waits for them, and re-layouts: 16.4 us -> 12.1 us
  transfers between devices with their start and end apart: 7 -> 6, of which waited for: 0 -> 2; matrix products, arithmetic and copies ran while one was open for 17% -> 11% of each run, Pallas kernels for 66% -> 30%
where the time goes in v4:
time: 740 us; the launch traced here: 735 us
  Pallas kernels  438 us (59%)
  waiting for transfers between devices  131 us (18%)
  matrix products  97.3 us (13%)
  other arithmetic  28.7 us (4%)
  local copies, waits for them, and re-layouts  23.8 us (3%)
  between operations  15 us (2%)
    pallas_call x8, Pallas kernels, call(): pl.pallas_call(kernel, out_shape=tuple((job.out for job in jobs)) + tuple...  438 us
    reduce_scatter x3, waiting for transfers between devices, scatter(): return lax.psum_scatter(values, axes, scatter_dimension=0, tiled=True)  129 us
    dot_general x4, matrix products, dot(): return jnp.dot(left, right, preferred_element_type=jnp.float32)  31.8 us
    dot_general x4, matrix products, times_transposed(): lax.dot_general(left, right, (((1,), (1,)), ((), ())), preferred_element_...  30.4 us
    dot_general x3, matrix products, column_product(): lax.dot_general(left, right, (((0,), (0,)), ((), ())), preferred_element_...  17.9 us
  transfers between devices with their start and end apart: 6, of which 2 were waited for; matrix products, arithmetic and copies ran while one was open for 11% of the time, Pallas kernels for 30%

profile of v4, /device:TPU:9, one launch (start us, length us, event | category | flops | bytes accessed | tf_op | source)
XLA Modules:
  0.0 734.7 jit_solution(6154392184616581126)
XLA Ops:
  20.1 104.9 %start.1 = (bf16[4,8,64,768]{3,2,1,0:T(8,128)(2,1)}, bf16[8,128,2048]{2,1,0:T(8,128)(2,1)}, bf16[8,64,2048]{2,1,0:T(8,128)(2,1)}) custom-call(bf16[8,64,768]{2,1,0:T(8,128)(2,1)} %reshape.346.refs_0_, bf16[128,2048]{1,0:T(8,128)(2,1)} %fusion.21.refs_1_, bf16[8,64,2048]{2,1,0:T(8,128)(2,1)} %reshape.348.refs_2_), custom_call_target="tpu_custom_call" | custom-call | tf_op jit(solution)/shard_map/start/pallas_call | solution.py:551
  125.4 6.2 fusion.69
  145.7 3.7 fusion.68
  149.4 10.7 %swap.1 = bf16[2,128,2048]{2,1,0:T(8,128)(2,1)} custom-call(bf16[2,128,2048]{2,1,0:T(8,128)(2,1)} %bitcast.116), custom_call_target="tpu_custom_call" | custom-call | tf_op jit(solution)/shard_map/swap/pallas_call | solution.py:551
  162.4 3.3 convolution_convert_fusion.1
  165.7 63.9 %out.1 = (f32[128,2048]{1,0:T(8,128)}, bf16[8,128,2048]{2,1,0:T(8,128)(2,1)}) custom-call(bf16[8,128,2048]{2,1,0:T(8,128)(2,1)} %bitcast.90, bf16[128,2048]{1,0:T(8,128)(2,1)} %refs_1_.1), custom_call_target="tpu_custom_call" | custom-call | tf_op jit(solution)/shard_map/out/pallas_call | solution.py:551
  232.3 41.0 %mid.1 = bf16[8,128,2048]{2,1,0:T(8,128)(2,1)} custom-call(bf16[128,2048]{1,0:T(8,128)(2,1)} %fusion.37.refs_0_), custom_call_target="tpu_custom_call" | custom-call | tf_op jit(solution)/shard_map/mid/pallas_call | solution.py:551
  273.3 14.6 %fusion.70 = f32[1024,2048]{1,0:T(8,128)} fusion(bf16[1024,2048]{1,0:T(8,128)(2,1)} %bitcast.91, bf16[2048,2048]{1,0:T(8,128)(2,1)} %all-gather.8.cloned.1.call-done), kind=kOutput, calls=%fused_computation.124 | convolution fusion | flops 8589934592 | bytes 20971520 | tf_op jit(solution)/shard_map/dot_general | solution.py:67
  287.9 11.0 %multiply_convert_fusion.3 = (bf16[1024,1024]{1,0:T(8,128)(2,1)S(1)}, bf16[1024,1024]{1,0:T(8,128)(2,1)S(1)}, bf16[1024,1024]{1,0:T(8,128)(2,1)}) fusion(f32[1024,2048]{1,0:T(8,128)} %fusion.70, bf16[1024,2048]{1,0:T(8,128)(2,1)} %bitcast.133, bf16[1024,2048]{1,0:T(8,128)(2,1)S(1)} %copy-done.29), kind=kOutput, calls=%fused_computation.11 | convolution fusion | flops 4310695936 | bytes 23068672 | tf_op jit(solution)/shard_map/dot_general | solution.py:71
  298.9 7.7 %convolution_convert_fusion.4 = bf16[1024,2048]{1,0:T(8,128)(2,1)} fusion(bf16[1024,1024]{1,0:T(8,128)(2,1)} %get-tuple-element.48, bf16[1024,2048]{1,0:T(8,128)(2,1)S(1)} %copy-done.29), kind=kOutput, calls=%fused_computation.23 | convolution fusion | flops 4297064448 | bytes 10485760 | tf_op jit(solution)/shard_map/dot_general | solution.py:67
  309.0 10.4 %convolution_convert_fusion = bf16[1024,2048]{1,0:T(8,128)(2,1)} fusion(bf16[2048,2048]{1,0:T(8,128)(2,1)S(1)} %bitcast.130, bf16[1024,1024]{1,0:T(8,128)(2,1)S(1)} %get-tuple-element.47, bf16[1024,1024]{1,0:T(8,128)(2,1)S(1)} %get-tuple-element.46), kind=kOutput, calls=%fused_computation.19 | convolution fusion | flops 8600420352 | bytes 16777216 | tf_op jit(solution)/shard_map/dot_general | solution.py:71
  319.4 47.9 %mid_back.1 = (f32[128,2048]{1,0:T(8,128)}, bf16[2048,2048]{1,0:T(8,128)(2,1)}) custom-call(bf16[8,128,2048]{2,1,0:T(8,128)(2,1)} %bitcast.101, bf16[1024,2048]{1,0:T(8,128)(2,1)} %bitcast.92, bf16[1024,2048]{1,0:T(8,128)(2,1)} %pad_maximum_fusion.refs_2_), custom_call_target="tpu_custom_call" | custom-call | tf_op jit(solution)/shard_map/mid_back/pallas_call | solution.py:551
  368.8 3.0 fusion.61
  371.8 67.4 %proj_back.1 = (bf16[8,128,2048]{2,1,0:T(8,128)(2,1)}, f32[128,2048]{1,0:T(8,128)}) custom-call(bf16[128,2048]{1,0:T(8,128)(2,1)} %get-tuple-element.40.refs_0_, bf16[8,128,2048]{2,1,0:T(8,128)(2,1)} %bitcast.102), custom_call_target="tpu_custom_call" | custom-call | tf_op jit(solution)/shard_map/proj_back/pallas_call | solution.py:551
  439.2 3.6 convolution_convert_fusion.6
  443.9 6.2 swap_back.1
  450.3 9.4 %convolution_convert_fusion.3 = bf16[1024,2048]{1,0:T(8,128)(2,1)} fusion(bf16[1024,1024]{1,0:T(8,128)(2,1)} %get-tuple-element.48, bf16[1024,2048]{1,0:T(8,128)(2,1)} %bitcast.134), kind=kOutput, calls=%fused_computation.22 | convolution fusion | flops 4297064448 | bytes 10485760 | tf_op jit(solution)/shard_map/dot_general | solution.py:77
  460.9 4.0 fusion.33
  464.9 6.1 multiply_convert_fusion
  480.0 5.0 convolution_convert_fusion.2
  485.0 4.9 convolution_convert_fusion.5
  491.7 42.6 %reduce-scatter.8.cloned.1.call-done = bf16[256,2048]{1,0:T(8,128)(2,1)} async-done(((bf16[1024,2048]{1,0:T(8,128)(2,1)}), bf16[256,2048]{1,0:T(8,128)(2,1)}) %reduce-scatter.8.cloned.1.call-update) | async-done | bytes 1048592 | tf_op jit(solution)/shard_map/reduce_scatter | solution.py:87
  537.0 86.5 %reduce-scatter.4.cloned.1.call-done = bf16[512,2048]{1,0:T(8,128)(2,1)} async-done(((bf16[2048,2048]{1,0:T(8,128)(2,1)}), bf16[512,2048]{1,0:T(8,128)(2,1)}) %reduce-scatter.4.cloned.1.call-update) | async-done | bytes 2097168 | tf_op jit(solution)/shard_map/reduce_scatter | solution.py:87
  623.5 96.4 %in_back.1 = (f32[128,2048]{1,0:T(8,128)}, f32[64,6144]{1,0:T(8,128)}, f32[64,16384]{1,0:T(8,128)}) custom-call(bf16[8,128,2048]{2,1,0:T(8,128)(2,1)} %bitcast.103, bf16[4,8,64,768]{3,2,1,0:T(8,128)(2,1)} %bitcast.110, bf16[8,64,2048]{2,1,0:T(8,128)(2,1)} %bitcast.113), custom_call_target="tpu_custom_call" | custom-call | tf_op jit(solution)/shard_map/in_back/pallas_call | solution.py:551
  (143 shorter events, 59.5 us)
Async XLA Ops:
  7.2 117.9 %all-gather.6.cloned.1.call-start = ((), (), s32[]{:S(2)}) async-start(), calls=%async_computation.4 | async-start | bytes 1310720 | tf_op jit(solution)/shard_map/all_gather | solution.py:83
  7.9 117.2 %all-gather.4.cloned.1.call-start = ((), (), s32[]{:S(2)}) async-start(), calls=%async_computation.3 | async-start | bytes 5242880 | tf_op jit(solution)/shard_map/all_gather | solution.py:83
  8.6 264.6 %all-gather.8.cloned.1.call-start = ((), (), s32[]{:S(2)}) async-start(), calls=%async_computation.5 | async-start | bytes 10485760 | tf_op jit(solution)/shard_map/all_gather | solution.py:83
  125.1 364.8 %reduce-scatter.6.cloned.1.call-start = ((), (), s32[]{:S(2)}) async-start(), calls=%async_computation.7 | async-start | bytes 1310720 | tf_op jit(solution)/shard_map/reduce_scatter | solution.py:87
  125.3 8.0 %copy-start.27 = (s32[1,2]{1,0:T(1,128)S(1)}, s32[1,2]{1,0:T(1,128)}, u32[]{:S(2)}) copy-start(s32[1,2]{1,0:T(1,128)} %param.13) | copy-start | bytes 28
  125.4 8.2 %copy-start.26 = (s32[1,8]{1,0:T(1,128)S(1)}, s32[1,8]{1,0:T(1,128)}, u32[]{:S(2)}) copy-start(s32[1,8]{1,0:T(1,128)} %param.14) | copy-start | bytes 100
  133.3 11.3 %copy-start.20 = (bf16[1024,256]{0,1:T(8,128)(2,1)}, bf16[1024,256]{0,1:T(8,128)(2,1)S(1)}, u32[]{:S(2)}) copy-start(bf16[1024,256]{0,1:T(8,128)(2,1)S(1)} %slice.79) | copy-start | bytes 1572868
  140.3 4.3 copy-start.6
  149.4 16.3 %copy-start.18 = (bf16[1024,2,128]{0,2,1:T(8,128)(2,1)}, bf16[1024,2,128]{0,2,1:T(8,128)(2,1)S(1)}, u32[]{:S(2)}) copy-start(bf16[1024,2,128]{0,2,1:T(8,128)(2,1)S(1)} %get-tuple-element.69) | copy-start | bytes 1572868
  273.3 14.6 %copy-start.29 = (bf16[1024,2048]{1,0:T(8,128)(2,1)S(1)}, bf16[1024,2048]{1,0:T(8,128)(2,1)}, u32[]{:S(2)}) copy-start(bf16[1024,2048]{1,0:T(8,128)(2,1)} %all-gather.4.cloned.1.call-done) | copy-start | bytes 12582916
  273.3 35.7 %slice-start.2 = ((s8[8388608]{0:T(1024)(128)(4,1)}), s8[4194304]{0:T(1024)(128)(4,1)S(1)}, s32[]{:S(2)}) async-start(s8[8388608]{0:T(1024)(128)(4,1)} %bitcast.129), calls=%async_computation.11 | async-start | bytes 8388608
  287.9 21.1 %slice-start.3 = ((s8[8388608]{0:T(1024)(128)(4,1)}), s8[4194304]{0:T(1024)(128)(4,1)S(1)}, s32[]{:S(2)}) async-start(s8[8388608]{0:T(1024)(128)(4,1)} %bitcast.129), calls=%async_computation.12 | async-start | bytes 8388608
  450.1 84.2 %reduce-scatter.8.cloned.1.call-start = ((), (), s32[]{:S(2)}) async-start(), calls=%async_computation.8 | async-start | bytes 5242880 | tf_op jit(solution)/shard_map/reduce_scatter | solution.py:87
  459.7 163.8 %reduce-scatter.4.cloned.1.call-start = ((), (), s32[]{:S(2)}) async-start(), calls=%async_computation.6 | async-start | bytes 10485760 | tf_op jit(solution)/shard_map/reduce_scatter | solution.py:87
  460.2 4.7 copy-start.7
  460.3 4.7 copy-start.21
  464.9 6.1 copy-start.16
  472.6 4.0 slice-start
  480.0 5.1 copy-start.28
  623.5 96.4 %copy-start.23 = (f32[128]{0:T(128)S(1)}, f32[128]{0:T(128)}, u32[]{:S(2)}) copy-start(f32[128]{0:T(128)} %copy-done.22) | copy-start | bytes 1540
  623.5 96.4 %copy-start.25 = (f32[128]{0:T(128)S(1)}, f32[128]{0:T(128)}, u32[]{:S(2)}) copy-start(f32[128]{0:T(128)} %copy-done.24) | copy-start | bytes 1540
  623.5 98.2 %copy-start.9 = (f32[128,2048]{1,0:T(8,128)S(1)}, f32[128,2048]{1,0:T(8,128)}, u32[]{:S(2)}) copy-start(f32[128,2048]{1,0:T(8,128)} %get-tuple-element.41) | copy-start | bytes 3145732
  719.9 4.6 copy-start.17
  719.9 5.7 copy-start.8
  (17 other events, 35.9 us)
Sparse Core Ops, SparseCore 0:
  9.8 39.4 all-gather.5
  51.2 63.2 all-gather.3
  125.2 92.0 all-gather.7
  450.2 28.4 reduce-scatter.5
  481.5 52.6 reduce-scatter.7
  537.2 86.2 reduce-scatter.3

commit v5 on v4

--- a/solution.py
+++ b/solution.py
@@ -513,7 +513,7 @@
             copy.wait_send()
 
 
-def call(jobs, operands, name, identity, axes, work=None):
+def call(jobs, operands, name, identity, axes, work=None, micros=50):
     counts = [len(job.scratch) for job in jobs]
     jobs_n = len(jobs)
     extra = work.operands if work else []
@@ -556,6 +556,9 @@
         scratch_shapes=[shape for job in jobs for shape in job.scratch] + list(extra_scratch),
         compiler_params=pltpu.CompilerParams(
             collective_id=identity, has_side_effects=True, vmem_limit_bytes=62 << 20
+        ),
+        cost_estimate=pl.CostEstimate(
+            flops=0, bytes_accessed=micros * 3_000_000, transcendentals=0
         ),
         name=name,
     )(*operands, *extra)
@@ -692,6 +695,7 @@
         "start",
         2,
         plane,
+        micros=110,
     )
     gate_up_cols, down_rows, out_rows = lax.optimization_barrier(
         (gate_up_cols, down_rows, out_rows)
@@ -703,6 +707,7 @@
         "swap",
         1,
         line,
+        micros=6,
     )
     qkv_cols = qkv_cols.reshape(width, 3 * head_width)
     normed_in_full = normed_in_full.reshape(length, width)
@@ -738,11 +743,12 @@
         "out",
         3,
         line,
+        micros=64,
     )
     cot_full = cot_full.reshape(length, width)
     residual = inputs + attn_out
     normed_mid, root_mid = normalize(residual)
-    (normed_mid_full,) = call([Gather(parts, block)], [normed_mid.astype(LOW)], "mid", 4, line)
+    (normed_mid_full,) = call([Gather(parts, block)], [normed_mid.astype(LOW)], "mid", 4, line, micros=45)
     normed_mid_full = normed_mid_full.reshape(length, width)
 
     gate_up = dot(normed_mid_full, gate_up_cols)
@@ -766,6 +772,7 @@
         line,
         Grads([(normed_mid_full, gate_up_back)]),
     )
+    gate_up_grad, down_grad = lax.optimization_barrier((gate_up_grad, down_grad))
     gate_up_grad = scatter(gate_up_grad, "fsdp")
     residual_back = cotangent.astype(jnp.float32) + norm_back(mid_back, normed_mid, root_mid)
     proj_back = residual_back.astype(LOW)
@@ -777,6 +784,7 @@
         "proj_back",
         6,
         line,
+        micros=70,
     )
     layer_out = (residual + down_out).astype(LOW)
     proj_back_full = proj_back_full.reshape(length, width)
@@ -789,7 +797,9 @@
         "swap_back",
         8,
         line,
-    )
+        micros=6,
+    )
+    out_grad, gate_up_grad = lax.optimization_barrier((out_grad, gate_up_grad))
     out_grad = scatter(out_grad.reshape(groups * shard, width), "fsdp").astype(jnp.float32)
     back_heads = times_transposed(proj_back_full, out_cols).astype(LOW).reshape(head_shape)
     delta = jnp.einsum("qhd,qhd->hq", back_heads.astype(jnp.float32), attn_heads)
@@ -825,6 +835,7 @@
         "in_back",
         7,
         plane,
+        micros=90,
     )
     tokens_grad = residual_back + norm_back(in_back, normed_in, root_in)
     return (

time: 740 us -> 620 us (0.84)
  waiting for transfers between devices: 131 us -> 1.55 us
    reduce_scatter x3, waiting for transfers between devices: 129 us -> 0.04 us  [scatter(): return lax.psum_scatter(values, axes, scatter_dimension=0, tiled=True)]
    unnamed x73 -> x81, local copies, waits for them, and re-layouts: 12.1 us -> 19.2 us
  transfers between devices with their start and end apart: 6 -> 6, of which waited for: 2 -> 0; matrix products, arithmetic and copies ran while one was open for 11% -> 17% of each run, Pallas kernels for 30% -> 71%
where the time goes in v5:
time: 620 us; the launch traced here: 616 us
  Pallas kernels  440 us (71%)
  matrix products  97.2 us (16%)
  local copies, waits for them, and re-layouts  30.9 us (5%)
  other arithmetic  29.9 us (5%)
  between operations  15 us (2%)
    pallas_call x8, Pallas kernels, call(): pl.pallas_call(kernel, out_shape=tuple((job.out for job in jobs)) + tuple...  440 us
    dot_general x4, matrix products, times_transposed(): lax.dot_general(left, right, (((1,), (1,)), ((), ())), preferred_element_...  32 us
    dot_general x4, matrix products, dot(): return jnp.dot(left, right, preferred_element_type=jnp.float32)  30.2 us
    unnamed x81, local copies, waits for them, and re-layouts  19.2 us
    dot_general x3, matrix products, column_product(): lax.dot_general(left, right, (((0,), (0,)), ((), ())), preferred_element_...  17.8 us
  transfers between devices with their start and end apart: 6, of which 0 were waited for; matrix products, arithmetic and copies ran while one was open for 17% of the time, Pallas kernels for 71%

profile of v5, /device:TPU:9, one launch (start us, length us, event | category | flops | bytes accessed | tf_op | source)
XLA Modules:
  0.0 615.6 jit_solution(481476208264646180)
XLA Ops:
  20.2 104.9 %start.1 = (bf16[4,8,64,768]{3,2,1,0:T(8,128)(2,1)}, bf16[8,128,2048]{2,1,0:T(8,128)(2,1)}, bf16[8,64,2048]{2,1,0:T(8,128)(2,1)}) custom-call(bf16[8,64,768]{2,1,0:T(8,128)(2,1)} %reshape.346.refs_0_, bf16[128,2048]{1,0:T(8,128)(2,1)} %fusion.21.refs_1_, bf16[8,64,2048]{2,1,0:T(8,128)(2,1)} %reshape.348.refs_2_), custom_call_target="tpu_custom_call" | custom-call | bytes 330000000 | tf_op jit(solution)/shard_map/start/pallas_call | solution.py:551
  125.8 6.2 %fusion.69 = f32[1024,768]{0,1:T(8,128)S(1)} fusion(bf16[1024,2048]{1,0:T(8,128)(2,1)} %bitcast.129, bf16[2048,768]{1,0:T(8,128)(2,1)} %bitcast.135), kind=kOutput, calls=%fused_computation.123 | convolution fusion | flops 3221225472 | bytes 10485760 | tf_op jit(solution)/shard_map/dot_general | solution.py:67
  146.1 3.7 fusion.68
  149.9 10.7 %swap.1 = bf16[2,128,2048]{2,1,0:T(8,128)(2,1)} custom-call(bf16[2,128,2048]{2,1,0:T(8,128)(2,1)} %bitcast.116), custom_call_target="tpu_custom_call" | custom-call | bytes 18000000 | tf_op jit(solution)/shard_map/swap/pallas_call | solution.py:551
  162.9 3.3 convolution_convert_fusion.1
  166.3 63.9 %out.1 = (f32[128,2048]{1,0:T(8,128)}, bf16[8,128,2048]{2,1,0:T(8,128)(2,1)}) custom-call(bf16[8,128,2048]{2,1,0:T(8,128)(2,1)} %bitcast.90, bf16[128,2048]{1,0:T(8,128)(2,1)} %refs_1_.1), custom_call_target="tpu_custom_call" | custom-call | bytes 192000000 | tf_op jit(solution)/shard_map/out/pallas_call | solution.py:551
  232.9 41.1 %mid.1 = bf16[8,128,2048]{2,1,0:T(8,128)(2,1)} custom-call(bf16[128,2048]{1,0:T(8,128)(2,1)} %fusion.37.refs_0_), custom_call_target="tpu_custom_call" | custom-call | bytes 135000000 | tf_op jit(solution)/shard_map/mid/pallas_call | solution.py:551
  274.0 14.6 %fusion.70 = f32[1024,2048]{1,0:T(8,128)} fusion(bf16[1024,2048]{1,0:T(8,128)(2,1)} %bitcast.91, bf16[2048,2048]{1,0:T(8,128)(2,1)} %all-gather.8.cloned.1.call-done), kind=kOutput, calls=%fused_computation.124 | convolution fusion | flops 8589934592 | bytes 20971520 | tf_op jit(solution)/shard_map/dot_general | solution.py:67
  288.6 10.0 %multiply_convert_fusion.3 = (bf16[1024,1024]{1,0:T(8,128)(2,1)}, bf16[1024,1024]{1,0:T(8,128)(2,1)}, bf16[1024,1024]{1,0:T(8,128)(2,1)S(1)}) fusion(f32[1024,2048]{1,0:T(8,128)} %fusion.70, bf16[1024,2048]{1,0:T(8,128)(2,1)S(1)} %bitcast.131, bf16[1024,2048]{1,0:T(8,128)(2,1)S(1)} %copy-done.30), kind=kOutput, calls=%fused_computation.11 | convolution fusion | flops 4310695936 | bytes 23068672 | tf_op jit(solution)/shard_map/dot_general | solution.py:71
  299.9 6.3 %convolution_convert_fusion.3 = bf16[1024,2048]{1,0:T(8,128)(2,1)} fusion(bf16[1024,1024]{1,0:T(8,128)(2,1)S(1)} %get-tuple-element.56, bf16[1024,2048]{1,0:T(8,128)(2,1)S(1)} %bitcast.132), kind=kOutput, calls=%fused_computation.22 | convolution fusion | flops 4297064448 | bytes 10485760 | tf_op jit(solution)/shard_map/dot_general | solution.py:77
  306.5 4.9 pad_maximum_fusion.refs_2_
  311.4 12.6 %convolution_convert_fusion = bf16[1024,2048]{1,0:T(8,128)(2,1)} fusion(bf16[2048,2048]{1,0:T(8,128)(2,1)} %all-gather.8.cloned.1.call-done, bf16[1024,1024]{1,0:T(8,128)(2,1)S(1)} %copy-done.15, bf16[1024,1024]{1,0:T(8,128)(2,1)S(1)} %copy-done.14), kind=kOutput, calls=%fused_computation.19 | convolution fusion | flops 8600420352 | bytes 16777216 | tf_op jit(solution)/shard_map/dot_general | solution.py:71
  324.0 48.2 %mid_back.1 = (f32[128,2048]{1,0:T(8,128)}, bf16[2048,2048]{1,0:T(8,128)(2,1)}) custom-call(bf16[8,128,2048]{2,1,0:T(8,128)(2,1)} %bitcast.101, bf16[1024,2048]{1,0:T(8,128)(2,1)} %bitcast.92, bf16[1024,2048]{1,0:T(8,128)(2,1)} %pad_maximum_fusion.refs_2_), custom_call_target="tpu_custom_call" | custom-call | bytes 150000000 | tf_op jit(solution)/shard_map/mid_back/pallas_call | solution.py:551
  376.5 3.3 fusion.61
  379.9 6.0 convolution_convert_fusion.4
  385.9 67.7 %proj_back.1 = (bf16[8,128,2048]{2,1,0:T(8,128)(2,1)}, f32[128,2048]{1,0:T(8,128)}) custom-call(bf16[128,2048]{1,0:T(8,128)(2,1)} %get-tuple-element.48.refs_0_, bf16[8,128,2048]{2,1,0:T(8,128)(2,1)} %bitcast.102), custom_call_target="tpu_custom_call" | custom-call | bytes 210000000 | tf_op jit(solution)/shard_map/proj_back/pallas_call | solution.py:551
  453.6 3.7 convolution_convert_fusion.6
  458.3 6.7 %swap_back.1 = bf16[2,128,2048]{2,1,0:T(8,128)(2,1)} custom-call(bf16[2,128,2048]{2,1,0:T(8,128)(2,1)} %bitcast.106), custom_call_target="tpu_custom_call" | custom-call | bytes 18000000 | tf_op jit(solution)/shard_map/swap_back/pallas_call | solution.py:551
  465.0 4.2 fusion.33
  469.3 6.0 multiply_convert_fusion
  484.6 5.2 convolution_convert_fusion.2
  490.7 7.9 %convolution_convert_fusion.5 = bf16[2048,768]{1,0:T(8,128)(2,1)} fusion(bf16[1024,2048]{1,0:T(8,128)(2,1)} %bitcast.130, bf16[1024,256]{0,1:T(8,128)(2,1)} %bitcast.140, bf16[1024,256]{0,1:T(8,128)(2,1)} %bitcast.123, bf16[1024,256]{0,1:T(8,128)(2,1)} %bitcast.121), kind=kOutput, calls=%fused_computation.24 | convolution fusion | flops 3227516928 | bytes 8912896 | tf_op jit(solution)/shard_map/dot_general | solution.py:77
  498.6 96.8 %in_back.1 = (f32[128,2048]{1,0:T(8,128)}, f32[64,6144]{1,0:T(8,128)}, f32[64,16384]{1,0:T(8,128)}) custom-call(bf16[8,128,2048]{2,1,0:T(8,128)(2,1)} %bitcast.103, bf16[4,8,64,768]{3,2,1,0:T(8,128)(2,1)} %bitcast.110, bf16[8,64,2048]{2,1,0:T(8,128)(2,1)} %bitcast.113), custom_call_target="tpu_custom_call" | custom-call | bytes 270000000 | tf_op jit(solution)/shard_map/in_back/pallas_call | solution.py:551
  604.0 4.5 copy.83
  (150 shorter events, 58.1 us)
Async XLA Ops:
  7.2 118.0 %all-gather.6.cloned.1.call-start = ((), (), s32[]{:S(2)}) async-start(), calls=%async_computation.4 | async-start | bytes 1310720 | tf_op jit(solution)/shard_map/all_gather | solution.py:83
  7.9 117.3 %all-gather.4.cloned.1.call-start = ((), (), s32[]{:S(2)}) async-start(), calls=%async_computation.3 | async-start | bytes 5242880 | tf_op jit(solution)/shard_map/all_gather | solution.py:83
  8.6 265.3 %all-gather.8.cloned.1.call-start = ((), (), s32[]{:S(2)}) async-start(), calls=%async_computation.5 | async-start | bytes 10485760 | tf_op jit(solution)/shard_map/all_gather | solution.py:83
  125.2 247.0 %reduce-scatter.4.cloned.1.call-start = ((), (), s32[]{:S(2)}) async-start(), calls=%async_computation.6 | async-start | bytes 5242880 | tf_op jit(solution)/shard_map/reduce_scatter | solution.py:87
  125.8 8.0 %copy-start.29 = (s32[1,2]{1,0:T(1,128)S(1)}, s32[1,2]{1,0:T(1,128)}, u32[]{:S(2)}) copy-start(s32[1,2]{1,0:T(1,128)} %param.13) | copy-start | bytes 28
  125.8 8.2 %copy-start.28 = (s32[1,8]{1,0:T(1,128)S(1)}, s32[1,8]{1,0:T(1,128)}, u32[]{:S(2)}) copy-start(s32[1,8]{1,0:T(1,128)} %param.14) | copy-start | bytes 100
  133.8 11.3 %copy-start.20 = (bf16[1024,256]{0,1:T(8,128)(2,1)}, bf16[1024,256]{0,1:T(8,128)(2,1)S(1)}, u32[]{:S(2)}) copy-start(bf16[1024,256]{0,1:T(8,128)(2,1)S(1)} %slice.79) | copy-start | bytes 1572868
  140.8 4.3 copy-start.6
  149.9 16.4 %copy-start.18 = (bf16[1024,2,128]{0,2,1:T(8,128)(2,1)}, bf16[1024,2,128]{0,2,1:T(8,128)(2,1)S(1)}, u32[]{:S(2)}) copy-start(bf16[1024,2,128]{0,2,1:T(8,128)(2,1)S(1)} %get-tuple-element.77) | copy-start | bytes 1572868
  274.0 14.6 %copy-start.30 = (bf16[1024,2048]{1,0:T(8,128)(2,1)S(1)}, bf16[1024,2048]{1,0:T(8,128)(2,1)}, u32[]{:S(2)}) copy-start(bf16[1024,2048]{1,0:T(8,128)(2,1)} %all-gather.4.cloned.1.call-done) | copy-start | bytes 12582916
  274.0 14.6 %copy-start.32 = (bf16[8,128,2048]{2,1,0:T(8,128)(2,1)S(1)}, bf16[8,128,2048]{2,1,0:T(8,128)(2,1)}, u32[]{:S(2)}) copy-start(bf16[8,128,2048]{2,1,0:T(8,128)(2,1)} %get-tuple-element.30) | copy-start | bytes 12582916
  306.2 183.5 %reduce-scatter.6.cloned.1.call-start = ((), (), s32[]{:S(2)}) async-start(), calls=%async_computation.7 | async-start | bytes 10485760 | tf_op jit(solution)/shard_map/reduce_scatter | solution.py:87
  306.5 4.9 copy-start.14
  306.5 4.9 copy-start.15
  375.0 224.6 %reduce-scatter.8.cloned.1.call-start = ((), (), s32[]{:S(2)}) async-start(), calls=%async_computation.8 | async-start | bytes 1310720 | tf_op jit(solution)/shard_map/reduce_scatter | solution.py:87
  375.1 4.8 copy-start.31
  375.1 4.8 copy-start.36
  465.0 4.2 copy-start.7
  465.0 4.2 copy-start.21
  469.2 6.1 copy-start.17
  484.6 5.2 copy-start.19
  498.6 96.8 %copy-start.25 = (f32[128]{0:T(128)S(1)}, f32[128]{0:T(128)}, u32[]{:S(2)}) copy-start(f32[128]{0:T(128)} %copy-done.24) | copy-start | bytes 1540
  498.6 96.8 %copy-start.27 = (f32[128]{0:T(128)S(1)}, f32[128]{0:T(128)}, u32[]{:S(2)}) copy-start(f32[128]{0:T(128)} %copy-done.26) | copy-start | bytes 1540
  498.6 98.4 %copy-start.8 = (f32[128,2048]{1,0:T(8,128)S(1)}, f32[128,2048]{1,0:T(8,128)}, u32[]{:S(2)}) copy-start(f32[128,2048]{1,0:T(8,128)} %get-tuple-element.49) | copy-start | bytes 3145732
  (21 other events, 45.3 us)
Sparse Core Ops, SparseCore 0:
  9.8 39.3 all-gather.5
  51.1 63.4 all-gather.3
  125.4 92.0 all-gather.7
  306.4 56.6 reduce-scatter.3
  375.2 86.0 reduce-scatter.5
  489.9 33.4 reduce-scatter.7

commit v6 on v5

--- a/solution.py
+++ b/solution.py
@@ -618,6 +618,204 @@
             copy.wait()
 
 
+def product(left, right):
+    return jnp.dot(left, right, preferred_element_type=jnp.float32)
+
+
+class Puts:
+    def __init__(self, made, put):
+        self.made, self.put, self.copies = made, put, []
+
+    def buffer(self):
+        if len(self.copies) >= 2:
+            self.copies[-2].wait()
+        return self.made.at[len(self.copies) % 2]
+
+    def send(self, source, target):
+        copy = pltpu.make_async_copy(source, target, self.put.at[len(self.copies) % 2])
+        copy.start()
+        self.copies.append(copy)
+
+    def finish(self):
+        for copy in self.copies[-2:]:
+            copy.wait()
+
+
+def softmax_block(query, keys, ok):
+    scores = times_transposed(query, keys) * HEAD_DIM ** (-0.5)
+    scores = jnp.where(ok, scores, -1e30)
+    weights = jnp.exp(scores - jnp.max(scores, axis=-1, keepdims=True))
+    weights = jnp.where(ok, weights, 0.0)
+    return weights, jnp.sum(weights, axis=-1, keepdims=True)
+
+
+class Attend:
+    tile = 256
+
+    def __init__(self, rows, weight, tables, heads):
+        self.heads = heads
+        self.operands = [rows, weight] + list(tables)
+        length, wide = rows.shape[0], weight.shape[1]
+        self.outs = [
+            jax.ShapeDtypeStruct((length, wide), LOW),
+            jax.ShapeDtypeStruct((length, wide // 3), LOW),
+        ]
+        self.scratch = [pltpu.VMEM(array.shape, array.dtype) for array in self.operands]
+        self.scratch += [pltpu.VMEM(out.shape, out.dtype) for out in self.outs]
+        self.scratch += [
+            pltpu.SemaphoreType.DMA((len(self.operands),)),
+            pltpu.SemaphoreType.DMA((2,)),
+        ]
+
+    def run(self, *refs):
+        n, tile, heads = len(self.operands), self.tile, self.heads
+        sources, results, held = refs[:n], refs[n : n + 2], refs[n + 2 : 2 * n + 2]
+        qkv, mix, get, put = refs[2 * n + 2 :]
+        rows, weight, cosine, sine, first, last, keys = held
+        gets = [pltpu.make_async_copy(s, h, get.at[i]) for i, (s, h) in enumerate(zip(sources, held))]
+        for copy in gets:
+            copy.start()
+        yield
+        for copy in gets:
+            copy.wait()
+        width = heads * HEAD_DIM
+
+        def project(index, carry):
+            at = pl.ds(pl.multiple_of(index * tile, tile), tile)
+            value = product(rows[at, :], weight[...])
+            for head in range(3 * heads):
+                block = value[:, head * HEAD_DIM : (head + 1) * HEAD_DIM]
+                if head < 2 * heads:
+                    turned = pltpu.roll(block, HEAD_DIM // 2, 1)
+                    block = block * cosine[at, :] + turned * sine[at, :]
+                qkv[at, head * HEAD_DIM : (head + 1) * HEAD_DIM] = block.astype(LOW)
+            return carry
+
+        lax.fori_loop(0, rows.shape[0] // tile, project, 0)
+        send = pltpu.make_async_copy(qkv, results[0], put.at[0])
+        send.start()
+        yield
+
+        def attend(index, carry):
+            at = pl.ds(pl.multiple_of(index * tile, tile), tile)
+            ok = (keys[:1, :] >= first[at, :1]) & (keys[:1, :] <= last[at, :1])
+            for head in range(heads):
+                lo = head * HEAD_DIM
+                weights, total = softmax_block(
+                    qkv[at, lo : lo + HEAD_DIM], qkv[:, width + lo : width + lo + HEAD_DIM], ok
+                )
+                value = qkv[:, 2 * width + lo : 2 * width + lo + HEAD_DIM]
+                mixed = product(weights.astype(LOW), value) / total
+                mix[at, lo : lo + HEAD_DIM] = mixed.astype(LOW)
+            return carry
+
+        lax.fori_loop(0, rows.shape[0] // tile, attend, 0)
+        send_mix = pltpu.make_async_copy(mix, results[1], put.at[1])
+        send_mix.start()
+        yield
+        send.wait()
+        send_mix.wait()
+
+
+class AttendBack:
+    tile = 256
+
+    def __init__(self, upstream, out_rows, qkv, rows, weight, tables, heads):
+        self.heads = heads
+        self.operands = [upstream, out_rows, qkv, weight] + list(tables) + [rows]
+        length, wide, width = rows.shape[0], weight.shape[1], rows.shape[1]
+        self.outs = [
+            jax.ShapeDtypeStruct((length, width), LOW),
+            jax.ShapeDtypeStruct((width, wide), LOW),
+        ]
+        self.scratch = [pltpu.VMEM(array.shape, array.dtype) for array in self.operands[:-1]]
+        self.scratch += [
+            pltpu.VMEM((length, wide // 3), LOW),
+            pltpu.VMEM((length, wide), LOW),
+            pltpu.VMEM((2, length, HEAD_DIM), jnp.float32),
+            pltpu.VMEM((2, self.tile, width), LOW),
+            pltpu.SemaphoreType.DMA((len(self.operands),)),
+            pltpu.SemaphoreType.DMA((2,)),
+        ]
+
+    def run(self, *refs):
+        n, tile, heads = len(self.operands), self.tile, self.heads
+        sources, results, held = refs[:n], refs[n : n + 2], refs[n + 2 : 2 * n + 1]
+        back, grads, sums, made, get, put = refs[2 * n + 1 :]
+        upstream, out_rows, qkv, weight, cosine, sine, first, last, keys = held
+        length, width = back.shape
+        gets = [pltpu.make_async_copy(s, h, get.at[i]) for i, (s, h) in enumerate(zip(sources, held))]
+        for copy in gets:
+            copy.start()
+        yield
+        for copy in gets:
+            copy.wait()
+
+        def project(index, carry):
+            at = pl.ds(pl.multiple_of(index * tile, tile), tile)
+            back[at, :] = times_transposed(upstream[at, :], out_rows[...]).astype(LOW)
+            return carry
+
+        lax.fori_loop(0, length // tile, project, 0)
+        rows = upstream
+        fetch = pltpu.make_async_copy(sources[n - 1], rows, get.at[n - 1])
+        fetch.start()
+        yield
+
+        def unrotated(value, at):
+            return value * cosine[at, :] - pltpu.roll(value, HEAD_DIM // 2, 1) * sine[at, :]
+
+        for head in range(heads):
+            lo = head * HEAD_DIM
+            mine = slice(lo, lo + HEAD_DIM)
+            key = slice(width + lo, width + lo + HEAD_DIM)
+            val = slice(2 * width + lo, 2 * width + lo + HEAD_DIM)
+            sums[...] = jnp.zeros_like(sums)
+
+            def attend(index, carry):
+                at = pl.ds(pl.multiple_of(index * tile, tile), tile)
+                ok = (keys[:1, :] >= first[at, :1]) & (keys[:1, :] <= last[at, :1])
+                weights, total = softmax_block(qkv[at, mine], qkv[:, key], ok)
+                probs = weights / total
+                upper = back[at, mine]
+                prob_back = times_transposed(upper, qkv[:, val])
+                delta = jnp.sum(probs * prob_back, axis=-1, keepdims=True)
+                score_back = HEAD_DIM ** (-0.5) * probs * (prob_back - delta)
+                score_low = score_back.astype(LOW)
+                query_back = product(score_low, qkv[:, key])
+                grads[at, mine] = unrotated(query_back, at).astype(LOW)
+                sums[0] += product(score_low.T, qkv[at, mine])
+                sums[1] += product(probs.astype(LOW).T, upper)
+                return carry
+
+            half = max(1, length // tile // 2)
+            for begin in range(0, length // tile, half):
+                lax.fori_loop(begin, begin + half, attend, 0)
+                yield
+
+            def settle(index, carry):
+                at = pl.ds(pl.multiple_of(index * tile, tile), tile)
+                grads[at, key] = unrotated(sums[0, at, :], at).astype(LOW)
+                grads[at, val] = sums[1, at, :].astype(LOW)
+                return carry
+
+            lax.fori_loop(0, length // tile, settle, 0)
+        puts = Puts(made, put)
+        for at in range(0, length, tile):
+            buffer = puts.buffer()
+            buffer[...] = times_transposed(grads[at : at + tile, :], weight[...]).astype(LOW)
+            puts.send(buffer, results[0].at[at : at + tile, :])
+            yield
+        fetch.wait()
+        wide = grads.shape[1]
+        for at in range(0, rows.shape[1], tile):
+            buffer = puts.buffer().at[:, :wide]
+            buffer[...] = product(rows[:, at : at + tile].T, grads[...]).astype(LOW)
+            puts.send(buffer, results[1].at[at : at + tile, :])
+            yield
+        puts.finish()
+
+
 class Plan:
     def __init__(self, parts, groups, width):
         self.parts, self.groups = parts, groups
@@ -674,7 +872,6 @@
     plan = Plan(parts, groups, width)
     heads, shard, run = plan.heads, plan.shard, plan.run
     head_width = heads * HEAD_DIM
-    score_scale = HEAD_DIM ** (-0.5)
     line = (("ctx", parts),)
     plane = (("ctx", parts), ("fsdp", groups))
     block = (rows, width)
@@ -685,56 +882,42 @@
     inputs = tokens.astype(jnp.float32)
     normed_in, root_in = normalize(inputs)
     qkv_pieces = plan.qkv_pieces(w_qkv)
-    qkv_cols, normed_in_full, gate_up_cols = call(
-        [
-            Spread(parts, groups, qkv_pieces.shape[1:]),
-            Gather(parts, block),
-            Exchange(parts, gate_up_pieces.shape[1:]),
-        ],
-        [qkv_pieces, normed_in.astype(LOW), gate_up_pieces],
+    qkv_cols, normed_in_full = call(
+        [Spread(parts, groups, qkv_pieces.shape[1:]), Gather(parts, block)],
+        [qkv_pieces, normed_in.astype(LOW)],
         "start",
         2,
         plane,
-        micros=110,
-    )
-    gate_up_cols, down_rows, out_rows = lax.optimization_barrier(
-        (gate_up_cols, down_rows, out_rows)
-    )
-    gate_up_cols = gather(gate_up_cols.reshape(width // groups, -1), "fsdp")
-    (out_cols,) = call(
-        [Exchange(run, (heads * shard, width))],
-        [out_rows.reshape(run, heads * shard, width)],
-        "swap",
+        micros=70,
+    )
+    qkv_cols = qkv_cols.reshape(width, 3 * head_width)
+    normed_in_full = normed_in_full.reshape(length, width)
+
+    row_index = jnp.arange(length, dtype=jnp.int32)
+    packed = initial_index(row_index, order_row)
+    _, pos = places(packed, lengths)
+    cosine_table, sine_table = angle_tables(pos)
+    half_sign = jnp.where(jnp.arange(HEAD_DIM) < HEAD_DIM // 2, -1.0, 1.0)
+    tables = (
+        cosine_table[:, 0, :],
+        sine_table[:, 0, :] * half_sign,
+        jnp.broadcast_to((packed - pos)[:, None], (length, HEAD_DIM)),
+        jnp.broadcast_to(packed[:, None], (length, HEAD_DIM)),
+        jnp.broadcast_to(packed[None, :], (8, length)),
+    )
+    gate_up_cols, out_cols, qkv_low, mix_low = call(
+        [Exchange(parts, gate_up_pieces.shape[1:]), Exchange(run, (heads * shard, width))],
+        [gate_up_pieces, out_rows.reshape(run, heads * shard, width)],
+        "attend",
         1,
         line,
-        micros=6,
-    )
-    qkv_cols = qkv_cols.reshape(width, 3 * head_width)
-    normed_in_full = normed_in_full.reshape(length, width)
+        Attend(normed_in_full, qkv_cols, tables, heads),
+        micros=55,
+    )
+    gate_up_cols, down_rows = lax.optimization_barrier((gate_up_cols, down_rows))
+    gate_up_cols = gather(gate_up_cols.reshape(width // groups, -1), "fsdp")
     out_cols = out_cols.reshape(run, heads, shard, width).transpose(1, 0, 2, 3)
     out_cols = out_cols.reshape(head_width, width)
-
-    row_index = jnp.arange(length, dtype=jnp.int32)
-    seq, pos = places(initial_index(row_index, order_row), lengths)
-    cosine_table, sine_table = angle_tables(pos)
-    allowed = ((seq[:, None] == seq[None, :]) & (pos[None, :] <= pos[:, None]))[None]
-
-    qkv = dot(normed_in_full, qkv_cols)
-    head_shape = (length, heads, HEAD_DIM)
-    queries = rotate(qkv[:, :head_width].reshape(head_shape), cosine_table, sine_table).astype(LOW)
-    keys = rotate(
-        qkv[:, head_width : 2 * head_width].reshape(head_shape), cosine_table, sine_table
-    ).astype(LOW)
-    values = qkv[:, 2 * head_width :].astype(LOW).reshape(head_shape)
-    scores = jnp.einsum("qhd,khd->hqk", queries, keys, preferred_element_type=jnp.float32)
-    scores = jnp.where(allowed, scores * score_scale, -1e30)
-    row_max = jnp.max(scores, axis=-1)
-    weights = jnp.where(allowed, jnp.exp(scores - row_max[..., None]), 0.0)
-    row_total = jnp.sum(weights, axis=-1)
-    mixed = jnp.einsum("hqk,khd->qhd", weights.astype(LOW), values, preferred_element_type=jnp.float32)
-    log_total = row_max + jnp.log(row_total)
-    attn_heads = mixed / jnp.transpose(row_total)[..., None]
-    mix_low = attn_heads.astype(LOW).reshape(length, head_width)
 
     out_terms = dot(mix_low, out_cols).astype(LOW)
     attn_out, cot_full = call(
@@ -778,49 +961,22 @@
     proj_back = residual_back.astype(LOW)
 
     down_terms = dot(activated, down_rows).astype(LOW)
-    proj_back_full, down_out = call(
-        [Gather(parts, block), Scatter(parts, block)],
-        [proj_back, down_terms.reshape((parts,) + block)],
-        "proj_back",
-        6,
-        line,
-        micros=70,
-    )
-    layer_out = (residual + down_out).astype(LOW)
+    (proj_back_full,) = call([Gather(parts, block)], [proj_back], "proj_back", 6, line, micros=45)
     proj_back_full = proj_back_full.reshape(length, width)
-
     out_grad = column_product(mix_low, proj_back_full).astype(LOW)
     out_grad = out_grad.reshape(heads, run, shard, width).transpose(1, 0, 2, 3)
-    (out_grad,) = call(
-        [Exchange(run, (heads * shard, width))],
-        [out_grad.reshape(run, heads * shard, width)],
-        "swap_back",
+    down_out, out_grad, in_back_terms, qkv_grad = call(
+        [Scatter(parts, block), Exchange(run, (heads * shard, width))],
+        [down_terms.reshape((parts,) + block), out_grad.reshape(run, heads * shard, width)],
+        "attend_back",
         8,
         line,
-        micros=6,
-    )
+        AttendBack(proj_back_full, out_cols, qkv_low, normed_in_full, qkv_cols, tables, heads),
+        micros=60,
+    )
+    layer_out = (residual + down_out).astype(LOW)
     out_grad, gate_up_grad = lax.optimization_barrier((out_grad, gate_up_grad))
     out_grad = scatter(out_grad.reshape(groups * shard, width), "fsdp").astype(jnp.float32)
-    back_heads = times_transposed(proj_back_full, out_cols).astype(LOW).reshape(head_shape)
-    delta = jnp.einsum("qhd,qhd->hq", back_heads.astype(jnp.float32), attn_heads)
-    probs = jnp.where(allowed, jnp.exp(scores - log_total[..., None]), 0.0)
-    value_back = jnp.einsum(
-        "hqk,qhd->khd", probs.astype(LOW), back_heads, preferred_element_type=jnp.float32
-    )
-    prob_back = jnp.einsum("qhd,khd->hqk", back_heads, values, preferred_element_type=jnp.float32)
-    score_back = (score_scale * probs * (prob_back - delta[..., None])).astype(LOW)
-    query_back = jnp.einsum("hqk,khd->qhd", score_back, keys, preferred_element_type=jnp.float32)
-    key_back = jnp.einsum("hqk,qhd->khd", score_back, queries, preferred_element_type=jnp.float32)
-    qkv_back = jnp.concatenate(
-        [
-            unrotate(query_back, cosine_table, sine_table).reshape(length, head_width),
-            unrotate(key_back, cosine_table, sine_table).reshape(length, head_width),
-            value_back.reshape(length, head_width),
-        ],
-        axis=1,
-    ).astype(LOW)
-    qkv_grad = column_product(normed_in_full, qkv_back).astype(LOW)
-    in_back_terms = times_transposed(qkv_back, qkv_cols).astype(LOW)
     in_back, qkv_grad, gate_up_grad = call(
         [
             Scatter(parts, block),

time: 620 us -> 596 us (0.961)
  matrix products: 97.2 us -> 56.6 us
  Pallas kernels: 440 us -> 462 us
  local copies, waits for them, and re-layouts: 30.9 us -> 24.6 us
    pallas_call x8, Pallas kernels: 440 us -> 462 us  [call(): pl.pallas_call(kernel, out_shape=tuple((job.out for job in jobs)) + tuple...]
    dot_general x6 -> x0, matrix products: 17.2 us -> none  [the longest x1 6.04 us: per_device(): jnp.einsum('qhd,khd->hqk', back_heads, values, preferred_element_type=jnp...]
    dot_general x4 -> x2, matrix products: 32 us -> 22.6 us  [times_transposed(): lax.dot_general(left, right, (((1,), (1,)), ((), ())), preferred_element_...]
    dot_general x3 -> x2, matrix products: 17.8 us -> 10.1 us  [column_product(): lax.dot_general(left, right, (((0,), (0,)), ((), ())), preferred_element_...]
    unnamed x81 -> x31, local copies, waits for them, and re-layouts: 19.2 us -> 12.6 us
    dot_general x4 -> x3, matrix products: 30.2 us -> 23.9 us  [dot(): return jnp.dot(left, right, preferred_element_type=jnp.float32)]
  transfers between devices with their start and end apart: 6 -> 6, of which waited for: 0 -> 0; matrix products, arithmetic and copies ran while one was open for 17% -> 11% of each run, Pallas kernels for 71% -> 79%
where the time goes in v6:
time: 596 us; the launch traced here: 587 us
  Pallas kernels  462 us (78%)
  matrix products  56.6 us (9%)
  other arithmetic  26.5 us (4%)
  local copies, waits for them, and re-layouts  24.6 us (4%)
  between operations  14.9 us (2%)
    pallas_call x8, Pallas kernels, call(): pl.pallas_call(kernel, out_shape=tuple((job.out for job in jobs)) + tuple...  462 us
    dot_general x3, matrix products, dot(): return jnp.dot(left, right, preferred_element_type=jnp.float32)  23.9 us
    dot_general x2, matrix products, times_transposed(): lax.dot_general(left, right, (((1,), (1,)), ((), ())), preferred_element_...  22.6 us
    unnamed x31, local copies, waits for them, and re-layouts  12.6 us
  transfers between devices with their start and end apart: 6, of which 0 were waited for; matrix products, arithmetic and copies ran while one was open for 11% of the time, Pallas kernels for 79%

profile of v6, /device:TPU:9, one launch (start us, length us, event | category | flops | bytes accessed | tf_op | source)
XLA Modules:
  0.0 587.0 jit_solution(17980937727358580364)
XLA Ops:
  8.7 2.3 reshape.205
  15.5 2.3 reshape.203.refs_0_
  19.6 58.6 %start.1 = (bf16[4,8,64,768]{3,2,1,0:T(8,128)(2,1)}, bf16[8,128,2048]{2,1,0:T(8,128)(2,1)}) custom-call(bf16[8,64,768]{2,1,0:T(8,128)(2,1)} %reshape.206.refs_0_, bf16[128,2048]{1,0:T(8,128)(2,1)} %fusion.5.refs_1_), custom_call_target="tpu_custom_call" | custom-call | bytes 210000000 | tf_op jit(solution)/shard_map/start/pallas_call | solution.py:551
  78.7 2.9 sine_multiply_fusion
  84.2 57.0 %attend.1 = (bf16[8,64,2048]{2,1,0:T(8,128)(2,1)}, bf16[2,128,2048]{2,1,0:T(8,128)(2,1)}, bf16[1024,768]{1,0:T(8,128)(2,1)}, bf16[1024,256]{1,0:T(8,128)(2,1)}) custom-call(bf16[8,64,2048]{2,1,0:T(8,128)(2,1)} %reshape.203.refs_0_, bf16[2,128,2048]{2,1,0:T(8,128)(2,1)} %bitcast.72, bf16[1024,2048]{1,0:T(8,128)(2,1)} %bitcast.53, bf16[2048,768]{1,0:T(8,128)(2,1)} %bitcast.57, ...), custom_call_target="tpu_custom_call" | custom-call | bytes 165000000 | tf_op jit(solution)/shard_map/attend/pallas_call | solution.py:551
  143.8 3.3 convolution_convert_fusion.1
  147.0 64.0 %out.1 = (f32[128,2048]{1,0:T(8,128)}, bf16[8,128,2048]{2,1,0:T(8,128)(2,1)}) custom-call(bf16[8,128,2048]{2,1,0:T(8,128)(2,1)} %bitcast.50, bf16[128,2048]{1,0:T(8,128)(2,1)} %refs_1_.1), custom_call_target="tpu_custom_call" | custom-call | bytes 192000000 | tf_op jit(solution)/shard_map/out/pallas_call | solution.py:551
  213.7 40.9 %mid.1 = bf16[8,128,2048]{2,1,0:T(8,128)(2,1)} custom-call(bf16[128,2048]{1,0:T(8,128)(2,1)} %fusion.11.refs_0_), custom_call_target="tpu_custom_call" | custom-call | bytes 135000000 | tf_op jit(solution)/shard_map/mid/pallas_call | solution.py:551
  254.7 14.6 %fusion.27 = f32[1024,2048]{1,0:T(8,128)} fusion(bf16[1024,2048]{1,0:T(8,128)(2,1)} %bitcast.51, bf16[2048,2048]{1,0:T(8,128)(2,1)} %all-gather.8.cloned.1.call-done), kind=kOutput, calls=%fused_computation.69 | convolution fusion | flops 8589934592 | bytes 20971520 | tf_op jit(solution)/shard_map/dot_general | solution.py:67
  269.3 10.0 %multiply_convert_fusion.1 = (bf16[1024,1024]{1,0:T(8,128)(2,1)}, bf16[1024,1024]{1,0:T(8,128)(2,1)}, bf16[1024,1024]{1,0:T(8,128)(2,1)S(1)}) fusion(f32[1024,2048]{1,0:T(8,128)} %fusion.27, bf16[1024,2048]{1,0:T(8,128)(2,1)S(1)} %bitcast.80, bf16[1024,2048]{1,0:T(8,128)(2,1)S(1)} %copy-done.9), kind=kOutput, calls=%fused_computation.2 | convolution fusion | flops 4310695936 | bytes 23068672 | tf_op jit(solution)/shard_map/dot_general | solution.py:71
  280.7 6.3 %convolution_convert_fusion.2 = bf16[1024,2048]{1,0:T(8,128)(2,1)} fusion(bf16[1024,1024]{1,0:T(8,128)(2,1)S(1)} %get-tuple-element.62, bf16[1024,2048]{1,0:T(8,128)(2,1)S(1)} %bitcast.81), kind=kOutput, calls=%fused_computation.8 | convolution fusion | flops 4297064448 | bytes 10485760 | tf_op jit(solution)/shard_map/dot_general | solution.py:77
  287.2 4.8 pad_maximum_fusion.refs_2_
  292.1 12.6 %convolution_convert_fusion = bf16[1024,2048]{1,0:T(8,128)(2,1)} fusion(bf16[2048,2048]{1,0:T(8,128)(2,1)} %all-gather.8.cloned.1.call-done, bf16[1024,1024]{1,0:T(8,128)(2,1)S(1)} %copy-done.5, bf16[1024,1024]{1,0:T(8,128)(2,1)S(1)} %copy-done.4), kind=kOutput, calls=%fused_computation.6 | convolution fusion | flops 8600420352 | bytes 16777216 | tf_op jit(solution)/shard_map/dot_general | solution.py:71
  304.6 48.7 %mid_back.1 = (f32[128,2048]{1,0:T(8,128)}, bf16[2048,2048]{1,0:T(8,128)(2,1)}) custom-call(bf16[8,128,2048]{2,1,0:T(8,128)(2,1)} %bitcast.63, bf16[1024,2048]{1,0:T(8,128)(2,1)} %bitcast.52, bf16[1024,2048]{1,0:T(8,128)(2,1)} %pad_maximum_fusion.refs_2_), custom_call_target="tpu_custom_call" | custom-call | bytes 150000000 | tf_op jit(solution)/shard_map/mid_back/pallas_call | solution.py:551
  353.3 2.8 convert_element_type.67
  357.7 2.7 fusion.25
  360.4 40.2 %proj_back.1 = bf16[8,128,2048]{2,1,0:T(8,128)(2,1)} custom-call(bf16[128,2048]{1,0:T(8,128)(2,1)} %get-tuple-element.56.refs_0_), custom_call_target="tpu_custom_call" | custom-call | bytes 135000000 | tf_op jit(solution)/shard_map/proj_back/pallas_call | solution.py:551
  400.6 3.9 convolution_convert_fusion.4
  405.5 6.0 %convolution_convert_fusion.3 = bf16[1024,2048]{1,0:T(8,128)(2,1)} fusion(bf16[1024,1024]{1,0:T(8,128)(2,1)S(1)} %copy-done.13, bf16[1024,2048]{1,0:T(8,128)(2,1)S(1)} %copy-done.10), kind=kOutput, calls=%fused_computation.9 | convolution fusion | flops 4297064448 | bytes 10485760 | tf_op jit(solution)/shard_map/dot_general | solution.py:67
  411.5 57.0 %attend_back.1 = (f32[128,2048]{1,0:T(8,128)}, bf16[2,128,2048]{2,1,0:T(8,128)(2,1)}, bf16[1024,2048]{1,0:T(8,128)(2,1)}, bf16[2048,768]{1,0:T(8,128)(2,1)}) custom-call(bf16[8,128,2048]{2,1,0:T(8,128)(2,1)} %bitcast.65, bf16[2,128,2048]{2,1,0:T(8,128)(2,1)} %bitcast.66, bf16[1024,2048]{1,0:T(8,128)(2,1)} %bitcast.56, bf16[256,2048]{1,0:T(8,128)(2,1)} %bitcast.60, ...), custom_call_target="tpu_custom_call" | custom-call | bytes 180000000 | tf_op jit(solution)/shard_map/attend_back/pallas_call | solution.py:551
  470.7 95.8 %in_back.1 = (f32[128,2048]{1,0:T(8,128)}, f32[64,6144]{1,0:T(8,128)}, f32[64,16384]{1,0:T(8,128)}) custom-call(bf16[8,128,2048]{2,1,0:T(8,128)(2,1)} %bitcast.64, bf16[4,8,64,768]{3,2,1,0:T(8,128)(2,1)} %bitcast.68, bf16[8,64,2048]{2,1,0:T(8,128)(2,1)} %bitcast.71), custom_call_target="tpu_custom_call" | custom-call | bytes 270000000 | tf_op jit(solution)/shard_map/in_back/pallas_call | solution.py:551
  568.1 2.6 fusion.9
  572.5 2.7 copy.34
  575.2 4.5 copy.35
  (82 shorter events, 25.6 us)
Async XLA Ops:
  7.2 74.4 %all-gather.4.cloned.1.call-start = ((), (), s32[]{:S(2)}) async-start(), calls=%async_computation.3 | async-start | bytes 1310720 | tf_op jit(solution)/shard_map/all_gather | solution.py:83
  7.9 133.4 %all-gather.6.cloned.1.call-start = ((), (), s32[]{:S(2)}) async-start(), calls=%async_computation.4 | async-start | bytes 5242880 | tf_op jit(solution)/shard_map/all_gather | solution.py:83
  8.6 246.0 %all-gather.8.cloned.1.call-start = ((), (), s32[]{:S(2)}) async-start(), calls=%async_computation.5 | async-start | bytes 10485760 | tf_op jit(solution)/shard_map/all_gather | solution.py:83
  15.0 2.8 copy-start.8
  15.0 3.0 copy-start
  15.5 62.7 %copy-start.7 = (s32[1,8]{1,0:T(1,128)S(1)}, s32[1,8]{1,0:T(1,128)}, u32[]{:S(2)}) copy-start(s32[1,8]{1,0:T(1,128)} %param.14) | copy-start | bytes 100
  141.3 2.5 copy-start.6
  141.3 212.0 %reduce-scatter.4.cloned.1.call-start = ((), (), s32[]{:S(2)}) async-start(), calls=%async_computation.6 | async-start | bytes 5242880 | tf_op jit(solution)/shard_map/reduce_scatter | solution.py:87
  142.8 1.0 copy-start.1
  254.6 14.7 %copy-start.9 = (bf16[1024,2048]{1,0:T(8,128)(2,1)S(1)}, bf16[1024,2048]{1,0:T(8,128)(2,1)}, u32[]{:S(2)}) copy-start(bf16[1024,2048]{1,0:T(8,128)(2,1)} %all-gather.6.cloned.1.call-done) | copy-start | bytes 12582916
  254.7 14.7 %copy-start.11 = (bf16[8,128,2048]{2,1,0:T(8,128)(2,1)S(1)}, bf16[8,128,2048]{2,1,0:T(8,128)(2,1)}, u32[]{:S(2)}) copy-start(bf16[8,128,2048]{2,1,0:T(8,128)(2,1)} %get-tuple-element.37) | copy-start | bytes 12582916
  279.3 1.3 copy-start.12
  287.0 181.6 %reduce-scatter.6.cloned.1.call-start = ((), (), s32[]{:S(2)}) async-start(), calls=%async_computation.7 | async-start | bytes 10485760 | tf_op jit(solution)/shard_map/reduce_scatter | solution.py:87
  287.2 4.9 copy-start.4
  287.2 4.9 copy-start.5
  356.1 1.2 copy-start.3
  356.2 214.6 %reduce-scatter.8.cloned.1.call-start = ((), (), s32[]{:S(2)}) async-start(), calls=%async_computation.8 | async-start | bytes 1310720 | tf_op jit(solution)/shard_map/reduce_scatter | solution.py:87
  400.6 4.9 copy-start.10
  400.6 4.9 copy-start.13
  470.7 97.4 %copy-start.2 = (f32[128,2048]{1,0:T(8,128)S(1)}, f32[128,2048]{1,0:T(8,128)}, u32[]{:S(2)}) copy-start(f32[128,2048]{1,0:T(8,128)} %get-tuple-element.57) | copy-start | bytes 3145732
Sparse Core Ops, SparseCore 0:
  9.8 39.2 all-gather.3
  51.0 57.2 all-gather.5
  141.5 86.9 all-gather.7
  287.1 57.1 reduce-scatter.3
  356.3 85.5 reduce-scatter.5
  468.7 42.1 reduce-scatter.7

commit v7 on v6

--- a/solution.py
+++ b/solution.py
@@ -141,8 +141,8 @@
 
 
 class Gather:
-    def __init__(self, parts, shape):
-        self.parts = parts
+    def __init__(self, parts, shape, watched=False):
+        self.parts, self.watched = parts, watched
         self.out = jax.ShapeDtypeStruct((parts,) + shape, LOW)
         chips = parts // 2
         self.scratch = [
@@ -168,6 +168,17 @@
             return remote(block, slot, pair_send.at[origin], pair_recv.at[origin], "ctx", partner)
 
         mine = dst.at[me]
+        own = pltpu.make_async_copy(src, mine, local)
+
+        def arrived(origin):
+            other = dst.at[2 * origin + 1 - core]
+            across(other, other, origin).wait_recv()
+
+            @pl.when(origin == chip)
+            def _():
+                own.wait()
+
+        self.dst, self.arrived = dst, arrived
 
         @pl.when(chip < chips - 1)
         def _():
@@ -178,9 +189,10 @@
             line(src, mine, chip, 1).start()
 
         across(src, mine, chip).start()
-        own = pltpu.make_async_copy(src, mine, local)
         own.start()
         yield
+        if self.watched:
+            yield
         for step in range(1, chips):
             for way in range(2):
                 origin = chip - step if way == 0 else chip + step
@@ -209,9 +221,8 @@
 
         for origin in range(chips):
             across(dst.at[2 * origin + core], dst.at[2 * origin + core], origin).wait_send()
-            other = dst.at[2 * origin + 1 - core]
-            across(other, other, origin).wait_recv()
-        own.wait()
+            if not self.watched:
+                arrived(origin)
 
 
 class Scatter:
@@ -816,6 +827,100 @@
         puts.finish()
 
 
+def near_first(chips):
+    table = []
+    for chip in range(chips):
+        order = [chip]
+        for step in range(1, chips):
+            order += [at for at in (chip + step, chip - step) if 0 <= at < chips]
+        table.append(order)
+    return table
+
+
+class FeedForward:
+    def __init__(self, job, upstream, gate_up, down):
+        self.job = job
+        self.operands = [upstream, gate_up, down]
+        length, width = upstream.shape
+        wide = gate_up.shape[1]
+        self.outs = [
+            jax.ShapeDtypeStruct((length, wide // 2), LOW),
+            jax.ShapeDtypeStruct((length, wide), LOW),
+            jax.ShapeDtypeStruct((length, width), LOW),
+        ]
+        self.tile = length // (job.parts // 2)
+        self.scratch = [pltpu.VMEM(array.shape, array.dtype) for array in self.operands]
+        self.scratch += [pltpu.VMEM((2, self.tile) + out.shape[1:], LOW) for out in self.outs]
+        self.scratch += [pltpu.SemaphoreType.DMA((3,)), pltpu.SemaphoreType.DMA((3, 2))]
+
+    def run(self, *refs):
+        job, tile = self.job, self.tile
+        sources, results, held, made = refs[:3], refs[3:6], refs[6:9], refs[9:12]
+        get, put = refs[12:]
+        upstream, gate_up, down = held
+        acts, backs, terms = made
+        rows = tile // 2
+        width, wide = gate_up.shape
+        units = wide // 2
+        step = min(units, 256)
+        span = min(width, 512)
+        chip = lax.axis_index("ctx") // 2
+        gets = [pltpu.make_async_copy(sources[i], held[i], get.at[i]) for i in (1, 2, 0)]
+        for copy in gets:
+            copy.start()
+        yield
+        for copy in gets:
+            copy.wait()
+        table = near_first(job.parts // 2)
+        puts = []
+        for turn in range(len(table)):
+            origin = sum(jnp.where(chip == at, order[turn], 0) for at, order in enumerate(table))
+            slot = turn % 2
+            if turn >= 2:
+                for copy in puts[turn - 2]:
+                    copy.wait()
+            job.arrived(origin)
+            at = pl.ds(pl.multiple_of(origin * tile, tile), tile)
+            normed = job.dst.at[pl.ds(2 * origin, 2)]
+
+            def forward(index, carry):
+                left = pl.ds(pl.multiple_of(index * step, step), step)
+                right = pl.ds(pl.multiple_of(units + index * step, step), step)
+                value = normed[...].reshape(tile, width)
+                gate = product(value, gate_up[:, left])
+                up = product(value, gate_up[:, right])
+                act_grad = times_transposed(upstream[at, :], down[left, :])
+                sigmoid = jax.nn.sigmoid(gate)
+                silu = gate * sigmoid
+                acts[slot, :, left] = (silu * up).astype(LOW)
+                gate_grad = act_grad * up * sigmoid * (1.0 + gate * (1.0 - sigmoid))
+                backs[slot, :, left] = gate_grad.astype(LOW)
+                backs[slot, :, right] = (act_grad * silu).astype(LOW)
+                return carry
+
+            lax.fori_loop(0, units // step, forward, 0)
+
+            def backward(index, carry):
+                where = pl.ds(pl.multiple_of(index * span, span), span)
+                value = times_transposed(backs[slot], gate_up[where, :])
+                terms[slot, :, where] = value.astype(LOW)
+                return carry
+
+            lax.fori_loop(0, width // span, backward, 0)
+            puts.append(
+                [
+                    pltpu.make_async_copy(made[i].at[slot], results[i].at[at, :], put.at[i, slot])
+                    for i in range(3)
+                ]
+            )
+            for copy in puts[-1]:
+                copy.start()
+            yield
+        for copies in puts[-2:]:
+            for copy in copies:
+                copy.wait()
+
+
 class Plan:
     def __init__(self, parts, groups, width):
         self.parts, self.groups = parts, groups
@@ -931,22 +1036,18 @@
     cot_full = cot_full.reshape(length, width)
     residual = inputs + attn_out
     normed_mid, root_mid = normalize(residual)
-    (normed_mid_full,) = call([Gather(parts, block)], [normed_mid.astype(LOW)], "mid", 4, line, micros=45)
+    mid_job = Gather(parts, block, watched=True)
+    normed_mid_full, activated, gate_up_back, mid_back_terms = call(
+        [mid_job],
+        [normed_mid.astype(LOW)],
+        "mid",
+        4,
+        line,
+        FeedForward(mid_job, cot_full, gate_up_cols, down_rows),
+        micros=60,
+    )
     normed_mid_full = normed_mid_full.reshape(length, width)
-
-    gate_up = dot(normed_mid_full, gate_up_cols)
-    units = gate_up.shape[1] // 2
-    gate_part = gate_up[:, :units]
-    up_part = gate_up[:, units:]
-    sigmoid_gate = jax.nn.sigmoid(gate_part)
-    silu_gate = gate_part * sigmoid_gate
-    activated = (silu_gate * up_part).astype(LOW)
-    act_grad = times_transposed(cot_full, down_rows)
-    gate_grad = act_grad * up_part * sigmoid_gate * (1.0 + gate_part * (1.0 - sigmoid_gate))
-    up_grad = act_grad * silu_gate
-    gate_up_back = jnp.concatenate([gate_grad, up_grad], axis=1).astype(LOW)
     down_grad = scatter(column_product(activated, cot_full).astype(LOW), "fsdp").astype(jnp.float32)
-    mid_back_terms = times_transposed(gate_up_back, gate_up_cols).astype(LOW)
     mid_back, gate_up_grad = call(
         [Scatter(parts, block)],
         [mid_back_terms.reshape((parts,) + block)],

time: 596 us -> 587 us (0.985)
  matrix products: 56.6 us -> 22.6 us
  waiting for transfers between devices: 1.53 us -> 24.1 us
  Pallas kernels: 462 us -> 472 us
    dot_general x2 -> x0, matrix products: 22.6 us -> none  [times_transposed(): lax.dot_general(left, right, (((1,), (1,)), ((), ())), preferred_element_...]
    all_gather x3, waiting for transfers between devices: 0.04 us -> 15.1 us  [gather(): return lax.all_gather(values, axes, axis=0, tiled=True)]
    dot_general x3 -> x2, matrix products: 23.9 us -> 9.29 us  [dot(): return jnp.dot(left, right, preferred_element_type=jnp.float32)]
    pallas_call x8, Pallas kernels: 462 us -> 472 us  [call(): pl.pallas_call(kernel, out_shape=tuple((job.out for job in jobs)) + tuple...]
    reduce_scatter x3, waiting for transfers between devices: 0.04 us -> 7.64 us  [scatter(): return lax.psum_scatter(values, axes, scatter_dimension=0, tiled=True)]
    unnamed x31 -> x21, local copies, waits for them, and re-layouts: 12.6 us -> 11.4 us
  transfers between devices with their start and end apart: 6 -> 6, of which waited for: 0 -> 2; matrix products, arithmetic and copies ran while one was open for 11% -> 8% of each run, Pallas kernels for 79% -> 74%
where the time goes in v7:
time: 587 us; the launch traced here: 578 us
  Pallas kernels  472 us (80%)
  waiting for transfers between devices  24.1 us (4%)
  local copies, waits for them, and re-layouts  23.4 us (4%)
  matrix products  22.6 us (4%)
  other arithmetic  21.6 us (4%)
  between operations  14.6 us (2%)
    pallas_call x8, Pallas kernels, call(): pl.pallas_call(kernel, out_shape=tuple((job.out for job in jobs)) + tuple...  472 us
    all_gather x3, waiting for transfers between devices, gather(): return lax.all_gather(values, axes, axis=0, tiled=True)  15.1 us
    dot_general x2, matrix products, column_product(): lax.dot_general(left, right, (((0,), (0,)), ((), ())), preferred_element_...  13.3 us
  transfers between devices with their start and end apart: 6, of which 2 were waited for; matrix products, arithmetic and copies ran while one was open for 8% of the time, Pallas kernels for 74%

profile of v7, /device:TPU:9, one launch (start us, length us, event | category | flops | bytes accessed | tf_op | source)
XLA Modules:
  0.0 578.4 jit_solution(8688642613282593429)
XLA Ops:
  8.7 2.3 reshape.205
  12.9 2.1 copy.22
  15.5 2.3 reshape.203.refs_0_
  19.6 58.6 %start.1 = (bf16[4,8,64,768]{3,2,1,0:T(8,128)(2,1)}, bf16[8,128,2048]{2,1,0:T(8,128)(2,1)}) custom-call(bf16[8,64,768]{2,1,0:T(8,128)(2,1)} %reshape.206.refs_0_, bf16[128,2048]{1,0:T(8,128)(2,1)} %fusion.4.refs_1_), custom_call_target="tpu_custom_call" | custom-call | bytes 210000000 | tf_op jit(solution)/shard_map/start/pallas_call | solution.py:562
  78.7 2.9 sine_multiply_fusion
  84.2 57.1 %attend.1 = (bf16[8,64,2048]{2,1,0:T(8,128)(2,1)}, bf16[2,128,2048]{2,1,0:T(8,128)(2,1)}, bf16[1024,768]{1,0:T(8,128)(2,1)}, bf16[1024,256]{1,0:T(8,128)(2,1)}) custom-call(bf16[8,64,2048]{2,1,0:T(8,128)(2,1)} %reshape.203.refs_0_, bf16[2,128,2048]{2,1,0:T(8,128)(2,1)} %bitcast.68, bf16[1024,2048]{1,0:T(8,128)(2,1)} %bitcast.46, bf16[2048,768]{1,0:T(8,128)(2,1)} %bitcast.50, ...), custom_call_target="tpu_custom_call" | custom-call | bytes 165000000 | tf_op jit(solution)/shard_map/attend/pallas_call | solution.py:562
  143.8 3.3 convolution_convert_fusion
  147.1 63.8 %out.1 = (f32[128,2048]{1,0:T(8,128)}, bf16[8,128,2048]{2,1,0:T(8,128)(2,1)}) custom-call(bf16[8,128,2048]{2,1,0:T(8,128)(2,1)} %bitcast.45, bf16[128,2048]{1,0:T(8,128)(2,1)} %refs_1_.1), custom_call_target="tpu_custom_call" | custom-call | bytes 192000000 | tf_op jit(solution)/shard_map/out/pallas_call | solution.py:562
  213.5 15.0 %all-gather.8.cloned.1.call-done.refs_2_ = bf16[2048,2048]{1,0:T(8,128)(2,1)} async-done(((bf16[512,2048]{1,0:T(8,128)(2,1)}), bf16[2048,2048]{1,0:T(8,128)(2,1)}) %all-gather.8.cloned.1.call-update) | async-done | bytes 8388624 | tf_op jit(solution)/shard_map/all_gather | solution.py:83
  228.5 46.3 %mid.1 = (bf16[8,128,2048]{2,1,0:T(8,128)(2,1)}, bf16[1024,1024]{1,0:T(8,128)(2,1)}, bf16[1024,2048]{1,0:T(8,128)(2,1)}, bf16[1024,2048]{1,0:T(8,128)(2,1)}) custom-call(bf16[128,2048]{1,0:T(8,128)(2,1)} %fusion.10.refs_0_, bf16[1024,2048]{1,0:T(8,128)(2,1)} %bitcast.59, bf16[2048,2048]{1,0:T(8,128)(2,1)} %all-gather.8.cloned.1.call-done.refs_2_, ...), custom_call_target="tpu_custom_call" | custom-call | bytes 180000000 | tf_op jit(solution)/shard_map/mid/pallas_call | solution.py:562
  274.8 9.4 %convolution_convert_fusion.1 = bf16[1024,2048]{1,0:T(8,128)(2,1)} fusion(bf16[1024,1024]{1,0:T(8,128)(2,1)} %get-tuple-element.42, bf16[1024,2048]{1,0:T(8,128)(2,1)} %bitcast.60), kind=kOutput, calls=%fused_computation.1 | convolution fusion | flops 4297064448 | bytes 10485760 | tf_op jit(solution)/shard_map/dot_general | solution.py:77
  284.3 51.8 %mid_back.1 = (f32[128,2048]{1,0:T(8,128)}, bf16[2048,2048]{1,0:T(8,128)(2,1)}) custom-call(bf16[8,128,2048]{2,1,0:T(8,128)(2,1)} %bitcast.57, bf16[1024,2048]{1,0:T(8,128)(2,1)} %bitcast.56, bf16[1024,2048]{1,0:T(8,128)(2,1)} %get-tuple-element.45.refs_2_), custom_call_target="tpu_custom_call" | custom-call | bytes 150000000 | tf_op jit(solution)/shard_map/mid_back/pallas_call | solution.py:562
  336.0 7.6 %reduce-scatter.4.cloned.1.call-done = bf16[256,2048]{1,0:T(8,128)(2,1)} async-done(((bf16[1024,2048]{1,0:T(8,128)(2,1)}), bf16[256,2048]{1,0:T(8,128)(2,1)}) %reduce-scatter.4.cloned.1.call-update) | async-done | bytes 1048592 | tf_op jit(solution)/shard_map/reduce_scatter | solution.py:87
  343.6 2.8 convert_element_type.58
  348.0 2.7 fusion.24
  350.7 41.2 %proj_back.1 = bf16[8,128,2048]{2,1,0:T(8,128)(2,1)} custom-call(bf16[128,2048]{1,0:T(8,128)(2,1)} %get-tuple-element.64.refs_0_), custom_call_target="tpu_custom_call" | custom-call | bytes 135000000 | tf_op jit(solution)/shard_map/proj_back/pallas_call | solution.py:562
  391.9 3.9 convolution_convert_fusion.3
  396.8 6.0 %convolution_convert_fusion.2 = bf16[1024,2048]{1,0:T(8,128)(2,1)} fusion(bf16[1024,1024]{1,0:T(8,128)(2,1)S(1)} %copy-done.8, bf16[1024,2048]{1,0:T(8,128)(2,1)S(1)} %copy-done.4), kind=kOutput, calls=%fused_computation.2 | convolution fusion | flops 4297064448 | bytes 10485760 | tf_op jit(solution)/shard_map/dot_general | solution.py:67
  402.8 57.9 %attend_back.1 = (f32[128,2048]{1,0:T(8,128)}, bf16[2,128,2048]{2,1,0:T(8,128)(2,1)}, bf16[1024,2048]{1,0:T(8,128)(2,1)}, bf16[2048,768]{1,0:T(8,128)(2,1)}) custom-call(bf16[8,128,2048]{2,1,0:T(8,128)(2,1)} %bitcast.61, bf16[2,128,2048]{2,1,0:T(8,128)(2,1)} %bitcast.62, bf16[1024,2048]{1,0:T(8,128)(2,1)} %bitcast.49, bf16[256,2048]{1,0:T(8,128)(2,1)} %bitcast.53, ...), custom_call_target="tpu_custom_call" | custom-call | bytes 180000000 | tf_op jit(solution)/shard_map/attend_back/pallas_call | solution.py:562
  460.8 2.1 add_convert_fusion
  463.0 95.2 %in_back.1 = (f32[128,2048]{1,0:T(8,128)}, f32[64,6144]{1,0:T(8,128)}, f32[64,16384]{1,0:T(8,128)}) custom-call(bf16[8,128,2048]{2,1,0:T(8,128)(2,1)} %bitcast.58, bf16[4,8,64,768]{3,2,1,0:T(8,128)(2,1)} %bitcast.64, bf16[8,64,2048]{2,1,0:T(8,128)(2,1)} %bitcast.67), custom_call_target="tpu_custom_call" | custom-call | bytes 270000000 | tf_op jit(solution)/shard_map/in_back/pallas_call | solution.py:562
  559.8 2.6 fusion.8
  564.2 2.7 copy.29
  566.8 4.5 copy.30
  (68 shorter events, 19.7 us)
Async XLA Ops:
  7.2 74.4 %all-gather.4.cloned.1.call-start = ((), (), s32[]{:S(2)}) async-start(), calls=%async_computation.3 | async-start | bytes 1310720 | tf_op jit(solution)/shard_map/all_gather | solution.py:83
  7.9 133.4 %all-gather.6.cloned.1.call-start = ((), (), s32[]{:S(2)}) async-start(), calls=%async_computation.4 | async-start | bytes 5242880 | tf_op jit(solution)/shard_map/all_gather | solution.py:83
  8.6 219.9 %all-gather.8.cloned.1.call-start = ((), (), s32[]{:S(2)}) async-start(), calls=%async_computation.5 | async-start | bytes 10485760 | tf_op jit(solution)/shard_map/all_gather | solution.py:83
  15.0 2.8 copy-start.7
  15.0 3.0 copy-start
  15.5 62.7 %copy-start.6 = (s32[1,8]{1,0:T(1,128)S(1)}, s32[1,8]{1,0:T(1,128)}, u32[]{:S(2)}) copy-start(s32[1,8]{1,0:T(1,128)} %param.14) | copy-start | bytes 100
  141.3 2.5 copy-start.5
  141.4 202.3 %reduce-scatter.4.cloned.1.call-start = ((), (), s32[]{:S(2)}) async-start(), calls=%async_computation.6 | async-start | bytes 5242880 | tf_op jit(solution)/shard_map/reduce_scatter | solution.py:87
  142.8 1.0 copy-start.1
  284.2 176.6 %reduce-scatter.6.cloned.1.call-start = ((), (), s32[]{:S(2)}) async-start(), calls=%async_computation.7 | async-start | bytes 10485760 | tf_op jit(solution)/shard_map/reduce_scatter | solution.py:87
  346.4 1.2 copy-start.3
  346.5 215.9 %reduce-scatter.8.cloned.1.call-start = ((), (), s32[]{:S(2)}) async-start(), calls=%async_computation.8 | async-start | bytes 1310720 | tf_op jit(solution)/shard_map/reduce_scatter | solution.py:87
  391.9 4.9 copy-start.4
  391.9 4.9 copy-start.8
  463.0 96.8 %copy-start.2 = (f32[128,2048]{1,0:T(8,128)S(1)}, f32[128,2048]{1,0:T(8,128)}, u32[]{:S(2)}) copy-start(f32[128,2048]{1,0:T(8,128)} %get-tuple-element.65) | copy-start | bytes 3145732
Sparse Core Ops, SparseCore 0:
  9.8 39.2 all-gather.3
  51.0 57.2 all-gather.5
  141.5 86.9 all-gather.7
  284.3 59.2 reduce-scatter.3
  346.6 86.3 reduce-scatter.5
  460.9 38.9 reduce-scatter.7

commit v8 on v7

--- a/solution.py
+++ b/solution.py
@@ -141,74 +141,97 @@
 
 
 class Gather:
-    def __init__(self, parts, shape, watched=False):
-        self.parts, self.watched = parts, watched
+    def __init__(self, parts, shape, watched=False, cuts=2):
+        self.parts, self.watched, self.shape, self.cuts = parts, watched, shape, cuts
         self.out = jax.ShapeDtypeStruct((parts,) + shape, LOW)
         chips = parts // 2
         self.scratch = [
-            pltpu.SemaphoreType.DMA((2, chips)),
-            pltpu.SemaphoreType.DMA((chips,)),
-            pltpu.SemaphoreType.DMA((chips,)),
-            pltpu.SemaphoreType.DMA((chips,)),
+            pltpu.SemaphoreType.DMA((2, chips, self.cuts)),
+            pltpu.SemaphoreType.DMA((chips, self.cuts)),
+            pltpu.SemaphoreType.DMA((chips, self.cuts)),
+            pltpu.SemaphoreType.DMA((chips, self.cuts)),
             pltpu.SemaphoreType.DMA,
         ]
 
     def run(self, src, dst, send, recv, pair_send, pair_recv, local):
-        chips = self.parts // 2
+        chips, cuts = self.parts // 2, self.cuts
+        rows = self.shape[0] // cuts
         me = lax.axis_index("ctx")
         chip, core = me // 2, lax.rem(me, 2)
         partner = me + 1 - 2 * core
 
-        def line(block, slot, origin, way):
+        def piece(block, cut):
+            return block.at[pl.ds(cut * rows, rows)]
+
+        def line(block, slot, origin, way, cut):
             return remote(
-                block, slot, send.at[way, origin], recv.at[origin], "ctx", me + 2 - 4 * way
+                piece(block, cut),
+                piece(slot, cut),
+                send.at[way, origin, cut],
+                recv.at[origin, cut],
+                "ctx",
+                me + 2 - 4 * way,
             )
 
-        def across(block, slot, origin):
-            return remote(block, slot, pair_send.at[origin], pair_recv.at[origin], "ctx", partner)
+        def across(block, slot, origin, cut):
+            return remote(
+                piece(block, cut),
+                piece(slot, cut),
+                pair_send.at[origin, cut],
+                pair_recv.at[origin, cut],
+                "ctx",
+                partner,
+            )
 
         mine = dst.at[me]
         own = pltpu.make_async_copy(src, mine, local)
 
         def arrived(origin):
             other = dst.at[2 * origin + 1 - core]
-            across(other, other, origin).wait_recv()
+            for cut in range(cuts):
+                across(other, other, origin, cut).wait_recv()
 
             @pl.when(origin == chip)
             def _():
                 own.wait()
 
-        self.dst, self.arrived = dst, arrived
-
-        @pl.when(chip < chips - 1)
-        def _():
-            line(src, mine, chip, 0).start()
-
-        @pl.when(chip > 0)
-        def _():
-            line(src, mine, chip, 1).start()
-
-        across(src, mine, chip).start()
+        def relay(step):
+            for cut in range(cuts):
+                for way in range(2):
+                    origin = chip - step if way == 0 else chip + step
+
+                    @pl.when((origin >= 0) & (origin < chips))
+                    def _():
+                        slot = dst.at[2 * origin + core]
+                        line(slot, slot, origin, way, cut).wait_recv()
+
+                        @pl.when((chip < chips - 1) if way == 0 else (chip > 0))
+                        def _():
+                            line(slot, slot, origin, way, cut).start()
+
+                        across(slot, slot, origin, cut).start()
+
+        self.dst, self.arrived, self.relay = dst, arrived, relay
+        for cut in range(cuts):
+
+            @pl.when(chip < chips - 1)
+            def _():
+                line(src, mine, chip, 0, cut).start()
+
+            @pl.when(chip > 0)
+            def _():
+                line(src, mine, chip, 1, cut).start()
+
+        for cut in range(cuts):
+            across(src, mine, chip, cut).start()
         own.start()
         yield
         if self.watched:
             yield
         for step in range(1, chips):
-            for way in range(2):
-                origin = chip - step if way == 0 else chip + step
-
-                @pl.when((origin >= 0) & (origin < chips))
-                def _():
-                    slot = dst.at[2 * origin + core]
-                    line(slot, slot, origin, way).wait_recv()
-
-                    @pl.when((chip < chips - 1) if way == 0 else (chip > 0))
-                    def _():
-                        line(slot, slot, origin, way).start()
-
-                    across(slot, slot, origin).start()
-
-            yield
+            if not self.watched:
+                relay(step)
+                yield
         for step in range(chips):
             for way in range(2):
                 origin = chip - step if way == 0 else chip + step
@@ -217,19 +240,20 @@
                 @pl.when((origin >= 0) & (origin < chips) & ahead)
                 def _():
                     slot = dst.at[2 * origin + core]
-                    line(slot, slot, origin, way).wait_send()
+                    for cut in range(cuts):
+                        line(slot, slot, origin, way, cut).wait_send()
 
         for origin in range(chips):
-            across(dst.at[2 * origin + core], dst.at[2 * origin + core], origin).wait_send()
+            slot = dst.at[2 * origin + core]
+            for cut in range(cuts):
+                across(slot, slot, origin, cut).wait_send()
             if not self.watched:
                 arrived(origin)
 
 
 class Scatter:
-    cuts = 2
-
-    def __init__(self, parts, shape):
-        self.parts, self.shape = parts, shape
+    def __init__(self, parts, shape, cuts=2):
+        self.parts, self.shape, self.cuts = parts, shape, cuts
         self.out = jax.ShapeDtypeStruct(shape, jnp.float32)
         chips = parts // 2
         piece = (self.cuts, shape[0] // self.cuts, shape[1])
@@ -575,6 +599,236 @@
     )(*operands, *extra)
 
 
+def product(left, right):
+    return jnp.dot(left, right, preferred_element_type=jnp.float32)
+
+
+class Puts:
+    def __init__(self, made, put):
+        self.made, self.put, self.copies = made, put, []
+
+    def pair(self, fill, columns, out, at, tile):
+        for copy in self.copies:
+            copy.wait()
+        lax.fori_loop(0, 2, fill, 0)
+        self.copies = []
+        for half in range(2):
+            begin = at + half * tile
+            copy = pltpu.make_async_copy(
+                self.made.at[half, :, pl.ds(0, columns)],
+                out.at[begin : begin + tile, :],
+                self.put.at[half],
+            )
+            copy.start()
+            self.copies.append(copy)
+
+    def finish(self):
+        for copy in self.copies:
+            copy.wait()
+
+
+class Grads:
+    tile = 256
+
+    def __init__(self, pairs):
+        self.pairs = pairs
+        length, wide = pairs[0][0].shape[0], max(right.shape[1] for _, right in pairs)
+        self.operands = [array for pair in pairs for array in pair]
+        self.outs = [jax.ShapeDtypeStruct((l.shape[1], r.shape[1]), LOW) for l, r in pairs]
+        self.scratch = [pltpu.VMEM(array.shape, LOW) for array in self.operands]
+        self.scratch += [
+            pltpu.VMEM((self.tile, length), LOW),
+            pltpu.VMEM((2, self.tile, wide), LOW),
+            pltpu.SemaphoreType.DMA((2 * len(pairs),)),
+            pltpu.SemaphoreType.DMA((2,)),
+        ]
+
+    def run(self, *refs):
+        n, tile = len(self.pairs), self.tile
+        sources, outs = refs[: 2 * n], refs[2 * n : 3 * n]
+        held = refs[3 * n : 5 * n]
+        turned, made, get, put = refs[5 * n :]
+        gets = [pltpu.make_async_copy(s, h, get.at[i]) for i, (s, h) in enumerate(zip(sources, held))]
+        for copy in gets:
+            copy.start()
+        yield
+        puts = Puts(made, put)
+        for which in range(n):
+            left, right, out = held[2 * which], held[2 * which + 1], outs[which]
+            gets[2 * which].wait()
+            gets[2 * which + 1].wait()
+            columns = right.shape[1]
+            step = min(columns, 256)
+            for at in range(0, left.shape[1], 2 * tile):
+                def pair(half, carry):
+                    begin = pl.multiple_of(at + half * tile, tile)
+                    turned[...] = left[:, pl.ds(begin, tile)].T
+
+                    def one(index, carry):
+                        where = pl.ds(pl.multiple_of(index * step, step), step)
+                        made[half, :, where] = product(turned[...], right[:, where]).astype(LOW)
+                        return carry
+
+                    return lax.fori_loop(0, columns // step, one, carry)
+
+                puts.pair(pair, columns, out, at, tile)
+                yield
+        puts.finish()
+
+
+class Deliver:
+    def __init__(self, parts, shape, offsets):
+        self.parts, self.shape, self.offsets = parts, shape, offsets
+        self.out = jax.ShapeDtypeStruct((shape[0], parts * shape[1]), jnp.float32)
+        self.scratch = [
+            pltpu.VMEM((parts - 1,) + shape, LOW),
+            pltpu.SemaphoreType.DMA((parts - 1,)),
+            pltpu.SemaphoreType.DMA((parts - 1,)),
+        ]
+
+    def place(self, out, origin, read):
+        starts = self.offsets(origin)
+        step = self.shape[1] // len(starts)
+        for index, start in enumerate(starts):
+            out[:, pl.ds(pl.multiple_of(start, HEAD_DIM), step)] = read(
+                index * step, (index + 1) * step
+            )
+
+    def send(self, me, step, block, came, send, recv):
+        return remote(
+            block,
+            came.at[step - 1],
+            send.at[step - 1],
+            recv.at[step - 1],
+            "ctx",
+            lax.rem(me + step, self.parts),
+        )
+
+    def run(self, src, out, came, send, recv):
+        me = lax.axis_index("ctx")
+        copies = []
+        for step in range(1, self.parts):
+            block = src.at[lax.rem(me + step, self.parts)]
+            copies.append(self.send(me, step, block, came, send, recv))
+            copies[-1].start()
+        self.place(out, me, lambda lo, hi: src[me, :, lo:hi].astype(jnp.float32))
+        yield
+        yield from self.finish(me, out, copies, came)
+
+    def finish(self, me, out, copies, came):
+        for step in range(1, self.parts):
+            copies[step - 1].wait_recv()
+            origin = lax.rem(me - step + self.parts, self.parts)
+            self.place(out, origin, lambda lo, hi: came[step - 1, :, lo:hi].astype(jnp.float32))
+            yield
+        for copy in copies:
+            copy.wait_send()
+
+
+class Collect(Deliver):
+    def __init__(self, parts, groups, shape, offsets):
+        super().__init__(parts, shape, offsets)
+        self.groups = groups
+        self.scratch = self.scratch + [
+            pltpu.VMEM((groups - 1, parts) + shape, LOW),
+            pltpu.VMEM((parts,) + shape, LOW),
+            pltpu.VMEM(shape, jnp.float32),
+            pltpu.SemaphoreType.DMA((groups - 1, parts)),
+            pltpu.SemaphoreType.DMA((groups - 1, parts)),
+        ]
+
+    def run(self, src, out, came, send, recv, far, stage, mine, far_send, far_recv):
+        parts, groups = self.parts, self.groups
+        me, group = lax.axis_index("ctx"), lax.axis_index("fsdp")
+        goals = [lax.rem(me + step, parts) for step in range(1, parts + 1)]
+        hops = []
+        for goal in goals:
+            for hop in range(1, groups):
+                peer = lax.rem(group + hop, groups)
+                hops.append(
+                    remote(
+                        src.at[peer, goal],
+                        far.at[hop - 1, goal],
+                        far_send.at[hop - 1, goal],
+                        far_recv.at[hop - 1, goal],
+                        "fsdp",
+                        peer,
+                    )
+                )
+                hops[-1].start()
+        yield
+        copies = []
+        for step in range(1, parts + 1):
+            goal = goals[step - 1]
+            for copy in hops[(step - 1) * (groups - 1) : step * (groups - 1)]:
+                copy.wait_recv()
+            value = src[group, goal].astype(jnp.float32)
+            for hop in range(groups - 1):
+                value += far[hop, goal].astype(jnp.float32)
+            if step < parts:
+                stage[goal] = value.astype(LOW)
+                copies.append(self.send(me, step, stage.at[goal], came, send, recv))
+                copies[-1].start()
+            else:
+                mine[...] = value
+            yield
+        self.place(out, me, lambda lo, hi: mine[:, lo:hi])
+        yield from self.finish(me, out, copies, came)
+        for copy in hops:
+            copy.wait_send()
+
+
+def call(jobs, operands, name, identity, axes, work=None, micros=50):
+    counts = [len(job.scratch) for job in jobs]
+    jobs_n = len(jobs)
+    extra = work.operands if work else []
+    extra_out = work.outs if work else []
+    extra_scratch = work.scratch if work else []
+
+    def kernel(*refs):
+        refs = list(refs)
+
+        def take(count):
+            taken = refs[:count]
+            del refs[:count]
+            return taken
+
+        ins, more = take(jobs_n), take(len(extra))
+        outs, more_outs = take(jobs_n), take(len(extra_out))
+        runs = []
+        for job, src, dst, count in zip(jobs, ins, outs, counts):
+            runs.append(job.run(src, dst, *take(count)))
+        if work:
+            runs.append(work.run(*more, *more_outs, *refs))
+        enter(axes)
+        while runs:
+            going = []
+            for run in runs:
+                try:
+                    next(run)
+                    going.append(run)
+                except StopIteration:
+                    pass
+            runs = going
+
+    vmem = pl.BlockSpec(memory_space=pltpu.VMEM)
+    anywhere = pl.BlockSpec(memory_space=pl.ANY)
+    return pl.pallas_call(
+        kernel,
+        out_shape=tuple(job.out for job in jobs) + tuple(extra_out),
+        in_specs=[vmem] * jobs_n + [anywhere] * len(extra),
+        out_specs=(vmem,) * jobs_n + (anywhere,) * len(extra_out),
+        scratch_shapes=[shape for job in jobs for shape in job.scratch] + list(extra_scratch),
+        compiler_params=pltpu.CompilerParams(
+            collective_id=identity, has_side_effects=True, vmem_limit_bytes=62 << 20
+        ),
+        cost_estimate=pl.CostEstimate(
+            flops=0, bytes_accessed=micros * 3_000_000, transcendentals=0
+        ),
+        name=name,
+    )(*operands, *extra)
+
+
 class Grads:
     tile = 256
 
@@ -629,29 +883,6 @@
             copy.wait()
 
 
-def product(left, right):
-    return jnp.dot(left, right, preferred_element_type=jnp.float32)
-
-
-class Puts:
-    def __init__(self, made, put):
-        self.made, self.put, self.copies = made, put, []
-
-    def buffer(self):
-        if len(self.copies) >= 2:
-            self.copies[-2].wait()
-        return self.made.at[len(self.copies) % 2]
-
-    def send(self, source, target):
-        copy = pltpu.make_async_copy(source, target, self.put.at[len(self.copies) % 2])
-        copy.start()
-        self.copies.append(copy)
-
-    def finish(self):
-        for copy in self.copies[-2:]:
-            copy.wait()
-
-
 def softmax_block(query, keys, ok):
     scores = times_transposed(query, keys) * HEAD_DIM ** (-0.5)
     scores = jnp.where(ok, scores, -1e30)
@@ -744,6 +975,7 @@
             pltpu.VMEM((length, wide // 3), LOW),
             pltpu.VMEM((length, wide), LOW),
             pltpu.VMEM((2, length, HEAD_DIM), jnp.float32),
+            pltpu.VMEM((self.tile, length), LOW),
             pltpu.VMEM((2, self.tile, width), LOW),
             pltpu.SemaphoreType.DMA((len(self.operands),)),
             pltpu.SemaphoreType.DMA((2,)),
@@ -752,7 +984,7 @@
     def run(self, *refs):
         n, tile, heads = len(self.operands), self.tile, self.heads
         sources, results, held = refs[:n], refs[n : n + 2], refs[n + 2 : 2 * n + 1]
-        back, grads, sums, made, get, put = refs[2 * n + 1 :]
+        back, grads, sums, turned, made, get, put = refs[2 * n + 1 :]
         upstream, out_rows, qkv, weight, cosine, sine, first, last, keys = held
         length, width = back.shape
         gets = [pltpu.make_async_copy(s, h, get.at[i]) for i, (s, h) in enumerate(zip(sources, held))]
@@ -799,10 +1031,8 @@
                 sums[1] += product(probs.astype(LOW).T, upper)
                 return carry
 
-            half = max(1, length // tile // 2)
-            for begin in range(0, length // tile, half):
-                lax.fori_loop(begin, begin + half, attend, 0)
-                yield
+            lax.fori_loop(0, length // tile, attend, 0)
+            yield
 
             def settle(index, carry):
                 at = pl.ds(pl.multiple_of(index * tile, tile), tile)
@@ -812,17 +1042,38 @@
 
             lax.fori_loop(0, length // tile, settle, 0)
         puts = Puts(made, put)
-        for at in range(0, length, tile):
-            buffer = puts.buffer()
-            buffer[...] = times_transposed(grads[at : at + tile, :], weight[...]).astype(LOW)
-            puts.send(buffer, results[0].at[at : at + tile, :])
+        wide = grads.shape[1]
+        part = tile if wide % tile == 0 else HEAD_DIM
+        for at in range(0, length, 2 * tile):
+
+            def terms(half, carry):
+                where = pl.ds(pl.multiple_of(at + half * tile, tile), tile)
+
+                def one(index, carry):
+                    span = pl.ds(pl.multiple_of(index * tile, tile), tile)
+                    value = times_transposed(grads[where, :], weight[span, :])
+                    made[half, :, span] = value.astype(LOW)
+                    return carry
+
+                return lax.fori_loop(0, made.shape[2] // tile, one, carry)
+
+            puts.pair(terms, made.shape[2], results[0], at, tile)
             yield
         fetch.wait()
-        wide = grads.shape[1]
-        for at in range(0, rows.shape[1], tile):
-            buffer = puts.buffer().at[:, :wide]
-            buffer[...] = product(rows[:, at : at + tile].T, grads[...]).astype(LOW)
-            puts.send(buffer, results[1].at[at : at + tile, :])
+        for at in range(0, rows.shape[1], 2 * tile):
+
+            def weights(half, carry):
+                where = pl.ds(pl.multiple_of(at + half * tile, tile), tile)
+                turned[...] = rows[:, where].T
+
+                def one(index, carry):
+                    span = pl.ds(pl.multiple_of(index * part, part), part)
+                    made[half, :, span] = product(turned[...], grads[:, span]).astype(LOW)
+                    return carry
+
+                return lax.fori_loop(0, wide // part, one, carry)
+
+            puts.pair(weights, wide, results[1], at, tile)
             yield
         puts.finish()
 
@@ -838,47 +1089,64 @@
 
 
 class FeedForward:
-    def __init__(self, job, upstream, gate_up, down):
+    def __init__(self, job, upstream, gate, up, down):
         self.job = job
-        self.operands = [upstream, gate_up, down]
+        self.operands = [upstream, gate, up, down]
         length, width = upstream.shape
-        wide = gate_up.shape[1]
+        units = gate.shape[1]
         self.outs = [
-            jax.ShapeDtypeStruct((length, wide // 2), LOW),
-            jax.ShapeDtypeStruct((length, wide), LOW),
+            jax.ShapeDtypeStruct((length, units), LOW),
+            jax.ShapeDtypeStruct((length, 2 * units), LOW),
             jax.ShapeDtypeStruct((length, width), LOW),
         ]
         self.tile = length // (job.parts // 2)
         self.scratch = [pltpu.VMEM(array.shape, array.dtype) for array in self.operands]
         self.scratch += [pltpu.VMEM((2, self.tile) + out.shape[1:], LOW) for out in self.outs]
-        self.scratch += [pltpu.SemaphoreType.DMA((3,)), pltpu.SemaphoreType.DMA((3, 2))]
+        self.scratch += [pltpu.SemaphoreType.DMA((4,)), pltpu.SemaphoreType.DMA((3, 2))]
 
     def run(self, *refs):
         job, tile = self.job, self.tile
-        sources, results, held, made = refs[:3], refs[3:6], refs[6:9], refs[9:12]
-        get, put = refs[12:]
-        upstream, gate_up, down = held
+        sources, results, held, made = refs[:4], refs[4:7], refs[7:11], refs[11:14]
+        get, put = refs[14:]
+        upstream, gate_w, up_w, down = held
         acts, backs, terms = made
-        rows = tile // 2
-        width, wide = gate_up.shape
-        units = wide // 2
+        width, units = gate_w.shape
         step = min(units, 256)
         span = min(width, 512)
         chip = lax.axis_index("ctx") // 2
-        gets = [pltpu.make_async_copy(sources[i], held[i], get.at[i]) for i in (1, 2, 0)]
+        gets = [pltpu.make_async_copy(sources[i], held[i], get.at[i]) for i in (1, 2, 3, 0)]
         for copy in gets:
             copy.start()
         yield
         for copy in gets:
             copy.wait()
         table = near_first(job.parts // 2)
-        puts = []
-        for turn in range(len(table)):
-            origin = sum(jnp.where(chip == at, order[turn], 0) for at, order in enumerate(table))
-            slot = turn % 2
-            if turn >= 2:
-                for copy in puts[turn - 2]:
+        chips = len(table)
+
+        def leave(slot, origin):
+            at = pl.ds(pl.multiple_of(origin * tile, tile), tile)
+            return [
+                pltpu.make_async_copy(made[i].at[slot], results[i].at[at, :], put.at[i, slot])
+                for i in range(3)
+            ]
+
+        def one_chip(turn, carry):
+            origin = sum(
+                jnp.where((chip == at) & (turn == when), order[when], 0)
+                for at, order in enumerate(table)
+                for when in range(chips)
+            )
+            slot = lax.rem(turn, 2)
+
+            @pl.when(turn > 0)
+            def _():
+                job.relay(turn)
+
+            @pl.when(turn >= 2)
+            def _():
+                for copy in leave(slot, 0):
                     copy.wait()
+
             job.arrived(origin)
             at = pl.ds(pl.multiple_of(origin * tile, tile), tile)
             normed = job.dst.at[pl.ds(2 * origin, 2)]
@@ -887,8 +1155,8 @@
                 left = pl.ds(pl.multiple_of(index * step, step), step)
                 right = pl.ds(pl.multiple_of(units + index * step, step), step)
                 value = normed[...].reshape(tile, width)
-                gate = product(value, gate_up[:, left])
-                up = product(value, gate_up[:, right])
+                gate = product(value, gate_w[:, left])
+                up = product(value, up_w[:, left])
                 act_grad = times_transposed(upstream[at, :], down[left, :])
                 sigmoid = jax.nn.sigmoid(gate)
                 silu = gate * sigmoid
@@ -902,22 +1170,19 @@
 
             def backward(index, carry):
                 where = pl.ds(pl.multiple_of(index * span, span), span)
-                value = times_transposed(backs[slot], gate_up[where, :])
+                value = times_transposed(backs[slot, :, :units], gate_w[where, :])
+                value += times_transposed(backs[slot, :, units:], up_w[where, :])
                 terms[slot, :, where] = value.astype(LOW)
                 return carry
 
             lax.fori_loop(0, width // span, backward, 0)
-            puts.append(
-                [
-                    pltpu.make_async_copy(made[i].at[slot], results[i].at[at, :], put.at[i, slot])
-                    for i in range(3)
-                ]
-            )
-            for copy in puts[-1]:
+            for copy in leave(slot, origin):
                 copy.start()
-            yield
-        for copies in puts[-2:]:
-            for copy in copies:
+            return carry
+
+        lax.fori_loop(0, chips, one_chip, 0)
+        for slot in range(min(2, chips)):
+            for copy in leave(slot, 0):
                 copy.wait()
 
 
@@ -984,17 +1249,24 @@
     out_rows = gather(w_out, "fsdp")
     down_rows = gather(w_down, "fsdp")
     gate_up_pieces = plan.unit_pieces(w_gate_up)
+    unit_columns = gate_up_pieces.shape[2] // 2
+    unit_shape = (w_gate_up.shape[0], unit_columns)
     inputs = tokens.astype(jnp.float32)
     normed_in, root_in = normalize(inputs)
     qkv_pieces = plan.qkv_pieces(w_qkv)
-    qkv_cols, normed_in_full = call(
-        [Spread(parts, groups, qkv_pieces.shape[1:]), Gather(parts, block)],
-        [qkv_pieces, normed_in.astype(LOW)],
+    qkv_cols, normed_in_full, gate_cols = call(
+        [
+            Spread(parts, groups, qkv_pieces.shape[1:]),
+            Gather(parts, block, cuts=1),
+            Exchange(parts, unit_shape),
+        ],
+        [qkv_pieces, normed_in.astype(LOW), gate_up_pieces[:, :, :unit_columns]],
         "start",
         2,
         plane,
-        micros=70,
+        micros=90,
     )
+    gate_cols = gather(gate_cols.reshape(width // groups, -1), "fsdp")
     qkv_cols = qkv_cols.reshape(width, 3 * head_width)
     normed_in_full = normed_in_full.reshape(length, width)
 
@@ -1010,23 +1282,22 @@
         jnp.broadcast_to(packed[:, None], (length, HEAD_DIM)),
         jnp.broadcast_to(packed[None, :], (8, length)),
     )
-    gate_up_cols, out_cols, qkv_low, mix_low = call(
-        [Exchange(parts, gate_up_pieces.shape[1:]), Exchange(run, (heads * shard, width))],
-        [gate_up_pieces, out_rows.reshape(run, heads * shard, width)],
+    up_cols, out_cols, qkv_low, mix_low = call(
+        [Exchange(parts, unit_shape), Exchange(run, (heads * shard, width))],
+        [gate_up_pieces[:, :, unit_columns:], out_rows.reshape(run, heads * shard, width)],
         "attend",
         1,
         line,
         Attend(normed_in_full, qkv_cols, tables, heads),
-        micros=55,
+        micros=40,
     )
-    gate_up_cols, down_rows = lax.optimization_barrier((gate_up_cols, down_rows))
-    gate_up_cols = gather(gate_up_cols.reshape(width // groups, -1), "fsdp")
+    up_cols = gather(up_cols.reshape(width // groups, -1), "fsdp")
     out_cols = out_cols.reshape(run, heads, shard, width).transpose(1, 0, 2, 3)
     out_cols = out_cols.reshape(head_width, width)
 
     out_terms = dot(mix_low, out_cols).astype(LOW)
     attn_out, cot_full = call(
-        [Scatter(parts, block), Gather(parts, block)],
+        [Scatter(parts, block, cuts=1), Gather(parts, block, cuts=1)],
         [out_terms.reshape((parts,) + block), cotangent],
         "out",
         3,
@@ -1043,21 +1314,20 @@
         "mid",
         4,
         line,
-        FeedForward(mid_job, cot_full, gate_up_cols, down_rows),
+        FeedForward(mid_job, cot_full, gate_cols, up_cols, down_rows),
         micros=60,
     )
     normed_mid_full = normed_mid_full.reshape(length, width)
-    down_grad = scatter(column_product(activated, cot_full).astype(LOW), "fsdp").astype(jnp.float32)
-    mid_back, gate_up_grad = call(
+    mid_back, gate_up_grad, down_grad = call(
         [Scatter(parts, block)],
         [mid_back_terms.reshape((parts,) + block)],
         "mid_back",
         5,
         line,
-        Grads([(normed_mid_full, gate_up_back)]),
+        Grads([(normed_mid_full, gate_up_back), (activated, cot_full)]),
     )
-    gate_up_grad, down_grad = lax.optimization_barrier((gate_up_grad, down_grad))
     gate_up_grad = scatter(gate_up_grad, "fsdp")
+    down_grad = scatter(down_grad, "fsdp")
     residual_back = cotangent.astype(jnp.float32) + norm_back(mid_back, normed_mid, root_mid)
     proj_back = residual_back.astype(LOW)
 
@@ -1077,7 +1347,7 @@
     )
     layer_out = (residual + down_out).astype(LOW)
     out_grad, gate_up_grad = lax.optimization_barrier((out_grad, gate_up_grad))
-    out_grad = scatter(out_grad.reshape(groups * shard, width), "fsdp").astype(jnp.float32)
+    out_grad = scatter(out_grad.reshape(groups * shard, width), "fsdp")
     in_back, qkv_grad, gate_up_grad = call(
         [
             Scatter(parts, block),
@@ -1094,14 +1364,15 @@
         plane,
         micros=90,
     )
+    in_back, down_grad, out_grad = lax.optimization_barrier((in_back, down_grad, out_grad))
     tokens_grad = residual_back + norm_back(in_back, normed_in, root_in)
     return (
         layer_out,
         tokens_grad,
         qkv_grad,
-        out_grad,
+        out_grad.astype(jnp.float32),
         plan.unit_rows(gate_up_grad),
-        down_grad,
+        down_grad.astype(jnp.float32),
     )
 
 

time: 587 us -> 554 us (0.944); the launches traced: 578 us -> 553 us
  waiting for transfers between devices: 24.1 us -> 12.8 us
  matrix products: 22.6 us -> 14.1 us
    dot_general x2 -> x1, matrix products: 13.3 us -> 3.76 us  [column_product(): lax.dot_general(left, right, (((0,), (0,)), ((), ())), preferred_element_...]
    reduce_scatter x3, waiting for transfers between devices: 7.64 us -> 0.06 us  [scatter(): return lax.psum_scatter(values, axes, scatter_dimension=0, tiled=True)]
    all_gather x3 -> x4, waiting for transfers between devices: 15.1 us -> 10.8 us  [gather(): return lax.all_gather(values, axes, axis=0, tiled=True)]
  transfers between devices with their start and end apart: 6 -> 7, of which waited for: 2 -> 1; matrix products, arithmetic and copies ran while one was open for 8% -> 8% of each run, Pallas kernels for 74% -> 66%
where the time goes in v8:
time: 554 us; the launch traced here: 553 us
  Pallas kernels  468 us (84%)
  local copies, waits for them, and re-layouts  22.5 us (4%)
  other arithmetic  20.7 us (4%)
  between operations  14.4 us (3%)
  matrix products  14.1 us (3%)
  waiting for transfers between devices  12.8 us (2%)
    pallas_call x8, Pallas kernels, call(): pl.pallas_call(kernel, out_shape=tuple((job.out for job in jobs)) + tuple...  468 us
  transfers between devices with their start and end apart: 7, of which 1 were waited for; matrix products, arithmetic and copies ran while one was open for 8% of the time, Pallas kernels for 66%

profile of v8, /device:TPU:9, one launch (start us, length us, event | category | flops | bytes accessed | tf_op | source)
XLA Modules:
  0.0 553.1 jit_solution(13193572163730628786)
XLA Ops:
  8.7 2.3 reshape.208
  12.9 2.1 copy.22
  15.0 1.7 copy.25
  16.8 2.9 reshape.206
  20.2 1.6 fusion.26
  22.8 81.7 %start.1 = (bf16[4,8,64,768]{3,2,1,0:T(8,128)(2,1)}, bf16[8,128,2048]{2,1,0:T(8,128)(2,1)}, bf16[8,64,1024]{2,1,0:T(8,128)(2,1)}) custom-call(bf16[8,64,768]{2,1,0:T(8,128)(2,1)} %reshape.209.refs_0_, bf16[128,2048]{1,0:T(8,128)(2,1)} %fusion.4.refs_1_, bf16[8,64,1024]{2,1,0:T(8,128)(2,1)} %get-tuple-element.70.refs_2_), custom_call_target="tpu_custom_call" | custom-call | bytes 270000000 | tf_op jit(solution)/shard_map/start/pallas_call | solution.py:816
  105.3 2.9 sine_multiply_fusion
  110.8 33.5 %attend.1 = (bf16[8,64,1024]{2,1,0:T(8,128)(2,1)}, bf16[2,128,2048]{2,1,0:T(8,128)(2,1)}, bf16[1024,768]{1,0:T(8,128)(2,1)}, bf16[1024,256]{1,0:T(8,128)(2,1)}) custom-call(bf16[8,64,1024]{2,1,0:T(8,128)(2,1)} %get-tuple-element.71.refs_0_, bf16[2,128,2048]{2,1,0:T(8,128)(2,1)} %bitcast.71, bf16[1024,2048]{1,0:T(8,128)(2,1)} %bitcast.47, ...), custom_call_target="tpu_custom_call" | custom-call | bytes 120000000 | tf_op jit(solution)/shard_map/attend/pallas_call | solution.py:816
  146.6 4.3 convolution_convert_fusion
  150.9 55.1 %out.1 = (f32[128,2048]{1,0:T(8,128)}, bf16[8,128,2048]{2,1,0:T(8,128)(2,1)}) custom-call(bf16[8,128,2048]{2,1,0:T(8,128)(2,1)} %bitcast.44, bf16[128,2048]{1,0:T(8,128)(2,1)} %refs_1_.1), custom_call_target="tpu_custom_call" | custom-call | bytes 192000000 | tf_op jit(solution)/shard_map/out/pallas_call | solution.py:816
  208.7 10.8 %all-gather.9.cloned.1.call-done.refs_3_ = bf16[2048,1024]{1,0:T(8,128)(2,1)} async-done(((bf16[512,1024]{1,0:T(8,128)(2,1)}), bf16[2048,1024]{1,0:T(8,128)(2,1)}) %all-gather.9.cloned.1.call-update) | async-done | bytes 4194320 | tf_op jit(solution)/shard_map/all_gather | solution.py:83
  219.5 47.2 %mid.1 = (bf16[8,128,2048]{2,1,0:T(8,128)(2,1)}, bf16[1024,1024]{1,0:T(8,128)(2,1)}, bf16[1024,2048]{1,0:T(8,128)(2,1)}, bf16[1024,2048]{1,0:T(8,128)(2,1)}) custom-call(bf16[128,2048]{1,0:T(8,128)(2,1)} %fusion.10.refs_0_, bf16[1024,2048]{1,0:T(8,128)(2,1)} %bitcast.49, bf16[2048,1024]{1,0:T(8,128)(2,1)} %all-gather.7.cloned.1.call-done.refs_2_, ...), custom_call_target="tpu_custom_call" | custom-call | bytes 180000000 | tf_op jit(solution)/shard_map/mid/pallas_call | solution.py:816
  266.7 58.0 %mid_back.1 = (f32[128,2048]{1,0:T(8,128)}, bf16[2048,2048]{1,0:T(8,128)(2,1)}, bf16[1024,2048]{1,0:T(8,128)(2,1)}) custom-call(bf16[8,128,2048]{2,1,0:T(8,128)(2,1)} %bitcast.60, bf16[1024,2048]{1,0:T(8,128)(2,1)} %bitcast.59, bf16[1024,2048]{1,0:T(8,128)(2,1)} %get-tuple-element.45.refs_2_, bf16[1024,1024]{1,0:T(8,128)(2,1)} %get-tuple-element.42.refs_3_, ...), custom_call_target="tpu_custom_call" | custom-call | bytes 150000000 | tf_op jit(solution)/shard_map/mid_back/pallas_call | solution.py:816
  326.2 2.7 fusion.24
  328.9 38.0 %proj_back.1 = bf16[8,128,2048]{2,1,0:T(8,128)(2,1)} custom-call(bf16[128,2048]{1,0:T(8,128)(2,1)} %get-tuple-element.66.refs_0_), custom_call_target="tpu_custom_call" | custom-call | bytes 135000000 | tf_op jit(solution)/shard_map/proj_back/pallas_call | solution.py:816
  367.0 3.8 convolution_convert_fusion.2
  371.8 6.0 %convolution_convert_fusion.1 = bf16[1024,2048]{1,0:T(8,128)(2,1)} fusion(bf16[1024,1024]{1,0:T(8,128)(2,1)S(1)} %copy-done.7, bf16[1024,2048]{1,0:T(8,128)(2,1)S(1)} %copy-done.6), kind=kOutput, calls=%fused_computation.1 | convolution fusion | flops 4297064448 | bytes 10485760 | tf_op jit(solution)/shard_map/dot_general | solution.py:67
  377.8 58.4 %attend_back.1 = (f32[128,2048]{1,0:T(8,128)}, bf16[2,128,2048]{2,1,0:T(8,128)(2,1)}, bf16[1024,2048]{1,0:T(8,128)(2,1)}, bf16[2048,768]{1,0:T(8,128)(2,1)}) custom-call(bf16[8,128,2048]{2,1,0:T(8,128)(2,1)} %bitcast.58, bf16[2,128,2048]{2,1,0:T(8,128)(2,1)} %bitcast.61, bf16[1024,2048]{1,0:T(8,128)(2,1)} %bitcast.46, bf16[256,2048]{1,0:T(8,128)(2,1)} %bitcast.54, ...), custom_call_target="tpu_custom_call" | custom-call | bytes 180000000 | tf_op jit(solution)/shard_map/attend_back/pallas_call | solution.py:816
  436.3 2.1 add_convert_fusion
  438.4 96.3 %in_back.1 = (f32[128,2048]{1,0:T(8,128)}, f32[64,6144]{1,0:T(8,128)}, f32[64,16384]{1,0:T(8,128)}) custom-call(bf16[8,128,2048]{2,1,0:T(8,128)(2,1)} %bitcast.57, bf16[4,8,64,768]{3,2,1,0:T(8,128)(2,1)} %bitcast.63, bf16[8,64,2048]{2,1,0:T(8,128)(2,1)} %bitcast.65), custom_call_target="tpu_custom_call" | custom-call | bytes 270000000 | tf_op jit(solution)/shard_map/in_back/pallas_call | solution.py:816
  534.8 1.7 fusion.22
  536.5 1.9 convert_element_type.54
  538.4 2.8 convert_element_type.55
  544.3 2.0 copy.30
  (75 shorter events, 19.0 us)
Async XLA Ops:
  7.2 101.0 %all-gather.5.cloned.1.call-start = ((), (), s32[]{:S(2)}) async-start(), calls=%async_computation.3 | async-start | bytes 1310720 | tf_op jit(solution)/shard_map/all_gather | solution.py:83
  7.9 200.8 %all-gather.11.cloned.1.call-start = ((), (), s32[]{:S(2)}) async-start(), calls=%async_computation.6 | async-start | bytes 5242880 | tf_op jit(solution)/shard_map/all_gather | solution.py:83
  8.6 200.0 %all-gather.7.cloned.1.call-start = ((), (), s32[]{:S(2)}) async-start(), calls=%async_computation.4 | async-start | bytes 5242880 | tf_op jit(solution)/shard_map/all_gather | solution.py:83
  15.0 4.7 copy-start
  20.1 84.4 %copy-start.10 = (s32[1,2]{1,0:T(1,128)S(1)}, s32[1,2]{1,0:T(1,128)}, u32[]{:S(2)}) copy-start(s32[1,2]{1,0:T(1,128)} %param.13) | copy-start | bytes 28
  20.1 84.6 %copy-start.9 = (s32[1,8]{1,0:T(1,128)S(1)}, s32[1,8]{1,0:T(1,128)}, u32[]{:S(2)}) copy-start(s32[1,8]{1,0:T(1,128)} %param.14) | copy-start | bytes 100
  104.5 114.9 %all-gather.9.cloned.1.call-start = ((), (), s32[]{:S(2)}) async-start(), calls=%async_computation.5 | async-start | bytes 5242880 | tf_op jit(solution)/shard_map/all_gather | solution.py:83
  144.3 292.0 %reduce-scatter.4.cloned.1.call-start = ((), (), s32[]{:S(2)}) async-start(), calls=%async_computation.7 | async-start | bytes 10485760 | tf_op jit(solution)/shard_map/reduce_scatter | solution.py:87
  145.7 1.0 copy-start.1
  324.7 1.2 copy-start.5
  324.7 210.0 %reduce-scatter.6.cloned.1.call-start = ((), (), s32[]{:S(2)}) async-start(), calls=%async_computation.8 | async-start | bytes 5242880 | tf_op jit(solution)/shard_map/reduce_scatter | solution.py:87
  325.3 209.5 %reduce-scatter.8.cloned.1.call-start = ((), (), s32[]{:S(2)}) async-start(), calls=%async_computation.9 | async-start | bytes 1310720 | tf_op jit(solution)/shard_map/reduce_scatter | solution.py:87
  367.0 4.8 copy-start.6
  367.0 4.8 copy-start.7
  534.7 6.5 %copy-start.2 = (f32[128,2048]{1,0:T(8,128)S(1)}, f32[128,2048]{1,0:T(8,128)}, u32[]{:S(2)}) copy-start(f32[128,2048]{1,0:T(8,128)} %get-tuple-element.57) | copy-start | bytes 3145732
  534.7 6.5 %copy-start.4 = (f32[128,2048]{1,0:T(8,128)S(1)}, f32[128,2048]{1,0:T(8,128)}, u32[]{:S(2)}) copy-start(f32[128,2048]{1,0:T(8,128)} %get-tuple-element.67) | copy-start | bytes 3145732
  536.5 6.1 %copy-start.8 = (f32[64,6144]{1,0:T(8,128)S(1)}, f32[64,6144]{1,0:T(8,128)}, u32[]{:S(2)}) copy-start(f32[64,6144]{1,0:T(8,128)} %get-tuple-element.84) | copy-start | bytes 4718596
  541.2 3.1 copy-start.3
Sparse Core Ops, SparseCore 0:
  9.8 38.8 all-gather.4
  50.5 60.1 all-gather.10
  112.6 52.5 all-gather.6
  166.9 52.5 all-gather.8
  324.8 84.4 reduce-scatter.3
  412.1 75.3 reduce-scatter.5
  490.4 27.6 reduce-scatter.7

commit v9 on v8

--- a/solution.py
+++ b/solution.py
@@ -105,8 +105,8 @@
 
 
 class Exchange:
-    def __init__(self, parts, shape):
-        self.parts = parts
+    def __init__(self, parts, shape, delay=0):
+        self.parts, self.delay = parts, delay
         self.out = jax.ShapeDtypeStruct((parts,) + shape, LOW)
         self.scratch = [
             pltpu.SemaphoreType.DMA((parts - 1,)),
@@ -115,6 +115,8 @@
         ]
 
     def run(self, src, dst, send, recv, local):
+        for _ in range(self.delay):
+            yield
         place = lax.axis_index("ctx")
         me = lax.rem(place, self.parts)
         copies = []
@@ -379,6 +381,36 @@
             def _():
                 for cut in range(cuts):
                     line(goal, cut, 0).wait_send()
+
+
+class Fan:
+    def __init__(self, groups, shape):
+        self.groups = groups
+        self.out = jax.ShapeDtypeStruct((groups,) + shape, LOW)
+        self.scratch = [
+            pltpu.SemaphoreType.DMA((groups - 1,)),
+            pltpu.SemaphoreType.DMA((groups - 1,)),
+            pltpu.SemaphoreType.DMA,
+        ]
+
+    def run(self, src, dst, send, recv, local):
+        groups = self.groups
+        group = lax.axis_index("fsdp")
+        copies = []
+        for hop in range(1, groups):
+            peer = lax.rem(group + hop, groups)
+            copies.append(
+                remote(src, dst.at[group], send.at[hop - 1], recv.at[hop - 1], "fsdp", peer)
+            )
+            copies[-1].start()
+        own = pltpu.make_async_copy(src, dst.at[group], local)
+        own.start()
+        yield
+        yield
+        yield
+        for copy in copies:
+            copy.wait()
+        own.wait()
 
 
 class Spread:
@@ -447,8 +479,9 @@
 
 
 class Deliver:
-    def __init__(self, parts, shape, offsets):
+    def __init__(self, parts, shape, offsets, delay=0, eager=1):
         self.parts, self.shape, self.offsets = parts, shape, offsets
+        self.delay, self.eager = delay, eager
         self.out = jax.ShapeDtypeStruct((shape[0], parts * shape[1]), jnp.float32)
         self.scratch = [
             pltpu.VMEM((parts - 1,) + shape, LOW),
@@ -475,6 +508,8 @@
         )
 
     def run(self, src, out, came, send, recv):
+        for _ in range(self.delay):
+            yield
         me = lax.axis_index("ctx")
         copies = []
         for step in range(1, self.parts):
@@ -490,14 +525,15 @@
             copies[step - 1].wait_recv()
             origin = lax.rem(me - step + self.parts, self.parts)
             self.place(out, origin, lambda lo, hi: came[step - 1, :, lo:hi].astype(jnp.float32))
-            yield
+            if step % self.eager == 0:
+                yield
         for copy in copies:
             copy.wait_send()
 
 
 class Collect(Deliver):
-    def __init__(self, parts, groups, shape, offsets):
-        super().__init__(parts, shape, offsets)
+    def __init__(self, parts, groups, shape, offsets, delay=0, eager=1):
+        super().__init__(parts, shape, offsets, delay, eager)
         self.groups = groups
         self.scratch = self.scratch + [
             pltpu.VMEM((groups - 1, parts) + shape, LOW),
@@ -541,7 +577,8 @@
                 copies[-1].start()
             else:
                 mine[...] = value
-            yield
+            if step % self.eager == 0:
+                yield
         self.place(out, me, lambda lo, hi: mine[:, lo:hi])
         yield from self.finish(me, out, copies, came)
         for copy in hops:
@@ -635,28 +672,33 @@
         length, wide = pairs[0][0].shape[0], max(right.shape[1] for _, right in pairs)
         self.operands = [array for pair in pairs for array in pair]
         self.outs = [jax.ShapeDtypeStruct((l.shape[1], r.shape[1]), LOW) for l, r in pairs]
+        self.slots = [[id(array) for array in self.operands].index(id(a)) for a in self.operands]
+        self.operands = [a for i, a in enumerate(self.operands) if self.slots[i] == i]
+        self.slots = [sorted(set(self.slots)).index(slot) for slot in self.slots]
         self.scratch = [pltpu.VMEM(array.shape, LOW) for array in self.operands]
         self.scratch += [
             pltpu.VMEM((self.tile, length), LOW),
             pltpu.VMEM((2, self.tile, wide), LOW),
-            pltpu.SemaphoreType.DMA((2 * len(pairs),)),
+            pltpu.SemaphoreType.DMA((len(self.operands),)),
             pltpu.SemaphoreType.DMA((2,)),
         ]
 
     def run(self, *refs):
-        n, tile = len(self.pairs), self.tile
-        sources, outs = refs[: 2 * n], refs[2 * n : 3 * n]
-        held = refs[3 * n : 5 * n]
-        turned, made, get, put = refs[5 * n :]
+        n, tile, count = len(self.pairs), self.tile, len(self.operands)
+        sources, outs = refs[:count], refs[count : count + n]
+        held = refs[count + n : 2 * count + n]
+        turned, made, get, put = refs[2 * count + n :]
         gets = [pltpu.make_async_copy(s, h, get.at[i]) for i, (s, h) in enumerate(zip(sources, held))]
         for copy in gets:
             copy.start()
         yield
         puts = Puts(made, put)
         for which in range(n):
-            left, right, out = held[2 * which], held[2 * which + 1], outs[which]
-            gets[2 * which].wait()
-            gets[2 * which + 1].wait()
+            first, second = self.slots[2 * which : 2 * which + 2]
+            left, right, out = held[first], held[second], outs[which]
+            for slot in (first, second):
+                if slot not in self.slots[: 2 * which]:
+                    gets[slot].wait()
             columns = right.shape[1]
             step = min(columns, 256)
             for at in range(0, left.shape[1], 2 * tile):
@@ -677,8 +719,9 @@
 
 
 class Deliver:
-    def __init__(self, parts, shape, offsets):
+    def __init__(self, parts, shape, offsets, delay=0, eager=1):
         self.parts, self.shape, self.offsets = parts, shape, offsets
+        self.delay, self.eager = delay, eager
         self.out = jax.ShapeDtypeStruct((shape[0], parts * shape[1]), jnp.float32)
         self.scratch = [
             pltpu.VMEM((parts - 1,) + shape, LOW),
@@ -705,6 +748,8 @@
         )
 
     def run(self, src, out, came, send, recv):
+        for _ in range(self.delay):
+            yield
         me = lax.axis_index("ctx")
         copies = []
         for step in range(1, self.parts):
@@ -720,14 +765,15 @@
             copies[step - 1].wait_recv()
             origin = lax.rem(me - step + self.parts, self.parts)
             self.place(out, origin, lambda lo, hi: came[step - 1, :, lo:hi].astype(jnp.float32))
-            yield
+            if step % self.eager == 0:
+                yield
         for copy in copies:
             copy.wait_send()
 
 
 class Collect(Deliver):
-    def __init__(self, parts, groups, shape, offsets):
-        super().__init__(parts, shape, offsets)
+    def __init__(self, parts, groups, shape, offsets, delay=0, eager=1):
+        super().__init__(parts, shape, offsets, delay, eager)
         self.groups = groups
         self.scratch = self.scratch + [
             pltpu.VMEM((groups - 1, parts) + shape, LOW),
@@ -771,7 +817,8 @@
                 copies[-1].start()
             else:
                 mine[...] = value
-            yield
+            if step % self.eager == 0:
+                yield
         self.place(out, me, lambda lo, hi: mine[:, lo:hi])
         yield from self.finish(me, out, copies, came)
         for copy in hops:
@@ -837,28 +884,33 @@
         length, wide = pairs[0][0].shape[0], max(right.shape[1] for _, right in pairs)
         self.operands = [array for pair in pairs for array in pair]
         self.outs = [jax.ShapeDtypeStruct((l.shape[1], r.shape[1]), LOW) for l, r in pairs]
+        self.slots = [[id(array) for array in self.operands].index(id(a)) for a in self.operands]
+        self.operands = [a for i, a in enumerate(self.operands) if self.slots[i] == i]
+        self.slots = [sorted(set(self.slots)).index(slot) for slot in self.slots]
         self.scratch = [pltpu.VMEM(array.shape, LOW) for array in self.operands]
         self.scratch += [
             pltpu.VMEM((self.tile, length), LOW),
             pltpu.VMEM((2, self.tile, wide), LOW),
-            pltpu.SemaphoreType.DMA((2 * len(pairs),)),
+            pltpu.SemaphoreType.DMA((len(self.operands),)),
             pltpu.SemaphoreType.DMA((2,)),
         ]
 
     def run(self, *refs):
-        n, tile = len(self.pairs), self.tile
-        sources, outs = refs[: 2 * n], refs[2 * n : 3 * n]
-        held = refs[3 * n : 5 * n]
-        turned, made, get, put = refs[5 * n :]
+        n, tile, count = len(self.pairs), self.tile, len(self.operands)
+        sources, outs = refs[:count], refs[count : count + n]
+        held = refs[count + n : 2 * count + n]
+        turned, made, get, put = refs[2 * count + n :]
         gets = [pltpu.make_async_copy(s, h, get.at[i]) for i, (s, h) in enumerate(zip(sources, held))]
         for copy in gets:
             copy.start()
         yield
         puts = []
         for which in range(n):
-            left, right, out = held[2 * which], held[2 * which + 1], outs[which]
-            gets[2 * which].wait()
-            gets[2 * which + 1].wait()
+            first, second = self.slots[2 * which : 2 * which + 2]
+            left, right, out = held[first], held[second], outs[which]
+            for slot in (first, second):
+                if slot not in self.slots[: 2 * which]:
+                    gets[slot].wait()
             columns = right.shape[1]
             step = min(columns, 512)
             for at in range(0, left.shape[1], tile):
@@ -962,17 +1014,16 @@
 class AttendBack:
     tile = 256
 
-    def __init__(self, upstream, out_rows, qkv, rows, weight, tables, heads):
+    def __init__(self, back, qkv, rows, weight, tables, heads):
         self.heads = heads
-        self.operands = [upstream, out_rows, qkv, weight] + list(tables) + [rows]
+        self.operands = [back, qkv] + list(tables) + [weight, rows]
         length, wide, width = rows.shape[0], weight.shape[1], rows.shape[1]
         self.outs = [
             jax.ShapeDtypeStruct((length, width), LOW),
             jax.ShapeDtypeStruct((width, wide), LOW),
         ]
-        self.scratch = [pltpu.VMEM(array.shape, array.dtype) for array in self.operands[:-1]]
+        self.scratch = [pltpu.VMEM(array.shape, array.dtype) for array in self.operands]
         self.scratch += [
-            pltpu.VMEM((length, wide // 3), LOW),
             pltpu.VMEM((length, wide), LOW),
             pltpu.VMEM((2, length, HEAD_DIM), jnp.float32),
             pltpu.VMEM((self.tile, length), LOW),
@@ -983,27 +1034,16 @@
 
     def run(self, *refs):
         n, tile, heads = len(self.operands), self.tile, self.heads
-        sources, results, held = refs[:n], refs[n : n + 2], refs[n + 2 : 2 * n + 1]
-        back, grads, sums, turned, made, get, put = refs[2 * n + 1 :]
-        upstream, out_rows, qkv, weight, cosine, sine, first, last, keys = held
+        sources, results, held = refs[:n], refs[n : n + 2], refs[n + 2 : 2 * n + 2]
+        grads, sums, turned, made, get, put = refs[2 * n + 2 :]
+        back, qkv, cosine, sine, first, last, keys, weight, rows = held
         length, width = back.shape
         gets = [pltpu.make_async_copy(s, h, get.at[i]) for i, (s, h) in enumerate(zip(sources, held))]
         for copy in gets:
             copy.start()
         yield
-        for copy in gets:
+        for copy in gets[:-2]:
             copy.wait()
-
-        def project(index, carry):
-            at = pl.ds(pl.multiple_of(index * tile, tile), tile)
-            back[at, :] = times_transposed(upstream[at, :], out_rows[...]).astype(LOW)
-            return carry
-
-        lax.fori_loop(0, length // tile, project, 0)
-        rows = upstream
-        fetch = pltpu.make_async_copy(sources[n - 1], rows, get.at[n - 1])
-        fetch.start()
-        yield
 
         def unrotated(value, at):
             return value * cosine[at, :] - pltpu.roll(value, HEAD_DIM // 2, 1) * sine[at, :]
@@ -1044,6 +1084,7 @@
         puts = Puts(made, put)
         wide = grads.shape[1]
         part = tile if wide % tile == 0 else HEAD_DIM
+        gets[-2].wait()
         for at in range(0, length, 2 * tile):
 
             def terms(half, carry):
@@ -1059,7 +1100,7 @@
 
             puts.pair(terms, made.shape[2], results[0], at, tile)
             yield
-        fetch.wait()
+        gets[-1].wait()
         for at in range(0, rows.shape[1], 2 * tile):
 
             def weights(half, carry):
@@ -1088,6 +1129,98 @@
     return table
 
 
+def next_chip(chips, turn):
+    chip = lax.axis_index("ctx") // 2
+    return sum(
+        jnp.where((chip == at) & (turn == when), order[when], 0)
+        for at, order in enumerate(near_first(chips))
+        for when in range(chips)
+    )
+
+
+class ProjectBack:
+    tile = 256
+
+    def __init__(self, job, activated, down, out_rows, mix):
+        self.job = job
+        self.operands = [activated, down, out_rows, mix]
+        length, heads_width = mix.shape
+        width = down.shape[1]
+        self.outs = [
+            jax.ShapeDtypeStruct((length, width), LOW),
+            jax.ShapeDtypeStruct((length, heads_width), LOW),
+            jax.ShapeDtypeStruct((heads_width, width), LOW),
+        ]
+        self.scratch = [pltpu.VMEM(array.shape, array.dtype) for array in self.operands]
+        self.scratch += [
+            pltpu.VMEM((2, self.tile, width), LOW),
+            pltpu.VMEM((length, heads_width), LOW),
+            pltpu.VMEM((heads_width, width), jnp.float32),
+            pltpu.VMEM((heads_width, width), LOW),
+            pltpu.SemaphoreType.DMA((4,)),
+            pltpu.SemaphoreType.DMA((2,)),
+            pltpu.SemaphoreType.DMA((2,)),
+        ]
+
+    def run(self, *refs):
+        job, tile = self.job, self.tile
+        sources, results, held = refs[:4], refs[4:7], refs[7:11]
+        made, back, total, total_low, get, put, leave = refs[11:]
+        activated, down, out_rows, mix = held
+        length, width = mix.shape[0], down.shape[1]
+        gets = [pltpu.make_async_copy(s, h, get.at[i]) for i, (s, h) in enumerate(zip(sources, held))]
+        for copy in gets:
+            copy.start()
+        yield
+        for copy in gets:
+            copy.wait()
+        total[...] = jnp.zeros_like(total)
+        puts = Puts(made, put)
+        for at in range(0, length, 2 * tile):
+
+            def terms(half, carry):
+                where = pl.ds(pl.multiple_of(at + half * tile, tile), tile)
+
+                def one(index, carry):
+                    span = pl.ds(pl.multiple_of(index * tile, tile), tile)
+                    value = product(activated[where, :], down[:, span])
+                    made[half, :, span] = value.astype(LOW)
+                    return carry
+
+                return lax.fori_loop(0, width // tile, one, carry)
+
+            puts.pair(terms, width, results[0], at, tile)
+        chips = job.parts // 2
+        rows = length // chips
+
+        def one_chip(turn, carry):
+            origin = next_chip(chips, turn)
+
+            @pl.when(turn > 0)
+            def _():
+                job.relay(turn)
+
+            job.arrived(origin)
+            at = pl.ds(pl.multiple_of(origin * rows, rows), rows)
+            block = job.dst.at[pl.ds(2 * origin, 2)]
+            value = block[...].reshape(rows, width)
+            back[at, :] = times_transposed(value, out_rows[...]).astype(LOW)
+            total[...] += product(mix[at, :].T, value)
+            return carry
+
+        lax.fori_loop(0, chips, one_chip, 0)
+        total_low[...] = total[...].astype(LOW)
+        out = [
+            pltpu.make_async_copy(back, results[1], leave.at[0]),
+            pltpu.make_async_copy(total_low, results[2], leave.at[1]),
+        ]
+        for copy in out:
+            copy.start()
+        puts.finish()
+        for copy in out:
+            copy.wait()
+
+
 class FeedForward:
     def __init__(self, job, upstream, gate, up, down):
         self.job = job
@@ -1096,46 +1229,41 @@
         units = gate.shape[1]
         self.outs = [
             jax.ShapeDtypeStruct((length, units), LOW),
-            jax.ShapeDtypeStruct((length, 2 * units), LOW),
+            jax.ShapeDtypeStruct((length, units), LOW),
+            jax.ShapeDtypeStruct((length, units), LOW),
             jax.ShapeDtypeStruct((length, width), LOW),
         ]
         self.tile = length // (job.parts // 2)
         self.scratch = [pltpu.VMEM(array.shape, array.dtype) for array in self.operands]
         self.scratch += [pltpu.VMEM((2, self.tile) + out.shape[1:], LOW) for out in self.outs]
-        self.scratch += [pltpu.SemaphoreType.DMA((4,)), pltpu.SemaphoreType.DMA((3, 2))]
+        self.scratch += [pltpu.SemaphoreType.DMA((4,)), pltpu.SemaphoreType.DMA((4, 2))]
 
     def run(self, *refs):
         job, tile = self.job, self.tile
-        sources, results, held, made = refs[:4], refs[4:7], refs[7:11], refs[11:14]
-        get, put = refs[14:]
+        sources, results, held, made = refs[:4], refs[4:8], refs[8:12], refs[12:16]
+        get, put = refs[16:]
         upstream, gate_w, up_w, down = held
-        acts, backs, terms = made
+        acts, gate_backs, up_backs, terms = made
         width, units = gate_w.shape
         step = min(units, 256)
         span = min(width, 512)
-        chip = lax.axis_index("ctx") // 2
         gets = [pltpu.make_async_copy(sources[i], held[i], get.at[i]) for i in (1, 2, 3, 0)]
         for copy in gets:
             copy.start()
         yield
         for copy in gets:
             copy.wait()
-        table = near_first(job.parts // 2)
-        chips = len(table)
+        chips = job.parts // 2
 
         def leave(slot, origin):
             at = pl.ds(pl.multiple_of(origin * tile, tile), tile)
             return [
                 pltpu.make_async_copy(made[i].at[slot], results[i].at[at, :], put.at[i, slot])
-                for i in range(3)
+                for i in range(4)
             ]
 
         def one_chip(turn, carry):
-            origin = sum(
-                jnp.where((chip == at) & (turn == when), order[when], 0)
-                for at, order in enumerate(table)
-                for when in range(chips)
-            )
+            origin = next_chip(chips, turn)
             slot = lax.rem(turn, 2)
 
             @pl.when(turn > 0)
@@ -1153,7 +1281,6 @@
 
             def forward(index, carry):
                 left = pl.ds(pl.multiple_of(index * step, step), step)
-                right = pl.ds(pl.multiple_of(units + index * step, step), step)
                 value = normed[...].reshape(tile, width)
                 gate = product(value, gate_w[:, left])
                 up = product(value, up_w[:, left])
@@ -1162,16 +1289,16 @@
                 silu = gate * sigmoid
                 acts[slot, :, left] = (silu * up).astype(LOW)
                 gate_grad = act_grad * up * sigmoid * (1.0 + gate * (1.0 - sigmoid))
-                backs[slot, :, left] = gate_grad.astype(LOW)
-                backs[slot, :, right] = (act_grad * silu).astype(LOW)
+                gate_backs[slot, :, left] = gate_grad.astype(LOW)
+                up_backs[slot, :, left] = (act_grad * silu).astype(LOW)
                 return carry
 
             lax.fori_loop(0, units // step, forward, 0)
 
             def backward(index, carry):
                 where = pl.ds(pl.multiple_of(index * span, span), span)
-                value = times_transposed(backs[slot, :, :units], gate_w[where, :])
-                value += times_transposed(backs[slot, :, units:], up_w[where, :])
+                value = times_transposed(gate_backs[slot], gate_w[where, :])
+                value += times_transposed(up_backs[slot], up_w[where, :])
                 terms[slot, :, where] = value.astype(LOW)
                 return carry
 
@@ -1214,20 +1341,20 @@
         return pieces.reshape(self.parts, rows, 2 * self.groups * inner)
 
     def unit_job(self, shape):
-        step = shape[1] // (2 * self.groups)
+        step = shape[1] // self.groups
         if step % HEAD_DIM:
             return Exchange(self.parts, shape)
         return Deliver(
             self.parts,
             shape,
-            lambda part: [(at * self.parts + part) * step for at in range(2 * self.groups)],
+            lambda part: [(at * self.parts + part) * step for at in range(self.groups)],
         )
 
     def unit_rows(self, pieces):
         if pieces.ndim == 2:
             return pieces
         parts, rows, columns = pieces.shape
-        outer = 2 * self.groups
+        outer = self.groups
         pieces = pieces.reshape(parts, rows, outer, columns // outer).transpose(1, 2, 0, 3)
         return pieces.reshape(rows, parts * columns).astype(jnp.float32)
 
@@ -1246,7 +1373,6 @@
     plane = (("ctx", parts), ("fsdp", groups))
     block = (rows, width)
 
-    out_rows = gather(w_out, "fsdp")
     down_rows = gather(w_down, "fsdp")
     gate_up_pieces = plan.unit_pieces(w_gate_up)
     unit_columns = gate_up_pieces.shape[2] // 2
@@ -1254,13 +1380,14 @@
     inputs = tokens.astype(jnp.float32)
     normed_in, root_in = normalize(inputs)
     qkv_pieces = plan.qkv_pieces(w_qkv)
-    qkv_cols, normed_in_full, gate_cols = call(
+    qkv_cols, normed_in_full, gate_cols, out_rows = call(
         [
             Spread(parts, groups, qkv_pieces.shape[1:]),
             Gather(parts, block, cuts=1),
-            Exchange(parts, unit_shape),
+            Exchange(parts, unit_shape, delay=2),
+            Fan(groups, w_out.shape),
         ],
-        [qkv_pieces, normed_in.astype(LOW), gate_up_pieces[:, :, :unit_columns]],
+        [qkv_pieces, normed_in.astype(LOW), gate_up_pieces[:, :, :unit_columns], w_out],
         "start",
         2,
         plane,
@@ -1308,7 +1435,7 @@
     residual = inputs + attn_out
     normed_mid, root_mid = normalize(residual)
     mid_job = Gather(parts, block, watched=True)
-    normed_mid_full, activated, gate_up_back, mid_back_terms = call(
+    normed_mid_full, activated, gate_back, up_back, mid_back_terms = call(
         [mid_job],
         [normed_mid.astype(LOW)],
         "mid",
@@ -1318,46 +1445,61 @@
         micros=60,
     )
     normed_mid_full = normed_mid_full.reshape(length, width)
-    mid_back, gate_up_grad, down_grad = call(
+    mid_back, gate_grad, up_grad, down_grad = call(
         [Scatter(parts, block)],
         [mid_back_terms.reshape((parts,) + block)],
         "mid_back",
         5,
         line,
-        Grads([(normed_mid_full, gate_up_back), (activated, cot_full)]),
+        Grads([(normed_mid_full, gate_back), (normed_mid_full, up_back), (activated, cot_full)]),
     )
-    gate_up_grad = scatter(gate_up_grad, "fsdp")
+    gate_grad = scatter(gate_grad, "fsdp")
+    up_grad = scatter(up_grad, "fsdp")
     down_grad = scatter(down_grad, "fsdp")
     residual_back = cotangent.astype(jnp.float32) + norm_back(mid_back, normed_mid, root_mid)
     proj_back = residual_back.astype(LOW)
 
-    down_terms = dot(activated, down_rows).astype(LOW)
-    (proj_back_full,) = call([Gather(parts, block)], [proj_back], "proj_back", 6, line, micros=45)
-    proj_back_full = proj_back_full.reshape(length, width)
-    out_grad = column_product(mix_low, proj_back_full).astype(LOW)
+    proj_job = Gather(parts, block, watched=True)
+    _, down_terms, back_heads, out_grad = call(
+        [proj_job],
+        [proj_back],
+        "proj_back",
+        6,
+        line,
+        ProjectBack(proj_job, activated, down_rows, out_cols, mix_low),
+        micros=45,
+    )
     out_grad = out_grad.reshape(heads, run, shard, width).transpose(1, 0, 2, 3)
-    down_out, out_grad, in_back_terms, qkv_grad = call(
-        [Scatter(parts, block), Exchange(run, (heads * shard, width))],
-        [down_terms.reshape((parts,) + block), out_grad.reshape(run, heads * shard, width)],
+    down_out, out_grad, gate_grad, in_back_terms, qkv_grad = call(
+        [
+            Scatter(parts, block, cuts=1),
+            Exchange(run, (heads * shard, width)),
+            plan.unit_job(unit_shape),
+        ],
+        [
+            down_terms.reshape((parts,) + block),
+            out_grad.reshape(run, heads * shard, width),
+            gate_grad.reshape((parts,) + unit_shape),
+        ],
         "attend_back",
         8,
         line,
-        AttendBack(proj_back_full, out_cols, qkv_low, normed_in_full, qkv_cols, tables, heads),
+        AttendBack(back_heads, qkv_low, normed_in_full, qkv_cols, tables, heads),
         micros=60,
     )
     layer_out = (residual + down_out).astype(LOW)
-    out_grad, gate_up_grad = lax.optimization_barrier((out_grad, gate_up_grad))
+    out_grad, up_grad = lax.optimization_barrier((out_grad, up_grad))
     out_grad = scatter(out_grad.reshape(groups * shard, width), "fsdp")
-    in_back, qkv_grad, gate_up_grad = call(
+    in_back, qkv_grad, up_grad = call(
         [
             Scatter(parts, block),
             Collect(parts, groups, qkv_pieces.shape[1:], plan.qkv_starts),
-            plan.unit_job(gate_up_pieces.shape[1:]),
+            plan.unit_job(unit_shape),
         ],
         [
             in_back_terms.reshape((parts,) + block),
             qkv_grad.reshape((groups,) + qkv_pieces.shape),
-            gate_up_grad.reshape(gate_up_pieces.shape),
+            up_grad.reshape((parts,) + unit_shape),
         ],
         "in_back",
         7,
@@ -1371,7 +1513,7 @@
         tokens_grad,
         qkv_grad,
         out_grad.astype(jnp.float32),
-        plan.unit_rows(gate_up_grad),
+        jnp.concatenate([plan.unit_rows(gate_grad), plan.unit_rows(up_grad)], axis=1),
         down_grad.astype(jnp.float32),
     )
 

time: 554 us -> 559 us (level)
  matrix products: 14.1 us -> 4.31 us
  Pallas kernels: 468 us -> 477 us
    pallas_call x8, Pallas kernels: 468 us -> 477 us  [call(): pl.pallas_call(kernel, out_shape=tuple((job.out for job in jobs)) + tuple...]
    reduce_scatter x3 -> x4, waiting for transfers between devices: 0.06 us -> 7.14 us  [scatter(): return lax.psum_scatter(values, axes, scatter_dimension=0, tiled=True)]
    dot_general x2 -> x1, matrix products: 10.3 us -> 4.31 us  [dot(): return jnp.dot(left, right, preferred_element_type=jnp.float32)]
  transfers between devices with their start and end apart: 7 -> 7, of which waited for: 1 -> 3; matrix products, arithmetic and copies ran while one was open for 8% -> 7% of each run, Pallas kernels for 66% -> 65%
where the time goes in v9:
time: 559 us; the launch traced here: 557 us
  Pallas kernels  477 us (85%)
  other arithmetic  23.9 us (4%)
  local copies, waits for them, and re-layouts  20.9 us (4%)
  waiting for transfers between devices  15.5 us (3%)
  between operations  14.4 us (3%)
    pallas_call x8, Pallas kernels, call(): pl.pallas_call(kernel, out_shape=tuple((job.out for job in jobs)) + tuple...  477 us
  transfers between devices with their start and end apart: 7, of which 3 were waited for; matrix products, arithmetic and copies ran while one was open for 7% of the time, Pallas kernels for 65%

profile of v9, /device:TPU:9, one launch (start us, length us, event | category | flops | bytes accessed | tf_op | source)
XLA Modules:
  0.0 556.6 jit_solution(3758207477599952193)
XLA Ops:
  7.9 2.3 reshape.207
  12.1 2.1 copy.22
  14.3 1.7 copy.25
  16.0 2.9 reshape.206
  19.4 1.6 fusion.26
  22.1 82.9 %start.1 = (bf16[4,8,64,768]{3,2,1,0:T(8,128)(2,1)}, bf16[8,128,2048]{2,1,0:T(8,128)(2,1)}, bf16[8,64,1024]{2,1,0:T(8,128)(2,1)}, bf16[4,64,2048]{2,1,0:T(8,128)(2,1)}) custom-call(bf16[8,64,768]{2,1,0:T(8,128)(2,1)} %reshape.208.refs_0_, bf16[128,2048]{1,0:T(8,128)(2,1)} %fusion.4.refs_1_, bf16[8,64,1024]{2,1,0:T(8,128)(2,1)} %get-tuple-element.84.refs_2_, ...), custom_call_target="tpu_custom_call" | custom-call | bytes 270000000 | tf_op jit(solution)/shard_map/start/pallas_call | solution.py:863
  105.8 2.9 sine_multiply_fusion
  111.3 29.9 %attend.1 = (bf16[8,64,1024]{2,1,0:T(8,128)(2,1)}, bf16[2,128,2048]{2,1,0:T(8,128)(2,1)}, bf16[1024,768]{1,0:T(8,128)(2,1)}, bf16[1024,256]{1,0:T(8,128)(2,1)}) custom-call(bf16[8,64,1024]{2,1,0:T(8,128)(2,1)} %get-tuple-element.85.refs_0_, bf16[2,128,2048]{2,1,0:T(8,128)(2,1)} %bitcast.66, bf16[1024,2048]{1,0:T(8,128)(2,1)} %bitcast.41, ...), custom_call_target="tpu_custom_call" | custom-call | bytes 120000000 | tf_op jit(solution)/shard_map/attend/pallas_call | solution.py:863
  143.6 4.3 convolution_convert_fusion
  147.9 54.7 %out.1 = (f32[128,2048]{1,0:T(8,128)}, bf16[8,128,2048]{2,1,0:T(8,128)(2,1)}) custom-call(bf16[8,128,2048]{2,1,0:T(8,128)(2,1)} %bitcast.40, bf16[128,2048]{1,0:T(8,128)(2,1)} %refs_1_.1), custom_call_target="tpu_custom_call" | custom-call | bytes 192000000 | tf_op jit(solution)/shard_map/out/pallas_call | solution.py:863
  205.4 6.6 %all-gather.6.cloned.1.call-done.refs_3_ = bf16[2048,1024]{1,0:T(8,128)(2,1)} async-done(((bf16[512,1024]{1,0:T(8,128)(2,1)}), bf16[2048,1024]{1,0:T(8,128)(2,1)}) %all-gather.6.cloned.1.call-update) | async-done | bytes 4194320 | tf_op jit(solution)/shard_map/all_gather | solution.py:83
  212.0 47.0 %mid.1 = (bf16[8,128,2048]{2,1,0:T(8,128)(2,1)}, bf16[1024,1024]{1,0:T(8,128)(2,1)}, bf16[1024,1024]{1,0:T(8,128)(2,1)}, bf16[1024,1024]{1,0:T(8,128)(2,1)}, bf16[1024,2048]{1,0:T(8,128)(2,1)}) custom-call(bf16[128,2048]{1,0:T(8,128)(2,1)} %fusion.10.refs_0_, bf16[1024,2048]{1,0:T(8,128)(2,1)} %bitcast.43, ...), custom_call_target="tpu_custom_call" | custom-call | bytes 180000000 | tf_op jit(solution)/shard_map/mid/pallas_call | solution.py:863
  259.0 66.9 %mid_back.1 = (f32[128,2048]{1,0:T(8,128)}, bf16[2048,1024]{1,0:T(8,128)(2,1)}, bf16[2048,1024]{1,0:T(8,128)(2,1)}, bf16[1024,2048]{1,0:T(8,128)(2,1)}) custom-call(bf16[8,128,2048]{2,1,0:T(8,128)(2,1)} %bitcast.55, bf16[1024,2048]{1,0:T(8,128)(2,1)} %bitcast.54, bf16[1024,1024]{1,0:T(8,128)(2,1)} %get-tuple-element.52.refs_2_, ...), custom_call_target="tpu_custom_call" | custom-call | bytes 150000000 | tf_op jit(solution)/shard_map/mid_back/pallas_call | solution.py:863
  327.7 2.7 fusion.24
  330.4 42.5 %proj_back.1 = (bf16[8,128,2048]{2,1,0:T(8,128)(2,1)}, bf16[1024,2048]{1,0:T(8,128)(2,1)}, bf16[1024,256]{1,0:T(8,128)(2,1)}, bf16[256,2048]{1,0:T(8,128)(2,1)}) custom-call(bf16[128,2048]{1,0:T(8,128)(2,1)} %get-tuple-element.80.refs_0_, bf16[1024,1024]{1,0:T(8,128)(2,1)} %get-tuple-element.54.refs_4_.refs_1_, ...), custom_call_target="tpu_custom_call" | custom-call | bytes 135000000 | tf_op jit(solution)/shard_map/proj_back/pallas_call | solution.py:863
  372.9 2.3 copy.21
  375.2 1.6 reduce-scatter.5.cloned.1.call-done
  376.8 78.2 %attend_back.1 = (f32[128,2048]{1,0:T(8,128)}, bf16[2,128,2048]{2,1,0:T(8,128)(2,1)}, f32[64,8192]{1,0:T(8,128)}, bf16[1024,2048]{1,0:T(8,128)(2,1)}, bf16[2048,768]{1,0:T(8,128)(2,1)}) custom-call(bf16[8,128,2048]{2,1,0:T(8,128)(2,1)} %bitcast.51, bf16[2,128,2048]{2,1,0:T(8,128)(2,1)} %bitcast.52, bf16[8,64,1024]{2,1,0:T(8,128)(2,1)} %bitcast.59, ...), custom_call_target="tpu_custom_call" | custom-call | bytes 180000000 | tf_op jit(solution)/shard_map/attend_back/pallas_call | solution.py:863
  455.1 2.1 add_convert_fusion
  457.2 74.8 %in_back.1 = (f32[128,2048]{1,0:T(8,128)}, f32[64,6144]{1,0:T(8,128)}, f32[64,8192]{1,0:T(8,128)}) custom-call(bf16[8,128,2048]{2,1,0:T(8,128)(2,1)} %bitcast.53, bf16[4,8,64,768]{3,2,1,0:T(8,128)(2,1)} %bitcast.57, bf16[8,64,1024]{2,1,0:T(8,128)(2,1)} %bitcast.65), custom_call_target="tpu_custom_call" | custom-call | bytes 270000000 | tf_op jit(solution)/shard_map/in_back/pallas_call | solution.py:863
  532.0 4.6 pad_maximum_fusion
  536.7 5.5 reduce-scatter.11.cloned.1.call-done
  542.5 1.9 convert_element_type.46
  544.4 2.8 convert_element_type.47
  (67 shorter events, 17.1 us)
Async XLA Ops:
  7.2 198.2 %all-gather.8.cloned.1.call-start = ((), (), s32[]{:S(2)}) async-start(), calls=%async_computation.6 | async-start | bytes 5242880 | tf_op jit(solution)/shard_map/all_gather | solution.py:83
  7.9 197.5 %all-gather.4.cloned.1.call-start = ((), (), s32[]{:S(2)}) async-start(), calls=%async_computation.4 | async-start | bytes 5242880 | tf_op jit(solution)/shard_map/all_gather | solution.py:83
  14.3 4.7 copy-start
  19.4 85.7 %copy-start.7 = (s32[1,2]{1,0:T(1,128)S(1)}, s32[1,2]{1,0:T(1,128)}, u32[]{:S(2)}) copy-start(s32[1,2]{1,0:T(1,128)} %param.13) | copy-start | bytes 28
  19.4 85.9 %copy-start.6 = (s32[1,8]{1,0:T(1,128)S(1)}, s32[1,8]{1,0:T(1,128)}, u32[]{:S(2)}) copy-start(s32[1,8]{1,0:T(1,128)} %param.14) | copy-start | bytes 100
  105.1 106.9 %all-gather.6.cloned.1.call-start = ((), (), s32[]{:S(2)}) async-start(), calls=%async_computation.5 | async-start | bytes 5242880 | tf_op jit(solution)/shard_map/all_gather | solution.py:83
  141.3 235.5 %reduce-scatter.5.cloned.1.call-start = ((), (), s32[]{:S(2)}) async-start(), calls=%async_computation.7 | async-start | bytes 5242880 | tf_op jit(solution)/shard_map/reduce_scatter | solution.py:87
  142.7 1.0 copy-start.1
  326.0 129.1 %reduce-scatter.7.cloned.1.call-start = ((), (), s32[]{:S(2)}) async-start(), calls=%async_computation.8 | async-start | bytes 5242880 | tf_op jit(solution)/shard_map/reduce_scatter | solution.py:87
  326.0 1.4 copy-start.4
  326.6 210.1 %reduce-scatter.9.cloned.1.call-start = ((), (), s32[]{:S(2)}) async-start(), calls=%async_computation.9 | async-start | bytes 5242880 | tf_op jit(solution)/shard_map/reduce_scatter | solution.py:87
  327.1 215.0 %reduce-scatter.11.cloned.1.call-start = ((), (), s32[]{:S(2)}) async-start(), calls=%async_computation.10 | async-start | bytes 1310720 | tf_op jit(solution)/shard_map/reduce_scatter | solution.py:87
  532.0 10.1 %copy-start.2 = (f32[128,2048]{1,0:T(8,128)S(1)}, f32[128,2048]{1,0:T(8,128)}, u32[]{:S(2)}) copy-start(f32[128,2048]{1,0:T(8,128)} %get-tuple-element.70) | copy-start | bytes 3145732
  536.7 10.5 %copy-start.3 = (f32[128,2048]{1,0:T(8,128)S(1)}, f32[128,2048]{1,0:T(8,128)}, u32[]{:S(2)}) copy-start(f32[128,2048]{1,0:T(8,128)} %get-tuple-element.81) | copy-start | bytes 3145732
  542.5 6.1 %copy-start.5 = (f32[64,6144]{1,0:T(8,128)S(1)}, f32[64,6144]{1,0:T(8,128)}, u32[]{:S(2)}) copy-start(f32[64,6144]{1,0:T(8,128)} %get-tuple-element.98) | copy-start | bytes 4718596
Sparse Core Ops, SparseCore 0:
  9.8 91.2 all-gather.7
  105.2 52.2 all-gather.3
  159.4 52.5 all-gather.5
  326.1 50.6 reduce-scatter.4
  379.6 52.5 reduce-scatter.6
  435.1 77.4 reduce-scatter.8
  515.4 26.7 reduce-scatter.10

commit v10 on v9

--- a/solution.py
+++ b/solution.py
@@ -105,8 +105,8 @@
 
 
 class Exchange:
-    def __init__(self, parts, shape, delay=0):
-        self.parts, self.delay = parts, delay
+    def __init__(self, parts, shape, delay=0, columns=None):
+        self.parts, self.delay, self.columns = parts, delay, columns
         self.out = jax.ShapeDtypeStruct((parts,) + shape, LOW)
         self.scratch = [
             pltpu.SemaphoreType.DMA((parts - 1,)),
@@ -119,27 +119,38 @@
             yield
         place = lax.axis_index("ctx")
         me = lax.rem(place, self.parts)
+        slot = dst.at[me]
         copies = []
         for step in range(1, self.parts):
             peer = lax.rem(me + step, self.parts)
-            copies.append(
-                remote(
-                    src.at[peer],
-                    dst.at[me],
-                    send.at[step - 1],
-                    recv.at[step - 1],
-                    "ctx",
-                    place - me + peer,
-                )
-            )
-            copies[-1].start()
-        own = pltpu.make_async_copy(src.at[me], dst.at[me], local)
-        own.start()
+            whole = (send.at[step - 1], recv.at[step - 1], "ctx", place - me + peer)
+            for block, target in blocks_of(src, peer, slot, self.columns):
+                copies.append(remote(block, target, *whole))
+                copies[-1].start()
+            if self.columns:
+                del copies[step - 1 :]
+                copies.append(remote(slot, slot, *whole))
+        for block, target in blocks_of(src, me, slot, self.columns):
+            pltpu.make_async_copy(block, target, local).start()
         yield
         for copy in copies:
             copy.wait()
             yield
-        own.wait()
+        pltpu.make_async_copy(slot, slot, local).wait()
+
+
+def blocks_of(src, part, slot, columns):
+    if columns is None:
+        return [(src.at[part], slot)]
+    starts = columns(part)
+    wide = slot.shape[1] // len(starts)
+    return [
+        (
+            src.at[:, pl.ds(pl.multiple_of(start, HEAD_DIM), wide)],
+            slot.at[:, pl.ds(index * wide, wide)],
+        )
+        for index, start in enumerate(starts)
+    ]
 
 
 class Gather:
@@ -414,8 +425,8 @@
 
 
 class Spread:
-    def __init__(self, parts, groups, shape):
-        self.parts, self.groups = parts, groups
+    def __init__(self, parts, groups, shape, columns=None):
+        self.parts, self.groups, self.columns = parts, groups, columns
         self.out = jax.ShapeDtypeStruct((groups, parts) + shape, LOW)
         self.scratch = [
             pltpu.SemaphoreType.DMA((parts - 1,)),
@@ -428,22 +439,17 @@
     def run(self, src, dst, send, recv, far_send, far_recv, local):
         parts, groups = self.parts, self.groups
         me, group = lax.axis_index("ctx"), lax.axis_index("fsdp")
+        slot = dst.at[group, me]
+        for block, target in blocks_of(src, me, slot, self.columns):
+            pltpu.make_async_copy(block, target, local).start()
         copies = []
         for step in range(1, parts):
             peer = lax.rem(me + step, parts)
-            copies.append(
-                remote(
-                    src.at[peer],
-                    dst.at[group, me],
-                    send.at[step - 1],
-                    recv.at[step - 1],
-                    "ctx",
-                    peer,
-                )
-            )
-            copies[-1].start()
-        own = pltpu.make_async_copy(src.at[me], dst.at[group, me], local)
-        own.start()
+            whole = (send.at[step - 1], recv.at[step - 1], "ctx", peer)
+            for block, target in blocks_of(src, peer, slot, self.columns):
+                remote(block, target, *whole).start()
+            copies.append(remote(slot, slot, *whole))
+        pltpu.make_async_copy(slot, slot, local).wait()
 
         def pass_on(block, origin, step):
             out = []
@@ -460,7 +466,7 @@
                 out.append(copy)
             return out
 
-        far = pass_on(src.at[me], me, 0)
+        far = pass_on(slot, me, 0)
         eager = -(-parts // 2)
         yield
         for step in range(1, parts):
@@ -475,7 +481,6 @@
                 yield
         for copy in copies:
             copy.wait_send()
-        own.wait()
 
 
 class Deliver:
@@ -1229,21 +1234,20 @@
         units = gate.shape[1]
         self.outs = [
             jax.ShapeDtypeStruct((length, units), LOW),
-            jax.ShapeDtypeStruct((length, units), LOW),
-            jax.ShapeDtypeStruct((length, units), LOW),
+            jax.ShapeDtypeStruct((length, 2 * units), LOW),
             jax.ShapeDtypeStruct((length, width), LOW),
         ]
         self.tile = length // (job.parts // 2)
         self.scratch = [pltpu.VMEM(array.shape, array.dtype) for array in self.operands]
         self.scratch += [pltpu.VMEM((2, self.tile) + out.shape[1:], LOW) for out in self.outs]
-        self.scratch += [pltpu.SemaphoreType.DMA((4,)), pltpu.SemaphoreType.DMA((4, 2))]
+        self.scratch += [pltpu.SemaphoreType.DMA((4,)), pltpu.SemaphoreType.DMA((3, 2))]
 
     def run(self, *refs):
         job, tile = self.job, self.tile
-        sources, results, held, made = refs[:4], refs[4:8], refs[8:12], refs[12:16]
-        get, put = refs[16:]
+        sources, results, held, made = refs[:4], refs[4:7], refs[7:11], refs[11:14]
+        get, put = refs[14:]
         upstream, gate_w, up_w, down = held
-        acts, gate_backs, up_backs, terms = made
+        acts, backs, terms = made
         width, units = gate_w.shape
         step = min(units, 256)
         span = min(width, 512)
@@ -1259,7 +1263,7 @@
             at = pl.ds(pl.multiple_of(origin * tile, tile), tile)
             return [
                 pltpu.make_async_copy(made[i].at[slot], results[i].at[at, :], put.at[i, slot])
-                for i in range(4)
+                for i in range(3)
             ]
 
         def one_chip(turn, carry):
@@ -1281,6 +1285,7 @@
 
             def forward(index, carry):
                 left = pl.ds(pl.multiple_of(index * step, step), step)
+                right = pl.ds(pl.multiple_of(units + index * step, step), step)
                 value = normed[...].reshape(tile, width)
                 gate = product(value, gate_w[:, left])
                 up = product(value, up_w[:, left])
@@ -1289,16 +1294,16 @@
                 silu = gate * sigmoid
                 acts[slot, :, left] = (silu * up).astype(LOW)
                 gate_grad = act_grad * up * sigmoid * (1.0 + gate * (1.0 - sigmoid))
-                gate_backs[slot, :, left] = gate_grad.astype(LOW)
-                up_backs[slot, :, left] = (act_grad * silu).astype(LOW)
+                backs[slot, :, left] = gate_grad.astype(LOW)
+                backs[slot, :, right] = (act_grad * silu).astype(LOW)
                 return carry
 
             lax.fori_loop(0, units // step, forward, 0)
 
             def backward(index, carry):
                 where = pl.ds(pl.multiple_of(index * span, span), span)
-                value = times_transposed(gate_backs[slot], gate_w[where, :])
-                value += times_transposed(up_backs[slot], up_w[where, :])
+                value = times_transposed(backs[slot, :, :units], gate_w[where, :])
+                value += times_transposed(backs[slot, :, units:], up_w[where, :])
                 terms[slot, :, where] = value.astype(LOW)
                 return carry
 
@@ -1319,12 +1324,6 @@
         self.shard = width // (parts * groups)
         self.run = HEAD_DIM // self.shard
         self.heads = HEADS // parts
-        self.qkv_dims = (3, self.run, self.heads, parts // self.run, HEAD_DIM)
-
-    def qkv_pieces(self, weight):
-        rows = weight.shape[0]
-        pieces = weight.reshape((rows,) + self.qkv_dims).transpose(4, 2, 0, 1, 3, 5)
-        return pieces.reshape(self.parts, rows, 3 * self.heads * HEAD_DIM)
 
     def qkv_starts(self, part):
         at, index = part // self.run, lax.rem(part, self.run)
@@ -1334,27 +1333,33 @@
             for head in range(self.heads)
         ]
 
-    def unit_pieces(self, weight):
+    def unit_source(self, weight, kind):
         rows, columns = weight.shape
-        inner = columns // (2 * self.groups * self.parts)
-        pieces = weight.reshape(rows, 2 * self.groups, self.parts, inner).transpose(2, 0, 1, 3)
-        return pieces.reshape(self.parts, rows, 2 * self.groups * inner)
+        half = columns // 2
+        step = half // (self.groups * self.parts)
+        if step % HEAD_DIM == 0:
+            return weight, lambda part: [
+                kind * half + (at * self.parts + part) * step for at in range(self.groups)
+            ]
+        pieces = weight[:, kind * half : (kind + 1) * half]
+        pieces = pieces.reshape(rows, self.groups, self.parts, step).transpose(2, 0, 1, 3)
+        return pieces.reshape(self.parts, rows, self.groups * step), None
 
     def unit_job(self, shape):
-        step = shape[1] // self.groups
+        step = shape[1] // (2 * self.groups)
         if step % HEAD_DIM:
             return Exchange(self.parts, shape)
         return Deliver(
             self.parts,
             shape,
-            lambda part: [(at * self.parts + part) * step for at in range(self.groups)],
+            lambda part: [(at * self.parts + part) * step for at in range(2 * self.groups)],
         )
 
     def unit_rows(self, pieces):
         if pieces.ndim == 2:
             return pieces
         parts, rows, columns = pieces.shape
-        outer = self.groups
+        outer = 2 * self.groups
         pieces = pieces.reshape(parts, rows, outer, columns // outer).transpose(1, 2, 0, 3)
         return pieces.reshape(rows, parts * columns).astype(jnp.float32)
 
@@ -1374,20 +1379,22 @@
     block = (rows, width)
 
     down_rows = gather(w_down, "fsdp")
-    gate_up_pieces = plan.unit_pieces(w_gate_up)
-    unit_columns = gate_up_pieces.shape[2] // 2
+    unit_columns = w_gate_up.shape[1] // (2 * parts)
     unit_shape = (w_gate_up.shape[0], unit_columns)
+    both_shape = (w_gate_up.shape[0], 2 * unit_columns)
+    qkv_shape = (w_qkv.shape[0], 3 * head_width)
+    gate_source, gate_starts = plan.unit_source(w_gate_up, 0)
+    up_source, up_starts = plan.unit_source(w_gate_up, 1)
     inputs = tokens.astype(jnp.float32)
     normed_in, root_in = normalize(inputs)
-    qkv_pieces = plan.qkv_pieces(w_qkv)
     qkv_cols, normed_in_full, gate_cols, out_rows = call(
         [
-            Spread(parts, groups, qkv_pieces.shape[1:]),
+            Spread(parts, groups, qkv_shape, plan.qkv_starts),
             Gather(parts, block, cuts=1),
-            Exchange(parts, unit_shape, delay=2),
+            Exchange(parts, unit_shape, 2, gate_starts),
             Fan(groups, w_out.shape),
         ],
-        [qkv_pieces, normed_in.astype(LOW), gate_up_pieces[:, :, :unit_columns], w_out],
+        [w_qkv, normed_in.astype(LOW), gate_source, w_out],
         "start",
         2,
         plane,
@@ -1410,8 +1417,11 @@
         jnp.broadcast_to(packed[None, :], (8, length)),
     )
     up_cols, out_cols, qkv_low, mix_low = call(
-        [Exchange(parts, unit_shape), Exchange(run, (heads * shard, width))],
-        [gate_up_pieces[:, :, unit_columns:], out_rows.reshape(run, heads * shard, width)],
+        [
+            Exchange(parts, unit_shape, 0, up_starts),
+            Exchange(run, (heads * shard, width)),
+        ],
+        [up_source, out_rows.reshape(run, heads * shard, width)],
         "attend",
         1,
         line,
@@ -1435,7 +1445,7 @@
     residual = inputs + attn_out
     normed_mid, root_mid = normalize(residual)
     mid_job = Gather(parts, block, watched=True)
-    normed_mid_full, activated, gate_back, up_back, mid_back_terms = call(
+    normed_mid_full, activated, gate_up_back, mid_back_terms = call(
         [mid_job],
         [normed_mid.astype(LOW)],
         "mid",
@@ -1445,16 +1455,15 @@
         micros=60,
     )
     normed_mid_full = normed_mid_full.reshape(length, width)
-    mid_back, gate_grad, up_grad, down_grad = call(
+    mid_back, gate_up_grad, down_grad = call(
         [Scatter(parts, block)],
         [mid_back_terms.reshape((parts,) + block)],
         "mid_back",
         5,
         line,
-        Grads([(normed_mid_full, gate_back), (normed_mid_full, up_back), (activated, cot_full)]),
+        Grads([(normed_mid_full, gate_up_back), (activated, cot_full)]),
     )
-    gate_grad = scatter(gate_grad, "fsdp")
-    up_grad = scatter(up_grad, "fsdp")
+    gate_up_grad = scatter(gate_up_grad, "fsdp")
     down_grad = scatter(down_grad, "fsdp")
     residual_back = cotangent.astype(jnp.float32) + norm_back(mid_back, normed_mid, root_mid)
     proj_back = residual_back.astype(LOW)
@@ -1470,16 +1479,14 @@
         micros=45,
     )
     out_grad = out_grad.reshape(heads, run, shard, width).transpose(1, 0, 2, 3)
-    down_out, out_grad, gate_grad, in_back_terms, qkv_grad = call(
+    down_out, out_grad, in_back_terms, qkv_grad = call(
         [
-            Scatter(parts, block, cuts=1),
+            Scatter(parts, block),
             Exchange(run, (heads * shard, width)),
-            plan.unit_job(unit_shape),
         ],
         [
             down_terms.reshape((parts,) + block),
             out_grad.reshape(run, heads * shard, width),
-            gate_grad.reshape((parts,) + unit_shape),
         ],
         "attend_back",
         8,
@@ -1488,18 +1495,18 @@
         micros=60,
     )
     layer_out = (residual + down_out).astype(LOW)
-    out_grad, up_grad = lax.optimization_barrier((out_grad, up_grad))
+    out_grad, gate_up_grad = lax.optimization_barrier((out_grad, gate_up_grad))
     out_grad = scatter(out_grad.reshape(groups * shard, width), "fsdp")
-    in_back, qkv_grad, up_grad = call(
+    in_back, qkv_grad, gate_up_grad = call(
         [
             Scatter(parts, block),
-            Collect(parts, groups, qkv_pieces.shape[1:], plan.qkv_starts),
-            plan.unit_job(unit_shape),
+            Collect(parts, groups, qkv_shape, plan.qkv_starts),
+            plan.unit_job(both_shape),
         ],
         [
             in_back_terms.reshape((parts,) + block),
-            qkv_grad.reshape((groups,) + qkv_pieces.shape),
-            up_grad.reshape((parts,) + unit_shape),
+            qkv_grad.reshape((groups, parts) + qkv_shape),
+            gate_up_grad.reshape((parts,) + both_shape),
         ],
         "in_back",
         7,
@@ -1513,7 +1520,7 @@
         tokens_grad,
         qkv_grad,
         out_grad.astype(jnp.float32),
-        jnp.concatenate([plan.unit_rows(gate_grad), plan.unit_rows(up_grad)], axis=1),
+        plan.unit_rows(gate_up_grad),
         down_grad.astype(jnp.float32),
     )
 

time: 559 us -> 534 us (0.955)
  Pallas kernels: 477 us -> 466 us
  local copies, waits for them, and re-layouts: 20.9 us -> 11.5 us
    pallas_call x8, Pallas kernels: 477 us -> 466 us  [call(): pl.pallas_call(kernel, out_shape=tuple((job.out for job in jobs)) + tuple...]
    reshape x5 -> x0, local copies, waits for them, and re-layouts: 8.83 us -> none  [the longest x1 2.93 us: unit_pieces(): return pieces.reshape(self.parts, rows, 2 * self.groups * inner)]
    reduce_scatter x4 -> x3, waiting for transfers between devices: 7.14 us -> 0.06 us  [scatter(): return lax.psum_scatter(values, axes, scatter_dimension=0, tiled=True)]
  transfers between devices with their start and end apart: 7 -> 6, of which waited for: 3 -> 1; matrix products, arithmetic and copies ran while one was open for 7% -> 5% of each run, Pallas kernels for 65% -> 68%
where the time goes in v10:
time: 534 us; the launch traced here: 533 us
  Pallas kernels  466 us (87%)
  other arithmetic  23.8 us (4%)
  between operations  14.4 us (3%)
  waiting for transfers between devices  13.1 us (2%)
  local copies, waits for them, and re-layouts  11.5 us (2%)
    pallas_call x8, Pallas kernels, call(): pl.pallas_call(kernel, out_shape=tuple((job.out for job in jobs)) + tuple...  466 us
    all_gather x3, waiting for transfers between devices, gather(): return lax.all_gather(values, axes, axis=0, tiled=True)  11.7 us
  transfers between devices with their start and end apart: 6, of which 1 were waited for; matrix products, arithmetic and copies ran while one was open for 5% of the time, Pallas kernels for 68%

profile of v10, /device:TPU:9, one launch (start us, length us, event | category | flops | bytes accessed | tf_op | source)
XLA Modules:
  0.0 532.9 jit_solution(10261230931404348240)
XLA Ops:
  8.0 1.2 convert_reduce_fusion
  9.2 1.3 fusion.9
  10.5 2.2 fusion.4.refs_1_
  12.7 80.3 %start.1 = (bf16[4,8,64,768]{3,2,1,0:T(8,128)(2,1)}, bf16[8,128,2048]{2,1,0:T(8,128)(2,1)}, bf16[8,64,1024]{2,1,0:T(8,128)(2,1)}, bf16[4,64,2048]{2,1,0:T(8,128)(2,1)}) custom-call(bf16[64,6144]{1,0:T(8,128)(2,1)} %refs_0_.2, bf16[128,2048]{1,0:T(8,128)(2,1)} %fusion.4.refs_1_, bf16[64,16384]{1,0:T(8,128)(2,1)} %refs_0_.3, bf16[64,2048]{1,0:T(8,128)(2,1)} %refs_3_.1), custom_call_target="tpu_custom_call" | custom-call | bytes 270000000 | tf_op jit(solution)/shard_map/start/pallas_call | solution.py:868
  93.7 2.9 sine_multiply_fusion
  99.2 32.0 %attend.1 = (bf16[8,64,1024]{2,1,0:T(8,128)(2,1)}, bf16[2,128,2048]{2,1,0:T(8,128)(2,1)}, bf16[1024,768]{1,0:T(8,128)(2,1)}, bf16[1024,256]{1,0:T(8,128)(2,1)}) custom-call(bf16[64,16384]{1,0:T(8,128)(2,1)} %refs_0_.3, bf16[2,128,2048]{2,1,0:T(8,128)(2,1)} %bitcast.44, bf16[1024,2048]{1,0:T(8,128)(2,1)} %bitcast.29, bf16[2048,768]{1,0:T(8,128)(2,1)} %bitcast.33, ...), custom_call_target="tpu_custom_call" | custom-call | bytes 120000000 | tf_op jit(solution)/shard_map/attend/pallas_call | solution.py:868
  131.2 1.3 copy.16
  133.6 4.3 convolution_convert_fusion
  137.9 54.1 %out.1 = (f32[128,2048]{1,0:T(8,128)}, bf16[8,128,2048]{2,1,0:T(8,128)(2,1)}) custom-call(bf16[8,128,2048]{2,1,0:T(8,128)(2,1)} %bitcast.28, bf16[128,2048]{1,0:T(8,128)(2,1)} %refs_1_.1), custom_call_target="tpu_custom_call" | custom-call | bytes 192000000 | tf_op jit(solution)/shard_map/out/pallas_call | solution.py:868
  191.9 1.4 fusion.25
  194.6 11.7 %all-gather.6.cloned.1.call-done.refs_3_ = bf16[2048,1024]{1,0:T(8,128)(2,1)} async-done(((bf16[512,1024]{1,0:T(8,128)(2,1)}), bf16[2048,1024]{1,0:T(8,128)(2,1)}) %all-gather.6.cloned.1.call-update) | async-done | bytes 4194320 | tf_op jit(solution)/shard_map/all_gather | solution.py:83
  206.3 47.2 %mid.1 = (bf16[8,128,2048]{2,1,0:T(8,128)(2,1)}, bf16[1024,1024]{1,0:T(8,128)(2,1)}, bf16[1024,2048]{1,0:T(8,128)(2,1)}, bf16[1024,2048]{1,0:T(8,128)(2,1)}) custom-call(bf16[128,2048]{1,0:T(8,128)(2,1)} %fusion.10.refs_0_, bf16[1024,2048]{1,0:T(8,128)(2,1)} %bitcast.31, bf16[2048,1024]{1,0:T(8,128)(2,1)} %all-gather.4.cloned.1.call-done.refs_2_, ...), custom_call_target="tpu_custom_call" | custom-call | bytes 180000000 | tf_op jit(solution)/shard_map/mid/pallas_call | solution.py:868
  253.5 58.1 %mid_back.1 = (f32[128,2048]{1,0:T(8,128)}, bf16[2048,2048]{1,0:T(8,128)(2,1)}, bf16[1024,2048]{1,0:T(8,128)(2,1)}) custom-call(bf16[8,128,2048]{2,1,0:T(8,128)(2,1)} %bitcast.41, bf16[1024,2048]{1,0:T(8,128)(2,1)} %bitcast.40, bf16[1024,2048]{1,0:T(8,128)(2,1)} %get-tuple-element.49.refs_2_, bf16[1024,1024]{1,0:T(8,128)(2,1)} %get-tuple-element.50.refs_3_.refs_1_, ...), custom_call_target="tpu_custom_call" | custom-call | bytes 150000000 | tf_op jit(solution)/shard_map/mid_back/pallas_call | solution.py:868
  313.1 2.7 fusion.24
  315.8 42.6 %proj_back.1 = (bf16[8,128,2048]{2,1,0:T(8,128)(2,1)}, bf16[1024,2048]{1,0:T(8,128)(2,1)}, bf16[1024,256]{1,0:T(8,128)(2,1)}, bf16[256,2048]{1,0:T(8,128)(2,1)}) custom-call(bf16[128,2048]{1,0:T(8,128)(2,1)} %get-tuple-element.74.refs_0_, bf16[1024,1024]{1,0:T(8,128)(2,1)} %get-tuple-element.50.refs_3_.refs_1_, ...), custom_call_target="tpu_custom_call" | custom-call | bytes 135000000 | tf_op jit(solution)/shard_map/proj_back/pallas_call | solution.py:868
  358.4 2.4 copy.17
  360.8 55.3 %attend_back.1 = (f32[128,2048]{1,0:T(8,128)}, bf16[2,128,2048]{2,1,0:T(8,128)(2,1)}, bf16[1024,2048]{1,0:T(8,128)(2,1)}, bf16[2048,768]{1,0:T(8,128)(2,1)}) custom-call(bf16[8,128,2048]{2,1,0:T(8,128)(2,1)} %bitcast.39, bf16[2,128,2048]{2,1,0:T(8,128)(2,1)} %bitcast.37, bf16[1024,256]{1,0:T(8,128)(2,1)} %get-tuple-element.54.refs_2_, ...), custom_call_target="tpu_custom_call" | custom-call | bytes 180000000 | tf_op jit(solution)/shard_map/attend_back/pallas_call | solution.py:868
  416.2 2.1 add_convert_fusion
  418.3 96.2 %in_back.1 = (f32[128,2048]{1,0:T(8,128)}, f32[64,6144]{1,0:T(8,128)}, f32[64,16384]{1,0:T(8,128)}) custom-call(bf16[8,128,2048]{2,1,0:T(8,128)(2,1)} %bitcast.38, bf16[4,8,64,768]{3,2,1,0:T(8,128)(2,1)} %bitcast.42, bf16[8,64,2048]{2,1,0:T(8,128)(2,1)} %bitcast.43), custom_call_target="tpu_custom_call" | custom-call | bytes 270000000 | tf_op jit(solution)/shard_map/in_back/pallas_call | solution.py:868
  514.6 1.7 fusion.22
  516.3 1.9 convert_element_type.46
  518.2 2.8 convert_element_type.47
  521.0 1.4 fusion.8
  524.1 2.0 copy.21
  (59 shorter events, 9.6 us)
Async XLA Ops:
  7.2 85.9 %copy-start.8 = (s32[1,2]{1,0:T(1,128)S(1)}, s32[1,2]{1,0:T(1,128)}, u32[]{:S(2)}) copy-start(s32[1,2]{1,0:T(1,128)} %param.13) | copy-start | bytes 28
  7.2 86.1 %copy-start.7 = (s32[1,8]{1,0:T(1,128)S(1)}, s32[1,8]{1,0:T(1,128)}, u32[]{:S(2)}) copy-start(s32[1,8]{1,0:T(1,128)} %param.14) | copy-start | bytes 100
  7.2 187.4 %all-gather.8.cloned.1.call-start = ((), (), s32[]{:S(2)}) async-start(), calls=%async_computation.5 | async-start | bytes 5242880 | tf_op jit(solution)/shard_map/all_gather | solution.py:83
  7.9 186.7 %all-gather.4.cloned.1.call-start = ((), (), s32[]{:S(2)}) async-start(), calls=%async_computation.3 | async-start | bytes 5242880 | tf_op jit(solution)/shard_map/all_gather | solution.py:83
  93.0 113.3 %all-gather.6.cloned.1.call-start = ((), (), s32[]{:S(2)}) async-start(), calls=%async_computation.4 | async-start | bytes 5242880 | tf_op jit(solution)/shard_map/all_gather | solution.py:83
  131.2 284.9 %reduce-scatter.4.cloned.1.call-start = ((), (), s32[]{:S(2)}) async-start(), calls=%async_computation.6 | async-start | bytes 10485760 | tf_op jit(solution)/shard_map/reduce_scatter | solution.py:87
  132.6 1.0 copy-start.1
  137.9 54.1 %copy-start = (bf16[128,2048]{1,0:T(8,128)(2,1)S(1)}, bf16[128,2048]{1,0:T(8,128)(2,1)}, u32[]{:S(2)}) copy-start(bf16[128,2048]{1,0:T(8,128)(2,1)} %param.8) | copy-start | bytes 1572868
  311.6 1.2 copy-start.5
  311.6 202.9 %reduce-scatter.6.cloned.1.call-start = ((), (), s32[]{:S(2)}) async-start(), calls=%async_computation.7 | async-start | bytes 5242880 | tf_op jit(solution)/shard_map/reduce_scatter | solution.py:87
  312.2 202.4 %reduce-scatter.8.cloned.1.call-start = ((), (), s32[]{:S(2)}) async-start(), calls=%async_computation.8 | async-start | bytes 1310720 | tf_op jit(solution)/shard_map/reduce_scatter | solution.py:87
  514.5 6.5 %copy-start.2 = (f32[128,2048]{1,0:T(8,128)S(1)}, f32[128,2048]{1,0:T(8,128)}, u32[]{:S(2)}) copy-start(f32[128,2048]{1,0:T(8,128)} %get-tuple-element.65) | copy-start | bytes 3145732
  514.5 6.5 %copy-start.4 = (f32[128,2048]{1,0:T(8,128)S(1)}, f32[128,2048]{1,0:T(8,128)}, u32[]{:S(2)}) copy-start(f32[128,2048]{1,0:T(8,128)} %get-tuple-element.75) | copy-start | bytes 3145732
  516.3 6.1 %copy-start.6 = (f32[64,6144]{1,0:T(8,128)S(1)}, f32[64,6144]{1,0:T(8,128)}, u32[]{:S(2)}) copy-start(f32[64,6144]{1,0:T(8,128)} %get-tuple-element.90) | copy-start | bytes 4718596
  521.0 3.1 copy-start.3
Sparse Core Ops, SparseCore 0:
  9.8 89.4 all-gather.7
  101.2 50.6 all-gather.3
  153.7 52.5 all-gather.5
  311.7 84.4 reduce-scatter.3
  399.0 77.8 reduce-scatter.5
  479.7 26.6 reduce-scatter.7

commit v11 on v10

--- a/solution.py
+++ b/solution.py
@@ -105,9 +105,12 @@
 
 
 class Exchange:
-    def __init__(self, parts, shape, delay=0, columns=None):
-        self.parts, self.delay, self.columns = parts, delay, columns
-        self.out = jax.ShapeDtypeStruct((parts,) + shape, LOW)
+    outside = ("in", "out")
+
+    def __init__(self, parts, shape, delay=0, columns=None, second=""):
+        self.parts, self.delay, self.columns, self.second = parts, delay, columns, second
+        placed = shape[:1] + (parts,) + shape[1:] if second == "out" else (parts,) + shape
+        self.out = jax.ShapeDtypeStruct(placed, LOW)
         self.scratch = [
             pltpu.SemaphoreType.DMA((parts - 1,)),
             pltpu.SemaphoreType.DMA((parts - 1,)),
@@ -119,18 +122,24 @@
             yield
         place = lax.axis_index("ctx")
         me = lax.rem(place, self.parts)
-        slot = dst.at[me]
+        slot = dst.at[:, me] if self.second == "out" else dst.at[me]
+
+        def blocks(part):
+            if self.second == "in":
+                return [(src.at[:, part], slot)]
+            return blocks_of(src, part, slot, self.columns)
+
         copies = []
         for step in range(1, self.parts):
             peer = lax.rem(me + step, self.parts)
             whole = (send.at[step - 1], recv.at[step - 1], "ctx", place - me + peer)
-            for block, target in blocks_of(src, peer, slot, self.columns):
+            for block, target in blocks(peer):
                 copies.append(remote(block, target, *whole))
                 copies[-1].start()
             if self.columns:
                 del copies[step - 1 :]
                 copies.append(remote(slot, slot, *whole))
-        for block, target in blocks_of(src, me, slot, self.columns):
+        for block, target in blocks(me):
             pltpu.make_async_copy(block, target, local).start()
         yield
         for copy in copies:
@@ -155,6 +164,7 @@
 
 class Gather:
     def __init__(self, parts, shape, watched=False, cuts=2):
+        self.outside = ("in", "out")
         self.parts, self.watched, self.shape, self.cuts = parts, watched, shape, cuts
         self.out = jax.ShapeDtypeStruct((parts,) + shape, LOW)
         chips = parts // 2
@@ -165,8 +175,11 @@
             pltpu.SemaphoreType.DMA((chips, self.cuts)),
             pltpu.SemaphoreType.DMA,
         ]
-
-    def run(self, src, dst, send, recv, pair_send, pair_recv, local):
+        if watched:
+            self.scratch += [pltpu.VMEM(self.out.shape, LOW), pltpu.SemaphoreType.DMA((chips,))]
+
+    def run(self, src, out, send, recv, pair_send, pair_recv, local, *watch):
+        dst = watch[0] if self.watched else out
         chips, cuts = self.parts // 2, self.cuts
         rows = self.shape[0] // cuts
         me = lax.axis_index("ctx")
@@ -207,6 +220,13 @@
             @pl.when(origin == chip)
             def _():
                 own.wait()
+
+            if self.watched:
+                kept(origin).start()
+
+        def kept(origin):
+            rows = pl.ds(2 * origin, 2)
+            return pltpu.make_async_copy(dst.at[rows], out.at[rows], watch[1].at[origin])
 
         def relay(step):
             for cut in range(cuts):
@@ -260,11 +280,15 @@
             slot = dst.at[2 * origin + core]
             for cut in range(cuts):
                 across(slot, slot, origin, cut).wait_send()
-            if not self.watched:
+            if self.watched:
+                kept(origin).wait()
+            else:
                 arrived(origin)
 
 
 class Scatter:
+    outside = ()
+
     def __init__(self, parts, shape, cuts=2):
         self.parts, self.shape, self.cuts = parts, shape, cuts
         self.out = jax.ShapeDtypeStruct(shape, jnp.float32)
@@ -395,6 +419,8 @@
 
 
 class Fan:
+    outside = ("in", "out")
+
     def __init__(self, groups, shape):
         self.groups = groups
         self.out = jax.ShapeDtypeStruct((groups,) + shape, LOW)
@@ -425,6 +451,8 @@
 
 
 class Spread:
+    outside = ("in", "out")
+
     def __init__(self, parts, groups, shape, columns=None):
         self.parts, self.groups, self.columns = parts, groups, columns
         self.out = jax.ShapeDtypeStruct((groups, parts) + shape, LOW)
@@ -484,14 +512,16 @@
 
 
 class Deliver:
+    outside = ("in",)
+
     def __init__(self, parts, shape, offsets, delay=0, eager=1):
         self.parts, self.shape, self.offsets = parts, shape, offsets
         self.delay, self.eager = delay, eager
         self.out = jax.ShapeDtypeStruct((shape[0], parts * shape[1]), jnp.float32)
         self.scratch = [
-            pltpu.VMEM((parts - 1,) + shape, LOW),
+            pltpu.VMEM((parts,) + shape, LOW),
             pltpu.SemaphoreType.DMA((parts - 1,)),
-            pltpu.SemaphoreType.DMA((parts - 1,)),
+            pltpu.SemaphoreType.DMA((parts,)),
         ]
 
     def place(self, out, origin, read):
@@ -521,8 +551,12 @@
             block = src.at[lax.rem(me + step, self.parts)]
             copies.append(self.send(me, step, block, came, send, recv))
             copies[-1].start()
-        self.place(out, me, lambda lo, hi: src[me, :, lo:hi].astype(jnp.float32))
-        yield
+        last = self.parts - 1
+        own = pltpu.make_async_copy(src.at[me], came.at[last], recv.at[last])
+        own.start()
+        yield
+        own.wait()
+        self.place(out, me, lambda lo, hi: came[last, :, lo:hi].astype(jnp.float32))
         yield from self.finish(me, out, copies, came)
 
     def finish(self, me, out, copies, came):
@@ -537,6 +571,8 @@
 
 
 class Collect(Deliver):
+    outside = ()
+
     def __init__(self, parts, groups, shape, offsets, delay=0, eager=1):
         super().__init__(parts, shape, offsets, delay, eager)
         self.groups = groups
@@ -590,6 +626,34 @@
             copy.wait_send()
 
 
+def product(left, right):
+    return jnp.dot(left, right, preferred_element_type=jnp.float32)
+
+
+class Puts:
+    def __init__(self, made, put):
+        self.made, self.put, self.copies = made, put, []
+
+    def pair(self, fill, columns, out, at, tile):
+        for copy in self.copies:
+            copy.wait()
+        lax.fori_loop(0, 2, fill, 0)
+        self.copies = []
+        for half in range(2):
+            begin = at + half * tile
+            copy = pltpu.make_async_copy(
+                self.made.at[half, :, pl.ds(0, columns)],
+                out.at[begin : begin + tile, :],
+                self.put.at[half],
+            )
+            copy.start()
+            self.copies.append(copy)
+
+    def finish(self):
+        for copy in self.copies:
+            copy.wait()
+
+
 def call(jobs, operands, name, identity, axes, work=None, micros=50):
     counts = [len(job.scratch) for job in jobs]
     jobs_n = len(jobs)
@@ -625,251 +689,13 @@
 
     vmem = pl.BlockSpec(memory_space=pltpu.VMEM)
     anywhere = pl.BlockSpec(memory_space=pl.ANY)
+    in_specs = [anywhere if "in" in job.outside else vmem for job in jobs]
+    out_specs = [anywhere if "out" in job.outside else vmem for job in jobs]
     return pl.pallas_call(
         kernel,
         out_shape=tuple(job.out for job in jobs) + tuple(extra_out),
-        in_specs=[vmem] * jobs_n + [anywhere] * len(extra),
-        out_specs=(vmem,) * jobs_n + (anywhere,) * len(extra_out),
-        scratch_shapes=[shape for job in jobs for shape in job.scratch] + list(extra_scratch),
-        compiler_params=pltpu.CompilerParams(
-            collective_id=identity, has_side_effects=True, vmem_limit_bytes=62 << 20
-        ),
-        cost_estimate=pl.CostEstimate(
-            flops=0, bytes_accessed=micros * 3_000_000, transcendentals=0
-        ),
-        name=name,
-    )(*operands, *extra)
-
-
-def product(left, right):
-    return jnp.dot(left, right, preferred_element_type=jnp.float32)
-
-
-class Puts:
-    def __init__(self, made, put):
-        self.made, self.put, self.copies = made, put, []
-
-    def pair(self, fill, columns, out, at, tile):
-        for copy in self.copies:
-            copy.wait()
-        lax.fori_loop(0, 2, fill, 0)
-        self.copies = []
-        for half in range(2):
-            begin = at + half * tile
-            copy = pltpu.make_async_copy(
-                self.made.at[half, :, pl.ds(0, columns)],
-                out.at[begin : begin + tile, :],
-                self.put.at[half],
-            )
-            copy.start()
-            self.copies.append(copy)
-
-    def finish(self):
-        for copy in self.copies:
-            copy.wait()
-
-
-class Grads:
-    tile = 256
-
-    def __init__(self, pairs):
-        self.pairs = pairs
-        length, wide = pairs[0][0].shape[0], max(right.shape[1] for _, right in pairs)
-        self.operands = [array for pair in pairs for array in pair]
-        self.outs = [jax.ShapeDtypeStruct((l.shape[1], r.shape[1]), LOW) for l, r in pairs]
-        self.slots = [[id(array) for array in self.operands].index(id(a)) for a in self.operands]
-        self.operands = [a for i, a in enumerate(self.operands) if self.slots[i] == i]
-        self.slots = [sorted(set(self.slots)).index(slot) for slot in self.slots]
-        self.scratch = [pltpu.VMEM(array.shape, LOW) for array in self.operands]
-        self.scratch += [
-            pltpu.VMEM((self.tile, length), LOW),
-            pltpu.VMEM((2, self.tile, wide), LOW),
-            pltpu.SemaphoreType.DMA((len(self.operands),)),
-            pltpu.SemaphoreType.DMA((2,)),
-        ]
-
-    def run(self, *refs):
-        n, tile, count = len(self.pairs), self.tile, len(self.operands)
-        sources, outs = refs[:count], refs[count : count + n]
-        held = refs[count + n : 2 * count + n]
-        turned, made, get, put = refs[2 * count + n :]
-        gets = [pltpu.make_async_copy(s, h, get.at[i]) for i, (s, h) in enumerate(zip(sources, held))]
-        for copy in gets:
-            copy.start()
-        yield
-        puts = Puts(made, put)
-        for which in range(n):
-            first, second = self.slots[2 * which : 2 * which + 2]
-            left, right, out = held[first], held[second], outs[which]
-            for slot in (first, second):
-                if slot not in self.slots[: 2 * which]:
-                    gets[slot].wait()
-            columns = right.shape[1]
-            step = min(columns, 256)
-            for at in range(0, left.shape[1], 2 * tile):
-                def pair(half, carry):
-                    begin = pl.multiple_of(at + half * tile, tile)
-                    turned[...] = left[:, pl.ds(begin, tile)].T
-
-                    def one(index, carry):
-                        where = pl.ds(pl.multiple_of(index * step, step), step)
-                        made[half, :, where] = product(turned[...], right[:, where]).astype(LOW)
-                        return carry
-
-                    return lax.fori_loop(0, columns // step, one, carry)
-
-                puts.pair(pair, columns, out, at, tile)
-                yield
-        puts.finish()
-
-
-class Deliver:
-    def __init__(self, parts, shape, offsets, delay=0, eager=1):
-        self.parts, self.shape, self.offsets = parts, shape, offsets
-        self.delay, self.eager = delay, eager
-        self.out = jax.ShapeDtypeStruct((shape[0], parts * shape[1]), jnp.float32)
-        self.scratch = [
-            pltpu.VMEM((parts - 1,) + shape, LOW),
-            pltpu.SemaphoreType.DMA((parts - 1,)),
-            pltpu.SemaphoreType.DMA((parts - 1,)),
-        ]
-
-    def place(self, out, origin, read):
-        starts = self.offsets(origin)
-        step = self.shape[1] // len(starts)
-        for index, start in enumerate(starts):
-            out[:, pl.ds(pl.multiple_of(start, HEAD_DIM), step)] = read(
-                index * step, (index + 1) * step
-            )
-
-    def send(self, me, step, block, came, send, recv):
-        return remote(
-            block,
-            came.at[step - 1],
-            send.at[step - 1],
-            recv.at[step - 1],
-            "ctx",
-            lax.rem(me + step, self.parts),
-        )
-
-    def run(self, src, out, came, send, recv):
-        for _ in range(self.delay):
-            yield
-        me = lax.axis_index("ctx")
-        copies = []
-        for step in range(1, self.parts):
-            block = src.at[lax.rem(me + step, self.parts)]
-            copies.append(self.send(me, step, block, came, send, recv))
-            copies[-1].start()
-        self.place(out, me, lambda lo, hi: src[me, :, lo:hi].astype(jnp.float32))
-        yield
-        yield from self.finish(me, out, copies, came)
-
-    def finish(self, me, out, copies, came):
-        for step in range(1, self.parts):
-            copies[step - 1].wait_recv()
-            origin = lax.rem(me - step + self.parts, self.parts)
-            self.place(out, origin, lambda lo, hi: came[step - 1, :, lo:hi].astype(jnp.float32))
-            if step % self.eager == 0:
-                yield
-        for copy in copies:
-            copy.wait_send()
-
-
-class Collect(Deliver):
-    def __init__(self, parts, groups, shape, offsets, delay=0, eager=1):
-        super().__init__(parts, shape, offsets, delay, eager)
-        self.groups = groups
-        self.scratch = self.scratch + [
-            pltpu.VMEM((groups - 1, parts) + shape, LOW),
-            pltpu.VMEM((parts,) + shape, LOW),
-            pltpu.VMEM(shape, jnp.float32),
-            pltpu.SemaphoreType.DMA((groups - 1, parts)),
-            pltpu.SemaphoreType.DMA((groups - 1, parts)),
-        ]
-
-    def run(self, src, out, came, send, recv, far, stage, mine, far_send, far_recv):
-        parts, groups = self.parts, self.groups
-        me, group = lax.axis_index("ctx"), lax.axis_index("fsdp")
-        goals = [lax.rem(me + step, parts) for step in range(1, parts + 1)]
-        hops = []
-        for goal in goals:
-            for hop in range(1, groups):
-                peer = lax.rem(group + hop, groups)
-                hops.append(
-                    remote(
-                        src.at[peer, goal],
-                        far.at[hop - 1, goal],
-                        far_send.at[hop - 1, goal],
-                        far_recv.at[hop - 1, goal],
-                        "fsdp",
-                        peer,
-                    )
-                )
-                hops[-1].start()
-        yield
-        copies = []
-        for step in range(1, parts + 1):
-            goal = goals[step - 1]
-            for copy in hops[(step - 1) * (groups - 1) : step * (groups - 1)]:
-                copy.wait_recv()
-            value = src[group, goal].astype(jnp.float32)
-            for hop in range(groups - 1):
-                value += far[hop, goal].astype(jnp.float32)
-            if step < parts:
-                stage[goal] = value.astype(LOW)
-                copies.append(self.send(me, step, stage.at[goal], came, send, recv))
-                copies[-1].start()
-            else:
-                mine[...] = value
-            if step % self.eager == 0:
-                yield
-        self.place(out, me, lambda lo, hi: mine[:, lo:hi])
-        yield from self.finish(me, out, copies, came)
-        for copy in hops:
-            copy.wait_send()
-
-
-def call(jobs, operands, name, identity, axes, work=None, micros=50):
-    counts = [len(job.scratch) for job in jobs]
-    jobs_n = len(jobs)
-    extra = work.operands if work else []
-    extra_out = work.outs if work else []
-    extra_scratch = work.scratch if work else []
-
-    def kernel(*refs):
-        refs = list(refs)
-
-        def take(count):
-            taken = refs[:count]
-            del refs[:count]
-            return taken
-
-        ins, more = take(jobs_n), take(len(extra))
-        outs, more_outs = take(jobs_n), take(len(extra_out))
-        runs = []
-        for job, src, dst, count in zip(jobs, ins, outs, counts):
-            runs.append(job.run(src, dst, *take(count)))
-        if work:
-            runs.append(work.run(*more, *more_outs, *refs))
-        enter(axes)
-        while runs:
-            going = []
-            for run in runs:
-                try:
-                    next(run)
-                    going.append(run)
-                except StopIteration:
-                    pass
-            runs = going
-
-    vmem = pl.BlockSpec(memory_space=pltpu.VMEM)
-    anywhere = pl.BlockSpec(memory_space=pl.ANY)
-    return pl.pallas_call(
-        kernel,
-        out_shape=tuple(job.out for job in jobs) + tuple(extra_out),
-        in_specs=[vmem] * jobs_n + [anywhere] * len(extra),
-        out_specs=(vmem,) * jobs_n + (anywhere,) * len(extra_out),
+        in_specs=in_specs + [anywhere] * len(extra),
+        out_specs=tuple(out_specs) + (anywhere,) * len(extra_out),
         scratch_shapes=[shape for job in jobs for shape in job.scratch] + list(extra_scratch),
         compiler_params=pltpu.CompilerParams(
             collective_id=identity, has_side_effects=True, vmem_limit_bytes=62 << 20
@@ -1419,9 +1245,9 @@
     up_cols, out_cols, qkv_low, mix_low = call(
         [
             Exchange(parts, unit_shape, 0, up_starts),
-            Exchange(run, (heads * shard, width)),
+            Exchange(run, (heads, shard, width), second="out"),
         ],
-        [up_source, out_rows.reshape(run, heads * shard, width)],
+        [up_source, out_rows.reshape(run, heads, shard, width)],
         "attend",
         1,
         line,
@@ -1429,7 +1255,6 @@
         micros=40,
     )
     up_cols = gather(up_cols.reshape(width // groups, -1), "fsdp")
-    out_cols = out_cols.reshape(run, heads, shard, width).transpose(1, 0, 2, 3)
     out_cols = out_cols.reshape(head_width, width)
 
     out_terms = dot(mix_low, out_cols).astype(LOW)
@@ -1478,15 +1303,14 @@
         ProjectBack(proj_job, activated, down_rows, out_cols, mix_low),
         micros=45,
     )
-    out_grad = out_grad.reshape(heads, run, shard, width).transpose(1, 0, 2, 3)
     down_out, out_grad, in_back_terms, qkv_grad = call(
         [
             Scatter(parts, block),
-            Exchange(run, (heads * shard, width)),
+            Exchange(run, (heads, shard, width), second="in"),
         ],
         [
             down_terms.reshape((parts,) + block),
-            out_grad.reshape(run, heads * shard, width),
+            out_grad.reshape(heads, run, shard, width),
         ],
         "attend_back",
         8,

time: 534 us -> 532 us (level)
  waiting for transfers between devices: 13.1 us -> 19.9 us
    all_gather x3, waiting for transfers between devices: 11.7 us -> 18.6 us  [gather(): return lax.all_gather(values, axes, axis=0, tiled=True)]
  transfers between devices with their start and end apart: 6 -> 6, of which waited for: 1 -> 1; matrix products, arithmetic and copies ran while one was open for 5% -> 4% of each run, Pallas kernels for 68% -> 68%
where the time goes in v11:
time: 532 us
  Pallas kernels  462 us (87%)
  other arithmetic  23.9 us (4%)
  waiting for transfers between devices  19.9 us (4%)
  between operations  14.3 us (3%)
  local copies, waits for them, and re-layouts  6.92 us (1%)
    pallas_call x8, Pallas kernels, call(): pl.pallas_call(kernel, out_shape=tuple((job.out for job in jobs)) + tuple...  462 us
    all_gather x3, waiting for transfers between devices, gather(): return lax.all_gather(values, axes, axis=0, tiled=True)  18.6 us
  transfers between devices with their start and end apart: 6, of which 1 were waited for; matrix products, arithmetic and copies ran while one was open for 4% of the time, Pallas kernels for 68%

profile of v11, /device:TPU:9, one launch (start us, length us, event | category | flops | bytes accessed | tf_op | source)
XLA Modules:
  0.0 531.7 jit_solution(2922245099751702502)
XLA Ops:
  8.0 1.2 convert_reduce_fusion
  9.2 1.3 fusion.9
  10.5 2.2 fusion.4.refs_1_
  12.7 80.1 %start.1 = (bf16[4,8,64,768]{3,2,1,0:T(8,128)(2,1)}, bf16[8,128,2048]{2,1,0:T(8,128)(2,1)}, bf16[8,64,1024]{2,1,0:T(8,128)(2,1)}, bf16[4,64,2048]{2,1,0:T(8,128)(2,1)}) custom-call(bf16[64,6144]{1,0:T(8,128)(2,1)} %refs_0_.2, bf16[128,2048]{1,0:T(8,128)(2,1)} %fusion.4.refs_1_, bf16[64,16384]{1,0:T(8,128)(2,1)} %refs_0_.3, bf16[64,2048]{1,0:T(8,128)(2,1)} %refs_3_.1), custom_call_target="tpu_custom_call" | custom-call | bytes 270000000 | tf_op jit(solution)/shard_map/start/pallas_call | solution.py:694
  93.5 2.9 sine_multiply_fusion
  97.0 1.0 broadcast_in_dim.80.refs_7_
  99.0 29.4 %attend.1 = (bf16[8,64,1024]{2,1,0:T(8,128)(2,1)}, bf16[2,2,64,2048]{3,2,1,0:T(8,128)(2,1)}, bf16[1024,768]{1,0:T(8,128)(2,1)}, bf16[1024,256]{1,0:T(8,128)(2,1)}) custom-call(bf16[64,16384]{1,0:T(8,128)(2,1)} %refs_0_.3, bf16[2,2,64,2048]{3,2,1,0:T(8,128)(2,1)} %bitcast.37, bf16[1024,2048]{1,0:T(8,128)(2,1)} %bitcast.23, bf16[2048,768]{1,0:T(8,128)(2,1)} %bitcast.27, ...), custom_call_target="tpu_custom_call" | custom-call | bytes 120000000 | tf_op jit(solution)/shard_map/attend/pallas_call | solution.py:694
  128.5 4.7 convolution_convert_fusion
  133.2 53.9 %out.1 = (f32[128,2048]{1,0:T(8,128)}, bf16[8,128,2048]{2,1,0:T(8,128)(2,1)}) custom-call(bf16[8,128,2048]{2,1,0:T(8,128)(2,1)} %bitcast.22, bf16[128,2048]{1,0:T(8,128)(2,1)} %refs_1_.1), custom_call_target="tpu_custom_call" | custom-call | bytes 192000000 | tf_op jit(solution)/shard_map/out/pallas_call | solution.py:694
  187.1 1.4 fusion.25
  189.8 18.6 %all-gather.6.cloned.1.call-done.refs_3_ = bf16[2048,1024]{1,0:T(8,128)(2,1)} async-done(((bf16[512,1024]{1,0:T(8,128)(2,1)}), bf16[2048,1024]{1,0:T(8,128)(2,1)}) %all-gather.6.cloned.1.call-update) | async-done | bytes 4194320 | tf_op jit(solution)/shard_map/all_gather | solution.py:83
  208.3 44.3 %mid.1 = (bf16[8,128,2048]{2,1,0:T(8,128)(2,1)}, bf16[1024,1024]{1,0:T(8,128)(2,1)}, bf16[1024,2048]{1,0:T(8,128)(2,1)}, bf16[1024,2048]{1,0:T(8,128)(2,1)}) custom-call(bf16[128,2048]{1,0:T(8,128)(2,1)} %fusion.10.refs_0_, bf16[1024,2048]{1,0:T(8,128)(2,1)} %bitcast.25, bf16[2048,1024]{1,0:T(8,128)(2,1)} %all-gather.4.cloned.1.call-done.refs_2_, ...), custom_call_target="tpu_custom_call" | custom-call | bytes 180000000 | tf_op jit(solution)/shard_map/mid/pallas_call | solution.py:694
  252.7 58.1 %mid_back.1 = (f32[128,2048]{1,0:T(8,128)}, bf16[2048,2048]{1,0:T(8,128)(2,1)}, bf16[1024,2048]{1,0:T(8,128)(2,1)}) custom-call(bf16[8,128,2048]{2,1,0:T(8,128)(2,1)} %bitcast.32, bf16[1024,2048]{1,0:T(8,128)(2,1)} %bitcast.31, bf16[1024,2048]{1,0:T(8,128)(2,1)} %get-tuple-element.49.refs_2_, bf16[1024,1024]{1,0:T(8,128)(2,1)} %get-tuple-element.50.refs_3_.refs_1_, ...), custom_call_target="tpu_custom_call" | custom-call | bytes 150000000 | tf_op jit(solution)/shard_map/mid_back/pallas_call | solution.py:694
  312.3 2.7 fusion.24
  315.0 40.1 %proj_back.1 = (bf16[8,128,2048]{2,1,0:T(8,128)(2,1)}, bf16[1024,2048]{1,0:T(8,128)(2,1)}, bf16[1024,256]{1,0:T(8,128)(2,1)}, bf16[256,2048]{1,0:T(8,128)(2,1)}) custom-call(bf16[128,2048]{1,0:T(8,128)(2,1)} %get-tuple-element.74.refs_0_, bf16[1024,1024]{1,0:T(8,128)(2,1)} %get-tuple-element.50.refs_3_.refs_1_, ...), custom_call_target="tpu_custom_call" | custom-call | bytes 135000000 | tf_op jit(solution)/shard_map/proj_back/pallas_call | solution.py:694
  355.1 60.5 %attend_back.1 = (f32[128,2048]{1,0:T(8,128)}, bf16[2,2,64,2048]{3,2,1,0:T(8,128)(2,1)}, bf16[1024,2048]{1,0:T(8,128)(2,1)}, bf16[2048,768]{1,0:T(8,128)(2,1)}) custom-call(bf16[8,128,2048]{2,1,0:T(8,128)(2,1)} %bitcast.30, bf16[2,2,64,2048]{3,2,1,0:T(8,128)(2,1)} %bitcast.38, bf16[1024,256]{1,0:T(8,128)(2,1)} %get-tuple-element.54.refs_2_, ...), custom_call_target="tpu_custom_call" | custom-call | bytes 180000000 | tf_op jit(solution)/shard_map/attend_back/pallas_call | solution.py:694
  415.7 2.2 add_convert_fusion
  417.9 95.4 %in_back.1 = (f32[128,2048]{1,0:T(8,128)}, f32[64,6144]{1,0:T(8,128)}, f32[64,16384]{1,0:T(8,128)}) custom-call(bf16[8,128,2048]{2,1,0:T(8,128)(2,1)} %bitcast.29, bf16[4,8,64,768]{3,2,1,0:T(8,128)(2,1)} %bitcast.35, bf16[8,64,2048]{2,1,0:T(8,128)(2,1)} %bitcast.36), custom_call_target="tpu_custom_call" | custom-call | bytes 270000000 | tf_op jit(solution)/shard_map/in_back/pallas_call | solution.py:694
  513.3 1.7 fusion.22
  515.0 1.9 convert_element_type.46
  516.9 2.8 convert_element_type.47
  519.7 1.4 fusion.8
  521.1 1.1 copy.16
  522.8 2.0 copy.17
  (55 shorter events, 6.6 us)
Async XLA Ops:
  7.2 85.7 %copy-start.7 = (s32[1,2]{1,0:T(1,128)S(1)}, s32[1,2]{1,0:T(1,128)}, u32[]{:S(2)}) copy-start(s32[1,2]{1,0:T(1,128)} %param.13) | copy-start | bytes 28
  7.2 85.9 %copy-start.6 = (s32[1,8]{1,0:T(1,128)S(1)}, s32[1,8]{1,0:T(1,128)}, u32[]{:S(2)}) copy-start(s32[1,8]{1,0:T(1,128)} %param.14) | copy-start | bytes 100
  7.2 182.6 %all-gather.8.cloned.1.call-start = ((), (), s32[]{:S(2)}) async-start(), calls=%async_computation.5 | async-start | bytes 5242880 | tf_op jit(solution)/shard_map/all_gather | solution.py:83
  7.9 181.9 %all-gather.4.cloned.1.call-start = ((), (), s32[]{:S(2)}) async-start(), calls=%async_computation.3 | async-start | bytes 5242880 | tf_op jit(solution)/shard_map/all_gather | solution.py:83
  92.8 115.6 %all-gather.6.cloned.1.call-start = ((), (), s32[]{:S(2)}) async-start(), calls=%async_computation.4 | async-start | bytes 5242880 | tf_op jit(solution)/shard_map/all_gather | solution.py:83
  128.5 287.2 %reduce-scatter.4.cloned.1.call-start = ((), (), s32[]{:S(2)}) async-start(), calls=%async_computation.6 | async-start | bytes 10485760 | tf_op jit(solution)/shard_map/reduce_scatter | solution.py:87
  133.2 53.9 %copy-start = (bf16[128,2048]{1,0:T(8,128)(2,1)S(1)}, bf16[128,2048]{1,0:T(8,128)(2,1)}, u32[]{:S(2)}) copy-start(bf16[128,2048]{1,0:T(8,128)(2,1)} %param.8) | copy-start | bytes 1572868
  310.8 1.2 copy-start.4
  310.8 202.5 %reduce-scatter.6.cloned.1.call-start = ((), (), s32[]{:S(2)}) async-start(), calls=%async_computation.7 | async-start | bytes 5242880 | tf_op jit(solution)/shard_map/reduce_scatter | solution.py:87
  311.4 201.9 %reduce-scatter.8.cloned.1.call-start = ((), (), s32[]{:S(2)}) async-start(), calls=%async_computation.8 | async-start | bytes 1310720 | tf_op jit(solution)/shard_map/reduce_scatter | solution.py:87
  513.3 6.5 %copy-start.1 = (f32[128,2048]{1,0:T(8,128)S(1)}, f32[128,2048]{1,0:T(8,128)}, u32[]{:S(2)}) copy-start(f32[128,2048]{1,0:T(8,128)} %get-tuple-element.65) | copy-start | bytes 3145732
  513.3 6.5 %copy-start.3 = (f32[128,2048]{1,0:T(8,128)S(1)}, f32[128,2048]{1,0:T(8,128)}, u32[]{:S(2)}) copy-start(f32[128,2048]{1,0:T(8,128)} %get-tuple-element.75) | copy-start | bytes 3145732
  515.0 6.1 %copy-start.5 = (f32[64,6144]{1,0:T(8,128)S(1)}, f32[64,6144]{1,0:T(8,128)}, u32[]{:S(2)}) copy-start(f32[64,6144]{1,0:T(8,128)} %get-tuple-element.90) | copy-start | bytes 4718596
  519.7 3.1 copy-start.2
Sparse Core Ops, SparseCore 0:
  9.8 91.2 all-gather.7
  103.0 50.8 all-gather.3
  155.7 52.5 all-gather.5
  310.9 84.4 reduce-scatter.3
  398.2 77.8 reduce-scatter.5
  478.8 26.6 reduce-scatter.7

commit v12 on v11

--- a/solution.py
+++ b/solution.py
@@ -105,10 +105,9 @@
 
 
 class Exchange:
-    outside = ("in", "out")
-
     def __init__(self, parts, shape, delay=0, columns=None, second=""):
         self.parts, self.delay, self.columns, self.second = parts, delay, columns, second
+        self.outside = () if second else ("in", "out")
         placed = shape[:1] + (parts,) + shape[1:] if second == "out" else (parts,) + shape
         self.out = jax.ShapeDtypeStruct(placed, LOW)
         self.scratch = [
@@ -735,7 +734,7 @@
         for copy in gets:
             copy.start()
         yield
-        puts = []
+        puts = Puts(made, put)
         for which in range(n):
             first, second = self.slots[2 * which : 2 * which + 2]
             left, right, out = held[first], held[second], outs[which]
@@ -744,26 +743,22 @@
                     gets[slot].wait()
             columns = right.shape[1]
             step = min(columns, 512)
-            for at in range(0, left.shape[1], tile):
-                slot = len(puts) % 2
-                if len(puts) >= 2:
-                    puts[-2].wait()
-                turned[...] = left[:, at : at + tile].T
-
-                def one(index, carry):
-                    where = pl.ds(pl.multiple_of(index * step, step), step)
-                    made[slot, :, where] = jnp.dot(
-                        turned[...], right[:, where], preferred_element_type=jnp.float32
-                    ).astype(LOW)
-                    return carry
-
-                lax.fori_loop(0, columns // step, one, 0)
-                part = made.at[slot] if columns == made.shape[2] else made.at[slot, :, :columns]
-                puts.append(pltpu.make_async_copy(part, out.at[at : at + tile, :], put.at[slot]))
-                puts[-1].start()
+            for at in range(0, left.shape[1], 2 * tile):
+
+                def pair(half, carry):
+                    begin = pl.multiple_of(at + half * tile, tile)
+                    turned[...] = left[:, pl.ds(begin, tile)].T
+
+                    def one(index, carry):
+                        where = pl.ds(pl.multiple_of(index * step, step), step)
+                        made[half, :, where] = product(turned[...], right[:, where]).astype(LOW)
+                        return carry
+
+                    return lax.fori_loop(0, columns // step, one, carry)
+
+                puts.pair(pair, columns, out, at, tile)
                 yield
-        for copy in puts[-2:]:
-            copy.wait()
+        puts.finish()
 
 
 def softmax_block(query, keys, ok):
@@ -796,7 +791,7 @@
         n, tile, heads = len(self.operands), self.tile, self.heads
         sources, results, held = refs[:n], refs[n : n + 2], refs[n + 2 : 2 * n + 2]
         qkv, mix, get, put = refs[2 * n + 2 :]
-        rows, weight, cosine, sine, first, last, keys = held
+        rows, weight, cosine, sine, ends, keys = held
         gets = [pltpu.make_async_copy(s, h, get.at[i]) for i, (s, h) in enumerate(zip(sources, held))]
         for copy in gets:
             copy.start()
@@ -821,9 +816,11 @@
         send.start()
         yield
 
+        half = HEAD_DIM // 2
+
         def attend(index, carry):
             at = pl.ds(pl.multiple_of(index * tile, tile), tile)
-            ok = (keys[:1, :] >= first[at, :1]) & (keys[:1, :] <= last[at, :1])
+            ok = (keys[:1, :] >= ends[at, :1]) & (keys[:1, :] <= ends[at, half : half + 1])
             for head in range(heads):
                 lo = head * HEAD_DIM
                 weights, total = softmax_block(
@@ -867,7 +864,7 @@
         n, tile, heads = len(self.operands), self.tile, self.heads
         sources, results, held = refs[:n], refs[n : n + 2], refs[n + 2 : 2 * n + 2]
         grads, sums, turned, made, get, put = refs[2 * n + 2 :]
-        back, qkv, cosine, sine, first, last, keys, weight, rows = held
+        back, qkv, cosine, sine, ends, keys, weight, rows = held
         length, width = back.shape
         gets = [pltpu.make_async_copy(s, h, get.at[i]) for i, (s, h) in enumerate(zip(sources, held))]
         for copy in gets:
@@ -879,6 +876,7 @@
         def unrotated(value, at):
             return value * cosine[at, :] - pltpu.roll(value, HEAD_DIM // 2, 1) * sine[at, :]
 
+        half = HEAD_DIM // 2
         for head in range(heads):
             lo = head * HEAD_DIM
             mine = slice(lo, lo + HEAD_DIM)
@@ -888,7 +886,7 @@
 
             def attend(index, carry):
                 at = pl.ds(pl.multiple_of(index * tile, tile), tile)
-                ok = (keys[:1, :] >= first[at, :1]) & (keys[:1, :] <= last[at, :1])
+                ok = (keys[:1, :] >= ends[at, :1]) & (keys[:1, :] <= ends[at, half : half + 1])
                 weights, total = softmax_block(qkv[at, mine], qkv[:, key], ok)
                 probs = weights / total
                 upper = back[at, mine]
@@ -1053,11 +1051,11 @@
 
 
 class FeedForward:
-    def __init__(self, job, upstream, gate, up, down):
+    def __init__(self, job, act_grad, gate, up):
         self.job = job
-        self.operands = [upstream, gate, up, down]
-        length, width = upstream.shape
-        units = gate.shape[1]
+        self.operands = [act_grad, gate, up]
+        length = act_grad.shape[0]
+        width, units = gate.shape
         self.outs = [
             jax.ShapeDtypeStruct((length, units), LOW),
             jax.ShapeDtypeStruct((length, 2 * units), LOW),
@@ -1066,18 +1064,18 @@
         self.tile = length // (job.parts // 2)
         self.scratch = [pltpu.VMEM(array.shape, array.dtype) for array in self.operands]
         self.scratch += [pltpu.VMEM((2, self.tile) + out.shape[1:], LOW) for out in self.outs]
-        self.scratch += [pltpu.SemaphoreType.DMA((4,)), pltpu.SemaphoreType.DMA((3, 2))]
+        self.scratch += [pltpu.SemaphoreType.DMA((3,)), pltpu.SemaphoreType.DMA((3, 2))]
 
     def run(self, *refs):
         job, tile = self.job, self.tile
-        sources, results, held, made = refs[:4], refs[4:7], refs[7:11], refs[11:14]
-        get, put = refs[14:]
-        upstream, gate_w, up_w, down = held
+        sources, results, held, made = refs[:3], refs[3:6], refs[6:9], refs[9:12]
+        get, put = refs[12:]
+        act_grads, gate_w, up_w = held
         acts, backs, terms = made
         width, units = gate_w.shape
         step = min(units, 256)
         span = min(width, 512)
-        gets = [pltpu.make_async_copy(sources[i], held[i], get.at[i]) for i in (1, 2, 3, 0)]
+        gets = [pltpu.make_async_copy(sources[i], held[i], get.at[i]) for i in (1, 2, 0)]
         for copy in gets:
             copy.start()
         yield
@@ -1115,7 +1113,7 @@
                 value = normed[...].reshape(tile, width)
                 gate = product(value, gate_w[:, left])
                 up = product(value, up_w[:, left])
-                act_grad = times_transposed(upstream[at, :], down[left, :])
+                act_grad = act_grads[at, left]
                 sigmoid = jax.nn.sigmoid(gate)
                 silu = gate * sigmoid
                 acts[slot, :, left] = (silu * up).astype(LOW)
@@ -1238,8 +1236,7 @@
     tables = (
         cosine_table[:, 0, :],
         sine_table[:, 0, :] * half_sign,
-        jnp.broadcast_to((packed - pos)[:, None], (length, HEAD_DIM)),
-        jnp.broadcast_to(packed[:, None], (length, HEAD_DIM)),
+        packed[:, None] - jnp.where(jnp.arange(HEAD_DIM) < HEAD_DIM // 2, pos[:, None], 0),
         jnp.broadcast_to(packed[None, :], (8, length)),
     )
     up_cols, out_cols, qkv_low, mix_low = call(
@@ -1269,6 +1266,7 @@
     cot_full = cot_full.reshape(length, width)
     residual = inputs + attn_out
     normed_mid, root_mid = normalize(residual)
+    act_grad = times_transposed(cot_full, down_rows)
     mid_job = Gather(parts, block, watched=True)
     normed_mid_full, activated, gate_up_back, mid_back_terms = call(
         [mid_job],
@@ -1276,7 +1274,7 @@
         "mid",
         4,
         line,
-        FeedForward(mid_job, cot_full, gate_cols, up_cols, down_rows),
+        FeedForward(mid_job, act_grad, gate_cols, up_cols),
         micros=60,
     )
     normed_mid_full = normed_mid_full.reshape(length, width)

time: 532 us -> 519 us (0.976)
  Pallas kernels: 462 us -> 447 us
  matrix products: 4.66 us -> 14.7 us
  waiting for transfers between devices: 19.9 us -> 11.9 us
    pallas_call x8, Pallas kernels: 462 us -> 447 us  [call(): pl.pallas_call(kernel, out_shape=tuple((job.out for job in jobs)) + tuple...]
    dot_general x0 -> x1, matrix products: none -> 10 us  [times_transposed(): lax.dot_general(left, right, (((1,), (1,)), ((), ())), preferred_element_...]
    all_gather x3, waiting for transfers between devices: 18.6 us -> 10.5 us  [gather(): return lax.all_gather(values, axes, axis=0, tiled=True)]
  transfers between devices with their start and end apart: 6 -> 6, of which waited for: 1 -> 1; matrix products, arithmetic and copies ran while one was open for 4% -> 6% of each run, Pallas kernels for 68% -> 69%
where the time goes in v12:
time: 519 us; the launch traced here: 518 us
  Pallas kernels  447 us (86%)
  other arithmetic  25 us (5%)
  matrix products  14.7 us (3%)
  between operations  14.3 us (3%)
  waiting for transfers between devices  11.9 us (2%)
    pallas_call x8, Pallas kernels, call(): pl.pallas_call(kernel, out_shape=tuple((job.out for job in jobs)) + tuple...  447 us
    all_gather x3, waiting for transfers between devices, gather(): return lax.all_gather(values, axes, axis=0, tiled=True)  10.5 us
  transfers between devices with their start and end apart: 6, of which 1 were waited for; matrix products, arithmetic and copies ran while one was open for 6% of the time, Pallas kernels for 69%

profile of v12, /device:TPU:9, one launch (start us, length us, event | category | flops | bytes accessed | tf_op | source)
XLA Modules:
  0.0 518.1 jit_solution(10652418042975357822)
XLA Ops:
  8.0 1.2 convert_reduce_fusion
  9.2 1.3 fusion.9
  10.5 2.2 fusion.4.refs_1_
  12.7 80.1 %start.1 = (bf16[4,8,64,768]{3,2,1,0:T(8,128)(2,1)}, bf16[8,128,2048]{2,1,0:T(8,128)(2,1)}, bf16[8,64,1024]{2,1,0:T(8,128)(2,1)}, bf16[4,64,2048]{2,1,0:T(8,128)(2,1)}) custom-call(bf16[64,6144]{1,0:T(8,128)(2,1)} %refs_0_.2, bf16[128,2048]{1,0:T(8,128)(2,1)} %fusion.4.refs_1_, bf16[64,16384]{1,0:T(8,128)(2,1)} %refs_0_.3, bf16[64,2048]{1,0:T(8,128)(2,1)} %refs_3_.1), custom_call_target="tpu_custom_call" | custom-call | bytes 270000000 | tf_op jit(solution)/shard_map/start/pallas_call | solution.py:693
  94.7 2.9 sine_multiply_fusion
  98.1 28.5 %attend.1 = (bf16[8,64,1024]{2,1,0:T(8,128)(2,1)}, bf16[2,2,64,2048]{3,2,1,0:T(8,128)(2,1)}, bf16[1024,768]{1,0:T(8,128)(2,1)}, bf16[1024,256]{1,0:T(8,128)(2,1)}) custom-call(bf16[64,16384]{1,0:T(8,128)(2,1)} %refs_0_.3, bf16[2,2,64,2048]{3,2,1,0:T(8,128)(2,1)} %bitcast.39, bf16[1024,2048]{1,0:T(8,128)(2,1)} %bitcast.25, bf16[2048,768]{1,0:T(8,128)(2,1)} %bitcast.27, ...), custom_call_target="tpu_custom_call" | custom-call | bytes 120000000 | tf_op jit(solution)/shard_map/attend/pallas_call | solution.py:693
  126.7 4.7 convolution_convert_fusion
  131.4 53.7 %out.1 = (f32[128,2048]{1,0:T(8,128)}, bf16[8,128,2048]{2,1,0:T(8,128)(2,1)}) custom-call(bf16[8,128,2048]{2,1,0:T(8,128)(2,1)} %bitcast.24, bf16[128,2048]{1,0:T(8,128)(2,1)} %refs_1_.1), custom_call_target="tpu_custom_call" | custom-call | bytes 192000000 | tf_op jit(solution)/shard_map/out/pallas_call | solution.py:693
  185.1 1.4 fusion.26
  187.8 10.0 %fusion.29.refs_1_ = f32[1024,1024]{1,0:T(8,128)} fusion(bf16[1024,2048]{1,0:T(8,128)(2,1)} %bitcast.30, bf16[1024,2048]{1,0:T(8,128)(2,1)} %all-gather.4.cloned.1.call-done.refs_2_), kind=kOutput, calls=%fused_computation.60 | convolution fusion | flops 4294967296 | bytes 12582912 | tf_op jit(solution)/shard_map/dot_general | solution.py:71
  197.8 10.5 %all-gather.8.cloned.1.call-done.refs_3_ = bf16[2048,1024]{1,0:T(8,128)(2,1)} async-done(((bf16[512,1024]{1,0:T(8,128)(2,1)}), bf16[2048,1024]{1,0:T(8,128)(2,1)}) %all-gather.8.cloned.1.call-update) | async-done | bytes 4194320 | tf_op jit(solution)/shard_map/all_gather | solution.py:83
  208.3 40.9 %mid.1 = (bf16[8,128,2048]{2,1,0:T(8,128)(2,1)}, bf16[1024,1024]{1,0:T(8,128)(2,1)}, bf16[1024,2048]{1,0:T(8,128)(2,1)}, bf16[1024,2048]{1,0:T(8,128)(2,1)}) custom-call(bf16[128,2048]{1,0:T(8,128)(2,1)} %fusion.10.refs_0_, f32[1024,1024]{1,0:T(8,128)} %fusion.29.refs_1_, bf16[2048,1024]{1,0:T(8,128)(2,1)} %all-gather.6.cloned.1.call-done.refs_2_, ...), custom_call_target="tpu_custom_call" | custom-call | bytes 180000000 | tf_op jit(solution)/shard_map/mid/pallas_call | solution.py:693
  249.2 50.6 %mid_back.1 = (f32[128,2048]{1,0:T(8,128)}, bf16[2048,2048]{1,0:T(8,128)(2,1)}, bf16[1024,2048]{1,0:T(8,128)(2,1)}) custom-call(bf16[8,128,2048]{2,1,0:T(8,128)(2,1)} %bitcast.34, bf16[1024,2048]{1,0:T(8,128)(2,1)} %bitcast.33, bf16[1024,2048]{1,0:T(8,128)(2,1)} %get-tuple-element.49.refs_2_, bf16[1024,1024]{1,0:T(8,128)(2,1)} %get-tuple-element.50.refs_3_.refs_1_, ...), custom_call_target="tpu_custom_call" | custom-call | bytes 150000000 | tf_op jit(solution)/shard_map/mid_back/pallas_call | solution.py:693
  301.4 2.7 fusion.25
  304.1 41.5 %proj_back.1 = (bf16[8,128,2048]{2,1,0:T(8,128)(2,1)}, bf16[1024,2048]{1,0:T(8,128)(2,1)}, bf16[1024,256]{1,0:T(8,128)(2,1)}, bf16[256,2048]{1,0:T(8,128)(2,1)}) custom-call(bf16[128,2048]{1,0:T(8,128)(2,1)} %get-tuple-element.74.refs_0_, bf16[1024,1024]{1,0:T(8,128)(2,1)} %get-tuple-element.50.refs_3_.refs_1_, ...), custom_call_target="tpu_custom_call" | custom-call | bytes 135000000 | tf_op jit(solution)/shard_map/proj_back/pallas_call | solution.py:693
  345.5 55.5 %attend_back.1 = (f32[128,2048]{1,0:T(8,128)}, bf16[2,2,64,2048]{3,2,1,0:T(8,128)(2,1)}, bf16[1024,2048]{1,0:T(8,128)(2,1)}, bf16[2048,768]{1,0:T(8,128)(2,1)}) custom-call(bf16[8,128,2048]{2,1,0:T(8,128)(2,1)} %bitcast.32, bf16[2,2,64,2048]{3,2,1,0:T(8,128)(2,1)} %bitcast.40, bf16[1024,256]{1,0:T(8,128)(2,1)} %get-tuple-element.54.refs_2_, ...), custom_call_target="tpu_custom_call" | custom-call | bytes 180000000 | tf_op jit(solution)/shard_map/attend_back/pallas_call | solution.py:693
  401.1 2.2 add_convert_fusion
  403.4 96.3 %in_back.1 = (f32[128,2048]{1,0:T(8,128)}, f32[64,6144]{1,0:T(8,128)}, f32[64,16384]{1,0:T(8,128)}) custom-call(bf16[8,128,2048]{2,1,0:T(8,128)(2,1)} %bitcast.29, bf16[4,8,64,768]{3,2,1,0:T(8,128)(2,1)} %bitcast.37, bf16[8,64,2048]{2,1,0:T(8,128)(2,1)} %bitcast.38), custom_call_target="tpu_custom_call" | custom-call | bytes 270000000 | tf_op jit(solution)/shard_map/in_back/pallas_call | solution.py:693
  499.7 1.7 fusion.23
  501.4 1.9 convert_element_type.46
  503.3 2.8 convert_element_type.47
  506.1 1.4 fusion.8
  507.5 1.1 copy.16
  509.2 2.0 copy.17
  (56 shorter events, 6.7 us)
Async XLA Ops:
  7.2 85.7 %copy-start.7 = (s32[1,2]{1,0:T(1,128)S(1)}, s32[1,2]{1,0:T(1,128)}, u32[]{:S(2)}) copy-start(s32[1,2]{1,0:T(1,128)} %param.13) | copy-start | bytes 28
  7.2 85.9 %copy-start.6 = (s32[1,8]{1,0:T(1,128)S(1)}, s32[1,8]{1,0:T(1,128)}, u32[]{:S(2)}) copy-start(s32[1,8]{1,0:T(1,128)} %param.14) | copy-start | bytes 100
  7.2 180.6 %all-gather.4.cloned.1.call-start = ((), (), s32[]{:S(2)}) async-start(), calls=%async_computation.3 | async-start | bytes 5242880 | tf_op jit(solution)/shard_map/all_gather | solution.py:83
  7.9 189.9 %all-gather.6.cloned.1.call-start = ((), (), s32[]{:S(2)}) async-start(), calls=%async_computation.4 | async-start | bytes 5242880 | tf_op jit(solution)/shard_map/all_gather | solution.py:83
  92.8 115.6 %all-gather.8.cloned.1.call-start = ((), (), s32[]{:S(2)}) async-start(), calls=%async_computation.5 | async-start | bytes 5242880 | tf_op jit(solution)/shard_map/all_gather | solution.py:83
  126.7 274.4 %reduce-scatter.4.cloned.1.call-start = ((), (), s32[]{:S(2)}) async-start(), calls=%async_computation.6 | async-start | bytes 10485760 | tf_op jit(solution)/shard_map/reduce_scatter | solution.py:87
  131.4 53.7 %copy-start = (bf16[128,2048]{1,0:T(8,128)(2,1)S(1)}, bf16[128,2048]{1,0:T(8,128)(2,1)}, u32[]{:S(2)}) copy-start(bf16[128,2048]{1,0:T(8,128)(2,1)} %param.8) | copy-start | bytes 1572868
  299.9 1.2 copy-start.4
  299.9 199.8 %reduce-scatter.6.cloned.1.call-start = ((), (), s32[]{:S(2)}) async-start(), calls=%async_computation.7 | async-start | bytes 5242880 | tf_op jit(solution)/shard_map/reduce_scatter | solution.py:87
  300.5 199.3 %reduce-scatter.8.cloned.1.call-start = ((), (), s32[]{:S(2)}) async-start(), calls=%async_computation.8 | async-start | bytes 1310720 | tf_op jit(solution)/shard_map/reduce_scatter | solution.py:87
  499.6 6.5 %copy-start.1 = (f32[128,2048]{1,0:T(8,128)S(1)}, f32[128,2048]{1,0:T(8,128)}, u32[]{:S(2)}) copy-start(f32[128,2048]{1,0:T(8,128)} %get-tuple-element.65) | copy-start | bytes 3145732
  499.7 6.5 %copy-start.3 = (f32[128,2048]{1,0:T(8,128)S(1)}, f32[128,2048]{1,0:T(8,128)}, u32[]{:S(2)}) copy-start(f32[128,2048]{1,0:T(8,128)} %get-tuple-element.75) | copy-start | bytes 3145732
  501.4 6.1 %copy-start.5 = (f32[64,6144]{1,0:T(8,128)S(1)}, f32[64,6144]{1,0:T(8,128)}, u32[]{:S(2)}) copy-start(f32[64,6144]{1,0:T(8,128)} %get-tuple-element.92) | copy-start | bytes 4718596
  506.1 3.1 copy-start.2
Sparse Core Ops, SparseCore 0:
  9.8 91.2 all-gather.3
  103.0 50.8 all-gather.5
  155.7 52.5 all-gather.7
  300.0 85.7 reduce-scatter.3
  388.6 77.9 reduce-scatter.5
  469.3 27.6 reduce-scatter.7

commit v13 on v12

--- a/solution.py
+++ b/solution.py
@@ -506,6 +506,42 @@
             copy.wait()
             if at % 6 == 5:
                 yield
+        for copy in copies:
+            copy.wait_send()
+
+
+class Sum:
+    outside = ()
+
+    def __init__(self, groups, shape):
+        self.groups = groups
+        self.out = jax.ShapeDtypeStruct(shape, jnp.float32)
+        self.scratch = [
+            pltpu.VMEM((groups - 1,) + shape, LOW),
+            pltpu.SemaphoreType.DMA((groups - 1,)),
+            pltpu.SemaphoreType.DMA((groups - 1,)),
+        ]
+
+    def run(self, src, out, far, send, recv):
+        groups = self.groups
+        group = lax.axis_index("fsdp")
+        copies = []
+        for hop in range(1, groups):
+            peer = lax.rem(group + hop, groups)
+            copies.append(
+                remote(
+                    src.at[peer], far.at[hop - 1], send.at[hop - 1], recv.at[hop - 1], "fsdp", peer
+                )
+            )
+            copies[-1].start()
+        for _ in range(8):
+            yield
+        for copy in copies:
+            copy.wait_recv()
+        value = src[group].astype(jnp.float32)
+        for hop in range(groups - 1):
+            value += far[hop].astype(jnp.float32)
+        out[...] = value
         for copy in copies:
             copy.wait_send()
 
@@ -1317,31 +1353,31 @@
         micros=60,
     )
     layer_out = (residual + down_out).astype(LOW)
-    out_grad, gate_up_grad = lax.optimization_barrier((out_grad, gate_up_grad))
-    out_grad = scatter(out_grad.reshape(groups * shard, width), "fsdp")
-    in_back, qkv_grad, gate_up_grad = call(
+    in_back, qkv_grad, gate_up_grad, out_grad = call(
         [
             Scatter(parts, block),
             Collect(parts, groups, qkv_shape, plan.qkv_starts),
             plan.unit_job(both_shape),
+            Sum(groups, w_out.shape),
         ],
         [
             in_back_terms.reshape((parts,) + block),
             qkv_grad.reshape((groups, parts) + qkv_shape),
             gate_up_grad.reshape((parts,) + both_shape),
+            out_grad.reshape((groups,) + w_out.shape),
         ],
         "in_back",
         7,
         plane,
         micros=90,
     )
-    in_back, down_grad, out_grad = lax.optimization_barrier((in_back, down_grad, out_grad))
+    in_back, down_grad = lax.optimization_barrier((in_back, down_grad))
     tokens_grad = residual_back + norm_back(in_back, normed_in, root_in)
     return (
         layer_out,
         tokens_grad,
         qkv_grad,
-        out_grad.astype(jnp.float32),
+        out_grad,
         plan.unit_rows(gate_up_grad),
         down_grad.astype(jnp.float32),
     )

time: 519 us -> 517 us (level)
  transfers between devices with their start and end apart: 6 -> 5, of which waited for: 1 -> 1; matrix products, arithmetic and copies ran while one was open for 6% -> 6% of each run, Pallas kernels for 69% -> 69%
where the time goes in v13:
time: 517 us; the launch traced here: 516 us
  Pallas kernels  447 us (86%)
  other arithmetic  23.1 us (4%)
  matrix products  14.7 us (3%)
  between operations  14 us (3%)
  waiting for transfers between devices  11.8 us (2%)
  local copies, waits for them, and re-layouts  5.21 us (1%)
    pallas_call x8, Pallas kernels, call(): pl.pallas_call(kernel, out_shape=tuple((job.out for job in jobs)) + tuple...  447 us
    all_gather x3, waiting for transfers between devices, gather(): return lax.all_gather(values, axes, axis=0, tiled=True)  10.5 us
  transfers between devices with their start and end apart: 5, of which 1 were waited for; matrix products, arithmetic and copies ran while one was open for 6% of the time, Pallas kernels for 69%

profile of v13, /device:TPU:9, one launch (start us, length us, event | category | flops | bytes accessed | tf_op | source)
XLA Modules:
  0.0 516.1 jit_solution(2488697950216054507)
XLA Ops:
  8.0 1.2 convert_reduce_fusion
  9.2 1.3 fusion.9
  10.5 2.2 fusion.4.refs_1_
  12.7 80.1 %start.1 = (bf16[4,8,64,768]{3,2,1,0:T(8,128)(2,1)}, bf16[8,128,2048]{2,1,0:T(8,128)(2,1)}, bf16[8,64,1024]{2,1,0:T(8,128)(2,1)}, bf16[4,64,2048]{2,1,0:T(8,128)(2,1)}) custom-call(bf16[64,6144]{1,0:T(8,128)(2,1)} %refs_0_.2, bf16[128,2048]{1,0:T(8,128)(2,1)} %fusion.4.refs_1_, bf16[64,16384]{1,0:T(8,128)(2,1)} %refs_0_.3, bf16[64,2048]{1,0:T(8,128)(2,1)} %refs_3_.1), custom_call_target="tpu_custom_call" | custom-call | bytes 270000000 | tf_op jit(solution)/shard_map/start/pallas_call | solution.py:729
  93.5 1.1 select_subtract_fusion.refs_6_
  94.7 2.9 sine_multiply_fusion
  98.1 28.5 %attend.1 = (bf16[8,64,1024]{2,1,0:T(8,128)(2,1)}, bf16[2,2,64,2048]{3,2,1,0:T(8,128)(2,1)}, bf16[1024,768]{1,0:T(8,128)(2,1)}, bf16[1024,256]{1,0:T(8,128)(2,1)}) custom-call(bf16[64,16384]{1,0:T(8,128)(2,1)} %refs_0_.3, bf16[2,2,64,2048]{3,2,1,0:T(8,128)(2,1)} %bitcast.39, bf16[1024,2048]{1,0:T(8,128)(2,1)} %bitcast.25, bf16[2048,768]{1,0:T(8,128)(2,1)} %bitcast.27, ...), custom_call_target="tpu_custom_call" | custom-call | bytes 120000000 | tf_op jit(solution)/shard_map/attend/pallas_call | solution.py:729
  126.7 4.7 convolution_convert_fusion
  131.4 53.7 %out.1 = (f32[128,2048]{1,0:T(8,128)}, bf16[8,128,2048]{2,1,0:T(8,128)(2,1)}) custom-call(bf16[8,128,2048]{2,1,0:T(8,128)(2,1)} %bitcast.24, bf16[128,2048]{1,0:T(8,128)(2,1)} %refs_1_.1), custom_call_target="tpu_custom_call" | custom-call | bytes 192000000 | tf_op jit(solution)/shard_map/out/pallas_call | solution.py:729
  185.1 1.4 fusion.26
  187.8 10.0 %fusion.29.refs_1_ = f32[1024,1024]{1,0:T(8,128)} fusion(bf16[1024,2048]{1,0:T(8,128)(2,1)} %bitcast.30, bf16[1024,2048]{1,0:T(8,128)(2,1)} %all-gather.4.cloned.1.call-done.refs_2_), kind=kOutput, calls=%fused_computation.60 | convolution fusion | flops 4294967296 | bytes 12582912 | tf_op jit(solution)/shard_map/dot_general | solution.py:71
  197.8 10.5 %all-gather.8.cloned.1.call-done.refs_3_ = bf16[2048,1024]{1,0:T(8,128)(2,1)} async-done(((bf16[512,1024]{1,0:T(8,128)(2,1)}), bf16[2048,1024]{1,0:T(8,128)(2,1)}) %all-gather.8.cloned.1.call-update) | async-done | bytes 4194320 | tf_op jit(solution)/shard_map/all_gather | solution.py:83
  208.3 40.9 %mid.1 = (bf16[8,128,2048]{2,1,0:T(8,128)(2,1)}, bf16[1024,1024]{1,0:T(8,128)(2,1)}, bf16[1024,2048]{1,0:T(8,128)(2,1)}, bf16[1024,2048]{1,0:T(8,128)(2,1)}) custom-call(bf16[128,2048]{1,0:T(8,128)(2,1)} %fusion.10.refs_0_, f32[1024,1024]{1,0:T(8,128)} %fusion.29.refs_1_, bf16[2048,1024]{1,0:T(8,128)(2,1)} %all-gather.6.cloned.1.call-done.refs_2_, ...), custom_call_target="tpu_custom_call" | custom-call | bytes 180000000 | tf_op jit(solution)/shard_map/mid/pallas_call | solution.py:729
  249.2 50.6 %mid_back.1 = (f32[128,2048]{1,0:T(8,128)}, bf16[2048,2048]{1,0:T(8,128)(2,1)}, bf16[1024,2048]{1,0:T(8,128)(2,1)}) custom-call(bf16[8,128,2048]{2,1,0:T(8,128)(2,1)} %bitcast.34, bf16[1024,2048]{1,0:T(8,128)(2,1)} %bitcast.33, bf16[1024,2048]{1,0:T(8,128)(2,1)} %get-tuple-element.47.refs_2_, bf16[1024,1024]{1,0:T(8,128)(2,1)} %get-tuple-element.48.refs_3_.refs_1_, ...), custom_call_target="tpu_custom_call" | custom-call | bytes 150000000 | tf_op jit(solution)/shard_map/mid_back/pallas_call | solution.py:729
  301.4 2.7 fusion.25
  304.1 41.5 %proj_back.1 = (bf16[8,128,2048]{2,1,0:T(8,128)(2,1)}, bf16[1024,2048]{1,0:T(8,128)(2,1)}, bf16[1024,256]{1,0:T(8,128)(2,1)}, bf16[256,2048]{1,0:T(8,128)(2,1)}) custom-call(bf16[128,2048]{1,0:T(8,128)(2,1)} %get-tuple-element.70.refs_0_, bf16[1024,1024]{1,0:T(8,128)(2,1)} %get-tuple-element.48.refs_3_.refs_1_, ...), custom_call_target="tpu_custom_call" | custom-call | bytes 135000000 | tf_op jit(solution)/shard_map/proj_back/pallas_call | solution.py:729
  345.5 55.5 %attend_back.1 = (f32[128,2048]{1,0:T(8,128)}, bf16[2,2,64,2048]{3,2,1,0:T(8,128)(2,1)}, bf16[1024,2048]{1,0:T(8,128)(2,1)}, bf16[2048,768]{1,0:T(8,128)(2,1)}) custom-call(bf16[8,128,2048]{2,1,0:T(8,128)(2,1)} %bitcast.32, bf16[2,2,64,2048]{3,2,1,0:T(8,128)(2,1)} %bitcast.41, bf16[1024,256]{1,0:T(8,128)(2,1)} %get-tuple-element.52.refs_2_, ...), custom_call_target="tpu_custom_call" | custom-call | bytes 180000000 | tf_op jit(solution)/shard_map/attend_back/pallas_call | solution.py:729
  401.1 2.3 add_convert_fusion
  403.3 96.3 %in_back.1 = (f32[128,2048]{1,0:T(8,128)}, f32[64,6144]{1,0:T(8,128)}, f32[64,16384]{1,0:T(8,128)}, f32[64,2048]{1,0:T(8,128)}) custom-call(bf16[8,128,2048]{2,1,0:T(8,128)(2,1)} %bitcast.29, bf16[4,8,64,768]{3,2,1,0:T(8,128)(2,1)} %bitcast.37, bf16[8,64,2048]{2,1,0:T(8,128)(2,1)} %bitcast.38, bf16[4,64,2048]{2,1,0:T(8,128)(2,1)} %bitcast.40), custom_call_target="tpu_custom_call" | custom-call | bytes 270000000 | tf_op jit(solution)/shard_map/in_back/pallas_call | solution.py:729
  499.7 1.7 fusion.23
  501.4 2.8 convert_element_type.43
  504.2 1.4 fusion.8
  505.6 1.1 copy.17
  507.5 2.0 copy.19
  (55 shorter events, 5.8 us)
Async XLA Ops:
  7.2 85.7 %copy-start.8 = (s32[1,2]{1,0:T(1,128)S(1)}, s32[1,2]{1,0:T(1,128)}, u32[]{:S(2)}) copy-start(s32[1,2]{1,0:T(1,128)} %param.13) | copy-start | bytes 28
  7.2 85.9 %copy-start.7 = (s32[1,8]{1,0:T(1,128)S(1)}, s32[1,8]{1,0:T(1,128)}, u32[]{:S(2)}) copy-start(s32[1,8]{1,0:T(1,128)} %param.14) | copy-start | bytes 100
  7.2 180.6 %all-gather.4.cloned.1.call-start = ((), (), s32[]{:S(2)}) async-start(), calls=%async_computation.2 | async-start | bytes 5242880 | tf_op jit(solution)/shard_map/all_gather | solution.py:83
  7.9 189.9 %all-gather.6.cloned.1.call-start = ((), (), s32[]{:S(2)}) async-start(), calls=%async_computation.3 | async-start | bytes 5242880 | tf_op jit(solution)/shard_map/all_gather | solution.py:83
  92.8 115.6 %all-gather.8.cloned.1.call-start = ((), (), s32[]{:S(2)}) async-start(), calls=%async_computation.4 | async-start | bytes 5242880 | tf_op jit(solution)/shard_map/all_gather | solution.py:83
  126.7 276.6 %reduce-scatter.3.cloned.1.call-start = ((), (), s32[]{:S(2)}) async-start(), calls=%async_computation.5 | async-start | bytes 10485760 | tf_op jit(solution)/shard_map/reduce_scatter | solution.py:87
  131.4 53.7 %copy-start = (bf16[128,2048]{1,0:T(8,128)(2,1)S(1)}, bf16[128,2048]{1,0:T(8,128)(2,1)}, u32[]{:S(2)}) copy-start(bf16[128,2048]{1,0:T(8,128)(2,1)} %param.8) | copy-start | bytes 1572868
  299.9 1.2 copy-start.4
  299.9 199.8 %reduce-scatter.5.cloned.1.call-start = ((), (), s32[]{:S(2)}) async-start(), calls=%async_computation.6 | async-start | bytes 5242880 | tf_op jit(solution)/shard_map/reduce_scatter | solution.py:87
  499.6 4.6 copy-start.1
  499.6 4.6 copy-start.3
  499.7 5.9 %copy-start.5 = (f32[64,6144]{1,0:T(8,128)S(1)}, f32[64,6144]{1,0:T(8,128)}, u32[]{:S(2)}) copy-start(f32[64,6144]{1,0:T(8,128)} %get-tuple-element.88) | copy-start | bytes 4718596
  504.2 2.6 copy-start.6
  504.2 3.3 copy-start.2
Sparse Core Ops, SparseCore 0:
  9.8 91.2 all-gather.3
  103.0 50.8 all-gather.5
  155.7 52.5 all-gather.7
  300.0 85.7 reduce-scatter.2
  388.6 89.0 reduce-scatter.4

commit v14 on v13

--- a/solution.py
+++ b/solution.py
@@ -1339,7 +1339,7 @@
     )
     down_out, out_grad, in_back_terms, qkv_grad = call(
         [
-            Scatter(parts, block),
+            Scatter(parts, block, cuts=1),
             Exchange(run, (heads, shard, width), second="in"),
         ],
         [

time: 517 us -> 527 us (1.019)
  Pallas kernels: 447 us -> 457 us
    pallas_call x8, Pallas kernels: 447 us -> 457 us  [call(): pl.pallas_call(kernel, out_shape=tuple((job.out for job in jobs)) + tuple...]
  transfers between devices with their start and end apart: 5 -> 5, of which waited for: 1 -> 1; matrix products, arithmetic and copies ran while one was open for 6% -> 6% of each run, Pallas kernels for 69% -> 70%
where the time goes in v14:
time: 527 us; the launch traced here: 526 us
  Pallas kernels  457 us (87%)
  other arithmetic  23 us (4%)
  matrix products  14.7 us (3%)
  between operations  14 us (3%)
  waiting for transfers between devices  11.8 us (2%)
    pallas_call x8, Pallas kernels, call(): pl.pallas_call(kernel, out_shape=tuple((job.out for job in jobs)) + tuple...  457 us
  transfers between devices with their start and end apart: 5, of which 1 were waited for; matrix products, arithmetic and copies ran while one was open for 6% of the time, Pallas kernels for 70%

profile of v14, /device:TPU:9, one launch (start us, length us, event | category | flops | bytes accessed | tf_op | source)
XLA Modules:
  0.0 526.0 jit_solution(6069977124304708718)
XLA Ops:
  8.0 1.2 convert_reduce_fusion
  9.2 1.3 fusion.9
  10.5 2.2 fusion.4.refs_1_
  12.7 80.1 %start.1 = (bf16[4,8,64,768]{3,2,1,0:T(8,128)(2,1)}, bf16[8,128,2048]{2,1,0:T(8,128)(2,1)}, bf16[8,64,1024]{2,1,0:T(8,128)(2,1)}, bf16[4,64,2048]{2,1,0:T(8,128)(2,1)}) custom-call(bf16[64,6144]{1,0:T(8,128)(2,1)} %refs_0_.2, bf16[128,2048]{1,0:T(8,128)(2,1)} %fusion.4.refs_1_, bf16[64,16384]{1,0:T(8,128)(2,1)} %refs_0_.3, bf16[64,2048]{1,0:T(8,128)(2,1)} %refs_3_.1), custom_call_target="tpu_custom_call" | custom-call | bytes 270000000 | tf_op jit(solution)/shard_map/start/pallas_call | solution.py:729
  93.5 1.1 select_subtract_fusion.refs_6_
  94.7 2.9 sine_multiply_fusion
  98.1 28.5 %attend.1 = (bf16[8,64,1024]{2,1,0:T(8,128)(2,1)}, bf16[2,2,64,2048]{3,2,1,0:T(8,128)(2,1)}, bf16[1024,768]{1,0:T(8,128)(2,1)}, bf16[1024,256]{1,0:T(8,128)(2,1)}) custom-call(bf16[64,16384]{1,0:T(8,128)(2,1)} %refs_0_.3, bf16[2,2,64,2048]{3,2,1,0:T(8,128)(2,1)} %bitcast.39, bf16[1024,2048]{1,0:T(8,128)(2,1)} %bitcast.25, bf16[2048,768]{1,0:T(8,128)(2,1)} %bitcast.27, ...), custom_call_target="tpu_custom_call" | custom-call | bytes 120000000 | tf_op jit(solution)/shard_map/attend/pallas_call | solution.py:729
  126.7 4.7 convolution_convert_fusion
  131.4 53.7 %out.1 = (f32[128,2048]{1,0:T(8,128)}, bf16[8,128,2048]{2,1,0:T(8,128)(2,1)}) custom-call(bf16[8,128,2048]{2,1,0:T(8,128)(2,1)} %bitcast.24, bf16[128,2048]{1,0:T(8,128)(2,1)} %refs_1_.1), custom_call_target="tpu_custom_call" | custom-call | bytes 192000000 | tf_op jit(solution)/shard_map/out/pallas_call | solution.py:729
  185.1 1.4 fusion.26
  187.8 10.0 %fusion.29.refs_1_ = f32[1024,1024]{1,0:T(8,128)} fusion(bf16[1024,2048]{1,0:T(8,128)(2,1)} %bitcast.30, bf16[1024,2048]{1,0:T(8,128)(2,1)} %all-gather.4.cloned.1.call-done.refs_2_), kind=kOutput, calls=%fused_computation.60 | convolution fusion | flops 4294967296 | bytes 12582912 | tf_op jit(solution)/shard_map/dot_general | solution.py:71
  197.8 10.5 %all-gather.8.cloned.1.call-done.refs_3_ = bf16[2048,1024]{1,0:T(8,128)(2,1)} async-done(((bf16[512,1024]{1,0:T(8,128)(2,1)}), bf16[2048,1024]{1,0:T(8,128)(2,1)}) %all-gather.8.cloned.1.call-update) | async-done | bytes 4194320 | tf_op jit(solution)/shard_map/all_gather | solution.py:83
  208.3 40.9 %mid.1 = (bf16[8,128,2048]{2,1,0:T(8,128)(2,1)}, bf16[1024,1024]{1,0:T(8,128)(2,1)}, bf16[1024,2048]{1,0:T(8,128)(2,1)}, bf16[1024,2048]{1,0:T(8,128)(2,1)}) custom-call(bf16[128,2048]{1,0:T(8,128)(2,1)} %fusion.10.refs_0_, f32[1024,1024]{1,0:T(8,128)} %fusion.29.refs_1_, bf16[2048,1024]{1,0:T(8,128)(2,1)} %all-gather.6.cloned.1.call-done.refs_2_, ...), custom_call_target="tpu_custom_call" | custom-call | bytes 180000000 | tf_op jit(solution)/shard_map/mid/pallas_call | solution.py:729
  249.2 50.6 %mid_back.1 = (f32[128,2048]{1,0:T(8,128)}, bf16[2048,2048]{1,0:T(8,128)(2,1)}, bf16[1024,2048]{1,0:T(8,128)(2,1)}) custom-call(bf16[8,128,2048]{2,1,0:T(8,128)(2,1)} %bitcast.34, bf16[1024,2048]{1,0:T(8,128)(2,1)} %bitcast.33, bf16[1024,2048]{1,0:T(8,128)(2,1)} %get-tuple-element.47.refs_2_, bf16[1024,1024]{1,0:T(8,128)(2,1)} %get-tuple-element.48.refs_3_.refs_1_, ...), custom_call_target="tpu_custom_call" | custom-call | bytes 150000000 | tf_op jit(solution)/shard_map/mid_back/pallas_call | solution.py:729
  301.4 2.7 fusion.25
  304.1 41.5 %proj_back.1 = (bf16[8,128,2048]{2,1,0:T(8,128)(2,1)}, bf16[1024,2048]{1,0:T(8,128)(2,1)}, bf16[1024,256]{1,0:T(8,128)(2,1)}, bf16[256,2048]{1,0:T(8,128)(2,1)}) custom-call(bf16[128,2048]{1,0:T(8,128)(2,1)} %get-tuple-element.70.refs_0_, bf16[1024,1024]{1,0:T(8,128)(2,1)} %get-tuple-element.48.refs_3_.refs_1_, ...), custom_call_target="tpu_custom_call" | custom-call | bytes 135000000 | tf_op jit(solution)/shard_map/proj_back/pallas_call | solution.py:729
  345.5 64.9 %attend_back.1 = (f32[128,2048]{1,0:T(8,128)}, bf16[2,2,64,2048]{3,2,1,0:T(8,128)(2,1)}, bf16[1024,2048]{1,0:T(8,128)(2,1)}, bf16[2048,768]{1,0:T(8,128)(2,1)}) custom-call(bf16[8,128,2048]{2,1,0:T(8,128)(2,1)} %bitcast.32, bf16[2,2,64,2048]{3,2,1,0:T(8,128)(2,1)} %bitcast.41, bf16[1024,256]{1,0:T(8,128)(2,1)} %get-tuple-element.52.refs_2_, ...), custom_call_target="tpu_custom_call" | custom-call | bytes 180000000 | tf_op jit(solution)/shard_map/attend_back/pallas_call | solution.py:729
  410.4 2.1 add_convert_fusion
  412.6 97.0 %in_back.1 = (f32[128,2048]{1,0:T(8,128)}, f32[64,6144]{1,0:T(8,128)}, f32[64,16384]{1,0:T(8,128)}, f32[64,2048]{1,0:T(8,128)}) custom-call(bf16[8,128,2048]{2,1,0:T(8,128)(2,1)} %bitcast.29, bf16[4,8,64,768]{3,2,1,0:T(8,128)(2,1)} %bitcast.37, bf16[8,64,2048]{2,1,0:T(8,128)(2,1)} %bitcast.38, bf16[4,64,2048]{2,1,0:T(8,128)(2,1)} %bitcast.40), custom_call_target="tpu_custom_call" | custom-call | bytes 270000000 | tf_op jit(solution)/shard_map/in_back/pallas_call | solution.py:729
  509.6 1.7 fusion.23
  511.4 2.8 convert_element_type.43
  514.2 1.4 fusion.8
  515.6 1.1 copy.17
  517.5 2.0 copy.19
  (55 shorter events, 5.8 us)
Async XLA Ops:
  7.2 85.7 %copy-start.8 = (s32[1,2]{1,0:T(1,128)S(1)}, s32[1,2]{1,0:T(1,128)}, u32[]{:S(2)}) copy-start(s32[1,2]{1,0:T(1,128)} %param.13) | copy-start | bytes 28
  7.2 85.9 %copy-start.7 = (s32[1,8]{1,0:T(1,128)S(1)}, s32[1,8]{1,0:T(1,128)}, u32[]{:S(2)}) copy-start(s32[1,8]{1,0:T(1,128)} %param.14) | copy-start | bytes 100
  7.2 180.6 %all-gather.4.cloned.1.call-start = ((), (), s32[]{:S(2)}) async-start(), calls=%async_computation.2 | async-start | bytes 5242880 | tf_op jit(solution)/shard_map/all_gather | solution.py:83
  7.9 189.9 %all-gather.6.cloned.1.call-start = ((), (), s32[]{:S(2)}) async-start(), calls=%async_computation.3 | async-start | bytes 5242880 | tf_op jit(solution)/shard_map/all_gather | solution.py:83
  92.8 115.6 %all-gather.8.cloned.1.call-start = ((), (), s32[]{:S(2)}) async-start(), calls=%async_computation.4 | async-start | bytes 5242880 | tf_op jit(solution)/shard_map/all_gather | solution.py:83
  126.7 285.9 %reduce-scatter.3.cloned.1.call-start = ((), (), s32[]{:S(2)}) async-start(), calls=%async_computation.5 | async-start | bytes 10485760 | tf_op jit(solution)/shard_map/reduce_scatter | solution.py:87
  131.4 53.7 %copy-start = (bf16[128,2048]{1,0:T(8,128)(2,1)S(1)}, bf16[128,2048]{1,0:T(8,128)(2,1)}, u32[]{:S(2)}) copy-start(bf16[128,2048]{1,0:T(8,128)(2,1)} %param.8) | copy-start | bytes 1572868
  299.9 1.2 copy-start.4
  299.9 209.8 %reduce-scatter.5.cloned.1.call-start = ((), (), s32[]{:S(2)}) async-start(), calls=%async_computation.6 | async-start | bytes 5242880 | tf_op jit(solution)/shard_map/reduce_scatter | solution.py:87
  509.6 4.6 copy-start.1
  509.6 4.6 copy-start.3
  509.6 5.9 %copy-start.5 = (f32[64,6144]{1,0:T(8,128)S(1)}, f32[64,6144]{1,0:T(8,128)}, u32[]{:S(2)}) copy-start(f32[64,6144]{1,0:T(8,128)} %get-tuple-element.88) | copy-start | bytes 4718596
  514.1 2.6 copy-start.6
  514.1 3.3 copy-start.2
Sparse Core Ops, SparseCore 0:
  9.8 91.2 all-gather.3
  103.0 50.8 all-gather.5
  155.7 52.5 all-gather.7
  300.0 85.7 reduce-scatter.2
  388.6 74.6 reduce-scatter.4
